TPU v7x, 256 devices: a whole 4x4x8 slice. The times are simulated.
256 devices in a mesh: chan: 8 (over x_hi, y), tm: 32 (over x_lo, z, core).
Axes of the slice: x: 4 (x_hi: 2, x_lo: 2; x = x_hi * 2 + x_lo), y: 4, z: 8, core: 2. Of those that a mesh axis runs over, the one named last changes fastest.
Arguments:
- records: bfloat16 [1408, 1024, 1024], P('tm', 'chan'), may hold values from -2000 to 2000, as said below
Outputs:
- cross_near: float32 [32, 2, 4, 1024, 2, 128], P('tm', None, None, 'chan')
- cross_far: float32 [32, 1024, 2, 128], P('tm', 'chan')
Inputs may be any that keep to these rules, and one draw needn't show every extreme that they name: Raw strain-rate records.
All inputs are finite; a program needn't handle non-finite values.
Results may differ from a plain program's by a relative error of at most 0.009.
Values may be sent and summed in bfloat16 or wider, within the bound.
A program may use at most 128 MiB of HBM per device.

v0:
```python
import math

import jax
import jax.numpy as jnp
from jax import lax
from jax.sharding import PartitionSpec as P

FREQS = 64
FIRST_BIN = 32


EPSILON = 1e-06


def shifted(value, axis, steps):
    count = lax.axis_size(axis)
    pairs = [(source, (source + steps) % count) for source in range(count)]
    return lax.ppermute(value, axis, pairs)


def dft_table(sample_count, frequency_count, first_bin):
    positions = jnp.arange(sample_count, dtype=jnp.int32)
    bin_numbers = jnp.arange(frequency_count, dtype=jnp.int32) + first_bin
    phase_index = bin_numbers[:, None] * positions[None, :] % sample_count
    phase_angle = 2.0 * math.pi / sample_count * phase_index.astype(jnp.float32)
    hann_taper = 0.5 - 0.5 * jnp.cos(2.0 * math.pi / sample_count * positions.astype(jnp.float32))
    cosine = hann_taper[None, :] * jnp.cos(phase_angle)
    sine_part = -hann_taper[None, :] * jnp.sin(phase_angle)
    return (
        jnp.stack([cosine, sine_part], axis=1)
        .reshape(2 * frequency_count, sample_count)
        .astype(jnp.bfloat16)
    )


def whiten(records, taper_table, overall_scale):
    spectra = jnp.einsum("ks,wcs->kwc", taper_table, records, preferred_element_type=jnp.float32)
    mean_square = jnp.mean(spectra * spectra, axis=0)
    factor = overall_scale / jnp.sqrt(mean_square + EPSILON)
    return (spectra * factor[None]).astype(jnp.bfloat16)


def pair_stack(own_blocks, mate_blocks, window_count):
    halves, freq_rows, complex_parts, windows, block_width = own_blocks.shape
    rounds = mate_blocks.shape[0]
    groups = windows // window_count
    negated = jnp.stack([own_blocks[:, :, 1], -own_blocks[:, :, 0]], axis=2)
    row_side = jnp.stack([own_blocks, negated], axis=-1).reshape(
        halves, freq_rows, complex_parts, groups, window_count, 2 * block_width
    )
    column_side = mate_blocks.reshape(
        rounds, halves, freq_rows, complex_parts, groups, window_count, block_width
    )
    partial_value = jnp.einsum(
        "hgpnwi,rhgpnwj->ghrnij", row_side, column_side, preferred_element_type=jnp.float32
    )
    rounded = lax.optimization_barrier(partial_value.astype(jnp.bfloat16)).astype(jnp.float32)
    summed = jnp.sum(rounded, axis=3)
    return summed.reshape(freq_rows, halves, rounds, block_width, 2, block_width)


def find_partners(blocks):
    chan_count = lax.axis_size("chan")
    half_count = chan_count // 2
    picked = []
    for offset in range(1, half_count + 1):
        picked.append(shifted(blocks, "chan", chan_count - offset))
    near_mates = jnp.stack([blocks] + picked[: half_count - 1], axis=0)
    return (near_mates, picked[half_count - 1])


def far_stack(own_blocks, far_partner, window_count):
    lower_half = lax.axis_index("chan") < lax.axis_size("chan") // 2
    first_block = jnp.where(lower_half, own_blocks, far_partner)
    second_block = jnp.where(lower_half, far_partner, own_blocks)
    half_pick = jnp.where(lower_half, 0, 1).astype(jnp.int32)
    first_block = lax.dynamic_slice_in_dim(first_block, half_pick, 1, 0)
    second_block = lax.dynamic_slice_in_dim(second_block, half_pick, 1, 0)
    result = pair_stack(first_block, second_block[None], window_count)
    return result.reshape(result.shape[0], result.shape[3], 2, result.shape[5])


def body(records):
    window_count = records.shape[0]
    time_count = lax.axis_size("tm")
    taper_table = dft_table(records.shape[2], FREQS, FIRST_BIN)
    whitened = whiten(records, taper_table, float(window_count * time_count) ** (-0.25))
    half_freq = FREQS // 2
    blocks = whitened.reshape(2, half_freq, 2, window_count, records.shape[1])
    blocks = lax.all_to_all(blocks, "tm", split_axis=1, concat_axis=3, tiled=True)
    near_mates, far_mate = find_partners(blocks)
    cross_near = pair_stack(blocks, near_mates, window_count)
    cross_far = far_stack(blocks, far_mate, window_count)
    return (cross_near, cross_far)


def solution(mesh):
    return jax.shard_map(
        body,
        mesh=mesh,
        in_specs=(P("tm", "chan", None),),
        out_specs=(P("tm", None, None, "chan", None, None), P("tm", "chan", None, None)),
        check_vma=False,
    )
```

profile of v0, /device:TPU:2, one launch (start us, length us, event | category | flops | bytes accessed | tf_op | source)
XLA Modules:
  0.0 230.8 jit_solution(11211021000394437318)
XLA Ops:
  2.4 6.8 %multiply_reduce_fusion = (f32[44,128]{1,0:T(8,128)S(1)}, f32[128,44,128]{2,0,1:T(8,128)S(1)}) fusion(bf16[128,1024,1]{1,0,2:T(8,128)(2,1)S(1)} %reshape.217, bf16[44,128,1024]{2,1,0:T(8,128)(2,1)} %param.1), kind=kOutput, calls=%fused_computation.17 | convolution fusion | flops 1477831168 | bytes 14702592 | tf_op jit(solution)/shard_map/ks,wcs->kwc/dot_general | solution.py:37
  10.6 47.0 %all_to_all.18 = bf16[2,32,2,44,128]{4,2,3,0,1:T(2,128)(2,1)S(1)} all-to-all(bf16[2,32,2,44,128]{4,2,3,0,1:T(2,128)(2,1)S(1)} %copy.58), channel_id=1, replica_groups=mesh['chan'=8,'tm'=32] {'tm'}, dimensions={1} | all-to-all | bytes 2883584 | tf_op jit(solution)/shard_map/all_to_all | solution.py:90
  58.9 2.2 collective-permute-start.3
  61.1 2.4 %collective-permute-start.2 = (bf16[2,1,2,1408,128]{4,2,3,0,1:T(2,128)(2,1)S(1)}, bf16[2,1,2,1408,128]{4,2,3,0,1:T(2,128)(2,1)}, u32[]{:S(2)}, u32[]{:S(2)}) collective-permute-start(bf16[2,1,2,1408,128]{4,2,3,0,1:T(2,128)(2,1)S(1)} %bitcast.51), channel_id=1, source_target_pairs={{0,160},{32,192},{64,224},{96,0},{128,32},{160,64},{192,96},{224,1... | collective-permute-start | bytes 4325384 | tf_op jit(solution)/shard_map/ppermute | solution.py:18
  63.5 4.5 %collective-permute-start.1 = (bf16[2,1,2,1408,128]{4,2,3,0,1:T(2,128)(2,1)S(1)}, bf16[2,1,2,1408,128]{4,2,3,0,1:T(2,128)(2,1)}, u32[]{:S(2)}, u32[]{:S(2)}) collective-permute-start(bf16[2,1,2,1408,128]{4,2,3,0,1:T(2,128)(2,1)S(1)} %bitcast.52), channel_id=1, source_target_pairs={{0,192},{32,224},{64,0},{96,32},{128,64},{160,96},{192,128},{224,1... | collective-permute-start | bytes 4325384 | tf_op jit(solution)/shard_map/ppermute | solution.py:18
  68.0 1.3 collective-permute-start
  69.3 2.6 %fusion.22 = (bf16[2,1,1,1408,128]{4,2,3,0,1:T(2,128)(2,1)S(1)}, bf16[2,1,1,1408,128]{4,2,3,0,1:T(2,128)(2,1)S(1)}) fusion(bf16[2,1,2,1408,128]{4,2,3,0,1:T(2,128)(2,1)S(1)} %bitcast.54), kind=kLoop, calls=%fused_computation.46 | loop fusion | flops 360448 | bytes 2883584 | tf_op jit(solution)/shard_map/slice | solution.py:47
  72.0 3.3 %maximum_bitcast_fusion.2 = bf16[2,1,2,1408,128,1]{4,2,3,0,5,1:T(2,128)(2,1)S(1)} fusion(bf16[2,1,1,1408,128]{4,2,3,0,1:T(2,128)(2,1)S(1)} %get-tuple-element.9, bf16[2,1,1,1408,128]{4,2,3,0,1:T(2,128)(2,1)S(1)} %get-tuple-element.8), kind=kLoop, calls=%fused_computation.22 | loop fusion | flops 2883584 | bytes 2883584 | tf_op jit(solution)/shard_map/stack | solution.py:48
  75.4 5.3 %pad_maximum_fusion = bf16[2,1,2,1408,128,2]{4,2,3,0,5,1:T(2,128)(2,1)} fusion(bf16[2,1,2,1408,128,1]{4,2,3,0,5,1:T(2,128)(2,1)S(1)} %maximum_bitcast_fusion.2, bf16[2,1,2,1408,128,1]{4,2,3,0,5,1:T(2,128)(2,1)S(1)} %bitcast.55), kind=kLoop, calls=%fused_computation.15 | loop fusion | flops 1441792 | bytes 5767168 | tf_op jit(solution)/shard_map/stack | solution.py:48
  80.7 14.2 %copy.65 = bf16[2,1,2,1408,128,2]{3,5,4,2,0,1:T(2,128)(2,1)} copy(bf16[2,1,2,1408,128,2]{4,2,3,0,5,1:T(2,128)(2,1)} %pad_maximum_fusion) | data formatting | bytes 5767168 | tf_op jit(solution)/shard_map/stack | solution.py:48
  94.9 27.5 %reshape.213 = bf16[2,2,32,44,256]{3,2,4,1,0:T(8,128)(2,1)} reshape(bf16[2,1,2,1408,128,2]{3,5,4,2,0,1:T(2,128)(2,1)} %copy.65) | data formatting | bytes 5767168 | tf_op jit(solution)/shard_map/reshape.3
  122.3 3.0 %broadcast_select_fusion.1 = (bf16[1,1,2,1408,128]{4,2,3,0,1:T(2,128)(2,1)}, bf16[1,1,2,1408,128]{4,2,3,0,1:T(2,128)(2,1)S(1)}) fusion(pred[]{:T(512)S(6)} %lt.14, bf16[2,1,2,1408,128]{4,2,3,0,1:T(2,128)(2,1)S(1)} %bitcast.56, s32[]{:T(128)S(6)} %select_n.41, bf16[2,1,2,1408,128]{4,2,3,0,1:T(2,128)(2,1)} %collective-permute-done.3), kind=kLoop, calls=%fused_computation.25 | loop fusion | flops 720896 | bytes 2883589 | tf_op jit(solution)/shard_map/jit(_where)/select_n | solution.py:75
  126.6 1.7 maximum_bitcast_fusion.3
  128.3 3.0 %pad_maximum_fusion.1 = bf16[1,1,2,1408,128,2]{4,2,3,5,1,0:T(2,128)(2,1)} fusion(bf16[1,1,2,1408,128,1]{4,2,3,5,1,0:T(2,128)(2,1)S(1)} %maximum_bitcast_fusion.3, bf16[1,1,2,1408,128,1]{4,2,3,5,1,0:T(2,128)(2,1)S(1)} %bitcast.57), kind=kLoop, calls=%fused_computation.23 | loop fusion | flops 720896 | bytes 2883584 | tf_op jit(solution)/shard_map/stack | solution.py:48
  131.3 7.7 %copy.68 = bf16[1,1,2,1408,128,2]{3,5,4,2,1,0:T(2,128)(2,1)} copy(bf16[1,1,2,1408,128,2]{4,2,3,5,1,0:T(2,128)(2,1)} %pad_maximum_fusion.1) | data formatting | bytes 2883584 | tf_op jit(solution)/shard_map/stack | solution.py:48
  139.0 2.8 %copy.63 = bf16[1,2,1,2,32,44,128]{6,5,3,0,4,1,2:T(8,128)(2,1)} copy(bf16[1,2,1,2,32,44,128]{6,3,5,4,1,2,0:T(2,128)(2,1)} %bitcast.8) | data formatting | bytes 2883584 | tf_op jit(solution)/shard_map/stack | solution.py:68
  141.8 13.1 %collective-permute-done.1 = bf16[2,1,2,1408,128]{4,2,3,0,1:T(2,128)(2,1)} collective-permute-done((bf16[2,1,2,1408,128]{4,2,3,0,1:T(2,128)(2,1)S(1)}, bf16[2,1,2,1408,128]{4,2,3,0,1:T(2,128)(2,1)}, u32[]{:S(2)}, u32[]{:S(2)}) %collective-permute-start.1) | collective-permute-done | bytes 1441824 | tf_op jit(solution)/shard_map/ppermute | solution.py:18
  155.0 2.7 %copy.62 = bf16[1,2,1,2,32,44,128]{6,5,3,0,4,1,2:T(8,128)(2,1)} copy(bf16[1,2,1,2,32,44,128]{6,3,5,4,1,2,0:T(2,128)(2,1)} %bitcast.7) | data formatting | bytes 2883584 | tf_op jit(solution)/shard_map/stack | solution.py:68
  157.7 26.5 %collective-permute-done = bf16[2,1,2,1408,128]{4,2,3,0,1:T(2,128)(2,1)} collective-permute-done((bf16[2,1,2,1408,128]{4,2,3,0,1:T(2,128)(2,1)S(1)}, bf16[2,1,2,1408,128]{4,2,3,0,1:T(2,128)(2,1)}, u32[]{:S(2)}, u32[]{:S(2)}) %collective-permute-start) | collective-permute-done | bytes 1441824 | tf_op jit(solution)/shard_map/ppermute | solution.py:18
  184.2 2.9 %copy.61 = bf16[1,2,1,2,32,44,128]{6,5,3,0,4,1,2:T(8,128)(2,1)} copy(bf16[1,2,1,2,32,44,128]{6,3,5,4,1,2,0:T(2,128)(2,1)} %bitcast.6) | data formatting | bytes 2883584 | tf_op jit(solution)/shard_map/stack | solution.py:68
  187.1 13.3 %reshape.216 = bf16[2,32,44,256]{2,1,3,0:T(8,128)(2,1)} reshape(bf16[1,1,2,1408,128,2]{3,5,4,2,1,0:T(2,128)(2,1)S(1)} %copy-done) | data formatting | bytes 2883584 | tf_op jit(solution)/shard_map/reshape.12
  200.4 4.7 %fusion.10 = bf16[1,1,1,32,256,128]{4,5,3,2,1,0:T(8,128)(2,1)S(1)} fusion(bf16[2,32,44,256]{2,1,3,0:T(8,128)(2,1)} %reshape.216, bf16[2,32,44,128]{3,0,2,1:T(2,128)(2,1)} %bitcast.62), kind=kOutput, calls=%fused_computation.18 | convolution fusion | flops 185597952 | bytes 4259840 | tf_op jit(solution)/shard_map/hgpnwi,rhgpnwj->ghrnij/dot_general | solution.py:54
  206.1 16.6 %fusion = bf16[1,2,4,32,256,128]{4,5,2,3,1,0:T(8,128)(2,1)} fusion(bf16[2,2,32,44,256,1]{3,2,4,1,0,5:T(8,128)(2,1)} %bitcast.58, bf16[1,2,1,2,32,44,128]{6,5,3,0,4,1,2:T(8,128)(2,1)} %copy.63, bf16[1,2,1,2,32,44,128]{6,5,3,0,4,1,2:T(8,128)(2,1)} %copy.62, bf16[1,2,1,2,32,44,128]{6,5,3,0,4,1,2:T(8,128)(2,1)} %copy.61, ...), kind=kOutput, calls=%fused_computation.2 | convolution fusion | flops 1493434368 | bytes 25427968 | tf_op jit(solution)/shard_map/hgpnwi,rhgpnwj->ghrnij/dot_general | solution.py:54
  222.7 6.8 %convert_reduce_fusion = f32[2,4,256,128]{2,3,1,0:T(8,128)S(1)} fusion(bf16[1,2,4,32,256,128]{4,5,2,3,1,0:T(8,128)(2,1)} %fusion), kind=kLoop, calls=%fused_computation.1 | loop fusion | flops 16515072 | bytes 17825792 | tf_op jit(solution)/shard_map/reduce_sum | solution.py:58
  (19 shorter events, 8.1 us)
Async XLA Ops:
  58.9 63.4 %collective-permute-start.3 = (bf16[2,1,2,1408,128]{4,2,3,0,1:T(2,128)(2,1)S(1)}, bf16[2,1,2,1408,128]{4,2,3,0,1:T(2,128)(2,1)}, u32[]{:S(2)}, u32[]{:S(2)}) collective-permute-start(bf16[2,1,2,1408,128]{4,2,3,0,1:T(2,128)(2,1)S(1)} %bitcast.50), channel_id=1, source_target_pairs={{0,128},{32,160},{64,192},{96,224},{128,0},{160,32},{192,64},{224,... | collective-permute-start | bytes 4325384 | tf_op jit(solution)/shard_map/ppermute | solution.py:18
  61.1 77.9 %collective-permute-start.2 = (bf16[2,1,2,1408,128]{4,2,3,0,1:T(2,128)(2,1)S(1)}, bf16[2,1,2,1408,128]{4,2,3,0,1:T(2,128)(2,1)}, u32[]{:S(2)}, u32[]{:S(2)}) collective-permute-start(bf16[2,1,2,1408,128]{4,2,3,0,1:T(2,128)(2,1)S(1)} %bitcast.51), channel_id=1, source_target_pairs={{0,160},{32,192},{64,224},{96,0},{128,32},{160,64},{192,96},{224,1... | collective-permute-start | bytes 4325384 | tf_op jit(solution)/shard_map/ppermute | solution.py:18
  63.5 91.4 %collective-permute-start.1 = (bf16[2,1,2,1408,128]{4,2,3,0,1:T(2,128)(2,1)S(1)}, bf16[2,1,2,1408,128]{4,2,3,0,1:T(2,128)(2,1)}, u32[]{:S(2)}, u32[]{:S(2)}) collective-permute-start(bf16[2,1,2,1408,128]{4,2,3,0,1:T(2,128)(2,1)S(1)} %bitcast.52), channel_id=1, source_target_pairs={{0,192},{32,224},{64,0},{96,32},{128,64},{160,96},{192,128},{224,1... | collective-permute-start | bytes 4325384 | tf_op jit(solution)/shard_map/ppermute | solution.py:18
  68.0 116.2 %collective-permute-start = (bf16[2,1,2,1408,128]{4,2,3,0,1:T(2,128)(2,1)S(1)}, bf16[2,1,2,1408,128]{4,2,3,0,1:T(2,128)(2,1)}, u32[]{:S(2)}, u32[]{:S(2)}) collective-permute-start(bf16[2,1,2,1408,128]{4,2,3,0,1:T(2,128)(2,1)S(1)} %bitcast.53), channel_id=1, source_target_pairs={{0,224},{32,0},{64,32},{96,64},{128,96},{160,128},{192,160},{224,1... | collective-permute-start | bytes 4325384 | tf_op jit(solution)/shard_map/ppermute | solution.py:18
  184.2 2.9 %copy-start = (bf16[1,1,2,1408,128,2]{3,5,4,2,1,0:T(2,128)(2,1)S(1)}, bf16[1,1,2,1408,128,2]{3,5,4,2,1,0:T(2,128)(2,1)}, u32[]{:S(2)}) copy-start(bf16[1,1,2,1408,128,2]{3,5,4,2,1,0:T(2,128)(2,1)} %copy.68) | copy-start | bytes 4325380
where the time goes:
time: 234 us; the launch traced here: 231 us
  local copies, waits for them, and re-layouts  75.8 us (32%)
  blocking collectives  47 us (20%)
  waiting for transfers between devices  39.7 us (17%)
  other arithmetic  29.1 us (12%)
  matrix products  28 us (12%)
  starting transfers between devices  10.4 us (4%)
    all_to_all x1, blocking collectives, body(): lax.all_to_all(blocks, 'tm', split_axis=1, concat_axis=3, tiled=True)  47 us
    another operation x2, local copies, waits for them, and re-layouts  40.8 us
    ppermute x4, waiting for transfers between devices, shifted(): return lax.ppermute(value, axis, pairs)  39.7 us
    another operation x2, local copies, waits for them, and re-layouts, pair_stack(): jnp.stack([own_blocks, negated], axis=-1)  21.8 us
    dot_general x2, matrix products, pair_stack(): jnp.einsum('hgpnwi,rhgpnwj->ghrnij', row_side, column_side, preferred_ele...  21.3 us
    another operation x4, other arithmetic, pair_stack(): jnp.stack([own_blocks, negated], axis=-1)  13.4 us
    ppermute x4, starting transfers between devices, shifted(): return lax.ppermute(value, axis, pairs)  10.4 us
    another operation x3, local copies, waits for them, and re-layouts, find_partners(): near_mates = jnp.stack([blocks] + picked[:half_count - 1], axis=0)  8.45 us
  transfers between devices with their start and end apart: 4, of which 2 were waited for; matrix products, arithmetic and copies ran while one was open for 33% of the time, Pallas kernels for 0%

commit v1 on v0

v1 whole, which is shorter than its diff:
```python
import functools
import math

import jax
import jax.numpy as jnp
from jax import lax
from jax.experimental import pallas as pl
from jax.experimental.pallas import tpu as pltpu
from jax.sharding import PartitionSpec as P

FREQS = 64
FIRST_BIN = 32
EPSILON = 1e-06
GROUPS_PER_STEP = 8


def shifted(value, axis, steps):
    count = lax.axis_size(axis)
    pairs = [(source, (source + steps) % count) for source in range(count)]
    return lax.ppermute(value, axis, pairs)


def dft_table(sample_count, frequency_count, first_bin):
    positions = jnp.arange(sample_count, dtype=jnp.int32)
    bin_numbers = jnp.arange(frequency_count, dtype=jnp.int32) + first_bin
    phase_index = bin_numbers[:, None] * positions[None, :] % sample_count
    phase_angle = 2.0 * math.pi / sample_count * phase_index.astype(jnp.float32)
    hann_taper = 0.5 - 0.5 * jnp.cos(2.0 * math.pi / sample_count * positions.astype(jnp.float32))
    cosine = hann_taper[None, :] * jnp.cos(phase_angle)
    sine_part = -hann_taper[None, :] * jnp.sin(phase_angle)
    return (
        jnp.stack([cosine, sine_part], axis=1)
        .reshape(2 * frequency_count, sample_count)
        .astype(jnp.bfloat16)
    )


def whiten(records, taper_table, overall_scale):
    spectra = jnp.einsum("ks,wcs->kwc", taper_table, records, preferred_element_type=jnp.float32)
    mean_square = jnp.mean(spectra * spectra, axis=0)
    factor = overall_scale / jnp.sqrt(mean_square + EPSILON)
    return (spectra * factor[None]).astype(jnp.bfloat16)


def row_side(blocks):
    real, imag = blocks[..., 0, :, :], blocks[..., 1, :, :]
    turned = jnp.stack([imag, -real], axis=-3)
    both = jnp.stack([blocks, turned], axis=-4)
    lead = blocks.shape[:-3]
    width, chans = blocks.shape[-2], blocks.shape[-1]
    order = tuple(range(len(lead))) + tuple(len(lead) + d for d in (0, 3, 1, 2))
    return both.transpose(order).reshape(lead + (2 * chans, 2 * width))


def pair_kernel(lhs_ref, rhs_ref, out_ref):
    chans = out_ref.shape[1]

    @pl.when(pl.program_id(1) == 0)
    def _():
        out_ref[...] = jnp.zeros_like(out_ref)

    acc = out_ref[0]
    for group in range(lhs_ref.shape[1]):
        part = jnp.dot(lhs_ref[0, group], rhs_ref[0, group], preferred_element_type=jnp.float32)
        part = part.astype(jnp.bfloat16).astype(jnp.float32)
        acc = acc + jnp.concatenate([part[:chans], part[chans:]], axis=1)
    out_ref[0] = acc


def pair_stack(lhs, rhs):
    halves, groups, rows, depth = lhs.shape
    chans = rhs.shape[-1]
    step = GROUPS_PER_STEP
    return pl.pallas_call(
        pair_kernel,
        out_shape=jax.ShapeDtypeStruct((halves, chans, 2 * chans), jnp.float32),
        grid=(halves, groups // step),
        in_specs=[
            pl.BlockSpec((1, step, rows, depth), lambda h, n: (h, n, 0, 0)),
            pl.BlockSpec((1, step, depth, chans), lambda h, n: (h, n, 0, 0)),
        ],
        out_specs=pl.BlockSpec((1, chans, 2 * chans), lambda h, n: (h, 0, 0)),
        cost_estimate=pl.CostEstimate(
            flops=2 * halves * groups * rows * depth * chans,
            bytes_accessed=2 * halves * groups * depth * (rows + chans) + 4 * halves * chans * 2 * chans,
            transcendentals=0,
        ),
    )(lhs, rhs)


def body(records):
    window_count = records.shape[0]
    chans = records.shape[1]
    time_count = lax.axis_size("tm")
    chan_count = lax.axis_size("chan")
    half_count = chan_count // 2
    taper_table = dft_table(records.shape[2], FREQS, FIRST_BIN)
    whitened = whiten(records, taper_table, float(window_count * time_count) ** (-0.25))
    half_freq = FREQS // 2
    blocks = whitened.reshape(2, half_freq, 2, window_count, chans)
    blocks = lax.all_to_all(blocks, "tm", split_axis=1, concat_axis=1, tiled=True)
    depth = 2 * window_count
    rhs_own = blocks.reshape(2, time_count, depth, chans)
    lhs_own = row_side(blocks)

    lower_half = lax.axis_index("chan") < half_count
    send_half = jnp.where(lower_half, 1, 0).astype(jnp.int32)
    far_send = lax.dynamic_slice_in_dim(blocks, send_half, 1, 0)
    far_recv = shifted(far_send, "chan", -half_count)
    mates = [shifted(rhs_own, "chan", -offset) for offset in range(1, half_count)]

    near = [pair_stack(lhs_own, rhs_own)]
    for mate in mates:
        near.append(pair_stack(lhs_own, mate))
    cross_near = jnp.stack(near, axis=1).reshape(1, 2, half_count, chans, 2, chans)

    far_lhs = jnp.where(lower_half, lhs_own[:1], row_side(far_recv))
    far_rhs = jnp.where(lower_half, far_recv.reshape(1, time_count, depth, chans), rhs_own[1:])
    cross_far = pair_stack(far_lhs, far_rhs).reshape(1, chans, 2, chans)
    return (cross_near, cross_far)


def solution(mesh):
    return jax.shard_map(
        body,
        mesh=mesh,
        in_specs=(P("tm", "chan", None),),
        out_specs=(P("tm", None, None, "chan", None, None), P("tm", "chan", None, None)),
        check_vma=False,
    )
```

time: 234 us -> 235 us (level)
  waiting for transfers between devices: 39.7 us -> 126 us
  blocking collectives: 47 us -> 0 us
  local copies, waits for them, and re-layouts: 75.8 us -> 43.5 us
  Pallas kernels: 0 us -> 30.5 us
  other arithmetic: 29.1 us -> 4.12 us
  matrix products: 28 us -> 6.78 us
  starting transfers between devices: 10.4 us -> 19.3 us
    another operation x7 -> x4, local copies, waits for them, and re-layouts: 71 us -> 4.32 us  [body(): jnp.stack(near, axis=1).reshape(1, 2, half_count, chans, 2, chans)]
    ppermute x4, waiting for transfers between devices: 39.7 us -> 91 us  [shifted(): return lax.ppermute(value, axis, pairs)]
    all_to_all x1 -> x0, blocking collectives: 47 us -> none  [body(): lax.all_to_all(blocks, 'tm', split_axis=1, concat_axis=3, tiled=True)]
    all_to_all x0 -> x1, waiting for transfers between devices: none -> 35 us  [body(): lax.all_to_all(blocks, 'tm', split_axis=1, concat_axis=1, tiled=True)]
    pallas_call x0 -> x5, Pallas kernels: none -> 30.5 us  [pair_stack(): pl.pallas_call(pair_kernel, out_shape=jax.ShapeDtypeStruct((halves, chans...]
    dot_general x2 -> x0, matrix products: 21.3 us -> none  [pair_stack(): jnp.einsum('hgpnwi,rhgpnwj->ghrnij', row_side, column_side, preferred_ele...]
    reshape x1 -> x5, local copies, waits for them, and re-layouts: 0.99 us -> 18.5 us  [the longest x2 13.1 us: row_side(): return both.transpose(order).reshape(lead + (2 * chans, 2 * width))]
    select_n x0 -> x4, local copies, waits for them, and re-layouts: none -> 12.1 us  [the longest x3 11 us: body(): far_lhs = jnp.where(lower_half, lhs_own[:1], row_side(far_recv))]
  transfers between devices with their start and end apart: 4 -> 5, of which waited for: 2 -> 4; matrix products, arithmetic and copies ran while one was open for 33% -> 16% of each run, Pallas kernels for 0% -> 10%
where the time goes in v1:
time: 235 us; the launch traced here: 231 us
  waiting for transfers between devices  126 us (54%)
  local copies, waits for them, and re-layouts  43.5 us (19%)
  Pallas kernels  30.5 us (13%)
  starting transfers between devices  19.3 us (8%)
  matrix products  6.78 us (3%)
  other arithmetic  4.12 us (2%)
    ppermute x4, waiting for transfers between devices, shifted(): return lax.ppermute(value, axis, pairs)  91 us
    all_to_all x1, waiting for transfers between devices, body(): lax.all_to_all(blocks, 'tm', split_axis=1, concat_axis=1, tiled=True)  35 us
    pallas_call x5, Pallas kernels, pair_stack(): pl.pallas_call(pair_kernel, out_shape=jax.ShapeDtypeStruct((halves, chans...  30.5 us
    reshape x2, local copies, waits for them, and re-layouts, row_side(): return both.transpose(order).reshape(lead + (2 * chans, 2 * width))  13.1 us
    select_n x3, local copies, waits for them, and re-layouts, body(): far_lhs = jnp.where(lower_half, lhs_own[:1], row_side(far_recv))  11 us
    all_to_all x1, starting transfers between devices, body(): lax.all_to_all(blocks, 'tm', split_axis=1, concat_axis=1, tiled=True)  10.1 us
    ppermute x4, starting transfers between devices, shifted(): return lax.ppermute(value, axis, pairs)  9.23 us
    dot_general x1, matrix products, whiten(): jnp.einsum('ks,wcs->kwc', taper_table, records, preferred_element_type=jn...  6.78 us
  transfers between devices with their start and end apart: 5, of which 4 were waited for; matrix products, arithmetic and copies ran while one was open for 16% of the time, Pallas kernels for 10%

profile of v1, /device:TPU:2, one launch (start us, length us, event | category | flops | bytes accessed | tf_op | source)
XLA Modules:
  0.0 231.1 jit_solution(5114004747144842373)
XLA Ops:
  2.4 6.8 %multiply_reduce_fusion = (f32[44,128]{1,0:T(8,128)S(1)}, f32[128,44,128]{2,0,1:T(8,128)S(1)}) fusion(bf16[128,1024,1]{1,0,2:T(8,128)(2,1)S(1)} %reshape.241, bf16[44,128,1024]{2,1,0:T(8,128)(2,1)} %param.1), kind=kOutput, calls=%fused_computation.2 | convolution fusion | flops 1477831168 | bytes 14702592 | tf_op jit(solution)/shard_map/ks,wcs->kwc/dot_general | solution.py:39
  9.6 2.1 copy.97
  11.7 10.1 %all-to-all-start = ((bf16[2,32,2,44,128]{4,2,3,0,1:T(2,128)(2,1)}), bf16[2,32,2,44,128]{4,2,3,0,1:T(2,128)(2,1)S(1)}, u32[]{:S(2)}, u32[]{:S(2)}) async-start(bf16[2,32,2,44,128]{4,2,3,0,1:T(2,128)(2,1)} %copy.97), calls=%async_computation | async-start | bytes 2883584 | tf_op jit(solution)/shard_map/all_to_all | solution.py:101
  21.8 35.0 %all-to-all-done = bf16[2,32,2,44,128]{4,2,3,0,1:T(2,128)(2,1)S(1)} async-done(((bf16[2,32,2,44,128]{4,2,3,0,1:T(2,128)(2,1)}), bf16[2,32,2,44,128]{4,2,3,0,1:T(2,128)(2,1)S(1)}, u32[]{:S(2)}, u32[]{:S(2)}) %all-to-all-start) | async-done | bytes 1441824 | tf_op jit(solution)/shard_map/all_to_all | solution.py:101
  57.3 2.2 collective-permute-start.3
  59.5 1.7 copy.104.rhs_ref
  61.2 3.9 %collective-permute-start = (bf16[2,32,88,128]{3,2,1,0:T(8,128)(2,1)}, bf16[2,32,88,128]{3,2,1,0:T(8,128)(2,1)}, u32[]{:S(2)}, u32[]{:S(2)}) collective-permute-start(bf16[2,32,88,128]{3,2,1,0:T(8,128)(2,1)} %copy.104.rhs_ref), channel_id=1, source_target_pairs={{0,224},{32,0},{64,32},{96,64},{128,96},{160,128},{192,160},{224,1... | collective-permute-start | bytes 4325384 | tf_op jit(solution)/shard_map/ppermute | solution.py:20
  65.6 2.5 %collective-permute-start.2 = (bf16[2,32,88,128]{3,2,1,0:T(8,128)(2,1)}, bf16[2,32,88,128]{3,2,1,0:T(8,128)(2,1)}, u32[]{:S(2)}, u32[]{:S(2)}) collective-permute-start(bf16[2,32,88,128]{3,2,1,0:T(8,128)(2,1)} %copy.104.rhs_ref), channel_id=1, source_target_pairs={{0,160},{32,192},{64,224},{96,0},{128,32},{160,64},{192,96},{224,1... | collective-permute-start | bytes 4325384 | tf_op jit(solution)/shard_map/ppermute | solution.py:20
  70.3 4.5 %copy.101 = bf16[2,32,2,128,2,44]{3,2,5,4,1,0:T(2,128)(2,1)} copy(bf16[2,32,2,128,2,44]{3,1,5,4,2,0:T(8,128)(2,1)S(1)} %maximum_bitcast_fusion) | data formatting | bytes 5767168 | tf_op jit(solution)/shard_map/transpose | solution.py:52
  74.9 7.4 %reshape.238 = bf16[2,32,256,88]{2,3,1,0:T(8,128)(2,1)} reshape(bf16[2,32,2,128,2,44]{3,2,5,4,1,0:T(2,128)(2,1)} %copy.101) | data formatting | bytes 5767168 | tf_op jit(solution)/shard_map/reshape | solution.py:52
  82.3 5.7 %copy.103.lhs_ref = bf16[2,32,256,88]{3,2,1,0:T(8,128)(2,1)} copy(bf16[2,32,256,88]{2,3,1,0:T(8,128)(2,1)} %reshape.238) | data formatting | bytes 5767168 | tf_op jit(solution)/shard_map/reshape | solution.py:52
  88.0 6.7 %shard_map.30 = f32[2,128,256]{2,1,0:T(8,128)} custom-call(bf16[2,32,256,88]{3,2,1,0:T(8,128)(2,1)} %copy.103.lhs_ref, bf16[2,32,88,128]{3,2,1,0:T(8,128)(2,1)} %copy.104.rhs_ref), custom_call_target="tpu_custom_call" | custom-call | flops 369098752 | bytes 4587520 | tf_op jit(solution)/shard_map/pallas_call | solution.py:74
  95.9 1.6 copy-done.1
  97.8 2.6 %copy.116 = bf16[1,32,2,128,2,44]{3,2,5,4,1,0:T(2,128)(2,1)} copy(bf16[1,32,2,128,2,44]{3,1,5,4,2,0:T(8,128)(2,1)S(1)} %slice_select_fusion) | data formatting | bytes 2883584 | tf_op jit(solution)/shard_map/jit(_where)/select_n | solution.py:117
  100.4 4.6 %select_n.49 = bf16[1,32,256,88]{2,3,1,0:T(8,128)(2,1)} reshape(bf16[1,32,2,128,2,44]{3,2,5,4,1,0:T(2,128)(2,1)} %copy.116) | data formatting | bytes 2883584 | tf_op jit(solution)/shard_map/jit(_where)/select_n | solution.py:117
  105.0 3.8 %copy.118.lhs_ref = bf16[1,32,256,88]{3,2,1,0:T(8,128)(2,1)} copy(bf16[1,32,256,88]{2,3,1,0:T(8,128)(2,1)} %select_n.49) | data formatting | bytes 2883584 | tf_op jit(solution)/shard_map/jit(_where)/select_n | solution.py:117
  109.9 3.7 %shard_map.34 = f32[1,128,256]{2,1,0:T(8,128)} custom-call(bf16[1,32,256,88]{3,2,1,0:T(8,128)(2,1)} %copy.118.lhs_ref, bf16[1,32,88,128]{3,2,1,0:T(8,128)(2,1)} %copy.119.rhs_ref), custom_call_target="tpu_custom_call" | custom-call | flops 184549376 | bytes 2293760 | tf_op jit(solution)/shard_map/pallas_call | solution.py:74
  113.7 1.6 reshape.240
  115.3 17.3 %collective-permute-done.rhs_ref = bf16[2,32,88,128]{3,2,1,0:T(8,128)(2,1)} collective-permute-done((bf16[2,32,88,128]{3,2,1,0:T(8,128)(2,1)}, bf16[2,32,88,128]{3,2,1,0:T(8,128)(2,1)}, u32[]{:S(2)}, u32[]{:S(2)}) %collective-permute-start) | collective-permute-done | bytes 1441824 | tf_op jit(solution)/shard_map/ppermute | solution.py:20
  132.7 6.7 %shard_map.31 = f32[2,128,256]{2,1,0:T(8,128)} custom-call(bf16[2,32,256,88]{3,2,1,0:T(8,128)(2,1)} %copy.103.lhs_ref, bf16[2,32,88,128]{3,2,1,0:T(8,128)(2,1)} %collective-permute-done.rhs_ref), custom_call_target="tpu_custom_call" | custom-call | flops 369098752 | bytes 4587520 | tf_op jit(solution)/shard_map/pallas_call | solution.py:74
  140.4 49.8 %collective-permute-done.1.rhs_ref = bf16[2,32,88,128]{3,2,1,0:T(8,128)(2,1)} collective-permute-done((bf16[2,32,88,128]{3,2,1,0:T(8,128)(2,1)}, bf16[2,32,88,128]{3,2,1,0:T(8,128)(2,1)}, u32[]{:S(2)}, u32[]{:S(2)}) %collective-permute-start.1) | collective-permute-done | bytes 1441824 | tf_op jit(solution)/shard_map/ppermute | solution.py:20
  190.3 6.7 %shard_map.32 = f32[2,128,256]{2,1,0:T(8,128)} custom-call(bf16[2,32,256,88]{3,2,1,0:T(8,128)(2,1)} %copy.103.lhs_ref, bf16[2,32,88,128]{3,2,1,0:T(8,128)(2,1)} %collective-permute-done.1.rhs_ref), custom_call_target="tpu_custom_call" | custom-call | flops 369098752 | bytes 4587520 | tf_op jit(solution)/shard_map/pallas_call | solution.py:74
  198.0 23.8 %collective-permute-done.2.rhs_ref = bf16[2,32,88,128]{3,2,1,0:T(8,128)(2,1)} collective-permute-done((bf16[2,32,88,128]{3,2,1,0:T(8,128)(2,1)}, bf16[2,32,88,128]{3,2,1,0:T(8,128)(2,1)}, u32[]{:S(2)}, u32[]{:S(2)}) %collective-permute-start.2) | collective-permute-done | bytes 1441824 | tf_op jit(solution)/shard_map/ppermute | solution.py:20
  221.9 6.7 %shard_map.33 = f32[2,128,256]{2,1,0:T(8,128)} custom-call(bf16[2,32,256,88]{3,2,1,0:T(8,128)(2,1)} %copy.103.lhs_ref, bf16[2,32,88,128]{3,2,1,0:T(8,128)(2,1)} %collective-permute-done.2.rhs_ref), custom_call_target="tpu_custom_call" | custom-call | flops 369098752 | bytes 4587520 | tf_op jit(solution)/shard_map/pallas_call | solution.py:74
  (28 shorter events, 12.6 us)
Async XLA Ops:
  11.7 45.1 %all-to-all-start = ((bf16[2,32,2,44,128]{4,2,3,0,1:T(2,128)(2,1)}), bf16[2,32,2,44,128]{4,2,3,0,1:T(2,128)(2,1)S(1)}, u32[]{:S(2)}, u32[]{:S(2)}) async-start(bf16[2,32,2,44,128]{4,2,3,0,1:T(2,128)(2,1)} %copy.97), calls=%async_computation | async-start | bytes 2883584 | tf_op jit(solution)/shard_map/all_to_all | solution.py:101
  57.3 38.5 %collective-permute-start.3 = (bf16[1,32,2,44,128]{4,1,3,2,0:T(8,128)(2,1)S(1)}, bf16[1,32,2,44,128]{4,1,3,2,0:T(8,128)(2,1)S(1)}, u32[]{:S(2)}, u32[]{:S(2)}) collective-permute-start(bf16[1,32,2,44,128]{4,1,3,2,0:T(8,128)(2,1)S(1)} %constant_dynamic-slice_fusion), channel_id=1, source_target_pairs={{0,128},{32,160},{64,192},{96,224},{128,0},{160,32},{192,64},{224,... | collective-permute-start | bytes 2162696 | tf_op jit(solution)/shard_map/ppermute | solution.py:20
  61.2 71.5 %collective-permute-start = (bf16[2,32,88,128]{3,2,1,0:T(8,128)(2,1)}, bf16[2,32,88,128]{3,2,1,0:T(8,128)(2,1)}, u32[]{:S(2)}, u32[]{:S(2)}) collective-permute-start(bf16[2,32,88,128]{3,2,1,0:T(8,128)(2,1)} %copy.104.rhs_ref), channel_id=1, source_target_pairs={{0,224},{32,0},{64,32},{96,64},{128,96},{160,128},{192,160},{224,1... | collective-permute-start | bytes 4325384 | tf_op jit(solution)/shard_map/ppermute | solution.py:20
  65.0 125.3 %collective-permute-start.1 = (bf16[2,32,88,128]{3,2,1,0:T(8,128)(2,1)}, bf16[2,32,88,128]{3,2,1,0:T(8,128)(2,1)}, u32[]{:S(2)}, u32[]{:S(2)}) collective-permute-start(bf16[2,32,88,128]{3,2,1,0:T(8,128)(2,1)} %copy.104.rhs_ref), channel_id=1, source_target_pairs={{0,192},{32,224},{64,0},{96,32},{128,64},{160,96},{192,128},{224,1... | collective-permute-start | bytes 4325384 | tf_op jit(solution)/shard_map/ppermute | solution.py:20
  65.6 156.2 %collective-permute-start.2 = (bf16[2,32,88,128]{3,2,1,0:T(8,128)(2,1)}, bf16[2,32,88,128]{3,2,1,0:T(8,128)(2,1)}, u32[]{:S(2)}, u32[]{:S(2)}) collective-permute-start(bf16[2,32,88,128]{3,2,1,0:T(8,128)(2,1)} %copy.104.rhs_ref), channel_id=1, source_target_pairs={{0,160},{32,192},{64,224},{96,0},{128,32},{160,64},{192,96},{224,1... | collective-permute-start | bytes 4325384 | tf_op jit(solution)/shard_map/ppermute | solution.py:20
  68.7 1.6 copy-start
  95.8 1.8 copy-start.1

commit v2 on v1

--- a/solution.py
+++ b/solution.py
@@ -97,25 +97,31 @@
     taper_table = dft_table(records.shape[2], FREQS, FIRST_BIN)
     whitened = whiten(records, taper_table, float(window_count * time_count) ** (-0.25))
     half_freq = FREQS // 2
-    blocks = whitened.reshape(2, half_freq, 2, window_count, chans)
-    blocks = lax.all_to_all(blocks, "tm", split_axis=1, concat_axis=1, tiled=True)
     depth = 2 * window_count
-    rhs_own = blocks.reshape(2, time_count, depth, chans)
-    lhs_own = row_side(blocks)
+    lower_half = lax.axis_index("chan") < half_count
+    spectra = whitened.reshape(2, half_freq, 2, window_count, chans)
 
-    lower_half = lax.axis_index("chan") < half_count
-    send_half = jnp.where(lower_half, 1, 0).astype(jnp.int32)
-    far_send = lax.dynamic_slice_in_dim(blocks, send_half, 1, 0)
-    far_recv = shifted(far_send, "chan", -half_count)
-    mates = [shifted(rhs_own, "chan", -offset) for offset in range(1, half_count)]
+    near = []
+    own_h = []
+    far_recv = []
+    for half in range(2):
+        blocks = lax.all_to_all(spectra[half], "tm", split_axis=0, concat_axis=0, tiled=True)
+        own_h.append(blocks)
+        rhs = blocks.reshape(1, time_count, depth, chans)
+        lhs = row_side(blocks)[None]
+        if half == 0:
+            pairs = [(s, s - half_count) for s in range(half_count, chan_count)]
+        else:
+            pairs = [(s, s + half_count) for s in range(half_count)]
+        far_recv.append(lax.ppermute(blocks, "chan", pairs))
+        rounds = [pair_stack(lhs, rhs)]
+        for offset in range(1, half_count):
+            rounds.append(pair_stack(lhs, shifted(rhs, "chan", -offset)))
+        near.append(jnp.stack(rounds, axis=1))
+    cross_near = jnp.concatenate(near, axis=0).reshape(1, 2, half_count, chans, 2, chans)
 
-    near = [pair_stack(lhs_own, rhs_own)]
-    for mate in mates:
-        near.append(pair_stack(lhs_own, mate))
-    cross_near = jnp.stack(near, axis=1).reshape(1, 2, half_count, chans, 2, chans)
-
-    far_lhs = jnp.where(lower_half, lhs_own[:1], row_side(far_recv))
-    far_rhs = jnp.where(lower_half, far_recv.reshape(1, time_count, depth, chans), rhs_own[1:])
+    far_lhs = jnp.where(lower_half, row_side(own_h[0]), row_side(far_recv[1]))[None]
+    far_rhs = jnp.where(lower_half, far_recv[0], own_h[1]).reshape(1, time_count, depth, chans)
     cross_far = pair_stack(far_lhs, far_rhs).reshape(1, chans, 2, chans)
     return (cross_near, cross_far)
 

time: 235 us -> 191 us (0.81)
  the two profiles are of different devices: /device:TPU:2 before, /device:TPU:24 now
where the time goes in v2:
time: 191 us; the launch traced here: 190 us
  waiting for transfers between devices  69.7 us (36%)
  Pallas kernels  33.9 us (18%)
  local copies, waits for them, and re-layouts  31 us (16%)
  starting transfers between devices  26.5 us (14%)
  other arithmetic  20.9 us (11%)
  matrix products  6.78 us (4%)
    ppermute x6, waiting for transfers between devices, shifted(): return lax.ppermute(value, axis, pairs)  34 us
    pallas_call x9, Pallas kernels, pair_stack(): pl.pallas_call(pair_kernel, out_shape=jax.ShapeDtypeStruct((halves, chans...  33.9 us
    all_to_all x2, waiting for transfers between devices, body(): lax.all_to_all(spectra[half], 'tm', split_axis=0, concat_axis=0, tiled=True)  30.7 us
    all_to_all x2, starting transfers between devices, body(): lax.all_to_all(spectra[half], 'tm', split_axis=0, concat_axis=0, tiled=True)  13.7 us
    another operation x4, local copies, waits for them, and re-layouts, body(): lhs = row_side(blocks)[None]  10.5 us
    ppermute x6, starting transfers between devices, shifted(): return lax.ppermute(value, axis, pairs)  9.34 us
    dot_general x1, matrix products, whiten(): jnp.einsum('ks,wcs->kwc', taper_table, records, preferred_element_type=jn...  6.78 us
    transpose x3, local copies, waits for them, and re-layouts, row_side(): return both.transpose(order).reshape(lead + (2 * chans, 2 * width))  5.58 us
  transfers between devices with their start and end apart: 10, of which 6 were waited for; matrix products, arithmetic and copies ran while one was open for 20% of the time, Pallas kernels for 16%

profile of v2, /device:TPU:24, one launch (start us, length us, event | category | flops | bytes accessed | tf_op | source)
XLA Modules:
  0.0 189.6 jit_solution(3660222179888585967)
XLA Ops:
  2.4 6.8 %multiply_reduce_fusion = (f32[44,128]{1,0:T(8,128)S(1)}, f32[128,44,128]{2,0,1:T(8,128)S(1)}) fusion(bf16[128,1024,1]{1,0,2:T(8,128)(2,1)S(1)} %reshape.210, bf16[44,128,1024]{2,1,0:T(8,128)(2,1)} %param.1), kind=kOutput, calls=%fused_computation.1 | convolution fusion | flops 1477831168 | bytes 14702592 | tf_op jit(solution)/shard_map/ks,wcs->kwc/dot_general | solution.py:39
  11.0 9.8 %all-to-all-start = ((bf16[32,2,44,128]{3,1,2,0:T(2,128)(2,1)}), bf16[32,2,44,128]{3,1,2,0:T(2,128)(2,1)S(1)}, u32[]{:S(2)}, u32[]{:S(2)}) async-start(bf16[32,2,44,128]{3,1,2,0:T(2,128)(2,1)} %copy.119), calls=%async_computation | async-start | bytes 1441792 | tf_op jit(solution)/shard_map/all_to_all | solution.py:108
  22.2 20.7 %all-to-all-done = bf16[32,2,44,128]{3,1,2,0:T(2,128)(2,1)S(1)} async-done(((bf16[32,2,44,128]{3,1,2,0:T(2,128)(2,1)}), bf16[32,2,44,128]{3,1,2,0:T(2,128)(2,1)S(1)}, u32[]{:S(2)}, u32[]{:S(2)}) %all-to-all-start) | async-done | bytes 720928 | tf_op jit(solution)/shard_map/all_to_all | solution.py:108
  42.9 3.9 %all-to-all-start.1 = ((bf16[32,2,44,128]{3,1,2,0:T(2,128)(2,1)}), bf16[32,2,44,128]{3,1,2,0:T(2,128)(2,1)S(1)}, u32[]{:S(2)}, u32[]{:S(2)}) async-start(bf16[32,2,44,128]{3,1,2,0:T(2,128)(2,1)} %copy.130), calls=%async_computation.1 | async-start | bytes 1441792 | tf_op jit(solution)/shard_map/all_to_all | solution.py:108
  49.6 7.1 %collective-permute-start.1 = (bf16[1,32,88,128]{3,2,1,0:T(8,128)(2,1)}, bf16[1,32,88,128]{3,2,1,0:T(8,128)(2,1)}, u32[]{:S(2)}, u32[]{:S(2)}) collective-permute-start(bf16[1,32,88,128]{3,2,1,0:T(8,128)(2,1)} %copy.123.rhs_ref), channel_id=1, source_target_pairs={{0,192},{32,224},{64,0},{96,32},{128,64},{160,96},{192,128},{224,1... | collective-permute-start | bytes 2162696 | tf_op jit(solution)/shard_map/ppermute | solution.py:20
  58.8 10.0 %all-to-all-done.1 = bf16[32,2,44,128]{3,1,2,0:T(2,128)(2,1)S(1)} async-done(((bf16[32,2,44,128]{3,1,2,0:T(2,128)(2,1)}), bf16[32,2,44,128]{3,1,2,0:T(2,128)(2,1)S(1)}, u32[]{:S(2)}, u32[]{:S(2)}) %all-to-all-start.1) | async-done | bytes 720928 | tf_op jit(solution)/shard_map/all_to_all | solution.py:108
  70.1 5.0 %collective-permute-done.7 = bf16[32,2,44,128]{3,0,2,1:T(8,128)(2,1)} collective-permute-done((bf16[32,2,44,128]{3,0,2,1:T(8,128)(2,1)S(1)}, bf16[32,2,44,128]{3,0,2,1:T(8,128)(2,1)}, u32[]{:S(2)}, u32[]{:S(2)}) %collective-permute-start.7) | collective-permute-done | bytes 720928 | tf_op jit(solution)/shard_map/ppermute | solution.py:116
  83.1 8.2 %collective-permute-done.2.rhs_ref = bf16[1,32,88,128]{3,2,1,0:T(8,128)(2,1)} collective-permute-done((bf16[1,32,88,128]{3,2,1,0:T(8,128)(2,1)}, bf16[1,32,88,128]{3,2,1,0:T(8,128)(2,1)}, u32[]{:S(2)}, u32[]{:S(2)}) %collective-permute-start.2) | collective-permute-done | bytes 720928 | tf_op jit(solution)/shard_map/ppermute | solution.py:20
  91.7 16.5 %collective-permute-done.1.rhs_ref = bf16[1,32,88,128]{3,2,1,0:T(8,128)(2,1)} collective-permute-done((bf16[1,32,88,128]{3,2,1,0:T(8,128)(2,1)}, bf16[1,32,88,128]{3,2,1,0:T(8,128)(2,1)}, u32[]{:S(2)}, u32[]{:S(2)}) %collective-permute-start.1) | collective-permute-done | bytes 720928 | tf_op jit(solution)/shard_map/ppermute | solution.py:20
  112.4 2.6 %copy.131 = bf16[32,2,128,2,44]{2,1,4,3,0:T(2,128)(2,1)} copy(bf16[32,2,128,2,44]{2,3,4,0,1:T(2,128)(2,1)S(1)} %maximum_bitcast_fusion.1) | data formatting | bytes 2883584 | tf_op jit(solution)/shard_map/transpose | solution.py:52
  115.0 3.6 %broadcast_in_dim_reshape.7 = bf16[1,32,256,88]{2,3,1,0:T(8,128)(2,1)S(1)} reshape(bf16[32,2,128,2,44]{2,1,4,3,0:T(2,128)(2,1)} %copy.131) | data formatting | bytes 2883584 | tf_op jit(solution)/shard_map/broadcast_in_dim;reshape | solution.py:111
  118.7 2.9 %copy.133.lhs_ref = bf16[1,32,256,88]{3,2,1,0:T(8,128)(2,1)} copy(bf16[1,32,256,88]{2,3,1,0:T(8,128)(2,1)S(1)} %broadcast_in_dim_reshape.7) | data formatting | bytes 2883584 | tf_op jit(solution)/shard_map/broadcast_in_dim;reshape | solution.py:111
  128.7 2.9 %copy.122.lhs_ref = bf16[1,32,256,88]{3,2,1,0:T(8,128)(2,1)} copy(bf16[1,32,256,88]{2,3,1,0:T(8,128)(2,1)S(1)} %broadcast_in_dim_reshape.6) | data formatting | bytes 2883584 | tf_op jit(solution)/shard_map/broadcast_in_dim;reshape | solution.py:111
  131.7 3.8 %shard_map.30 = f32[1,128,256]{2,1,0:T(8,128)} custom-call(bf16[1,32,256,88]{3,2,1,0:T(8,128)(2,1)} %copy.122.lhs_ref, bf16[1,32,88,128]{3,2,1,0:T(8,128)(2,1)} %copy.123.rhs_ref), custom_call_target="tpu_custom_call" | custom-call | flops 184549376 | bytes 2293760 | tf_op jit(solution)/shard_map/pallas_call | solution.py:74
  136.6 3.8 %shard_map.34 = f32[1,128,256]{2,1,0:T(8,128)} custom-call(bf16[1,32,256,88]{3,2,1,0:T(8,128)(2,1)} %copy.133.lhs_ref, bf16[1,32,88,128]{3,2,1,0:T(8,128)(2,1)} %copy.134.rhs_ref), custom_call_target="tpu_custom_call" | custom-call | flops 184549376 | bytes 2293760 | tf_op jit(solution)/shard_map/pallas_call | solution.py:74
  140.4 3.8 %shard_map.33 = f32[1,128,256]{2,1,0:T(8,128)} custom-call(bf16[1,32,256,88]{3,2,1,0:T(8,128)(2,1)} %copy.122.lhs_ref, bf16[1,32,88,128]{3,2,1,0:T(8,128)(2,1)} %collective-permute-done.2.rhs_ref), custom_call_target="tpu_custom_call" | custom-call | flops 184549376 | bytes 2293760 | tf_op jit(solution)/shard_map/pallas_call | solution.py:74
  144.2 3.7 %shard_map.32 = f32[1,128,256]{2,1,0:T(8,128)} custom-call(bf16[1,32,256,88]{3,2,1,0:T(8,128)(2,1)} %copy.122.lhs_ref, bf16[1,32,88,128]{3,2,1,0:T(8,128)(2,1)} %collective-permute-done.1.rhs_ref), custom_call_target="tpu_custom_call" | custom-call | flops 184549376 | bytes 2293760 | tf_op jit(solution)/shard_map/pallas_call | solution.py:74
  147.9 3.8 %shard_map.31 = f32[1,128,256]{2,1,0:T(8,128)} custom-call(bf16[1,32,256,88]{3,2,1,0:T(8,128)(2,1)} %copy.122.lhs_ref, bf16[1,32,88,128]{3,2,1,0:T(8,128)(2,1)} %collective-permute-done.rhs_ref), custom_call_target="tpu_custom_call" | custom-call | flops 184549376 | bytes 2293760 | tf_op jit(solution)/shard_map/pallas_call | solution.py:74
  151.7 3.8 %shard_map.37 = f32[1,128,256]{2,1,0:T(8,128)} custom-call(bf16[1,32,256,88]{3,2,1,0:T(8,128)(2,1)} %copy.133.lhs_ref, bf16[1,32,88,128]{3,2,1,0:T(8,128)(2,1)} %collective-permute-done.5.rhs_ref), custom_call_target="tpu_custom_call" | custom-call | flops 184549376 | bytes 2293760 | tf_op jit(solution)/shard_map/pallas_call | solution.py:74
  155.4 3.8 %shard_map.36 = f32[1,128,256]{2,1,0:T(8,128)} custom-call(bf16[1,32,256,88]{3,2,1,0:T(8,128)(2,1)} %copy.133.lhs_ref, bf16[1,32,88,128]{3,2,1,0:T(8,128)(2,1)} %collective-permute-done.4.rhs_ref), custom_call_target="tpu_custom_call" | custom-call | flops 184549376 | bytes 2293760 | tf_op jit(solution)/shard_map/pallas_call | solution.py:74
  159.3 9.3 %collective-permute-done.3.rhs_ref = bf16[1,32,88,128]{3,2,1,0:T(8,128)(2,1)} collective-permute-done((bf16[1,32,88,128]{3,2,1,0:T(8,128)(2,1)}, bf16[1,32,88,128]{3,2,1,0:T(8,128)(2,1)}, u32[]{:S(2)}, u32[]{:S(2)}) %collective-permute-start.3) | collective-permute-done | bytes 720928 | tf_op jit(solution)/shard_map/ppermute | solution.py:20
  168.6 3.8 %shard_map.35 = f32[1,128,256]{2,1,0:T(8,128)} custom-call(bf16[1,32,256,88]{3,2,1,0:T(8,128)(2,1)} %copy.133.lhs_ref, bf16[1,32,88,128]{3,2,1,0:T(8,128)(2,1)} %collective-permute-done.3.rhs_ref), custom_call_target="tpu_custom_call" | custom-call | flops 184549376 | bytes 2293760 | tf_op jit(solution)/shard_map/pallas_call | solution.py:74
  179.8 2.9 %copy.144 = bf16[1,32,256,88]{3,2,1,0:T(8,128)(2,1)} copy(bf16[1,32,256,88]{2,3,1,0:T(8,128)(2,1)S(1)} %reshape.207) | data formatting | bytes 2883584 | tf_op jit(solution)/shard_map/reshape | solution.py:52
  184.3 3.8 %shard_map.38 = f32[1,128,256]{2,1,0:T(8,128)} custom-call(bf16[1,32,256,88]{3,2,1,0:T(8,128)(2,1)} %broadcast_select_fusion.lhs_ref, bf16[1,32,88,128]{3,2,1,0:T(8,128)(2,1)} %copy.147.rhs_ref), custom_call_target="tpu_custom_call" | custom-call | flops 184549376 | bytes 2293760 | tf_op jit(solution)/shard_map/pallas_call | solution.py:74
  (62 shorter events, 42.6 us)
Async XLA Ops:
  11.0 31.8 %all-to-all-start = ((bf16[32,2,44,128]{3,1,2,0:T(2,128)(2,1)}), bf16[32,2,44,128]{3,1,2,0:T(2,128)(2,1)S(1)}, u32[]{:S(2)}, u32[]{:S(2)}) async-start(bf16[32,2,44,128]{3,1,2,0:T(2,128)(2,1)} %copy.119), calls=%async_computation | async-start | bytes 1441792 | tf_op jit(solution)/shard_map/all_to_all | solution.py:108
  42.9 25.9 %all-to-all-start.1 = ((bf16[32,2,44,128]{3,1,2,0:T(2,128)(2,1)}), bf16[32,2,44,128]{3,1,2,0:T(2,128)(2,1)S(1)}, u32[]{:S(2)}, u32[]{:S(2)}) async-start(bf16[32,2,44,128]{3,1,2,0:T(2,128)(2,1)} %copy.130), calls=%async_computation.1 | async-start | bytes 1441792 | tf_op jit(solution)/shard_map/all_to_all | solution.py:108
  46.9 28.3 %collective-permute-start.7 = (bf16[32,2,44,128]{3,0,2,1:T(8,128)(2,1)S(1)}, bf16[32,2,44,128]{3,0,2,1:T(8,128)(2,1)}, u32[]{:S(2)}, u32[]{:S(2)}) collective-permute-start(bf16[32,2,44,128]{3,0,2,1:T(8,128)(2,1)S(1)} %copy.121), channel_id=1, source_target_pairs={{128,0},{160,32},{192,64},{224,96},{129,1},{161,33},{193,65},{225,... | collective-permute-start | bytes 2162696 | tf_op jit(solution)/shard_map/ppermute | solution.py:116
  49.4 41.9 %collective-permute-start.2 = (bf16[1,32,88,128]{3,2,1,0:T(8,128)(2,1)}, bf16[1,32,88,128]{3,2,1,0:T(8,128)(2,1)}, u32[]{:S(2)}, u32[]{:S(2)}) collective-permute-start(bf16[1,32,88,128]{3,2,1,0:T(8,128)(2,1)} %copy.123.rhs_ref), channel_id=1, source_target_pairs={{0,160},{32,192},{64,224},{96,0},{128,32},{160,64},{192,96},{224,1... | collective-permute-start | bytes 2162696 | tf_op jit(solution)/shard_map/ppermute | solution.py:20
  49.6 58.6 %collective-permute-start.1 = (bf16[1,32,88,128]{3,2,1,0:T(8,128)(2,1)}, bf16[1,32,88,128]{3,2,1,0:T(8,128)(2,1)}, u32[]{:S(2)}, u32[]{:S(2)}) collective-permute-start(bf16[1,32,88,128]{3,2,1,0:T(8,128)(2,1)} %copy.123.rhs_ref), channel_id=1, source_target_pairs={{0,192},{32,224},{64,0},{96,32},{128,64},{160,96},{192,128},{224,1... | collective-permute-start | bytes 2162696 | tf_op jit(solution)/shard_map/ppermute | solution.py:20
  56.6 91.3 %collective-permute-start = (bf16[1,32,88,128]{3,2,1,0:T(8,128)(2,1)}, bf16[1,32,88,128]{3,2,1,0:T(8,128)(2,1)}, u32[]{:S(2)}, u32[]{:S(2)}) collective-permute-start(bf16[1,32,88,128]{3,2,1,0:T(8,128)(2,1)} %copy.123.rhs_ref), channel_id=1, source_target_pairs={{0,224},{32,0},{64,32},{96,64},{128,96},{160,128},{192,160},{224,1... | collective-permute-start | bytes 2162696 | tf_op jit(solution)/shard_map/ppermute | solution.py:20
  79.8 71.9 %collective-permute-start.5 = (bf16[1,32,88,128]{3,2,1,0:T(8,128)(2,1)}, bf16[1,32,88,128]{3,2,1,0:T(8,128)(2,1)}, u32[]{:S(2)}, u32[]{:S(2)}) collective-permute-start(bf16[1,32,88,128]{3,2,1,0:T(8,128)(2,1)} %copy.134.rhs_ref), channel_id=1, source_target_pairs={{0,160},{32,192},{64,224},{96,0},{128,32},{160,64},{192,96},{224,1... | collective-permute-start | bytes 2162696 | tf_op jit(solution)/shard_map/ppermute | solution.py:20
  80.4 75.0 %collective-permute-start.4 = (bf16[1,32,88,128]{3,2,1,0:T(8,128)(2,1)}, bf16[1,32,88,128]{3,2,1,0:T(8,128)(2,1)}, u32[]{:S(2)}, u32[]{:S(2)}) collective-permute-start(bf16[1,32,88,128]{3,2,1,0:T(8,128)(2,1)} %copy.134.rhs_ref), channel_id=1, source_target_pairs={{0,192},{32,224},{64,0},{96,32},{128,64},{160,96},{192,128},{224,1... | collective-permute-start | bytes 2162696 | tf_op jit(solution)/shard_map/ppermute | solution.py:20
  91.2 77.3 %collective-permute-start.3 = (bf16[1,32,88,128]{3,2,1,0:T(8,128)(2,1)}, bf16[1,32,88,128]{3,2,1,0:T(8,128)(2,1)}, u32[]{:S(2)}, u32[]{:S(2)}) collective-permute-start(bf16[1,32,88,128]{3,2,1,0:T(8,128)(2,1)} %copy.134.rhs_ref), channel_id=1, source_target_pairs={{0,224},{32,0},{64,32},{96,64},{128,96},{160,128},{192,160},{224,1... | collective-permute-start | bytes 2162696 | tf_op jit(solution)/shard_map/ppermute | solution.py:20
  108.2 66.6 %collective-permute-start.6 = (bf16[32,2,44,128]{3,0,2,1:T(8,128)(2,1)}, bf16[32,2,44,128]{3,0,2,1:T(8,128)(2,1)}, u32[]{:S(2)}, u32[]{:S(2)}) collective-permute-start(bf16[32,2,44,128]{3,0,2,1:T(8,128)(2,1)} %get-tuple-element.5), channel_id=1, source_target_pairs={{0,128},{32,160},{64,192},{96,224},{1,129},{33,161},{65,193},{97,2... | collective-permute-start | bytes 2162696 | tf_op jit(solution)/shard_map/ppermute | solution.py:116
  131.7 3.8 %copy-start.1 = (bf16[32,2,44,128]{3,0,2,1:T(8,128)(2,1)S(1)}, bf16[32,2,44,128]{3,0,2,1:T(8,128)(2,1)}, u32[]{:S(2)}) copy-start(bf16[32,2,44,128]{3,0,2,1:T(8,128)(2,1)} %get-tuple-element.4) | copy-start | bytes 2162692
  159.2 13.1 %copy-start.2 = (f32[1,128,256]{2,1,0:T(8,128)S(1)}, f32[1,128,256]{2,1,0:T(8,128)}, u32[]{:S(2)}) copy-start(f32[1,128,256]{2,1,0:T(8,128)} %shard_map.30) | copy-start | bytes 393220
  159.2 13.1 %copy-start.3 = (f32[1,128,256]{2,1,0:T(8,128)S(1)}, f32[1,128,256]{2,1,0:T(8,128)}, u32[]{:S(2)}) copy-start(f32[1,128,256]{2,1,0:T(8,128)} %shard_map.34) | copy-start | bytes 393220
  159.2 13.1 %copy-start.4 = (f32[1,128,256]{2,1,0:T(8,128)S(1)}, f32[1,128,256]{2,1,0:T(8,128)}, u32[]{:S(2)}) copy-start(f32[1,128,256]{2,1,0:T(8,128)} %shard_map.33) | copy-start | bytes 393220
  159.2 13.1 %copy-start.5 = (f32[1,128,256]{2,1,0:T(8,128)S(1)}, f32[1,128,256]{2,1,0:T(8,128)}, u32[]{:S(2)}) copy-start(f32[1,128,256]{2,1,0:T(8,128)} %shard_map.32) | copy-start | bytes 393220
  159.2 13.1 %copy-start.6 = (f32[1,128,256]{2,1,0:T(8,128)S(1)}, f32[1,128,256]{2,1,0:T(8,128)}, u32[]{:S(2)}) copy-start(f32[1,128,256]{2,1,0:T(8,128)} %shard_map.31) | copy-start | bytes 393220
  159.2 13.1 %copy-start.7 = (f32[1,128,256]{2,1,0:T(8,128)S(1)}, f32[1,128,256]{2,1,0:T(8,128)}, u32[]{:S(2)}) copy-start(f32[1,128,256]{2,1,0:T(8,128)} %shard_map.37) | copy-start | bytes 393220
  159.3 13.1 %copy-start.8 = (f32[1,128,256]{2,1,0:T(8,128)S(1)}, f32[1,128,256]{2,1,0:T(8,128)}, u32[]{:S(2)}) copy-start(f32[1,128,256]{2,1,0:T(8,128)} %shard_map.36) | copy-start | bytes 393220
  179.8 2.9 %copy-start = (bf16[1,32,256,88]{3,2,1,0:T(8,128)(2,1)S(1)}, bf16[1,32,256,88]{3,2,1,0:T(8,128)(2,1)}, u32[]{:S(2)}) copy-start(bf16[1,32,256,88]{3,2,1,0:T(8,128)(2,1)} %copy.122.lhs_ref) | copy-start | bytes 4325380

commit v3 on v2

--- a/solution.py
+++ b/solution.py
@@ -11,7 +11,7 @@
 FREQS = 64
 FIRST_BIN = 32
 EPSILON = 1e-06
-GROUPS_PER_STEP = 8
+GROUPS_PER_STEP = 16
 
 
 def shifted(value, axis, steps):
@@ -59,12 +59,12 @@
     def _():
         out_ref[...] = jnp.zeros_like(out_ref)
 
-    acc = out_ref[0]
-    for group in range(lhs_ref.shape[1]):
+    def one_group(group, acc):
         part = jnp.dot(lhs_ref[0, group], rhs_ref[0, group], preferred_element_type=jnp.float32)
         part = part.astype(jnp.bfloat16).astype(jnp.float32)
-        acc = acc + jnp.concatenate([part[:chans], part[chans:]], axis=1)
-    out_ref[0] = acc
+        return acc + jnp.concatenate([part[:chans], part[chans:]], axis=1)
+
+    out_ref[0] = lax.fori_loop(0, lhs_ref.shape[1], one_group, out_ref[0], unroll=2)
 
 
 def pair_stack(lhs, rhs):
@@ -104,11 +104,13 @@
     near = []
     own_h = []
     far_recv = []
+    lhs_halves = []
     for half in range(2):
         blocks = lax.all_to_all(spectra[half], "tm", split_axis=0, concat_axis=0, tiled=True)
         own_h.append(blocks)
         rhs = blocks.reshape(1, time_count, depth, chans)
         lhs = row_side(blocks)[None]
+        lhs_halves.append(lhs)
         if half == 0:
             pairs = [(s, s - half_count) for s in range(half_count, chan_count)]
         else:
@@ -120,9 +122,11 @@
         near.append(jnp.stack(rounds, axis=1))
     cross_near = jnp.concatenate(near, axis=0).reshape(1, 2, half_count, chans, 2, chans)
 
-    far_lhs = jnp.where(lower_half, row_side(own_h[0]), row_side(far_recv[1]))[None]
-    far_rhs = jnp.where(lower_half, far_recv[0], own_h[1]).reshape(1, time_count, depth, chans)
-    cross_far = pair_stack(far_lhs, far_rhs).reshape(1, chans, 2, chans)
+    far_lhs = jnp.where(lower_half, lhs_halves[0], lhs_halves[1])
+    far_rhs = jnp.where(lower_half, far_recv[0], far_recv[1]).reshape(1, time_count, depth, chans)
+    product = pair_stack(far_lhs, far_rhs).reshape(chans, 2, chans)
+    turned = product.transpose(2, 1, 0) * jnp.array([1.0, -1.0], jnp.float32)[None, :, None]
+    cross_far = jnp.where(lower_half, product, turned).reshape(1, chans, 2, chans)
     return (cross_near, cross_far)
 
 

time: 191 us -> 186 us (0.974)
  the two profiles are of different devices: /device:TPU:24 before, /device:TPU:2 now
where the time goes in v3:
time: 186 us
  waiting for transfers between devices  47 us (25%)
  Pallas kernels  43.6 us (23%)
  starting transfers between devices  40 us (22%)
  local copies, waits for them, and re-layouts  31.7 us (17%)
  other arithmetic  15.5 us (8%)
  matrix products  6.78 us (4%)
    pallas_call x9, Pallas kernels, pair_stack(): pl.pallas_call(pair_kernel, out_shape=jax.ShapeDtypeStruct((halves, chans...  43.6 us
    all_to_all x2, waiting for transfers between devices, body(): lax.all_to_all(spectra[half], 'tm', split_axis=0, concat_axis=0, tiled=True)  30.1 us
    ppermute x6, waiting for transfers between devices, shifted(): return lax.ppermute(value, axis, pairs)  16.9 us
    ppermute x6, starting transfers between devices, shifted(): return lax.ppermute(value, axis, pairs)  16.6 us
    all_to_all x2, starting transfers between devices, body(): lax.all_to_all(spectra[half], 'tm', split_axis=0, concat_axis=0, tiled=True)  14.9 us
    another operation x4, local copies, waits for them, and re-layouts, body(): lhs = row_side(blocks)[None]  13.2 us
    ppermute x2, starting transfers between devices, body(): far_recv.append(lax.ppermute(blocks, 'chan', pairs))  8.53 us
    dot_general x1, matrix products, whiten(): jnp.einsum('ks,wcs->kwc', taper_table, records, preferred_element_type=jn...  6.78 us
  transfers between devices with their start and end apart: 10, of which 4 were waited for; matrix products, arithmetic and copies ran while one was open for 21% of the time, Pallas kernels for 21%

profile of v3, /device:TPU:2, one launch (start us, length us, event | category | flops | bytes accessed | tf_op | source)
XLA Modules:
  0.0 185.6 jit_solution(18055401138094155949)
XLA Ops:
  2.4 6.8 %multiply_reduce_fusion = (f32[44,128]{1,0:T(8,128)S(1)}, f32[128,44,128]{2,0,1:T(8,128)S(1)}) fusion(bf16[128,1024,1]{1,0,2:T(8,128)(2,1)S(1)} %reshape.213, bf16[44,128,1024]{2,1,0:T(8,128)(2,1)} %param.2), kind=kOutput, calls=%fused_computation.1 | convolution fusion | flops 1477831168 | bytes 14702592 | tf_op jit(solution)/shard_map/ks,wcs->kwc/dot_general | solution.py:39
  11.0 10.1 %all-to-all-start.1 = ((bf16[32,2,44,128]{3,1,2,0:T(2,128)(2,1)}), bf16[32,2,44,128]{3,1,2,0:T(2,128)(2,1)S(1)}, u32[]{:S(2)}, u32[]{:S(2)}) async-start(bf16[32,2,44,128]{3,1,2,0:T(2,128)(2,1)} %copy.131), calls=%async_computation.1 | async-start | bytes 1441792 | tf_op jit(solution)/shard_map/all_to_all | solution.py:109
  22.5 19.8 %all-to-all-done.1 = bf16[32,2,44,128]{3,1,2,0:T(2,128)(2,1)S(1)} async-done(((bf16[32,2,44,128]{3,1,2,0:T(2,128)(2,1)}), bf16[32,2,44,128]{3,1,2,0:T(2,128)(2,1)S(1)}, u32[]{:S(2)}, u32[]{:S(2)}) %all-to-all-start.1) | async-done | bytes 720928 | tf_op jit(solution)/shard_map/all_to_all | solution.py:109
  42.2 4.8 %all-to-all-start = ((bf16[32,2,44,128]{3,1,2,0:T(2,128)(2,1)}), bf16[32,2,44,128]{3,1,2,0:T(2,128)(2,1)S(1)}, u32[]{:S(2)}, u32[]{:S(2)}) async-start(bf16[32,2,44,128]{3,1,2,0:T(2,128)(2,1)} %copy.120), calls=%async_computation | async-start | bytes 1441792 | tf_op jit(solution)/shard_map/all_to_all | solution.py:109
  49.4 3.2 %collective-permute-start.5 = (bf16[1,32,88,128]{3,2,1,0:T(8,128)(2,1)S(1)}, bf16[1,32,88,128]{3,2,1,0:T(8,128)(2,1)S(1)}, u32[]{:S(2)}, u32[]{:S(2)}) collective-permute-start(bf16[1,32,88,128]{3,2,1,0:T(8,128)(2,1)S(1)} %copy.135.rhs_ref), channel_id=1, source_target_pairs={{0,160},{32,192},{64,224},{96,0},{128,32},{160,64},{192,96},{224,1... | collective-permute-start | bytes 2162696 | tf_op jit(solution)/shard_map/ppermute | solution.py:20
  52.7 3.7 %collective-permute-start.4 = (bf16[1,32,88,128]{3,2,1,0:T(8,128)(2,1)S(1)}, bf16[1,32,88,128]{3,2,1,0:T(8,128)(2,1)}, u32[]{:S(2)}, u32[]{:S(2)}) collective-permute-start(bf16[1,32,88,128]{3,2,1,0:T(8,128)(2,1)S(1)} %copy.135.rhs_ref), channel_id=1, source_target_pairs={{0,192},{32,224},{64,0},{96,32},{128,64},{160,96},{192,128},{224,1... | collective-permute-start | bytes 2162696 | tf_op jit(solution)/shard_map/ppermute | solution.py:20
  57.8 10.4 %all-to-all-done = bf16[32,2,44,128]{3,1,2,0:T(2,128)(2,1)S(1)} async-done(((bf16[32,2,44,128]{3,1,2,0:T(2,128)(2,1)}), bf16[32,2,44,128]{3,1,2,0:T(2,128)(2,1)S(1)}, u32[]{:S(2)}, u32[]{:S(2)}) %all-to-all-start) | async-done | bytes 720928 | tf_op jit(solution)/shard_map/all_to_all | solution.py:109
  71.4 3.1 %collective-permute-start.2 = (bf16[1,32,88,128]{3,2,1,0:T(8,128)(2,1)}, bf16[1,32,88,128]{3,2,1,0:T(8,128)(2,1)}, u32[]{:S(2)}, u32[]{:S(2)}) collective-permute-start(bf16[1,32,88,128]{3,2,1,0:T(8,128)(2,1)} %copy.124.rhs_ref), channel_id=1, source_target_pairs={{0,160},{32,192},{64,224},{96,0},{128,32},{160,64},{192,96},{224,1... | collective-permute-start | bytes 2162696 | tf_op jit(solution)/shard_map/ppermute | solution.py:20
  74.6 3.7 %collective-permute-start.1 = (bf16[1,32,88,128]{3,2,1,0:T(8,128)(2,1)}, bf16[1,32,88,128]{3,2,1,0:T(8,128)(2,1)}, u32[]{:S(2)}, u32[]{:S(2)}) collective-permute-start(bf16[1,32,88,128]{3,2,1,0:T(8,128)(2,1)} %copy.124.rhs_ref), channel_id=1, source_target_pairs={{0,192},{32,224},{64,0},{96,32},{128,64},{160,96},{192,128},{224,1... | collective-permute-start | bytes 2162696 | tf_op jit(solution)/shard_map/ppermute | solution.py:20
  87.7 16.4 %collective-permute-done.4.rhs_ref = bf16[1,32,88,128]{3,2,1,0:T(8,128)(2,1)} collective-permute-done((bf16[1,32,88,128]{3,2,1,0:T(8,128)(2,1)S(1)}, bf16[1,32,88,128]{3,2,1,0:T(8,128)(2,1)}, u32[]{:S(2)}, u32[]{:S(2)}) %collective-permute-start.4) | collective-permute-done | bytes 720928 | tf_op jit(solution)/shard_map/ppermute | solution.py:20
  105.9 7.3 %collective-permute-start.7 = (bf16[32,2,44,128]{3,0,2,1:T(8,128)(2,1)}, bf16[32,2,44,128]{3,0,2,1:T(8,128)(2,1)}, u32[]{:S(2)}, u32[]{:S(2)}) collective-permute-start(bf16[32,2,44,128]{3,0,2,1:T(8,128)(2,1)} %copy.133), channel_id=1, source_target_pairs={{0,128},{32,160},{64,192},{96,224},{1,129},{33,161},{65,193},{97,2... | collective-permute-start | bytes 2162696 | tf_op jit(solution)/shard_map/ppermute | solution.py:118
  117.8 3.6 %broadcast_in_dim_reshape.7 = bf16[1,32,256,88]{2,3,1,0:T(8,128)(2,1)S(1)} reshape(bf16[32,2,128,2,44]{2,1,4,3,0:T(2,128)(2,1)} %copy.132) | data formatting | bytes 2883584 | tf_op jit(solution)/shard_map/broadcast_in_dim;reshape | solution.py:112
  121.4 2.9 %copy.134.lhs_ref = bf16[1,32,256,88]{3,2,1,0:T(8,128)(2,1)} copy(bf16[1,32,256,88]{2,3,1,0:T(8,128)(2,1)S(1)} %broadcast_in_dim_reshape.7) | data formatting | bytes 2883584 | tf_op jit(solution)/shard_map/broadcast_in_dim;reshape | solution.py:112
  127.0 3.6 %broadcast_in_dim_reshape.6 = bf16[1,32,256,88]{2,3,1,0:T(8,128)(2,1)S(1)} reshape(bf16[32,2,128,2,44]{2,1,4,3,0:T(2,128)(2,1)} %copy.121) | data formatting | bytes 2883584 | tf_op jit(solution)/shard_map/broadcast_in_dim;reshape | solution.py:112
  130.6 2.9 %copy.123.lhs_ref = bf16[1,32,256,88]{3,2,1,0:T(8,128)(2,1)} copy(bf16[1,32,256,88]{2,3,1,0:T(8,128)(2,1)S(1)} %broadcast_in_dim_reshape.6) | data formatting | bytes 2883584 | tf_op jit(solution)/shard_map/broadcast_in_dim;reshape | solution.py:112
  133.6 4.8 %shard_map.45 = f32[1,128,256]{2,1,0:T(8,128)} custom-call(bf16[1,32,256,88]{3,2,1,0:T(8,128)(2,1)} %copy.134.lhs_ref, bf16[1,32,88,128]{3,2,1,0:T(8,128)(2,1)} %copy-done.1), custom_call_target="tpu_custom_call" | custom-call | flops 184549376 | bytes 2293760 | tf_op jit(solution)/shard_map/pallas_call | solution.py:74
  138.4 5.0 %shard_map.41 = f32[1,128,256]{2,1,0:T(8,128)} custom-call(bf16[1,32,256,88]{3,2,1,0:T(8,128)(2,1)} %copy.123.lhs_ref, bf16[1,32,88,128]{3,2,1,0:T(8,128)(2,1)} %copy.124.rhs_ref), custom_call_target="tpu_custom_call" | custom-call | flops 184549376 | bytes 2293760 | tf_op jit(solution)/shard_map/pallas_call | solution.py:74
  144.9 4.8 %shard_map.48 = f32[1,128,256]{2,1,0:T(8,128)} custom-call(bf16[1,32,256,88]{3,2,1,0:T(8,128)(2,1)} %copy.134.lhs_ref, bf16[1,32,88,128]{3,2,1,0:T(8,128)(2,1)} %copy-done.2), custom_call_target="tpu_custom_call" | custom-call | flops 184549376 | bytes 2293760 | tf_op jit(solution)/shard_map/pallas_call | solution.py:74
  149.7 4.8 %shard_map.47 = f32[1,128,256]{2,1,0:T(8,128)} custom-call(bf16[1,32,256,88]{3,2,1,0:T(8,128)(2,1)} %copy.134.lhs_ref, bf16[1,32,88,128]{3,2,1,0:T(8,128)(2,1)} %collective-permute-done.4.rhs_ref), custom_call_target="tpu_custom_call" | custom-call | flops 184549376 | bytes 2293760 | tf_op jit(solution)/shard_map/pallas_call | solution.py:74
  154.5 4.8 %shard_map.46 = f32[1,128,256]{2,1,0:T(8,128)} custom-call(bf16[1,32,256,88]{3,2,1,0:T(8,128)(2,1)} %copy.134.lhs_ref, bf16[1,32,88,128]{3,2,1,0:T(8,128)(2,1)} %collective-permute-done.3.rhs_ref), custom_call_target="tpu_custom_call" | custom-call | flops 184549376 | bytes 2293760 | tf_op jit(solution)/shard_map/pallas_call | solution.py:74
  159.3 4.8 %shard_map.44 = f32[1,128,256]{2,1,0:T(8,128)} custom-call(bf16[1,32,256,88]{3,2,1,0:T(8,128)(2,1)} %copy.123.lhs_ref, bf16[1,32,88,128]{3,2,1,0:T(8,128)(2,1)} %collective-permute-done.2.rhs_ref), custom_call_target="tpu_custom_call" | custom-call | flops 184549376 | bytes 2293760 | tf_op jit(solution)/shard_map/pallas_call | solution.py:74
  164.2 4.8 %shard_map.43 = f32[1,128,256]{2,1,0:T(8,128)} custom-call(bf16[1,32,256,88]{3,2,1,0:T(8,128)(2,1)} %copy.123.lhs_ref, bf16[1,32,88,128]{3,2,1,0:T(8,128)(2,1)} %collective-permute-done.1.rhs_ref), custom_call_target="tpu_custom_call" | custom-call | flops 184549376 | bytes 2293760 | tf_op jit(solution)/shard_map/pallas_call | solution.py:74
  169.0 4.9 %shard_map.42 = f32[1,128,256]{2,1,0:T(8,128)} custom-call(bf16[1,32,256,88]{3,2,1,0:T(8,128)(2,1)} %copy.123.lhs_ref, bf16[1,32,88,128]{3,2,1,0:T(8,128)(2,1)} %collective-permute-done.rhs_ref), custom_call_target="tpu_custom_call" | custom-call | flops 184549376 | bytes 2293760 | tf_op jit(solution)/shard_map/pallas_call | solution.py:74
  178.8 4.8 %shard_map.49 = f32[1,128,256]{2,1,0:T(8,128)} custom-call(bf16[1,32,256,88]{3,2,1,0:T(8,128)(2,1)} %broadcast_select_fusion.lhs_ref, bf16[1,32,88,128]{3,2,1,0:T(8,128)(2,1)} %copy.146.rhs_ref), custom_call_target="tpu_custom_call" | custom-call | flops 184549376 | bytes 2293760 | tf_op jit(solution)/shard_map/pallas_call | solution.py:74
  (64 shorter events, 38.6 us)
Async XLA Ops:
  11.0 31.2 %all-to-all-start.1 = ((bf16[32,2,44,128]{3,1,2,0:T(2,128)(2,1)}), bf16[32,2,44,128]{3,1,2,0:T(2,128)(2,1)S(1)}, u32[]{:S(2)}, u32[]{:S(2)}) async-start(bf16[32,2,44,128]{3,1,2,0:T(2,128)(2,1)} %copy.131), calls=%async_computation.1 | async-start | bytes 1441792 | tf_op jit(solution)/shard_map/all_to_all | solution.py:109
  42.2 25.9 %all-to-all-start = ((bf16[32,2,44,128]{3,1,2,0:T(2,128)(2,1)}), bf16[32,2,44,128]{3,1,2,0:T(2,128)(2,1)S(1)}, u32[]{:S(2)}, u32[]{:S(2)}) async-start(bf16[32,2,44,128]{3,1,2,0:T(2,128)(2,1)} %copy.120), calls=%async_computation | async-start | bytes 1441792 | tf_op jit(solution)/shard_map/all_to_all | solution.py:109
  49.4 22.0 %copy-start.1 = (bf16[1,32,88,128]{3,2,1,0:T(8,128)(2,1)}, bf16[1,32,88,128]{3,2,1,0:T(8,128)(2,1)S(1)}, u32[]{:S(2)}) copy-start(bf16[1,32,88,128]{3,2,1,0:T(8,128)(2,1)S(1)} %copy.135.rhs_ref) | copy-start | bytes 2162692
  49.4 36.8 %collective-permute-start.5 = (bf16[1,32,88,128]{3,2,1,0:T(8,128)(2,1)S(1)}, bf16[1,32,88,128]{3,2,1,0:T(8,128)(2,1)S(1)}, u32[]{:S(2)}, u32[]{:S(2)}) collective-permute-start(bf16[1,32,88,128]{3,2,1,0:T(8,128)(2,1)S(1)} %copy.135.rhs_ref), channel_id=1, source_target_pairs={{0,160},{32,192},{64,224},{96,0},{128,32},{160,64},{192,96},{224,1... | collective-permute-start | bytes 2162696 | tf_op jit(solution)/shard_map/ppermute | solution.py:20
  52.7 51.4 %collective-permute-start.4 = (bf16[1,32,88,128]{3,2,1,0:T(8,128)(2,1)S(1)}, bf16[1,32,88,128]{3,2,1,0:T(8,128)(2,1)}, u32[]{:S(2)}, u32[]{:S(2)}) collective-permute-start(bf16[1,32,88,128]{3,2,1,0:T(8,128)(2,1)S(1)} %copy.135.rhs_ref), channel_id=1, source_target_pairs={{0,192},{32,224},{64,0},{96,32},{128,64},{160,96},{192,128},{224,1... | collective-permute-start | bytes 2162696 | tf_op jit(solution)/shard_map/ppermute | solution.py:20
  56.4 49.5 %collective-permute-start.3 = (bf16[1,32,88,128]{3,2,1,0:T(8,128)(2,1)S(1)}, bf16[1,32,88,128]{3,2,1,0:T(8,128)(2,1)}, u32[]{:S(2)}, u32[]{:S(2)}) collective-permute-start(bf16[1,32,88,128]{3,2,1,0:T(8,128)(2,1)S(1)} %copy.135.rhs_ref), channel_id=1, source_target_pairs={{0,224},{32,0},{64,32},{96,64},{128,96},{160,128},{192,160},{224,1... | collective-permute-start | bytes 2162696 | tf_op jit(solution)/shard_map/ppermute | solution.py:20
  71.4 87.9 %collective-permute-start.2 = (bf16[1,32,88,128]{3,2,1,0:T(8,128)(2,1)}, bf16[1,32,88,128]{3,2,1,0:T(8,128)(2,1)}, u32[]{:S(2)}, u32[]{:S(2)}) collective-permute-start(bf16[1,32,88,128]{3,2,1,0:T(8,128)(2,1)} %copy.124.rhs_ref), channel_id=1, source_target_pairs={{0,160},{32,192},{64,224},{96,0},{128,32},{160,64},{192,96},{224,1... | collective-permute-start | bytes 2162696 | tf_op jit(solution)/shard_map/ppermute | solution.py:20
  74.6 89.6 %collective-permute-start.1 = (bf16[1,32,88,128]{3,2,1,0:T(8,128)(2,1)}, bf16[1,32,88,128]{3,2,1,0:T(8,128)(2,1)}, u32[]{:S(2)}, u32[]{:S(2)}) collective-permute-start(bf16[1,32,88,128]{3,2,1,0:T(8,128)(2,1)} %copy.124.rhs_ref), channel_id=1, source_target_pairs={{0,192},{32,224},{64,0},{96,32},{128,64},{160,96},{192,128},{224,1... | collective-permute-start | bytes 2162696 | tf_op jit(solution)/shard_map/ppermute | solution.py:20
  86.3 26.9 %copy-start.2 = (bf16[1,32,88,128]{3,2,1,0:T(8,128)(2,1)}, bf16[1,32,88,128]{3,2,1,0:T(8,128)(2,1)S(1)}, u32[]{:S(2)}) copy-start(bf16[1,32,88,128]{3,2,1,0:T(8,128)(2,1)S(1)} %collective-permute-done.5.rhs_ref) | copy-start | bytes 2162692
  86.3 82.8 %collective-permute-start = (bf16[1,32,88,128]{3,2,1,0:T(8,128)(2,1)}, bf16[1,32,88,128]{3,2,1,0:T(8,128)(2,1)}, u32[]{:S(2)}, u32[]{:S(2)}) collective-permute-start(bf16[1,32,88,128]{3,2,1,0:T(8,128)(2,1)} %copy.124.rhs_ref), channel_id=1, source_target_pairs={{0,224},{32,0},{64,32},{96,64},{128,96},{160,128},{192,160},{224,1... | collective-permute-start | bytes 2162696 | tf_op jit(solution)/shard_map/ppermute | solution.py:20
  104.1 72.4 %collective-permute-start.6 = (bf16[32,2,44,128]{3,0,2,1:T(8,128)(2,1)}, bf16[32,2,44,128]{3,0,2,1:T(8,128)(2,1)}, u32[]{:S(2)}, u32[]{:S(2)}) collective-permute-start(bf16[32,2,44,128]{3,0,2,1:T(8,128)(2,1)} %copy.122), channel_id=1, source_target_pairs={{128,0},{160,32},{192,64},{224,96},{129,1},{161,33},{193,65},{225,... | collective-permute-start | bytes 2162696 | tf_op jit(solution)/shard_map/ppermute | solution.py:118
  105.9 70.6 %collective-permute-start.7 = (bf16[32,2,44,128]{3,0,2,1:T(8,128)(2,1)}, bf16[32,2,44,128]{3,0,2,1:T(8,128)(2,1)}, u32[]{:S(2)}, u32[]{:S(2)}) collective-permute-start(bf16[32,2,44,128]{3,0,2,1:T(8,128)(2,1)} %copy.133), channel_id=1, source_target_pairs={{0,128},{32,160},{64,192},{96,224},{1,129},{33,161},{65,193},{97,2... | collective-permute-start | bytes 2162696 | tf_op jit(solution)/shard_map/ppermute | solution.py:118
  138.4 5.0 %copy-start = (bf16[1,32,256,88]{3,2,1,0:T(8,128)(2,1)S(1)}, bf16[1,32,256,88]{3,2,1,0:T(8,128)(2,1)}, u32[]{:S(2)}) copy-start(bf16[1,32,256,88]{3,2,1,0:T(8,128)(2,1)} %copy.123.lhs_ref) | copy-start | bytes 4325380
  169.0 5.0 %copy-start.3 = (f32[1,128,256]{2,1,0:T(8,128)S(1)}, f32[1,128,256]{2,1,0:T(8,128)}, u32[]{:S(2)}) copy-start(f32[1,128,256]{2,1,0:T(8,128)} %shard_map.45) | copy-start | bytes 393220
  169.0 5.0 %copy-start.4 = (f32[1,128,256]{2,1,0:T(8,128)S(1)}, f32[1,128,256]{2,1,0:T(8,128)}, u32[]{:S(2)}) copy-start(f32[1,128,256]{2,1,0:T(8,128)} %shard_map.41) | copy-start | bytes 393220
  169.0 5.0 %copy-start.5 = (f32[1,128,256]{2,1,0:T(8,128)S(1)}, f32[1,128,256]{2,1,0:T(8,128)}, u32[]{:S(2)}) copy-start(f32[1,128,256]{2,1,0:T(8,128)} %shard_map.48) | copy-start | bytes 393220
  169.0 5.0 %copy-start.6 = (f32[1,128,256]{2,1,0:T(8,128)S(1)}, f32[1,128,256]{2,1,0:T(8,128)}, u32[]{:S(2)}) copy-start(f32[1,128,256]{2,1,0:T(8,128)} %shard_map.47) | copy-start | bytes 393220
  169.0 5.0 %copy-start.7 = (f32[1,128,256]{2,1,0:T(8,128)S(1)}, f32[1,128,256]{2,1,0:T(8,128)}, u32[]{:S(2)}) copy-start(f32[1,128,256]{2,1,0:T(8,128)} %shard_map.46) | copy-start | bytes 393220
  169.0 5.0 %copy-start.8 = (f32[1,128,256]{2,1,0:T(8,128)S(1)}, f32[1,128,256]{2,1,0:T(8,128)}, u32[]{:S(2)}) copy-start(f32[1,128,256]{2,1,0:T(8,128)} %shard_map.44) | copy-start | bytes 393220
  169.0 5.0 %copy-start.9 = (f32[1,128,256]{2,1,0:T(8,128)S(1)}, f32[1,128,256]{2,1,0:T(8,128)}, u32[]{:S(2)}) copy-start(f32[1,128,256]{2,1,0:T(8,128)} %shard_map.43) | copy-start | bytes 393220
  178.8 5.9 %copy-start.10 = (f32[2]{0:T(128)S(1)}, f32[2]{0:T(128)}, u32[]{:S(2)}) copy-start(f32[2]{0:T(128)} %constant.41.clone) | copy-start | bytes 28

commit v4 on v2

v4 whole, which is shorter than its diff:
```python
import functools
import math

import jax
import jax.numpy as jnp
from jax import lax
from jax.experimental import pallas as pl
from jax.experimental.pallas import tpu as pltpu
from jax.sharding import PartitionSpec as P

FREQS = 64
FIRST_BIN = 32
EPSILON = 1e-06
GROUPS_PER_STEP = 8


def shifted(value, axis, steps):
    count = lax.axis_size(axis)
    pairs = [(source, (source + steps) % count) for source in range(count)]
    return lax.ppermute(value, axis, pairs)


def dft_table(sample_count, frequency_count, first_bin):
    positions = jnp.arange(sample_count, dtype=jnp.int32)
    bin_numbers = jnp.arange(frequency_count, dtype=jnp.int32) + first_bin
    phase_index = bin_numbers[:, None] * positions[None, :] % sample_count
    phase_angle = 2.0 * math.pi / sample_count * phase_index.astype(jnp.float32)
    hann_taper = 0.5 - 0.5 * jnp.cos(2.0 * math.pi / sample_count * positions.astype(jnp.float32))
    cosine = hann_taper[None, :] * jnp.cos(phase_angle)
    sine_part = -hann_taper[None, :] * jnp.sin(phase_angle)
    return (
        jnp.stack([cosine, sine_part], axis=1)
        .reshape(2 * frequency_count, sample_count)
        .astype(jnp.bfloat16)
    )


def whiten(records, taper_table, overall_scale):
    spectra = jnp.einsum("ks,wcs->kwc", taper_table, records, preferred_element_type=jnp.float32)
    mean_square = jnp.mean(spectra * spectra, axis=0)
    factor = overall_scale / jnp.sqrt(mean_square + EPSILON)
    return (spectra * factor[None]).astype(jnp.bfloat16)


def pair_kernel(group_count, own_ref, *refs):
    mate_refs, out_ref = refs[:-1], refs[-1]
    chans = out_ref.shape[-2]
    contract = (((0,), (0,)), ((), ()))

    @pl.when(pl.program_id(0) == 0)
    def _():
        out_ref[...] = jnp.zeros_like(out_ref)

    for group in range(group_count):
        rows = jnp.concatenate([own_ref[group, 0], own_ref[group, 1]], axis=1)
        for index, mate_ref in enumerate(mate_refs):
            cols = jnp.concatenate([mate_ref[group, 0], mate_ref[group, 1]], axis=1)
            prod = lax.dot_general(rows, cols, contract, preferred_element_type=jnp.float32)
            real = prod[:chans, :chans] + prod[chans:, chans:]
            imag = prod[chans:, :chans] - prod[:chans, chans:]
            both = jnp.concatenate([real, imag], axis=1)
            out_ref[index] += both.astype(jnp.bfloat16).astype(jnp.float32)


def pair_stack(own, mates):
    groups, _, width, chans = own.shape
    step = GROUPS_PER_STEP
    spec = pl.BlockSpec((step, 2, width, chans), lambda n: (n, 0, 0, 0))
    count = len(mates)
    return pl.pallas_call(
        functools.partial(pair_kernel, step),
        out_shape=jax.ShapeDtypeStruct((count, chans, 2 * chans), jnp.float32),
        grid=(groups // step,),
        in_specs=[spec] * (count + 1),
        out_specs=pl.BlockSpec((count, chans, 2 * chans), lambda n: (0, 0, 0)),
        cost_estimate=pl.CostEstimate(
            flops=2 * count * groups * 2 * width * 4 * chans * chans,
            bytes_accessed=2 * (count + 1) * groups * 2 * width * chans + 4 * count * chans * 2 * chans,
            transcendentals=0,
        ),
    )(own, *mates)


def body(records):
    window_count = records.shape[0]
    chans = records.shape[1]
    chan_count = lax.axis_size("chan")
    half_count = chan_count // 2
    time_count = lax.axis_size("tm")
    taper_table = dft_table(records.shape[2], FREQS, FIRST_BIN)
    whitened = whiten(records, taper_table, float(window_count * time_count) ** (-0.25))
    half_freq = FREQS // 2
    lower_half = lax.axis_index("chan") < half_count
    spectra = whitened.reshape(2, half_freq, 2, window_count, chans)

    near = []
    own_h = []
    far_recv = []
    for half in range(2):
        blocks = lax.all_to_all(spectra[half], "tm", split_axis=0, concat_axis=0, tiled=True)
        own_h.append(blocks)
        if half == 0:
            pairs = [(s, s - half_count) for s in range(half_count, chan_count)]
        else:
            pairs = [(s, s + half_count) for s in range(half_count)]
        far_recv.append(lax.ppermute(blocks, "chan", pairs))
        mates = [blocks] + [shifted(blocks, "chan", -offset) for offset in range(1, half_count)]
        near.append(pair_stack(blocks, mates))
    cross_near = jnp.stack(near, axis=0).reshape(1, 2, half_count, chans, 2, chans)

    far_own = jnp.where(lower_half, own_h[0], own_h[1])
    far_mate = jnp.where(lower_half, far_recv[0], far_recv[1])
    product = pair_stack(far_own, [far_mate]).reshape(chans, 2, chans)
    turned = product.transpose(2, 1, 0) * jnp.array([1.0, -1.0], jnp.float32)[None, :, None]
    cross_far = jnp.where(lower_half, product, turned).reshape(1, chans, 2, chans)
    return (cross_near, cross_far)


def solution(mesh):
    return jax.shard_map(
        body,
        mesh=mesh,
        in_specs=(P("tm", "chan", None),),
        out_specs=(P("tm", None, None, "chan", None, None), P("tm", "chan", None, None)),
        check_vma=False,
    )
```

time: 191 us -> 219 us (1.15)
  the two profiles are of different devices: /device:TPU:24 before, /device:TPU:44 now
where the time goes in v4:
time: 219 us; the launch traced here: 218 us
  waiting for transfers between devices  135 us (62%)
  starting transfers between devices  27.7 us (13%)
  local copies, waits for them, and re-layouts  23.3 us (11%)
  Pallas kernels  18.9 us (9%)
  matrix products  6.78 us (3%)
  other arithmetic  6.21 us (3%)
    ppermute x6, waiting for transfers between devices, shifted(): return lax.ppermute(value, axis, pairs)  82.1 us
    all_to_all x2, waiting for transfers between devices, body(): lax.all_to_all(spectra[half], 'tm', split_axis=0, concat_axis=0, tiled=True)  39.1 us
    pallas_call x3, Pallas kernels, pair_stack(): pl.pallas_call(functools.partial(pair_kernel, step), out_shape=jax.ShapeD...  18.9 us
    ppermute x6, local copies, waits for them, and re-layouts, shifted(): return lax.ppermute(value, axis, pairs)  13.7 us
    ppermute x2, waiting for transfers between devices, body(): far_recv.append(lax.ppermute(blocks, 'chan', pairs))  13.6 us
    all_to_all x2, starting transfers between devices, body(): lax.all_to_all(spectra[half], 'tm', split_axis=0, concat_axis=0, tiled=True)  13.2 us
    ppermute x6, starting transfers between devices, shifted(): return lax.ppermute(value, axis, pairs)  10.5 us
    dot_general x1, matrix products, whiten(): jnp.einsum('ks,wcs->kwc', taper_table, records, preferred_element_type=jn...  6.78 us
  transfers between devices with their start and end apart: 10, of which 6 were waited for; matrix products, arithmetic and copies ran while one was open for 10% of the time, Pallas kernels for 5%

profile of v4, /device:TPU:44, one launch (start us, length us, event | category | flops | bytes accessed | tf_op | source)
XLA Modules:
  0.0 218.5 jit_solution(9639307876012707786)
XLA Ops:
  2.4 6.8 %multiply_reduce_fusion = (f32[44,128]{1,0:T(8,128)S(1)}, f32[128,44,128]{2,0,1:T(8,128)S(1)}) fusion(bf16[128,1024,1]{1,0,2:T(8,128)(2,1)S(1)} %reshape.182, bf16[44,128,1024]{2,1,0:T(8,128)(2,1)} %param.2), kind=kOutput, calls=%fused_computation.1 | convolution fusion | flops 1477831168 | bytes 14702592 | tf_op jit(solution)/shard_map/ks,wcs->kwc/dot_general | solution.py:39
  11.0 9.4 %all-to-all-start = ((bf16[32,2,44,128]{3,1,2,0:T(2,128)(2,1)}), bf16[32,2,44,128]{3,1,2,0:T(2,128)(2,1)S(1)}, u32[]{:S(2)}, u32[]{:S(2)}) async-start(bf16[32,2,44,128]{3,1,2,0:T(2,128)(2,1)} %copy.60), calls=%async_computation | async-start | bytes 1441792 | tf_op jit(solution)/shard_map/all_to_all | solution.py:100
  21.8 20.6 %all-to-all-done = bf16[32,2,44,128]{3,1,2,0:T(2,128)(2,1)S(1)} async-done(((bf16[32,2,44,128]{3,1,2,0:T(2,128)(2,1)}), bf16[32,2,44,128]{3,1,2,0:T(2,128)(2,1)S(1)}, u32[]{:S(2)}, u32[]{:S(2)}) %all-to-all-start) | async-done | bytes 720928 | tf_op jit(solution)/shard_map/all_to_all | solution.py:100
  42.4 3.9 %all-to-all-start.1 = ((bf16[32,2,44,128]{3,1,2,0:T(2,128)(2,1)}), bf16[32,2,44,128]{3,1,2,0:T(2,128)(2,1)S(1)}, u32[]{:S(2)}, u32[]{:S(2)}) async-start(bf16[32,2,44,128]{3,1,2,0:T(2,128)(2,1)} %copy.69), calls=%async_computation.1 | async-start | bytes 1441792 | tf_op jit(solution)/shard_map/all_to_all | solution.py:100
  47.2 2.7 %collective-permute-start.6 = (bf16[32,2,44,128]{3,0,2,1:T(8,128)(2,1)}, bf16[32,2,44,128]{3,0,2,1:T(8,128)(2,1)S(1)}, u32[]{:S(2)}, u32[]{:S(2)}) collective-permute-start(bf16[32,2,44,128]{3,0,2,1:T(8,128)(2,1)} %copy.61), channel_id=1, source_target_pairs={{128,0},{160,32},{192,64},{224,96},{129,1},{161,33},{193,65},{225,... | collective-permute-start | bytes 2162696 | tf_op jit(solution)/shard_map/ppermute | solution.py:106
  50.0 18.5 %all-to-all-done.1 = bf16[32,2,44,128]{3,1,2,0:T(2,128)(2,1)S(1)} async-done(((bf16[32,2,44,128]{3,1,2,0:T(2,128)(2,1)}), bf16[32,2,44,128]{3,1,2,0:T(2,128)(2,1)S(1)}, u32[]{:S(2)}, u32[]{:S(2)}) %all-to-all-start.1) | async-done | bytes 720928 | tf_op jit(solution)/shard_map/all_to_all | solution.py:100
  71.2 6.2 %collective-permute-start.1 = (bf16[32,2,44,128]{3,0,2,1:T(8,128)(2,1)}, bf16[32,2,44,128]{3,0,2,1:T(8,128)(2,1)}, u32[]{:S(2)}, u32[]{:S(2)}) collective-permute-start(bf16[32,2,44,128]{3,0,2,1:T(8,128)(2,1)} %copy.61), channel_id=1, source_target_pairs={{0,192},{32,224},{64,0},{96,32},{128,64},{160,96},{192,128},{224,1... | collective-permute-start | bytes 2162696 | tf_op jit(solution)/shard_map/ppermute | solution.py:20
  78.5 13.6 %collective-permute-done.7 = bf16[32,2,44,128]{3,0,2,1:T(8,128)(2,1)S(1)} collective-permute-done((bf16[32,2,44,128]{3,0,2,1:T(8,128)(2,1)}, bf16[32,2,44,128]{3,0,2,1:T(8,128)(2,1)S(1)}, u32[]{:S(2)}, u32[]{:S(2)}) %collective-permute-start.7) | collective-permute-done | bytes 720928 | tf_op jit(solution)/shard_map/ppermute | solution.py:106
  92.1 12.5 %collective-permute-done = bf16[32,2,44,128]{3,0,2,1:T(8,128)(2,1)} collective-permute-done((bf16[32,2,44,128]{3,0,2,1:T(8,128)(2,1)}, bf16[32,2,44,128]{3,0,2,1:T(8,128)(2,1)}, u32[]{:S(2)}, u32[]{:S(2)}) %collective-permute-start) | collective-permute-done | bytes 720928 | tf_op jit(solution)/shard_map/ppermute | solution.py:20
  104.6 2.7 %collective-permute-start.5 = (bf16[32,2,44,128]{3,0,2,1:T(8,128)(2,1)}, bf16[32,2,44,128]{3,0,2,1:T(8,128)(2,1)}, u32[]{:S(2)}, u32[]{:S(2)}) collective-permute-start(bf16[32,2,44,128]{3,0,2,1:T(8,128)(2,1)} %copy.70), channel_id=1, source_target_pairs={{0,160},{32,192},{64,224},{96,0},{128,32},{160,64},{192,96},{224,1... | collective-permute-start | bytes 2162696 | tf_op jit(solution)/shard_map/ppermute | solution.py:20
  107.2 1.5 broadcast_select_fusion
  108.7 1.5 copy_select_fusion.refs_0_
  110.2 4.2 %shard_map.43 = f32[1,128,256]{2,1,0:T(8,128)} custom-call(bf16[32,2,44,128]{3,2,1,0:T(8,128)(2,1)} %get-tuple-element.8.own_ref, bf16[32,2,44,128]{3,2,1,0:T(8,128)(2,1)} %copy_select_fusion.refs_0_), custom_call_target="tpu_custom_call" | custom-call | flops 369098752 | bytes 1572864 | tf_op jit(solution)/shard_map/pallas_call | solution.py:70
  116.4 2.3 %copy.66.refs_1_ = bf16[32,2,44,128]{3,2,1,0:T(8,128)(2,1)} copy(bf16[32,2,44,128]{3,0,2,1:T(8,128)(2,1)} %collective-permute-done) | data formatting | bytes 1441792 | tf_op jit(solution)/shard_map/ppermute | solution.py:20
  118.7 2.3 %copy.67.refs_2_ = bf16[32,2,44,128]{3,2,1,0:T(8,128)(2,1)} copy(bf16[32,2,44,128]{3,0,2,1:T(8,128)(2,1)} %collective-permute-done.1) | data formatting | bytes 1441792 | tf_op jit(solution)/shard_map/ppermute | solution.py:20
  120.9 40.4 %collective-permute-done.2 = bf16[32,2,44,128]{3,0,2,1:T(8,128)(2,1)} collective-permute-done((bf16[32,2,44,128]{3,0,2,1:T(8,128)(2,1)}, bf16[32,2,44,128]{3,0,2,1:T(8,128)(2,1)}, u32[]{:S(2)}, u32[]{:S(2)}) %collective-permute-start.2) | collective-permute-done | bytes 720928 | tf_op jit(solution)/shard_map/ppermute | solution.py:20
  161.4 2.3 %copy.68.refs_3_ = bf16[32,2,44,128]{3,2,1,0:T(8,128)(2,1)} copy(bf16[32,2,44,128]{3,0,2,1:T(8,128)(2,1)} %collective-permute-done.2) | data formatting | bytes 1441792 | tf_op jit(solution)/shard_map/ppermute | solution.py:20
  163.7 7.3 %shard_map.41 = f32[4,128,256]{2,1,0:T(8,128)} custom-call(bf16[32,2,44,128]{3,2,1,0:T(8,128)(2,1)} %get-tuple-element.9.own_ref.refs_0_, bf16[32,2,44,128]{3,2,1,0:T(8,128)(2,1)} %get-tuple-element.9.own_ref.refs_0_, bf16[32,2,44,128]{3,2,1,0:T(8,128)(2,1)} %copy.66.refs_1_, bf16[32,2,44,128]{3,2,1,0:T(8,128)(2,1)} %copy.67.refs_2_, ...), custom_call_target="tpu_custom_call" | custom-call | flops 1476395008 | bytes 4128768 | tf_op jit(solution)/shard_map/pallas_call | solution.py:70
  172.3 2.3 %copy.75.refs_1_ = bf16[32,2,44,128]{3,2,1,0:T(8,128)(2,1)} copy(bf16[32,2,44,128]{3,0,2,1:T(8,128)(2,1)} %collective-permute-done.3) | data formatting | bytes 1441792 | tf_op jit(solution)/shard_map/ppermute | solution.py:20
  174.6 2.3 %copy.76.refs_2_ = bf16[32,2,44,128]{3,2,1,0:T(8,128)(2,1)} copy(bf16[32,2,44,128]{3,0,2,1:T(8,128)(2,1)} %collective-permute-done.4) | data formatting | bytes 1441792 | tf_op jit(solution)/shard_map/ppermute | solution.py:20
  176.9 29.2 %collective-permute-done.5 = bf16[32,2,44,128]{3,0,2,1:T(8,128)(2,1)} collective-permute-done((bf16[32,2,44,128]{3,0,2,1:T(8,128)(2,1)}, bf16[32,2,44,128]{3,0,2,1:T(8,128)(2,1)}, u32[]{:S(2)}, u32[]{:S(2)}) %collective-permute-start.5) | collective-permute-done | bytes 720928 | tf_op jit(solution)/shard_map/ppermute | solution.py:20
  206.1 2.3 %copy.77.refs_3_ = bf16[32,2,44,128]{3,2,1,0:T(8,128)(2,1)} copy(bf16[32,2,44,128]{3,0,2,1:T(8,128)(2,1)} %collective-permute-done.5) | data formatting | bytes 1441792 | tf_op jit(solution)/shard_map/ppermute | solution.py:20
  208.4 7.3 %shard_map.42 = f32[4,128,256]{2,1,0:T(8,128)} custom-call(bf16[32,2,44,128]{3,2,1,0:T(8,128)(2,1)} %get-tuple-element.10.own_ref.refs_0_, bf16[32,2,44,128]{3,2,1,0:T(8,128)(2,1)} %get-tuple-element.10.own_ref.refs_0_, bf16[32,2,44,128]{3,2,1,0:T(8,128)(2,1)} %copy.75.refs_1_, bf16[32,2,44,128]{3,2,1,0:T(8,128)(2,1)} %copy.76.refs_2_, ...), custom_call_target="tpu_custom_call" | custom-call | flops 1476395008 | bytes 4128768 | tf_op jit(solution)/shard_map/pallas_call | solution.py:70
  217.0 1.4 pad_maximum_fusion
  (30 shorter events, 14.3 us)
Async XLA Ops:
  11.0 31.3 %all-to-all-start = ((bf16[32,2,44,128]{3,1,2,0:T(2,128)(2,1)}), bf16[32,2,44,128]{3,1,2,0:T(2,128)(2,1)S(1)}, u32[]{:S(2)}, u32[]{:S(2)}) async-start(bf16[32,2,44,128]{3,1,2,0:T(2,128)(2,1)} %copy.60), calls=%async_computation | async-start | bytes 1441792 | tf_op jit(solution)/shard_map/all_to_all | solution.py:100
  42.4 26.0 %all-to-all-start.1 = ((bf16[32,2,44,128]{3,1,2,0:T(2,128)(2,1)}), bf16[32,2,44,128]{3,1,2,0:T(2,128)(2,1)S(1)}, u32[]{:S(2)}, u32[]{:S(2)}) async-start(bf16[32,2,44,128]{3,1,2,0:T(2,128)(2,1)} %copy.69), calls=%async_computation.1 | async-start | bytes 1441792 | tf_op jit(solution)/shard_map/all_to_all | solution.py:100
  47.2 30.9 %collective-permute-start.6 = (bf16[32,2,44,128]{3,0,2,1:T(8,128)(2,1)}, bf16[32,2,44,128]{3,0,2,1:T(8,128)(2,1)S(1)}, u32[]{:S(2)}, u32[]{:S(2)}) collective-permute-start(bf16[32,2,44,128]{3,0,2,1:T(8,128)(2,1)} %copy.61), channel_id=1, source_target_pairs={{128,0},{160,32},{192,64},{224,96},{129,1},{161,33},{193,65},{225,... | collective-permute-start | bytes 2162696 | tf_op jit(solution)/shard_map/ppermute | solution.py:106
  69.4 22.7 %collective-permute-start.7 = (bf16[32,2,44,128]{3,0,2,1:T(8,128)(2,1)}, bf16[32,2,44,128]{3,0,2,1:T(8,128)(2,1)S(1)}, u32[]{:S(2)}, u32[]{:S(2)}) collective-permute-start(bf16[32,2,44,128]{3,0,2,1:T(8,128)(2,1)} %copy.70), channel_id=1, source_target_pairs={{0,128},{32,160},{64,192},{96,224},{1,129},{33,161},{65,193},{97,2... | collective-permute-start | bytes 2162696 | tf_op jit(solution)/shard_map/ppermute | solution.py:106
  70.7 33.9 %collective-permute-start = (bf16[32,2,44,128]{3,0,2,1:T(8,128)(2,1)}, bf16[32,2,44,128]{3,0,2,1:T(8,128)(2,1)}, u32[]{:S(2)}, u32[]{:S(2)}) collective-permute-start(bf16[32,2,44,128]{3,0,2,1:T(8,128)(2,1)} %copy.61), channel_id=1, source_target_pairs={{0,224},{32,0},{64,32},{96,64},{128,96},{160,128},{192,160},{224,1... | collective-permute-start | bytes 2162696 | tf_op jit(solution)/shard_map/ppermute | solution.py:20
  71.2 47.4 %collective-permute-start.1 = (bf16[32,2,44,128]{3,0,2,1:T(8,128)(2,1)}, bf16[32,2,44,128]{3,0,2,1:T(8,128)(2,1)}, u32[]{:S(2)}, u32[]{:S(2)}) collective-permute-start(bf16[32,2,44,128]{3,0,2,1:T(8,128)(2,1)} %copy.61), channel_id=1, source_target_pairs={{0,192},{32,224},{64,0},{96,32},{128,64},{160,96},{192,128},{224,1... | collective-permute-start | bytes 2162696 | tf_op jit(solution)/shard_map/ppermute | solution.py:20
  77.4 83.9 %collective-permute-start.2 = (bf16[32,2,44,128]{3,0,2,1:T(8,128)(2,1)}, bf16[32,2,44,128]{3,0,2,1:T(8,128)(2,1)}, u32[]{:S(2)}, u32[]{:S(2)}) collective-permute-start(bf16[32,2,44,128]{3,0,2,1:T(8,128)(2,1)} %copy.61), channel_id=1, source_target_pairs={{0,160},{32,192},{64,224},{96,0},{128,32},{160,64},{192,96},{224,1... | collective-permute-start | bytes 2162696 | tf_op jit(solution)/shard_map/ppermute | solution.py:20
  78.1 94.2 %collective-permute-start.3 = (bf16[32,2,44,128]{3,0,2,1:T(8,128)(2,1)}, bf16[32,2,44,128]{3,0,2,1:T(8,128)(2,1)}, u32[]{:S(2)}, u32[]{:S(2)}) collective-permute-start(bf16[32,2,44,128]{3,0,2,1:T(8,128)(2,1)} %copy.70), channel_id=1, source_target_pairs={{0,224},{32,0},{64,32},{96,64},{128,96},{160,128},{192,160},{224,1... | collective-permute-start | bytes 2162696 | tf_op jit(solution)/shard_map/ppermute | solution.py:20
  92.1 82.5 %collective-permute-start.4 = (bf16[32,2,44,128]{3,0,2,1:T(8,128)(2,1)}, bf16[32,2,44,128]{3,0,2,1:T(8,128)(2,1)}, u32[]{:S(2)}, u32[]{:S(2)}) collective-permute-start(bf16[32,2,44,128]{3,0,2,1:T(8,128)(2,1)} %copy.70), channel_id=1, source_target_pairs={{0,192},{32,224},{64,0},{96,32},{128,64},{160,96},{192,128},{224,1... | collective-permute-start | bytes 2162696 | tf_op jit(solution)/shard_map/ppermute | solution.py:20
  104.6 101.5 %collective-permute-start.5 = (bf16[32,2,44,128]{3,0,2,1:T(8,128)(2,1)}, bf16[32,2,44,128]{3,0,2,1:T(8,128)(2,1)}, u32[]{:S(2)}, u32[]{:S(2)}) collective-permute-start(bf16[32,2,44,128]{3,0,2,1:T(8,128)(2,1)} %copy.70), channel_id=1, source_target_pairs={{0,160},{32,192},{64,224},{96,0},{128,32},{160,64},{192,96},{224,1... | collective-permute-start | bytes 2162696 | tf_op jit(solution)/shard_map/ppermute | solution.py:20
  108.7 6.8 %copy-start = (f32[2]{0:T(128)S(1)}, f32[2]{0:T(128)}, u32[]{:S(2)}) copy-start(f32[2]{0:T(128)} %constant.41.clone) | copy-start | bytes 28

commit v5 on v4

--- a/solution.py
+++ b/solution.py
@@ -105,7 +105,7 @@
             pairs = [(s, s + half_count) for s in range(half_count)]
         far_recv.append(lax.ppermute(blocks, "chan", pairs))
         mates = [blocks] + [shifted(blocks, "chan", -offset) for offset in range(1, half_count)]
-        near.append(pair_stack(blocks, mates))
+        near.append(jnp.concatenate([pair_stack(blocks, [mate]) for mate in mates], axis=0))
     cross_near = jnp.stack(near, axis=0).reshape(1, 2, half_count, chans, 2, chans)
 
     far_own = jnp.where(lower_half, own_h[0], own_h[1])

time: 219 us -> 180 us (0.82)
  the two profiles are of different devices: /device:TPU:44 before, /device:TPU:2 now
where the time goes in v5:
time: 180 us; the launch traced here: 178 us
  waiting for transfers between devices  64.5 us (36%)
  starting transfers between devices  39 us (22%)
  Pallas kernels  38.3 us (21%)
  local copies, waits for them, and re-layouts  20.2 us (11%)
  other arithmetic  8.23 us (5%)
  matrix products  6.78 us (4%)
    pallas_call x9, Pallas kernels, pair_stack(): pl.pallas_call(functools.partial(pair_kernel, step), out_shape=jax.ShapeD...  38.3 us
    ppermute x6, waiting for transfers between devices, shifted(): return lax.ppermute(value, axis, pairs)  32.1 us
    all_to_all x2, waiting for transfers between devices, body(): lax.all_to_all(spectra[half], 'tm', split_axis=0, concat_axis=0, tiled=True)  31.6 us
    ppermute x6, starting transfers between devices, shifted(): return lax.ppermute(value, axis, pairs)  18.8 us
    all_to_all x2, starting transfers between devices, body(): lax.all_to_all(spectra[half], 'tm', split_axis=0, concat_axis=0, tiled=True)  14.9 us
    ppermute x6, local copies, waits for them, and re-layouts, shifted(): return lax.ppermute(value, axis, pairs)  12.6 us
    dot_general x1, matrix products, whiten(): jnp.einsum('ks,wcs->kwc', taper_table, records, preferred_element_type=jn...  6.78 us
    ppermute x2, starting transfers between devices, body(): far_recv.append(lax.ppermute(blocks, 'chan', pairs))  5.27 us
  transfers between devices with their start and end apart: 10, of which 5 were waited for; matrix products, arithmetic and copies ran while one was open for 11% of the time, Pallas kernels for 19%

profile of v5, /device:TPU:2, one launch (start us, length us, event | category | flops | bytes accessed | tf_op | source)
XLA Modules:
  0.0 177.8 jit_solution(14137135009045891120)
XLA Ops:
  2.4 6.8 %multiply_reduce_fusion = (f32[44,128]{1,0:T(8,128)S(1)}, f32[128,44,128]{2,0,1:T(8,128)S(1)}) fusion(bf16[128,1024,1]{1,0,2:T(8,128)(2,1)S(1)} %reshape.182, bf16[44,128,1024]{2,1,0:T(8,128)(2,1)} %param.2), kind=kOutput, calls=%fused_computation.1 | convolution fusion | flops 1477831168 | bytes 14702592 | tf_op jit(solution)/shard_map/ks,wcs->kwc/dot_general | solution.py:39
  11.1 10.1 %all-to-all-start.1 = ((bf16[32,2,44,128]{3,1,2,0:T(2,128)(2,1)}), bf16[32,2,44,128]{3,1,2,0:T(2,128)(2,1)S(1)}, u32[]{:S(2)}, u32[]{:S(2)}) async-start(bf16[32,2,44,128]{3,1,2,0:T(2,128)(2,1)} %copy.84), calls=%async_computation.1 | async-start | bytes 1441792 | tf_op jit(solution)/shard_map/all_to_all | solution.py:100
  22.5 19.7 %all-to-all-done.1 = bf16[32,2,44,128]{3,1,2,0:T(2,128)(2,1)S(1)} async-done(((bf16[32,2,44,128]{3,1,2,0:T(2,128)(2,1)}), bf16[32,2,44,128]{3,1,2,0:T(2,128)(2,1)S(1)}, u32[]{:S(2)}, u32[]{:S(2)}) %all-to-all-start.1) | async-done | bytes 720928 | tf_op jit(solution)/shard_map/all_to_all | solution.py:100
  42.3 4.8 %all-to-all-start = ((bf16[32,2,44,128]{3,1,2,0:T(2,128)(2,1)}), bf16[32,2,44,128]{3,1,2,0:T(2,128)(2,1)S(1)}, u32[]{:S(2)}, u32[]{:S(2)}) async-start(bf16[32,2,44,128]{3,1,2,0:T(2,128)(2,1)} %copy.72), calls=%async_computation | async-start | bytes 1441792 | tf_op jit(solution)/shard_map/all_to_all | solution.py:100
  48.1 3.1 %collective-permute-start.5 = (bf16[32,2,44,128]{3,0,2,1:T(8,128)(2,1)}, bf16[32,2,44,128]{3,0,2,1:T(8,128)(2,1)S(1)}, u32[]{:S(2)}, u32[]{:S(2)}) collective-permute-start(bf16[32,2,44,128]{3,0,2,1:T(8,128)(2,1)} %copy.87), channel_id=1, source_target_pairs={{0,160},{32,192},{64,224},{96,0},{128,32},{160,64},{192,96},{224,1... | collective-permute-start | bytes 2162696 | tf_op jit(solution)/shard_map/ppermute | solution.py:20
  51.2 3.7 %collective-permute-start.4 = (bf16[32,2,44,128]{3,0,2,1:T(8,128)(2,1)}, bf16[32,2,44,128]{3,0,2,1:T(8,128)(2,1)}, u32[]{:S(2)}, u32[]{:S(2)}) collective-permute-start(bf16[32,2,44,128]{3,0,2,1:T(8,128)(2,1)} %copy.87), channel_id=1, source_target_pairs={{0,192},{32,224},{64,0},{96,32},{128,64},{160,96},{192,128},{224,1... | collective-permute-start | bytes 2162696 | tf_op jit(solution)/shard_map/ppermute | solution.py:20
  56.3 11.9 %all-to-all-done = bf16[32,2,44,128]{3,1,2,0:T(2,128)(2,1)S(1)} async-done(((bf16[32,2,44,128]{3,1,2,0:T(2,128)(2,1)}), bf16[32,2,44,128]{3,1,2,0:T(2,128)(2,1)S(1)}, u32[]{:S(2)}, u32[]{:S(2)}) %all-to-all-start) | async-done | bytes 720928 | tf_op jit(solution)/shard_map/all_to_all | solution.py:100
  69.1 3.1 %collective-permute-start.2 = (bf16[32,2,44,128]{3,0,2,1:T(8,128)(2,1)}, bf16[32,2,44,128]{3,0,2,1:T(8,128)(2,1)}, u32[]{:S(2)}, u32[]{:S(2)}) collective-permute-start(bf16[32,2,44,128]{3,0,2,1:T(8,128)(2,1)} %copy.75), channel_id=1, source_target_pairs={{0,160},{32,192},{64,224},{96,0},{128,32},{160,64},{192,96},{224,1... | collective-permute-start | bytes 2162696 | tf_op jit(solution)/shard_map/ppermute | solution.py:20
  72.3 3.7 %collective-permute-start.1 = (bf16[32,2,44,128]{3,0,2,1:T(8,128)(2,1)}, bf16[32,2,44,128]{3,0,2,1:T(8,128)(2,1)}, u32[]{:S(2)}, u32[]{:S(2)}) collective-permute-start(bf16[32,2,44,128]{3,0,2,1:T(8,128)(2,1)} %copy.75), channel_id=1, source_target_pairs={{0,192},{32,224},{64,0},{96,32},{128,64},{160,96},{192,128},{224,1... | collective-permute-start | bytes 2162696 | tf_op jit(solution)/shard_map/ppermute | solution.py:20
  76.0 3.7 %collective-permute-start = (bf16[32,2,44,128]{3,0,2,1:T(8,128)(2,1)}, bf16[32,2,44,128]{3,0,2,1:T(8,128)(2,1)}, u32[]{:S(2)}, u32[]{:S(2)}) collective-permute-start(bf16[32,2,44,128]{3,0,2,1:T(8,128)(2,1)} %copy.75), channel_id=1, source_target_pairs={{0,224},{32,0},{64,32},{96,64},{128,96},{160,128},{192,160},{224,1... | collective-permute-start | bytes 2162696 | tf_op jit(solution)/shard_map/ppermute | solution.py:20
  79.8 22.7 %collective-permute-done.4 = bf16[32,2,44,128]{3,0,2,1:T(8,128)(2,1)} collective-permute-done((bf16[32,2,44,128]{3,0,2,1:T(8,128)(2,1)}, bf16[32,2,44,128]{3,0,2,1:T(8,128)(2,1)}, u32[]{:S(2)}, u32[]{:S(2)}) %collective-permute-start.4) | collective-permute-done | bytes 720928 | tf_op jit(solution)/shard_map/ppermute | solution.py:20
  102.5 3.8 %collective-permute-start.7 = (bf16[32,2,44,128]{3,0,2,1:T(8,128)(2,1)}, bf16[32,2,44,128]{3,0,2,1:T(8,128)(2,1)S(1)}, u32[]{:S(2)}, u32[]{:S(2)}) collective-permute-start(bf16[32,2,44,128]{3,0,2,1:T(8,128)(2,1)} %copy.87), channel_id=1, source_target_pairs={{0,128},{32,160},{64,192},{96,224},{1,129},{33,161},{65,193},{97,2... | collective-permute-start | bytes 2162696 | tf_op jit(solution)/shard_map/ppermute | solution.py:106
  109.3 4.3 %shard_map.45 = f32[1,128,256]{2,1,0:T(8,128)} custom-call(bf16[32,2,44,128]{3,2,1,0:T(8,128)(2,1)} %get-tuple-element.10.own_ref.refs_0_, bf16[32,2,44,128]{3,2,1,0:T(8,128)(2,1)} %get-tuple-element.10.own_ref.refs_0_), custom_call_target="tpu_custom_call" | custom-call | flops 369098752 | bytes 1572864 | tf_op jit(solution)/shard_map/pallas_call | solution.py:70
  113.6 4.2 %shard_map.41 = f32[1,128,256]{2,1,0:T(8,128)} custom-call(bf16[32,2,44,128]{3,2,1,0:T(8,128)(2,1)} %get-tuple-element.9.own_ref.refs_0_, bf16[32,2,44,128]{3,2,1,0:T(8,128)(2,1)} %get-tuple-element.9.own_ref.refs_0_), custom_call_target="tpu_custom_call" | custom-call | flops 369098752 | bytes 1572864 | tf_op jit(solution)/shard_map/pallas_call | solution.py:70
  123.5 4.3 %shard_map.48 = f32[1,128,256]{2,1,0:T(8,128)} custom-call(bf16[32,2,44,128]{3,2,1,0:T(8,128)(2,1)} %get-tuple-element.10.own_ref.refs_0_, bf16[32,2,44,128]{3,2,1,0:T(8,128)(2,1)} %copy.95.refs_0_), custom_call_target="tpu_custom_call" | custom-call | flops 369098752 | bytes 1572864 | tf_op jit(solution)/shard_map/pallas_call | solution.py:70
  127.8 4.3 %shard_map.47 = f32[1,128,256]{2,1,0:T(8,128)} custom-call(bf16[32,2,44,128]{3,2,1,0:T(8,128)(2,1)} %get-tuple-element.10.own_ref.refs_0_, bf16[32,2,44,128]{3,2,1,0:T(8,128)(2,1)} %copy.92.refs_0_), custom_call_target="tpu_custom_call" | custom-call | flops 369098752 | bytes 1572864 | tf_op jit(solution)/shard_map/pallas_call | solution.py:70
  132.1 4.2 %shard_map.46 = f32[1,128,256]{2,1,0:T(8,128)} custom-call(bf16[32,2,44,128]{3,2,1,0:T(8,128)(2,1)} %get-tuple-element.10.own_ref.refs_0_, bf16[32,2,44,128]{3,2,1,0:T(8,128)(2,1)} %copy.89.refs_0_), custom_call_target="tpu_custom_call" | custom-call | flops 369098752 | bytes 1572864 | tf_op jit(solution)/shard_map/pallas_call | solution.py:70
  139.9 2.3 %copy.80.refs_0_ = bf16[32,2,44,128]{3,2,1,0:T(8,128)(2,1)} copy(bf16[32,2,44,128]{3,0,2,1:T(8,128)(2,1)} %collective-permute-done.1) | data formatting | bytes 1441792 | tf_op jit(solution)/shard_map/ppermute | solution.py:20
  142.2 9.4 %collective-permute-done = bf16[32,2,44,128]{3,0,2,1:T(8,128)(2,1)} collective-permute-done((bf16[32,2,44,128]{3,0,2,1:T(8,128)(2,1)}, bf16[32,2,44,128]{3,0,2,1:T(8,128)(2,1)}, u32[]{:S(2)}, u32[]{:S(2)}) %collective-permute-start) | collective-permute-done | bytes 720928 | tf_op jit(solution)/shard_map/ppermute | solution.py:20
  151.6 2.3 %copy.77.refs_0_ = bf16[32,2,44,128]{3,2,1,0:T(8,128)(2,1)} copy(bf16[32,2,44,128]{3,0,2,1:T(8,128)(2,1)} %collective-permute-done) | data formatting | bytes 1441792 | tf_op jit(solution)/shard_map/ppermute | solution.py:20
  153.9 4.3 %shard_map.44 = f32[1,128,256]{2,1,0:T(8,128)} custom-call(bf16[32,2,44,128]{3,2,1,0:T(8,128)(2,1)} %get-tuple-element.9.own_ref.refs_0_, bf16[32,2,44,128]{3,2,1,0:T(8,128)(2,1)} %copy.83.refs_0_), custom_call_target="tpu_custom_call" | custom-call | flops 369098752 | bytes 1572864 | tf_op jit(solution)/shard_map/pallas_call | solution.py:70
  158.2 4.3 %shard_map.43 = f32[1,128,256]{2,1,0:T(8,128)} custom-call(bf16[32,2,44,128]{3,2,1,0:T(8,128)(2,1)} %get-tuple-element.9.own_ref.refs_0_, bf16[32,2,44,128]{3,2,1,0:T(8,128)(2,1)} %copy.80.refs_0_), custom_call_target="tpu_custom_call" | custom-call | flops 369098752 | bytes 1572864 | tf_op jit(solution)/shard_map/pallas_call | solution.py:70
  162.4 4.2 %shard_map.42 = f32[1,128,256]{2,1,0:T(8,128)} custom-call(bf16[32,2,44,128]{3,2,1,0:T(8,128)(2,1)} %get-tuple-element.9.own_ref.refs_0_, bf16[32,2,44,128]{3,2,1,0:T(8,128)(2,1)} %copy.77.refs_0_), custom_call_target="tpu_custom_call" | custom-call | flops 369098752 | bytes 1572864 | tf_op jit(solution)/shard_map/pallas_call | solution.py:70
  170.2 4.2 %shard_map.49 = f32[1,128,256]{2,1,0:T(8,128)} custom-call(bf16[32,2,44,128]{3,2,1,0:T(8,128)(2,1)} %get-tuple-element.8.own_ref, bf16[32,2,44,128]{3,2,1,0:T(8,128)(2,1)} %copy_select_fusion.refs_0_), custom_call_target="tpu_custom_call" | custom-call | flops 369098752 | bytes 1572864 | tf_op jit(solution)/shard_map/pallas_call | solution.py:70
  (50 shorter events, 27.4 us)
Async XLA Ops:
  11.1 31.2 %all-to-all-start.1 = ((bf16[32,2,44,128]{3,1,2,0:T(2,128)(2,1)}), bf16[32,2,44,128]{3,1,2,0:T(2,128)(2,1)S(1)}, u32[]{:S(2)}, u32[]{:S(2)}) async-start(bf16[32,2,44,128]{3,1,2,0:T(2,128)(2,1)} %copy.84), calls=%async_computation.1 | async-start | bytes 1441792 | tf_op jit(solution)/shard_map/all_to_all | solution.py:100
  42.3 25.9 %all-to-all-start = ((bf16[32,2,44,128]{3,1,2,0:T(2,128)(2,1)}), bf16[32,2,44,128]{3,1,2,0:T(2,128)(2,1)S(1)}, u32[]{:S(2)}, u32[]{:S(2)}) async-start(bf16[32,2,44,128]{3,1,2,0:T(2,128)(2,1)} %copy.72), calls=%async_computation | async-start | bytes 1441792 | tf_op jit(solution)/shard_map/all_to_all | solution.py:100
  48.1 28.0 %collective-permute-start.5 = (bf16[32,2,44,128]{3,0,2,1:T(8,128)(2,1)}, bf16[32,2,44,128]{3,0,2,1:T(8,128)(2,1)S(1)}, u32[]{:S(2)}, u32[]{:S(2)}) collective-permute-start(bf16[32,2,44,128]{3,0,2,1:T(8,128)(2,1)} %copy.87), channel_id=1, source_target_pairs={{0,160},{32,192},{64,224},{96,0},{128,32},{160,64},{192,96},{224,1... | collective-permute-start | bytes 2162696 | tf_op jit(solution)/shard_map/ppermute | solution.py:20
  51.2 51.3 %collective-permute-start.4 = (bf16[32,2,44,128]{3,0,2,1:T(8,128)(2,1)}, bf16[32,2,44,128]{3,0,2,1:T(8,128)(2,1)}, u32[]{:S(2)}, u32[]{:S(2)}) collective-permute-start(bf16[32,2,44,128]{3,0,2,1:T(8,128)(2,1)} %copy.87), channel_id=1, source_target_pairs={{0,192},{32,224},{64,0},{96,32},{128,64},{160,96},{192,128},{224,1... | collective-permute-start | bytes 2162696 | tf_op jit(solution)/shard_map/ppermute | solution.py:20
  54.9 51.3 %collective-permute-start.3 = (bf16[32,2,44,128]{3,0,2,1:T(8,128)(2,1)}, bf16[32,2,44,128]{3,0,2,1:T(8,128)(2,1)}, u32[]{:S(2)}, u32[]{:S(2)}) collective-permute-start(bf16[32,2,44,128]{3,0,2,1:T(8,128)(2,1)} %copy.87), channel_id=1, source_target_pairs={{0,224},{32,0},{64,32},{96,64},{128,96},{160,128},{192,160},{224,1... | collective-permute-start | bytes 2162696 | tf_op jit(solution)/shard_map/ppermute | solution.py:20
  69.1 68.5 %collective-permute-start.2 = (bf16[32,2,44,128]{3,0,2,1:T(8,128)(2,1)}, bf16[32,2,44,128]{3,0,2,1:T(8,128)(2,1)}, u32[]{:S(2)}, u32[]{:S(2)}) collective-permute-start(bf16[32,2,44,128]{3,0,2,1:T(8,128)(2,1)} %copy.75), channel_id=1, source_target_pairs={{0,160},{32,192},{64,224},{96,0},{128,32},{160,64},{192,96},{224,1... | collective-permute-start | bytes 2162696 | tf_op jit(solution)/shard_map/ppermute | solution.py:20
  72.3 67.6 %collective-permute-start.1 = (bf16[32,2,44,128]{3,0,2,1:T(8,128)(2,1)}, bf16[32,2,44,128]{3,0,2,1:T(8,128)(2,1)}, u32[]{:S(2)}, u32[]{:S(2)}) collective-permute-start(bf16[32,2,44,128]{3,0,2,1:T(8,128)(2,1)} %copy.75), channel_id=1, source_target_pairs={{0,192},{32,224},{64,0},{96,32},{128,64},{160,96},{192,128},{224,1... | collective-permute-start | bytes 2162696 | tf_op jit(solution)/shard_map/ppermute | solution.py:20
  76.0 3.7 %copy-start = (bf16[32,2,44,128]{3,0,2,1:T(8,128)(2,1)}, bf16[32,2,44,128]{3,0,2,1:T(8,128)(2,1)S(1)}, u32[]{:S(2)}) copy-start(bf16[32,2,44,128]{3,0,2,1:T(8,128)(2,1)S(1)} %collective-permute-done.5) | copy-start | bytes 2162692
  76.0 75.6 %collective-permute-start = (bf16[32,2,44,128]{3,0,2,1:T(8,128)(2,1)}, bf16[32,2,44,128]{3,0,2,1:T(8,128)(2,1)}, u32[]{:S(2)}, u32[]{:S(2)}) collective-permute-start(bf16[32,2,44,128]{3,0,2,1:T(8,128)(2,1)} %copy.75), channel_id=1, source_target_pairs={{0,224},{32,0},{64,32},{96,64},{128,96},{160,128},{192,160},{224,1... | collective-permute-start | bytes 2162696 | tf_op jit(solution)/shard_map/ppermute | solution.py:20
  102.5 65.5 %collective-permute-start.7 = (bf16[32,2,44,128]{3,0,2,1:T(8,128)(2,1)}, bf16[32,2,44,128]{3,0,2,1:T(8,128)(2,1)S(1)}, u32[]{:S(2)}, u32[]{:S(2)}) collective-permute-start(bf16[32,2,44,128]{3,0,2,1:T(8,128)(2,1)} %copy.87), channel_id=1, source_target_pairs={{0,128},{32,160},{64,192},{96,224},{1,129},{33,161},{65,193},{97,2... | collective-permute-start | bytes 2162696 | tf_op jit(solution)/shard_map/ppermute | solution.py:106
  106.3 62.5 %collective-permute-start.6 = (bf16[32,2,44,128]{3,0,2,1:T(8,128)(2,1)}, bf16[32,2,44,128]{3,0,2,1:T(8,128)(2,1)S(1)}, u32[]{:S(2)}, u32[]{:S(2)}) collective-permute-start(bf16[32,2,44,128]{3,0,2,1:T(8,128)(2,1)} %copy.75), channel_id=1, source_target_pairs={{128,0},{160,32},{192,64},{224,96},{129,1},{161,33},{193,65},{225,... | collective-permute-start | bytes 2162696 | tf_op jit(solution)/shard_map/ppermute | solution.py:106
  109.3 8.6 %copy-start.1 = (bf16[32,2,44,128]{3,0,2,1:T(8,128)(2,1)S(1)}, bf16[32,2,44,128]{3,0,2,1:T(8,128)(2,1)}, u32[]{:S(2)}) copy-start(bf16[32,2,44,128]{3,0,2,1:T(8,128)(2,1)} %copy-done) | copy-start | bytes 2162692
  123.5 12.8 %copy-start.3 = (f32[1,128,256]{2,1,0:T(8,128)S(1)}, f32[1,128,256]{2,1,0:T(8,128)}, u32[]{:S(2)}) copy-start(f32[1,128,256]{2,1,0:T(8,128)} %shard_map.45) | copy-start | bytes 393220
  127.8 8.5 %copy-start.4 = (f32[1,128,256]{2,1,0:T(8,128)S(1)}, f32[1,128,256]{2,1,0:T(8,128)}, u32[]{:S(2)}) copy-start(f32[1,128,256]{2,1,0:T(8,128)} %shard_map.48) | copy-start | bytes 393220
  153.9 12.8 %copy-start.2 = (f32[1,128,256]{2,1,0:T(8,128)S(1)}, f32[1,128,256]{2,1,0:T(8,128)}, u32[]{:S(2)}) copy-start(f32[1,128,256]{2,1,0:T(8,128)} %shard_map.41) | copy-start | bytes 393220
  158.2 8.5 %copy-start.5 = (f32[1,128,256]{2,1,0:T(8,128)S(1)}, f32[1,128,256]{2,1,0:T(8,128)}, u32[]{:S(2)}) copy-start(f32[1,128,256]{2,1,0:T(8,128)} %shard_map.44) | copy-start | bytes 393220
  167.7 7.8 %copy-start.6 = (f32[2]{0:T(128)S(1)}, f32[2]{0:T(128)}, u32[]{:S(2)}) copy-start(f32[2]{0:T(128)} %constant.41.clone) | copy-start | bytes 28

commit v6 on v5

--- a/solution.py
+++ b/solution.py
@@ -11,7 +11,7 @@
 FREQS = 64
 FIRST_BIN = 32
 EPSILON = 1e-06
-GROUPS_PER_STEP = 8
+GROUPS_PER_STEP = 16
 
 
 def shifted(value, axis, steps):
@@ -105,7 +105,8 @@
             pairs = [(s, s + half_count) for s in range(half_count)]
         far_recv.append(lax.ppermute(blocks, "chan", pairs))
         mates = [blocks] + [shifted(blocks, "chan", -offset) for offset in range(1, half_count)]
-        near.append(jnp.concatenate([pair_stack(blocks, [mate]) for mate in mates], axis=0))
+        first = pair_stack(blocks, mates[:2])
+        near.append(jnp.concatenate([first] + [pair_stack(blocks, [mate]) for mate in mates[2:]], axis=0))
     cross_near = jnp.stack(near, axis=0).reshape(1, 2, half_count, chans, 2, chans)
 
     far_own = jnp.where(lower_half, own_h[0], own_h[1])

time: 180 us -> 178 us (0.989)
  Pallas kernels: 38.3 us -> 25.9 us
  waiting for transfers between devices: 64.5 us -> 75.8 us
    pallas_call x9 -> x7, Pallas kernels: 38.3 us -> 25.9 us  [pair_stack(): pl.pallas_call(functools.partial(pair_kernel, step), out_shape=jax.ShapeD...]
    ppermute x6, waiting for transfers between devices: 32.1 us -> 42 us  [shifted(): return lax.ppermute(value, axis, pairs)]
  transfers between devices with their start and end apart: 10 -> 10, of which waited for: 5 -> 7; matrix products, arithmetic and copies ran while one was open for 11% -> 11% of each run, Pallas kernels for 19% -> 13%
where the time goes in v6:
time: 178 us; the launch traced here: 177 us
  waiting for transfers between devices  75.8 us (43%)
  starting transfers between devices  39.1 us (22%)
  Pallas kernels  25.9 us (15%)
  local copies, waits for them, and re-layouts  20.2 us (11%)
  other arithmetic  8.32 us (5%)
  matrix products  6.78 us (4%)
    ppermute x6, waiting for transfers between devices, shifted(): return lax.ppermute(value, axis, pairs)  42 us
    all_to_all x2, waiting for transfers between devices, body(): lax.all_to_all(spectra[half], 'tm', split_axis=0, concat_axis=0, tiled=True)  31.6 us
    pallas_call x7, Pallas kernels, pair_stack(): pl.pallas_call(functools.partial(pair_kernel, step), out_shape=jax.ShapeD...  25.9 us
    ppermute x6, starting transfers between devices, shifted(): return lax.ppermute(value, axis, pairs)  18.8 us
    all_to_all x2, starting transfers between devices, body(): lax.all_to_all(spectra[half], 'tm', split_axis=0, concat_axis=0, tiled=True)  14.9 us
    ppermute x6, local copies, waits for them, and re-layouts, shifted(): return lax.ppermute(value, axis, pairs)  12.6 us
    dot_general x1, matrix products, whiten(): jnp.einsum('ks,wcs->kwc', taper_table, records, preferred_element_type=jn...  6.78 us
    ppermute x2, starting transfers between devices, body(): far_recv.append(lax.ppermute(blocks, 'chan', pairs))  5.4 us
  transfers between devices with their start and end apart: 10, of which 7 were waited for; matrix products, arithmetic and copies ran while one was open for 11% of the time, Pallas kernels for 13%

profile of v6, /device:TPU:2, one launch (start us, length us, event | category | flops | bytes accessed | tf_op | source)
XLA Modules:
  0.0 176.9 jit_solution(6838049646474842252)
XLA Ops:
  2.4 6.8 %multiply_reduce_fusion = (f32[44,128]{1,0:T(8,128)S(1)}, f32[128,44,128]{2,0,1:T(8,128)S(1)}) fusion(bf16[128,1024,1]{1,0,2:T(8,128)(2,1)S(1)} %reshape.182, bf16[44,128,1024]{2,1,0:T(8,128)(2,1)} %param.2), kind=kOutput, calls=%fused_computation.1 | convolution fusion | flops 1477831168 | bytes 14702592 | tf_op jit(solution)/shard_map/ks,wcs->kwc/dot_general | solution.py:39
  11.0 10.1 %all-to-all-start.1 = ((bf16[32,2,44,128]{3,1,2,0:T(2,128)(2,1)}), bf16[32,2,44,128]{3,1,2,0:T(2,128)(2,1)S(1)}, u32[]{:S(2)}, u32[]{:S(2)}) async-start(bf16[32,2,44,128]{3,1,2,0:T(2,128)(2,1)} %copy.79), calls=%async_computation.1 | async-start | bytes 1441792 | tf_op jit(solution)/shard_map/all_to_all | solution.py:100
  22.5 19.7 %all-to-all-done.1 = bf16[32,2,44,128]{3,1,2,0:T(2,128)(2,1)S(1)} async-done(((bf16[32,2,44,128]{3,1,2,0:T(2,128)(2,1)}), bf16[32,2,44,128]{3,1,2,0:T(2,128)(2,1)S(1)}, u32[]{:S(2)}, u32[]{:S(2)}) %all-to-all-start.1) | async-done | bytes 720928 | tf_op jit(solution)/shard_map/all_to_all | solution.py:100
  42.2 4.8 %all-to-all-start = ((bf16[32,2,44,128]{3,1,2,0:T(2,128)(2,1)}), bf16[32,2,44,128]{3,1,2,0:T(2,128)(2,1)S(1)}, u32[]{:S(2)}, u32[]{:S(2)}) async-start(bf16[32,2,44,128]{3,1,2,0:T(2,128)(2,1)} %copy.68), calls=%async_computation | async-start | bytes 1441792 | tf_op jit(solution)/shard_map/all_to_all | solution.py:100
  48.0 3.1 %collective-permute-start.5 = (bf16[32,2,44,128]{3,0,2,1:T(8,128)(2,1)}, bf16[32,2,44,128]{3,0,2,1:T(8,128)(2,1)S(1)}, u32[]{:S(2)}, u32[]{:S(2)}) collective-permute-start(bf16[32,2,44,128]{3,0,2,1:T(8,128)(2,1)} %copy.80), channel_id=1, source_target_pairs={{0,160},{32,192},{64,224},{96,0},{128,32},{160,64},{192,96},{224,1... | collective-permute-start | bytes 2162696 | tf_op jit(solution)/shard_map/ppermute | solution.py:20
  51.2 3.7 %collective-permute-start.4 = (bf16[32,2,44,128]{3,0,2,1:T(8,128)(2,1)}, bf16[32,2,44,128]{3,0,2,1:T(8,128)(2,1)}, u32[]{:S(2)}, u32[]{:S(2)}) collective-permute-start(bf16[32,2,44,128]{3,0,2,1:T(8,128)(2,1)} %copy.80), channel_id=1, source_target_pairs={{0,192},{32,224},{64,0},{96,32},{128,64},{160,96},{192,128},{224,1... | collective-permute-start | bytes 2162696 | tf_op jit(solution)/shard_map/ppermute | solution.py:20
  56.3 11.9 %all-to-all-done = bf16[32,2,44,128]{3,1,2,0:T(2,128)(2,1)S(1)} async-done(((bf16[32,2,44,128]{3,1,2,0:T(2,128)(2,1)}), bf16[32,2,44,128]{3,1,2,0:T(2,128)(2,1)S(1)}, u32[]{:S(2)}, u32[]{:S(2)}) %all-to-all-start) | async-done | bytes 720928 | tf_op jit(solution)/shard_map/all_to_all | solution.py:100
  69.1 3.1 %collective-permute-start.2 = (bf16[32,2,44,128]{3,0,2,1:T(8,128)(2,1)}, bf16[32,2,44,128]{3,0,2,1:T(8,128)(2,1)}, u32[]{:S(2)}, u32[]{:S(2)}) collective-permute-start(bf16[32,2,44,128]{3,0,2,1:T(8,128)(2,1)} %copy.69), channel_id=1, source_target_pairs={{0,160},{32,192},{64,224},{96,0},{128,32},{160,64},{192,96},{224,1... | collective-permute-start | bytes 2162696 | tf_op jit(solution)/shard_map/ppermute | solution.py:20
  72.3 3.7 %collective-permute-start.1 = (bf16[32,2,44,128]{3,0,2,1:T(8,128)(2,1)}, bf16[32,2,44,128]{3,0,2,1:T(8,128)(2,1)}, u32[]{:S(2)}, u32[]{:S(2)}) collective-permute-start(bf16[32,2,44,128]{3,0,2,1:T(8,128)(2,1)} %copy.69), channel_id=1, source_target_pairs={{0,192},{32,224},{64,0},{96,32},{128,64},{160,96},{192,128},{224,1... | collective-permute-start | bytes 2162696 | tf_op jit(solution)/shard_map/ppermute | solution.py:20
  76.0 3.7 %collective-permute-start = (bf16[32,2,44,128]{3,0,2,1:T(8,128)(2,1)}, bf16[32,2,44,128]{3,0,2,1:T(8,128)(2,1)}, u32[]{:S(2)}, u32[]{:S(2)}) collective-permute-start(bf16[32,2,44,128]{3,0,2,1:T(8,128)(2,1)} %copy.69), channel_id=1, source_target_pairs={{0,224},{32,0},{64,32},{96,64},{128,96},{160,128},{192,160},{224,1... | collective-permute-start | bytes 2162696 | tf_op jit(solution)/shard_map/ppermute | solution.py:20
  79.7 22.7 %collective-permute-done.4 = bf16[32,2,44,128]{3,0,2,1:T(8,128)(2,1)} collective-permute-done((bf16[32,2,44,128]{3,0,2,1:T(8,128)(2,1)}, bf16[32,2,44,128]{3,0,2,1:T(8,128)(2,1)}, u32[]{:S(2)}, u32[]{:S(2)}) %collective-permute-start.4) | collective-permute-done | bytes 720928 | tf_op jit(solution)/shard_map/ppermute | solution.py:20
  102.5 3.9 %collective-permute-start.7 = (bf16[32,2,44,128]{3,0,2,1:T(8,128)(2,1)}, bf16[32,2,44,128]{3,0,2,1:T(8,128)(2,1)S(1)}, u32[]{:S(2)}, u32[]{:S(2)}) collective-permute-start(bf16[32,2,44,128]{3,0,2,1:T(8,128)(2,1)} %copy.80), channel_id=1, source_target_pairs={{0,128},{32,160},{64,192},{96,224},{1,129},{33,161},{65,193},{97,2... | collective-permute-start | bytes 2162696 | tf_op jit(solution)/shard_map/ppermute | solution.py:106
  112.8 2.3 %copy.83.refs_1_ = bf16[32,2,44,128]{3,2,1,0:T(8,128)(2,1)} copy(bf16[32,2,44,128]{3,0,2,1:T(8,128)(2,1)} %collective-permute-done.3) | data formatting | bytes 1441792 | tf_op jit(solution)/shard_map/ppermute | solution.py:20
  115.1 3.3 %shard_map.46 = f32[1,128,256]{2,1,0:T(8,128)} custom-call(bf16[32,2,44,128]{3,2,1,0:T(8,128)(2,1)} %get-tuple-element.10.own_ref.refs_0_, bf16[32,2,44,128]{3,2,1,0:T(8,128)(2,1)} %copy.89.refs_0_), custom_call_target="tpu_custom_call" | custom-call | flops 369098752 | bytes 1572864 | tf_op jit(solution)/shard_map/pallas_call | solution.py:70
  118.4 3.3 %shard_map.45 = f32[1,128,256]{2,1,0:T(8,128)} custom-call(bf16[32,2,44,128]{3,2,1,0:T(8,128)(2,1)} %get-tuple-element.10.own_ref.refs_0_, bf16[32,2,44,128]{3,2,1,0:T(8,128)(2,1)} %copy.86.refs_0_), custom_call_target="tpu_custom_call" | custom-call | flops 369098752 | bytes 1572864 | tf_op jit(solution)/shard_map/pallas_call | solution.py:70
  121.8 4.6 %shard_map.44 = f32[2,128,256]{2,1,0:T(8,128)} custom-call(bf16[32,2,44,128]{3,2,1,0:T(8,128)(2,1)} %get-tuple-element.10.own_ref.refs_0_, bf16[32,2,44,128]{3,2,1,0:T(8,128)(2,1)} %get-tuple-element.10.own_ref.refs_0_, bf16[32,2,44,128]{3,2,1,0:T(8,128)(2,1)} %copy.83.refs_1_), custom_call_target="tpu_custom_call" | custom-call | flops 738197504 | bytes 2424832 | tf_op jit(solution)/shard_map/pallas_call | solution.py:70
  127.7 2.3 %copy.78.refs_0_ = bf16[32,2,44,128]{3,2,1,0:T(8,128)(2,1)} copy(bf16[32,2,44,128]{3,0,2,1:T(8,128)(2,1)} %collective-permute-done.2) | data formatting | bytes 1441792 | tf_op jit(solution)/shard_map/ppermute | solution.py:20
  130.0 6.1 %collective-permute-done.1 = bf16[32,2,44,128]{3,0,2,1:T(8,128)(2,1)} collective-permute-done((bf16[32,2,44,128]{3,0,2,1:T(8,128)(2,1)}, bf16[32,2,44,128]{3,0,2,1:T(8,128)(2,1)}, u32[]{:S(2)}, u32[]{:S(2)}) %collective-permute-start.1) | collective-permute-done | bytes 720928 | tf_op jit(solution)/shard_map/ppermute | solution.py:20
  138.4 13.2 %collective-permute-done = bf16[32,2,44,128]{3,0,2,1:T(8,128)(2,1)} collective-permute-done((bf16[32,2,44,128]{3,0,2,1:T(8,128)(2,1)}, bf16[32,2,44,128]{3,0,2,1:T(8,128)(2,1)}, u32[]{:S(2)}, u32[]{:S(2)}) %collective-permute-start) | collective-permute-done | bytes 720928 | tf_op jit(solution)/shard_map/ppermute | solution.py:20
  151.6 2.3 %copy.72.refs_1_ = bf16[32,2,44,128]{3,2,1,0:T(8,128)(2,1)} copy(bf16[32,2,44,128]{3,0,2,1:T(8,128)(2,1)} %collective-permute-done) | data formatting | bytes 1441792 | tf_op jit(solution)/shard_map/ppermute | solution.py:20
  153.9 3.3 %shard_map.43 = f32[1,128,256]{2,1,0:T(8,128)} custom-call(bf16[32,2,44,128]{3,2,1,0:T(8,128)(2,1)} %get-tuple-element.9.own_ref.refs_0_, bf16[32,2,44,128]{3,2,1,0:T(8,128)(2,1)} %copy.78.refs_0_), custom_call_target="tpu_custom_call" | custom-call | flops 369098752 | bytes 1572864 | tf_op jit(solution)/shard_map/pallas_call | solution.py:70
  157.2 3.3 %shard_map.42 = f32[1,128,256]{2,1,0:T(8,128)} custom-call(bf16[32,2,44,128]{3,2,1,0:T(8,128)(2,1)} %get-tuple-element.9.own_ref.refs_0_, bf16[32,2,44,128]{3,2,1,0:T(8,128)(2,1)} %copy.75.refs_0_), custom_call_target="tpu_custom_call" | custom-call | flops 369098752 | bytes 1572864 | tf_op jit(solution)/shard_map/pallas_call | solution.py:70
  160.5 4.6 %shard_map.41 = f32[2,128,256]{2,1,0:T(8,128)} custom-call(bf16[32,2,44,128]{3,2,1,0:T(8,128)(2,1)} %get-tuple-element.9.own_ref.refs_0_, bf16[32,2,44,128]{3,2,1,0:T(8,128)(2,1)} %get-tuple-element.9.own_ref.refs_0_, bf16[32,2,44,128]{3,2,1,0:T(8,128)(2,1)} %copy.72.refs_1_), custom_call_target="tpu_custom_call" | custom-call | flops 738197504 | bytes 2424832 | tf_op jit(solution)/shard_map/pallas_call | solution.py:70
  170.2 3.3 %shard_map.47 = f32[1,128,256]{2,1,0:T(8,128)} custom-call(bf16[32,2,44,128]{3,2,1,0:T(8,128)(2,1)} %get-tuple-element.8.own_ref, bf16[32,2,44,128]{3,2,1,0:T(8,128)(2,1)} %copy_select_fusion.refs_0_), custom_call_target="tpu_custom_call" | custom-call | flops 369098752 | bytes 1572864 | tf_op jit(solution)/shard_map/pallas_call | solution.py:70
  (44 shorter events, 26.7 us)
Async XLA Ops:
  11.0 31.2 %all-to-all-start.1 = ((bf16[32,2,44,128]{3,1,2,0:T(2,128)(2,1)}), bf16[32,2,44,128]{3,1,2,0:T(2,128)(2,1)S(1)}, u32[]{:S(2)}, u32[]{:S(2)}) async-start(bf16[32,2,44,128]{3,1,2,0:T(2,128)(2,1)} %copy.79), calls=%async_computation.1 | async-start | bytes 1441792 | tf_op jit(solution)/shard_map/all_to_all | solution.py:100
  42.2 25.9 %all-to-all-start = ((bf16[32,2,44,128]{3,1,2,0:T(2,128)(2,1)}), bf16[32,2,44,128]{3,1,2,0:T(2,128)(2,1)S(1)}, u32[]{:S(2)}, u32[]{:S(2)}) async-start(bf16[32,2,44,128]{3,1,2,0:T(2,128)(2,1)} %copy.68), calls=%async_computation | async-start | bytes 1441792 | tf_op jit(solution)/shard_map/all_to_all | solution.py:100
  48.0 28.0 %collective-permute-start.5 = (bf16[32,2,44,128]{3,0,2,1:T(8,128)(2,1)}, bf16[32,2,44,128]{3,0,2,1:T(8,128)(2,1)S(1)}, u32[]{:S(2)}, u32[]{:S(2)}) collective-permute-start(bf16[32,2,44,128]{3,0,2,1:T(8,128)(2,1)} %copy.80), channel_id=1, source_target_pairs={{0,160},{32,192},{64,224},{96,0},{128,32},{160,64},{192,96},{224,1... | collective-permute-start | bytes 2162696 | tf_op jit(solution)/shard_map/ppermute | solution.py:20
  51.2 51.3 %collective-permute-start.4 = (bf16[32,2,44,128]{3,0,2,1:T(8,128)(2,1)}, bf16[32,2,44,128]{3,0,2,1:T(8,128)(2,1)}, u32[]{:S(2)}, u32[]{:S(2)}) collective-permute-start(bf16[32,2,44,128]{3,0,2,1:T(8,128)(2,1)} %copy.80), channel_id=1, source_target_pairs={{0,192},{32,224},{64,0},{96,32},{128,64},{160,96},{192,128},{224,1... | collective-permute-start | bytes 2162696 | tf_op jit(solution)/shard_map/ppermute | solution.py:20
  54.9 51.5 %collective-permute-start.3 = (bf16[32,2,44,128]{3,0,2,1:T(8,128)(2,1)}, bf16[32,2,44,128]{3,0,2,1:T(8,128)(2,1)}, u32[]{:S(2)}, u32[]{:S(2)}) collective-permute-start(bf16[32,2,44,128]{3,0,2,1:T(8,128)(2,1)} %copy.80), channel_id=1, source_target_pairs={{0,224},{32,0},{64,32},{96,64},{128,96},{160,128},{192,160},{224,1... | collective-permute-start | bytes 2162696 | tf_op jit(solution)/shard_map/ppermute | solution.py:20
  69.1 58.6 %collective-permute-start.2 = (bf16[32,2,44,128]{3,0,2,1:T(8,128)(2,1)}, bf16[32,2,44,128]{3,0,2,1:T(8,128)(2,1)}, u32[]{:S(2)}, u32[]{:S(2)}) collective-permute-start(bf16[32,2,44,128]{3,0,2,1:T(8,128)(2,1)} %copy.69), channel_id=1, source_target_pairs={{0,160},{32,192},{64,224},{96,0},{128,32},{160,64},{192,96},{224,1... | collective-permute-start | bytes 2162696 | tf_op jit(solution)/shard_map/ppermute | solution.py:20
  72.3 63.8 %collective-permute-start.1 = (bf16[32,2,44,128]{3,0,2,1:T(8,128)(2,1)}, bf16[32,2,44,128]{3,0,2,1:T(8,128)(2,1)}, u32[]{:S(2)}, u32[]{:S(2)}) collective-permute-start(bf16[32,2,44,128]{3,0,2,1:T(8,128)(2,1)} %copy.69), channel_id=1, source_target_pairs={{0,192},{32,224},{64,0},{96,32},{128,64},{160,96},{192,128},{224,1... | collective-permute-start | bytes 2162696 | tf_op jit(solution)/shard_map/ppermute | solution.py:20
  76.0 3.7 %copy-start = (bf16[32,2,44,128]{3,0,2,1:T(8,128)(2,1)}, bf16[32,2,44,128]{3,0,2,1:T(8,128)(2,1)S(1)}, u32[]{:S(2)}) copy-start(bf16[32,2,44,128]{3,0,2,1:T(8,128)(2,1)S(1)} %collective-permute-done.5) | copy-start | bytes 2162692
  76.0 75.5 %collective-permute-start = (bf16[32,2,44,128]{3,0,2,1:T(8,128)(2,1)}, bf16[32,2,44,128]{3,0,2,1:T(8,128)(2,1)}, u32[]{:S(2)}, u32[]{:S(2)}) collective-permute-start(bf16[32,2,44,128]{3,0,2,1:T(8,128)(2,1)} %copy.69), channel_id=1, source_target_pairs={{0,224},{32,0},{64,32},{96,64},{128,96},{160,128},{192,160},{224,1... | collective-permute-start | bytes 2162696 | tf_op jit(solution)/shard_map/ppermute | solution.py:20
  102.5 6.9 %copy-start.1 = (bf16[32,2,44,128]{3,0,2,1:T(8,128)(2,1)S(1)}, bf16[32,2,44,128]{3,0,2,1:T(8,128)(2,1)}, u32[]{:S(2)}) copy-start(bf16[32,2,44,128]{3,0,2,1:T(8,128)(2,1)} %copy-done) | copy-start | bytes 2162692
  102.5 64.3 %collective-permute-start.7 = (bf16[32,2,44,128]{3,0,2,1:T(8,128)(2,1)}, bf16[32,2,44,128]{3,0,2,1:T(8,128)(2,1)S(1)}, u32[]{:S(2)}, u32[]{:S(2)}) collective-permute-start(bf16[32,2,44,128]{3,0,2,1:T(8,128)(2,1)} %copy.80), channel_id=1, source_target_pairs={{0,128},{32,160},{64,192},{96,224},{1,129},{33,161},{65,193},{97,2... | collective-permute-start | bytes 2162696 | tf_op jit(solution)/shard_map/ppermute | solution.py:106
  106.4 62.3 %collective-permute-start.6 = (bf16[32,2,44,128]{3,0,2,1:T(8,128)(2,1)}, bf16[32,2,44,128]{3,0,2,1:T(8,128)(2,1)S(1)}, u32[]{:S(2)}, u32[]{:S(2)}) collective-permute-start(bf16[32,2,44,128]{3,0,2,1:T(8,128)(2,1)} %copy.69), channel_id=1, source_target_pairs={{128,0},{160,32},{192,64},{224,96},{129,1},{161,33},{193,65},{225,... | collective-permute-start | bytes 2162696 | tf_op jit(solution)/shard_map/ppermute | solution.py:106
  118.4 8.0 %copy-start.2 = (f32[1,128,256]{2,1,0:T(8,128)S(1)}, f32[1,128,256]{2,1,0:T(8,128)}, u32[]{:S(2)}) copy-start(f32[1,128,256]{2,1,0:T(8,128)} %shard_map.46) | copy-start | bytes 393220
  157.2 8.0 %copy-start.3 = (f32[1,128,256]{2,1,0:T(8,128)S(1)}, f32[1,128,256]{2,1,0:T(8,128)}, u32[]{:S(2)}) copy-start(f32[1,128,256]{2,1,0:T(8,128)} %shard_map.43) | copy-start | bytes 393220
  166.2 8.4 %copy-start.4 = (f32[2]{0:T(128)S(1)}, f32[2]{0:T(128)}, u32[]{:S(2)}) copy-start(f32[2]{0:T(128)} %constant.41.clone) | copy-start | bytes 28

commit v7 on v6

--- a/solution.py
+++ b/solution.py
@@ -81,39 +81,73 @@
     )(own, *mates)
 
 
+def joint_permute(value, route):
+    chan_count, time_count = lax.axis_size("chan"), lax.axis_size("tm")
+    pairs = []
+    for chan in range(chan_count):
+        for time in range(time_count):
+            target = route(chan, time)
+            if target is not None:
+                pairs.append((chan * time_count + time, target[0] * time_count + target[1]))
+    return lax.ppermute(value, ("chan", "tm"), pairs)
+
+
 def body(records):
     window_count = records.shape[0]
     chans = records.shape[1]
     chan_count = lax.axis_size("chan")
     half_count = chan_count // 2
     time_count = lax.axis_size("tm")
+    half_time = time_count // 2
     taper_table = dft_table(records.shape[2], FREQS, FIRST_BIN)
     whitened = whiten(records, taper_table, float(window_count * time_count) ** (-0.25))
     half_freq = FREQS // 2
     lower_half = lax.axis_index("chan") < half_count
     spectra = whitened.reshape(2, half_freq, 2, window_count, chans)
 
+    def upper(chan):
+        return chan // half_count == 1
+
+    def flip(time):
+        return (time + half_time) % time_count
+
+    def mate_route(offset):
+        def route(chan, time):
+            target = (chan - offset) % chan_count
+            return (target, time if upper(target) == upper(chan) else flip(time))
+        return route
+
     near = []
     own_h = []
     far_recv = []
     for half in range(2):
-        blocks = lax.all_to_all(spectra[half], "tm", split_axis=0, concat_axis=0, tiled=True)
+        sent = jnp.where(lower_half, spectra[half], jnp.roll(spectra[half], half_time, axis=0))
+        blocks = lax.all_to_all(sent, "tm", split_axis=0, concat_axis=0, tiled=True)
         own_h.append(blocks)
-        if half == 0:
-            pairs = [(s, s - half_count) for s in range(half_count, chan_count)]
-        else:
-            pairs = [(s, s + half_count) for s in range(half_count)]
-        far_recv.append(lax.ppermute(blocks, "chan", pairs))
-        mates = [blocks] + [shifted(blocks, "chan", -offset) for offset in range(1, half_count)]
+
+        def far_route(chan, time, half=half):
+            if upper(chan) == (half == 0):
+                return ((chan + half_count) % chan_count, flip(time))
+            return None
+
+        far_recv.append(joint_permute(blocks, far_route))
+        mates = [blocks] + [joint_permute(blocks, mate_route(offset)) for offset in range(1, half_count)]
         first = pair_stack(blocks, mates[:2])
         near.append(jnp.concatenate([first] + [pair_stack(blocks, [mate]) for mate in mates[2:]], axis=0))
-    cross_near = jnp.stack(near, axis=0).reshape(1, 2, half_count, chans, 2, chans)
 
     far_own = jnp.where(lower_half, own_h[0], own_h[1])
     far_mate = jnp.where(lower_half, far_recv[0], far_recv[1])
     product = pair_stack(far_own, [far_mate]).reshape(chans, 2, chans)
     turned = product.transpose(2, 1, 0) * jnp.array([1.0, -1.0], jnp.float32)[None, :, None]
-    cross_far = jnp.where(lower_half, product, turned).reshape(1, chans, 2, chans)
+    far_part = jnp.where(lower_half, product, turned)
+
+    def home(chan, time):
+        return (chan, flip(time)) if upper(chan) else None
+
+    near = [jnp.where(lower_half, part, joint_permute(part, home)) for part in near]
+    far_part = jnp.where(lower_half, far_part, joint_permute(far_part, home))
+    cross_near = jnp.stack(near, axis=0).reshape(1, 2, half_count, chans, 2, chans)
+    cross_far = far_part.reshape(1, chans, 2, chans)
     return (cross_near, cross_far)
 
 

time: 178 us -> 212 us (1.19)
  the two profiles are of different devices: /device:TPU:2 before, /device:TPU:28 now
where the time goes in v7:
time: 212 us; the launch traced here: 211 us
  waiting for transfers between devices  101 us (48%)
  starting transfers between devices  41.5 us (20%)
  Pallas kernels  26 us (12%)
  local copies, waits for them, and re-layouts  25 us (12%)
  other arithmetic  9.71 us (5%)
  matrix products  6.78 us (3%)
    ppermute x11, waiting for transfers between devices, joint_permute(): return lax.ppermute(value, ('chan', 'tm'), pairs)  65.6 us
    all_to_all x2, waiting for transfers between devices, body(): blocks = lax.all_to_all(sent, 'tm', split_axis=0, concat_axis=0, tiled=True)  35.6 us
    ppermute x11, starting transfers between devices, joint_permute(): return lax.ppermute(value, ('chan', 'tm'), pairs)  28.1 us
    pallas_call x7, Pallas kernels, pair_stack(): pl.pallas_call(functools.partial(pair_kernel, step), out_shape=jax.ShapeD...  26 us
    ppermute x6, local copies, waits for them, and re-layouts, joint_permute(): return lax.ppermute(value, ('chan', 'tm'), pairs)  13.8 us
    all_to_all x2, starting transfers between devices, body(): blocks = lax.all_to_all(sent, 'tm', split_axis=0, concat_axis=0, tiled=True)  13.4 us
    dot_general x1, matrix products, whiten(): jnp.einsum('ks,wcs->kwc', taper_table, records, preferred_element_type=jn...  6.78 us
  transfers between devices with their start and end apart: 13, of which 6 were waited for; matrix products, arithmetic and copies ran while one was open for 12% of the time, Pallas kernels for 12%

profile of v7, /device:TPU:28, one launch (start us, length us, event | category | flops | bytes accessed | tf_op | source)
XLA Modules:
  0.0 211.1 jit_solution(1202437428522573200)
XLA Ops:
  2.4 6.8 %multiply_reduce_fusion = (f32[44,128]{1,0:T(8,128)S(1)}, f32[128,44,128]{2,0,1:T(8,128)S(1)}) fusion(bf16[128,1024,1]{1,0,2:T(8,128)(2,1)S(1)} %reshape.186, bf16[44,128,1024]{2,1,0:T(8,128)(2,1)} %param.2), kind=kOutput, calls=%fused_computation.1 | convolution fusion | flops 1477831168 | bytes 14702592 | tf_op jit(solution)/shard_map/ks,wcs->kwc/dot_general | solution.py:39
  14.0 9.5 %all-to-all-start.1 = ((bf16[32,2,44,128]{3,1,2,0:T(2,128)(2,1)}), bf16[32,2,44,128]{3,1,2,0:T(2,128)(2,1)S(1)}, u32[]{:S(2)}, u32[]{:S(2)}) async-start(bf16[32,2,44,128]{3,1,2,0:T(2,128)(2,1)} %copy.101), calls=%async_computation.1 | async-start | bytes 1441792 | tf_op jit(solution)/shard_map/all_to_all | solution.py:125
  25.8 19.7 %all-to-all-done.1 = bf16[32,2,44,128]{3,1,2,0:T(2,128)(2,1)S(1)} async-done(((bf16[32,2,44,128]{3,1,2,0:T(2,128)(2,1)}), bf16[32,2,44,128]{3,1,2,0:T(2,128)(2,1)S(1)}, u32[]{:S(2)}, u32[]{:S(2)}) %all-to-all-start.1) | async-done | bytes 720928 | tf_op jit(solution)/shard_map/all_to_all | solution.py:125
  45.5 3.9 %all-to-all-start = ((bf16[32,2,44,128]{3,1,2,0:T(2,128)(2,1)}), bf16[32,2,44,128]{3,1,2,0:T(2,128)(2,1)S(1)}, u32[]{:S(2)}, u32[]{:S(2)}) async-start(bf16[32,2,44,128]{3,1,2,0:T(2,128)(2,1)} %copy.87), calls=%async_computation | async-start | bytes 1441792 | tf_op jit(solution)/shard_map/all_to_all | solution.py:125
  50.6 2.4 %collective-permute-start.4 = (bf16[32,2,44,128]{3,0,2,1:T(8,128)(2,1)}, bf16[32,2,44,128]{3,0,2,1:T(8,128)(2,1)}, u32[]{:S(2)}, u32[]{:S(2)}) collective-permute-start(bf16[32,2,44,128]{3,0,2,1:T(8,128)(2,1)} %copy.102), channel_id=1, source_target_pairs={{0,240},{1,241},{2,242},{3,243},{4,244},{5,245},{6,246},{7,247},{8... | collective-permute-start | bytes 2162696 | tf_op jit(solution)/shard_map/ppermute | solution.py:92
  55.5 15.9 %all-to-all-done = bf16[32,2,44,128]{3,1,2,0:T(2,128)(2,1)S(1)} async-done(((bf16[32,2,44,128]{3,1,2,0:T(2,128)(2,1)}), bf16[32,2,44,128]{3,1,2,0:T(2,128)(2,1)S(1)}, u32[]{:S(2)}, u32[]{:S(2)}) %all-to-all-start) | async-done | bytes 720928 | tf_op jit(solution)/shard_map/all_to_all | solution.py:125
  76.3 2.3 %copy.111.refs_0_ = bf16[32,2,44,128]{3,2,1,0:T(8,128)(2,1)} copy(bf16[32,2,44,128]{3,0,2,1:T(8,128)(2,1)} %collective-permute-done.6) | data formatting | bytes 1441792 | tf_op jit(solution)/shard_map/ppermute | solution.py:92
  78.6 22.4 %collective-permute-done.4 = bf16[32,2,44,128]{3,0,2,1:T(8,128)(2,1)} collective-permute-done((bf16[32,2,44,128]{3,0,2,1:T(8,128)(2,1)}, bf16[32,2,44,128]{3,0,2,1:T(8,128)(2,1)}, u32[]{:S(2)}, u32[]{:S(2)}) %collective-permute-start.4) | collective-permute-done | bytes 720928 | tf_op jit(solution)/shard_map/ppermute | solution.py:92
  101.0 2.3 %copy.105.refs_1_ = bf16[32,2,44,128]{3,2,1,0:T(8,128)(2,1)} copy(bf16[32,2,44,128]{3,0,2,1:T(8,128)(2,1)} %collective-permute-done.4) | data formatting | bytes 1441792 | tf_op jit(solution)/shard_map/ppermute | solution.py:92
  103.3 4.7 %shard_map.44 = f32[2,128,256]{2,1,0:T(8,128)} custom-call(bf16[32,2,44,128]{3,2,1,0:T(8,128)(2,1)} %get-tuple-element.14.own_ref.refs_0_, bf16[32,2,44,128]{3,2,1,0:T(8,128)(2,1)} %get-tuple-element.14.own_ref.refs_0_, bf16[32,2,44,128]{3,2,1,0:T(8,128)(2,1)} %copy.105.refs_1_), custom_call_target="tpu_custom_call" | custom-call | flops 738197504 | bytes 2424832 | tf_op jit(solution)/shard_map/pallas_call | solution.py:70
  108.0 12.9 %collective-permute-start = (bf16[32,2,44,128]{3,0,2,1:T(8,128)(2,1)}, bf16[32,2,44,128]{3,0,2,1:T(8,128)(2,1)}, u32[]{:S(2)}, u32[]{:S(2)}) collective-permute-start(bf16[32,2,44,128]{3,0,2,1:T(8,128)(2,1)} %copy.88), channel_id=1, source_target_pairs={{0,240},{1,241},{2,242},{3,243},{4,244},{5,245},{6,246},{7,247},{8... | collective-permute-start | bytes 2162696 | tf_op jit(solution)/shard_map/ppermute | solution.py:92
  120.8 3.3 %shard_map.46 = f32[1,128,256]{2,1,0:T(8,128)} custom-call(bf16[32,2,44,128]{3,2,1,0:T(8,128)(2,1)} %get-tuple-element.14.own_ref.refs_0_, bf16[32,2,44,128]{3,2,1,0:T(8,128)(2,1)} %copy.111.refs_0_), custom_call_target="tpu_custom_call" | custom-call | flops 369098752 | bytes 1572864 | tf_op jit(solution)/shard_map/pallas_call | solution.py:70
  124.2 2.3 %copy.108.refs_0_ = bf16[32,2,44,128]{3,2,1,0:T(8,128)(2,1)} copy(bf16[32,2,44,128]{3,0,2,1:T(8,128)(2,1)} %collective-permute-done.5) | data formatting | bytes 1441792 | tf_op jit(solution)/shard_map/ppermute | solution.py:92
  126.5 3.3 %shard_map.45 = f32[1,128,256]{2,1,0:T(8,128)} custom-call(bf16[32,2,44,128]{3,2,1,0:T(8,128)(2,1)} %get-tuple-element.14.own_ref.refs_0_, bf16[32,2,44,128]{3,2,1,0:T(8,128)(2,1)} %copy.108.refs_0_), custom_call_target="tpu_custom_call" | custom-call | flops 369098752 | bytes 1572864 | tf_op jit(solution)/shard_map/pallas_call | solution.py:70
  134.2 3.3 %shard_map.47 = f32[1,128,256]{2,1,0:T(8,128)} custom-call(bf16[32,2,44,128]{3,2,1,0:T(8,128)(2,1)} %get-tuple-element.12.own_ref, bf16[32,2,44,128]{3,2,1,0:T(8,128)(2,1)} %copy_select_fusion.refs_0_), custom_call_target="tpu_custom_call" | custom-call | flops 369098752 | bytes 1572864 | tf_op jit(solution)/shard_map/pallas_call | solution.py:70
  138.7 3.9 %collective-permute-start.10 = (f32[128,2,128]{0,2,1:T(8,128)S(1)}, f32[128,2,128]{0,2,1:T(8,128)S(1)}, u32[]{:S(2)}, u32[]{:S(2)}) collective-permute-start(f32[128,2,128]{0,2,1:T(8,128)S(1)} %bitcast_select_fusion), channel_id=1, source_target_pairs={{128,144},{129,145},{130,146},{131,147},{132,148},{133,149},{134,1... | collective-permute-start | bytes 393224 | tf_op jit(solution)/shard_map/ppermute | solution.py:92
  144.9 2.5 %collective-permute-done.1 = bf16[32,2,44,128]{3,0,2,1:T(8,128)(2,1)} collective-permute-done((bf16[32,2,44,128]{3,0,2,1:T(8,128)(2,1)}, bf16[32,2,44,128]{3,0,2,1:T(8,128)(2,1)}, u32[]{:S(2)}, u32[]{:S(2)}) %collective-permute-start.1) | collective-permute-done | bytes 720928 | tf_op jit(solution)/shard_map/ppermute | solution.py:92
  147.5 2.3 %copy.94.refs_0_ = bf16[32,2,44,128]{3,2,1,0:T(8,128)(2,1)} copy(bf16[32,2,44,128]{3,0,2,1:T(8,128)(2,1)} %collective-permute-done.1) | data formatting | bytes 1441792 | tf_op jit(solution)/shard_map/ppermute | solution.py:92
  149.8 29.7 %collective-permute-done = bf16[32,2,44,128]{3,0,2,1:T(8,128)(2,1)} collective-permute-done((bf16[32,2,44,128]{3,0,2,1:T(8,128)(2,1)}, bf16[32,2,44,128]{3,0,2,1:T(8,128)(2,1)}, u32[]{:S(2)}, u32[]{:S(2)}) %collective-permute-start) | collective-permute-done | bytes 720928 | tf_op jit(solution)/shard_map/ppermute | solution.py:92
  179.5 2.3 %copy.91.refs_1_ = bf16[32,2,44,128]{3,2,1,0:T(8,128)(2,1)} copy(bf16[32,2,44,128]{3,0,2,1:T(8,128)(2,1)} %collective-permute-done) | data formatting | bytes 1441792 | tf_op jit(solution)/shard_map/ppermute | solution.py:92
  181.8 3.3 %shard_map.43 = f32[1,128,256]{2,1,0:T(8,128)} custom-call(bf16[32,2,44,128]{3,2,1,0:T(8,128)(2,1)} %get-tuple-element.13.own_ref.refs_0_, bf16[32,2,44,128]{3,2,1,0:T(8,128)(2,1)} %copy.97.refs_0_), custom_call_target="tpu_custom_call" | custom-call | flops 369098752 | bytes 1572864 | tf_op jit(solution)/shard_map/pallas_call | solution.py:70
  185.1 3.4 %shard_map.42 = f32[1,128,256]{2,1,0:T(8,128)} custom-call(bf16[32,2,44,128]{3,2,1,0:T(8,128)(2,1)} %get-tuple-element.13.own_ref.refs_0_, bf16[32,2,44,128]{3,2,1,0:T(8,128)(2,1)} %copy.94.refs_0_), custom_call_target="tpu_custom_call" | custom-call | flops 369098752 | bytes 1572864 | tf_op jit(solution)/shard_map/pallas_call | solution.py:70
  188.5 4.6 %shard_map.41 = f32[2,128,256]{2,1,0:T(8,128)} custom-call(bf16[32,2,44,128]{3,2,1,0:T(8,128)(2,1)} %get-tuple-element.13.own_ref.refs_0_, bf16[32,2,44,128]{3,2,1,0:T(8,128)(2,1)} %get-tuple-element.13.own_ref.refs_0_, bf16[32,2,44,128]{3,2,1,0:T(8,128)(2,1)} %copy.91.refs_1_), custom_call_target="tpu_custom_call" | custom-call | flops 738197504 | bytes 2424832 | tf_op jit(solution)/shard_map/pallas_call | solution.py:70
  198.3 10.9 %collective-permute-done.3 = f32[4,128,256]{2,1,0:T(8,128)S(1)} collective-permute-done((f32[4,128,256]{2,1,0:T(8,128)S(1)}, f32[4,128,256]{2,1,0:T(8,128)S(1)}, u32[]{:S(2)}, u32[]{:S(2)}) %collective-permute-start.3) | collective-permute-done | bytes 524320 | tf_op jit(solution)/shard_map/ppermute | solution.py:92
  (66 shorter events, 32.1 us)
Async XLA Ops:
  14.0 31.5 %all-to-all-start.1 = ((bf16[32,2,44,128]{3,1,2,0:T(2,128)(2,1)}), bf16[32,2,44,128]{3,1,2,0:T(2,128)(2,1)S(1)}, u32[]{:S(2)}, u32[]{:S(2)}) async-start(bf16[32,2,44,128]{3,1,2,0:T(2,128)(2,1)} %copy.101), calls=%async_computation.1 | async-start | bytes 1441792 | tf_op jit(solution)/shard_map/all_to_all | solution.py:125
  45.5 25.9 %all-to-all-start = ((bf16[32,2,44,128]{3,1,2,0:T(2,128)(2,1)}), bf16[32,2,44,128]{3,1,2,0:T(2,128)(2,1)S(1)}, u32[]{:S(2)}, u32[]{:S(2)}) async-start(bf16[32,2,44,128]{3,1,2,0:T(2,128)(2,1)} %copy.87), calls=%async_computation | async-start | bytes 1441792 | tf_op jit(solution)/shard_map/all_to_all | solution.py:125
  50.4 25.6 %collective-permute-start.6 = (bf16[32,2,44,128]{3,0,2,1:T(8,128)(2,1)}, bf16[32,2,44,128]{3,0,2,1:T(8,128)(2,1)}, u32[]{:S(2)}, u32[]{:S(2)}) collective-permute-start(bf16[32,2,44,128]{3,0,2,1:T(8,128)(2,1)} %copy.102), channel_id=1, source_target_pairs={{0,176},{1,177},{2,178},{3,179},{4,180},{5,181},{6,182},{7,183},{8... | collective-permute-start | bytes 2162696 | tf_op jit(solution)/shard_map/ppermute | solution.py:92
  50.6 50.3 %collective-permute-start.4 = (bf16[32,2,44,128]{3,0,2,1:T(8,128)(2,1)}, bf16[32,2,44,128]{3,0,2,1:T(8,128)(2,1)}, u32[]{:S(2)}, u32[]{:S(2)}) collective-permute-start(bf16[32,2,44,128]{3,0,2,1:T(8,128)(2,1)} %copy.102), channel_id=1, source_target_pairs={{0,240},{1,241},{2,242},{3,243},{4,244},{5,245},{6,246},{7,247},{8... | collective-permute-start | bytes 2162696 | tf_op jit(solution)/shard_map/ppermute | solution.py:92
  53.0 55.0 %collective-permute-start.5 = (bf16[32,2,44,128]{3,0,2,1:T(8,128)(2,1)}, bf16[32,2,44,128]{3,0,2,1:T(8,128)(2,1)}, u32[]{:S(2)}, u32[]{:S(2)}) collective-permute-start(bf16[32,2,44,128]{3,0,2,1:T(8,128)(2,1)} %copy.102), channel_id=1, source_target_pairs={{0,208},{1,209},{2,210},{3,211},{4,212},{5,213},{6,214},{7,215},{8... | collective-permute-start | bytes 2162696 | tf_op jit(solution)/shard_map/ppermute | solution.py:92
  54.2 76.5 %collective-permute-start.9 = (bf16[32,2,44,128]{3,0,2,1:T(8,128)(2,1)}, bf16[32,2,44,128]{3,0,2,1:T(8,128)(2,1)S(1)}, u32[]{:S(2)}, u32[]{:S(2)}) collective-permute-start(bf16[32,2,44,128]{3,0,2,1:T(8,128)(2,1)} %copy.102), channel_id=1, source_target_pairs={{0,144},{1,145},{2,146},{3,147},{4,148},{5,149},{6,150},{7,151},{8... | collective-permute-start | bytes 2162696 | tf_op jit(solution)/shard_map/ppermute | solution.py:92
  72.4 60.3 %collective-permute-start.8 = (bf16[32,2,44,128]{3,0,2,1:T(8,128)(2,1)}, bf16[32,2,44,128]{3,0,2,1:T(8,128)(2,1)S(1)}, u32[]{:S(2)}, u32[]{:S(2)}) collective-permute-start(bf16[32,2,44,128]{3,0,2,1:T(8,128)(2,1)} %copy.88), channel_id=1, source_target_pairs={{128,16},{129,17},{130,18},{131,19},{132,20},{133,21},{134,22},{13... | collective-permute-start | bytes 2162696 | tf_op jit(solution)/shard_map/ppermute | solution.py:92
  76.1 66.6 %collective-permute-start.2 = (bf16[32,2,44,128]{3,0,2,1:T(8,128)(2,1)}, bf16[32,2,44,128]{3,0,2,1:T(8,128)(2,1)}, u32[]{:S(2)}, u32[]{:S(2)}) collective-permute-start(bf16[32,2,44,128]{3,0,2,1:T(8,128)(2,1)} %copy.88), channel_id=1, source_target_pairs={{0,176},{1,177},{2,178},{3,179},{4,180},{5,181},{6,182},{7,183},{8... | collective-permute-start | bytes 2162696 | tf_op jit(solution)/shard_map/ppermute | solution.py:92
  101.0 46.5 %collective-permute-start.1 = (bf16[32,2,44,128]{3,0,2,1:T(8,128)(2,1)}, bf16[32,2,44,128]{3,0,2,1:T(8,128)(2,1)}, u32[]{:S(2)}, u32[]{:S(2)}) collective-permute-start(bf16[32,2,44,128]{3,0,2,1:T(8,128)(2,1)} %copy.88), channel_id=1, source_target_pairs={{0,208},{1,209},{2,210},{3,211},{4,212},{5,213},{6,214},{7,215},{8... | collective-permute-start | bytes 2162696 | tf_op jit(solution)/shard_map/ppermute | solution.py:92
  108.0 21.8 %copy-start.4 = (f32[2,128,256]{2,1,0:T(8,128)S(1)}, f32[2,128,256]{2,1,0:T(8,128)}, u32[]{:S(2)}) copy-start(f32[2,128,256]{2,1,0:T(8,128)} %shard_map.44) | copy-start | bytes 786436
  108.0 71.5 %collective-permute-start = (bf16[32,2,44,128]{3,0,2,1:T(8,128)(2,1)}, bf16[32,2,44,128]{3,0,2,1:T(8,128)(2,1)}, u32[]{:S(2)}, u32[]{:S(2)}) collective-permute-start(bf16[32,2,44,128]{3,0,2,1:T(8,128)(2,1)} %copy.88), channel_id=1, source_target_pairs={{0,240},{1,241},{2,242},{3,243},{4,244},{5,245},{6,246},{7,247},{8... | collective-permute-start | bytes 2162696 | tf_op jit(solution)/shard_map/ppermute | solution.py:92
  124.2 5.6 %copy-start = (f32[1,128,256]{2,1,0:T(8,128)S(1)}, f32[1,128,256]{2,1,0:T(8,128)}, u32[]{:S(2)}) copy-start(f32[1,128,256]{2,1,0:T(8,128)} %shard_map.46) | copy-start | bytes 393220
  129.8 8.8 %copy-start.6 = (f32[2]{0:T(128)S(1)}, f32[2]{0:T(128)}, u32[]{:S(2)}) copy-start(f32[2]{0:T(128)} %constant.41.clone) | copy-start | bytes 28
  130.8 66.2 %collective-permute-start.7 = (f32[4,128,256]{2,1,0:T(8,128)S(1)}, f32[4,128,256]{2,1,0:T(8,128)}, u32[]{:S(2)}, u32[]{:S(2)}) collective-permute-start(f32[4,128,256]{2,1,0:T(8,128)S(1)} %pad_maximum_fusion.2), channel_id=1, source_target_pairs={{128,144},{129,145},{130,146},{131,147},{132,148},{133,149},{134,1... | collective-permute-start | bytes 1572872 | tf_op jit(solution)/shard_map/ppermute | solution.py:92
  138.7 57.4 %collective-permute-start.10 = (f32[128,2,128]{0,2,1:T(8,128)S(1)}, f32[128,2,128]{0,2,1:T(8,128)S(1)}, u32[]{:S(2)}, u32[]{:S(2)}) collective-permute-start(f32[128,2,128]{0,2,1:T(8,128)S(1)} %bitcast_select_fusion), channel_id=1, source_target_pairs={{128,144},{129,145},{130,146},{131,147},{132,148},{133,149},{134,1... | collective-permute-start | bytes 393224 | tf_op jit(solution)/shard_map/ppermute | solution.py:92
  185.1 8.0 %copy-start.2 = (f32[1,128,256]{2,1,0:T(8,128)S(1)}, f32[1,128,256]{2,1,0:T(8,128)}, u32[]{:S(2)}) copy-start(f32[1,128,256]{2,1,0:T(8,128)} %shard_map.43) | copy-start | bytes 393220
  185.1 11.8 %copy-start.1 = (f32[1,128,256]{2,1,0:T(8,128)S(1)}, f32[1,128,256]{2,1,0:T(8,128)}, u32[]{:S(2)}) copy-start(f32[1,128,256]{2,1,0:T(8,128)} %shard_map.45) | copy-start | bytes 393220
  188.5 20.8 %copy-start.3 = (f32[1,128,256]{2,1,0:T(8,128)S(1)}, f32[1,128,256]{2,1,0:T(8,128)}, u32[]{:S(2)}) copy-start(f32[1,128,256]{2,1,0:T(8,128)} %shard_map.42) | copy-start | bytes 393220
  193.1 16.2 %copy-start.5 = (f32[2,128,256]{2,1,0:T(8,128)S(1)}, f32[2,128,256]{2,1,0:T(8,128)}, u32[]{:S(2)}) copy-start(f32[2,128,256]{2,1,0:T(8,128)} %shard_map.41) | copy-start | bytes 786436
  194.2 15.1 %collective-permute-start.3 = (f32[4,128,256]{2,1,0:T(8,128)S(1)}, f32[4,128,256]{2,1,0:T(8,128)S(1)}, u32[]{:S(2)}, u32[]{:S(2)}) collective-permute-start(f32[4,128,256]{2,1,0:T(8,128)S(1)} %pad_maximum_fusion.1), channel_id=1, source_target_pairs={{128,144},{129,145},{130,146},{131,147},{132,148},{133,149},{134,1... | collective-permute-start | bytes 1572872 | tf_op jit(solution)/shard_map/ppermute | solution.py:92

commit v8 on v6

--- a/solution.py
+++ b/solution.py
@@ -11,7 +11,8 @@
 FREQS = 64
 FIRST_BIN = 32
 EPSILON = 1e-06
-GROUPS_PER_STEP = 16
+GROUPS_PER_STEP = 32
+UNROLL = 8
 
 
 def shifted(value, axis, steps):
@@ -51,15 +52,20 @@
     def _():
         out_ref[...] = jnp.zeros_like(out_ref)
 
-    for group in range(group_count):
-        rows = jnp.concatenate([own_ref[group, 0], own_ref[group, 1]], axis=1)
-        for index, mate_ref in enumerate(mate_refs):
-            cols = jnp.concatenate([mate_ref[group, 0], mate_ref[group, 1]], axis=1)
-            prod = lax.dot_general(rows, cols, contract, preferred_element_type=jnp.float32)
-            real = prod[:chans, :chans] + prod[chans:, chans:]
-            imag = prod[chans:, :chans] - prod[:chans, chans:]
-            both = jnp.concatenate([real, imag], axis=1)
-            out_ref[index] += both.astype(jnp.bfloat16).astype(jnp.float32)
+    def chunk(index, carry):
+        for offset in range(UNROLL):
+            group = index * UNROLL + offset
+            rows = jnp.concatenate([own_ref[group, 0], own_ref[group, 1]], axis=1)
+            for slot, mate_ref in enumerate(mate_refs):
+                cols = jnp.concatenate([mate_ref[group, 0], mate_ref[group, 1]], axis=1)
+                prod = lax.dot_general(rows, cols, contract, preferred_element_type=jnp.float32)
+                real = prod[:chans, :chans] + prod[chans:, chans:]
+                imag = prod[chans:, :chans] - prod[:chans, chans:]
+                both = jnp.concatenate([real, imag], axis=1)
+                out_ref[slot] += both.astype(jnp.bfloat16).astype(jnp.float32)
+        return carry
+
+    lax.fori_loop(0, group_count // UNROLL, chunk, 0)
 
 
 def pair_stack(own, mates):

time: 178 us -> 180 us (1.011)
  Pallas kernels: 25.9 us -> 30.5 us
  waiting for transfers between devices: 75.8 us -> 71.8 us
    pallas_call x7, Pallas kernels: 25.9 us -> 30.5 us  [pair_stack(): pl.pallas_call(functools.partial(pair_kernel, step), out_shape=jax.ShapeD...]
    ppermute x6, waiting for transfers between devices: 42 us -> 40 us  [shifted(): return lax.ppermute(value, axis, pairs)]
    ppermute x2, waiting for transfers between devices: 2.23 us -> 0.25 us  [body(): far_recv.append(lax.ppermute(blocks, 'chan', pairs))]
  transfers between devices with their start and end apart: 10 -> 10, of which waited for: 7 -> 6; matrix products, arithmetic and copies ran while one was open for 11% -> 11% of each run, Pallas kernels for 13% -> 15%
where the time goes in v8:
time: 180 us; the launch traced here: 178 us
  waiting for transfers between devices  71.8 us (40%)
  starting transfers between devices  39.1 us (22%)
  Pallas kernels  30.5 us (17%)
  local copies, waits for them, and re-layouts  20.2 us (11%)
  other arithmetic  8.32 us (5%)
  matrix products  6.78 us (4%)
    ppermute x6, waiting for transfers between devices, shifted(): return lax.ppermute(value, axis, pairs)  40 us
    all_to_all x2, waiting for transfers between devices, body(): lax.all_to_all(spectra[half], 'tm', split_axis=0, concat_axis=0, tiled=True)  31.6 us
    pallas_call x7, Pallas kernels, pair_stack(): pl.pallas_call(functools.partial(pair_kernel, step), out_shape=jax.ShapeD...  30.5 us
    ppermute x6, starting transfers between devices, shifted(): return lax.ppermute(value, axis, pairs)  18.8 us
    all_to_all x2, starting transfers between devices, body(): lax.all_to_all(spectra[half], 'tm', split_axis=0, concat_axis=0, tiled=True)  14.9 us
    ppermute x6, local copies, waits for them, and re-layouts, shifted(): return lax.ppermute(value, axis, pairs)  12.6 us
    dot_general x1, matrix products, whiten(): jnp.einsum('ks,wcs->kwc', taper_table, records, preferred_element_type=jn...  6.78 us
    ppermute x2, starting transfers between devices, body(): far_recv.append(lax.ppermute(blocks, 'chan', pairs))  5.4 us
  transfers between devices with their start and end apart: 10, of which 6 were waited for; matrix products, arithmetic and copies ran while one was open for 11% of the time, Pallas kernels for 15%

profile of v8, /device:TPU:2, one launch (start us, length us, event | category | flops | bytes accessed | tf_op | source)
XLA Modules:
  0.0 177.6 jit_solution(513541421843396374)
XLA Ops:
  2.4 6.8 %multiply_reduce_fusion = (f32[44,128]{1,0:T(8,128)S(1)}, f32[128,44,128]{2,0,1:T(8,128)S(1)}) fusion(bf16[128,1024,1]{1,0,2:T(8,128)(2,1)S(1)} %reshape.182, bf16[44,128,1024]{2,1,0:T(8,128)(2,1)} %param.2), kind=kOutput, calls=%fused_computation.1 | convolution fusion | flops 1477831168 | bytes 14702592 | tf_op jit(solution)/shard_map/ks,wcs->kwc/dot_general | solution.py:40
  11.0 10.1 %all-to-all-start.1 = ((bf16[32,2,44,128]{3,1,2,0:T(2,128)(2,1)}), bf16[32,2,44,128]{3,1,2,0:T(2,128)(2,1)S(1)}, u32[]{:S(2)}, u32[]{:S(2)}) async-start(bf16[32,2,44,128]{3,1,2,0:T(2,128)(2,1)} %copy.79), calls=%async_computation.1 | async-start | bytes 1441792 | tf_op jit(solution)/shard_map/all_to_all | solution.py:106
  22.5 19.7 %all-to-all-done.1 = bf16[32,2,44,128]{3,1,2,0:T(2,128)(2,1)S(1)} async-done(((bf16[32,2,44,128]{3,1,2,0:T(2,128)(2,1)}), bf16[32,2,44,128]{3,1,2,0:T(2,128)(2,1)S(1)}, u32[]{:S(2)}, u32[]{:S(2)}) %all-to-all-start.1) | async-done | bytes 720928 | tf_op jit(solution)/shard_map/all_to_all | solution.py:106
  42.2 4.8 %all-to-all-start = ((bf16[32,2,44,128]{3,1,2,0:T(2,128)(2,1)}), bf16[32,2,44,128]{3,1,2,0:T(2,128)(2,1)S(1)}, u32[]{:S(2)}, u32[]{:S(2)}) async-start(bf16[32,2,44,128]{3,1,2,0:T(2,128)(2,1)} %copy.68), calls=%async_computation | async-start | bytes 1441792 | tf_op jit(solution)/shard_map/all_to_all | solution.py:106
  48.0 3.1 %collective-permute-start.5 = (bf16[32,2,44,128]{3,0,2,1:T(8,128)(2,1)}, bf16[32,2,44,128]{3,0,2,1:T(8,128)(2,1)S(1)}, u32[]{:S(2)}, u32[]{:S(2)}) collective-permute-start(bf16[32,2,44,128]{3,0,2,1:T(8,128)(2,1)} %copy.80), channel_id=1, source_target_pairs={{0,160},{32,192},{64,224},{96,0},{128,32},{160,64},{192,96},{224,1... | collective-permute-start | bytes 2162696 | tf_op jit(solution)/shard_map/ppermute | solution.py:21
  51.2 3.7 %collective-permute-start.4 = (bf16[32,2,44,128]{3,0,2,1:T(8,128)(2,1)}, bf16[32,2,44,128]{3,0,2,1:T(8,128)(2,1)}, u32[]{:S(2)}, u32[]{:S(2)}) collective-permute-start(bf16[32,2,44,128]{3,0,2,1:T(8,128)(2,1)} %copy.80), channel_id=1, source_target_pairs={{0,192},{32,224},{64,0},{96,32},{128,64},{160,96},{192,128},{224,1... | collective-permute-start | bytes 2162696 | tf_op jit(solution)/shard_map/ppermute | solution.py:21
  56.3 11.9 %all-to-all-done = bf16[32,2,44,128]{3,1,2,0:T(2,128)(2,1)S(1)} async-done(((bf16[32,2,44,128]{3,1,2,0:T(2,128)(2,1)}), bf16[32,2,44,128]{3,1,2,0:T(2,128)(2,1)S(1)}, u32[]{:S(2)}, u32[]{:S(2)}) %all-to-all-start) | async-done | bytes 720928 | tf_op jit(solution)/shard_map/all_to_all | solution.py:106
  69.1 3.1 %collective-permute-start.2 = (bf16[32,2,44,128]{3,0,2,1:T(8,128)(2,1)}, bf16[32,2,44,128]{3,0,2,1:T(8,128)(2,1)}, u32[]{:S(2)}, u32[]{:S(2)}) collective-permute-start(bf16[32,2,44,128]{3,0,2,1:T(8,128)(2,1)} %copy.69), channel_id=1, source_target_pairs={{0,160},{32,192},{64,224},{96,0},{128,32},{160,64},{192,96},{224,1... | collective-permute-start | bytes 2162696 | tf_op jit(solution)/shard_map/ppermute | solution.py:21
  72.3 3.7 %collective-permute-start.1 = (bf16[32,2,44,128]{3,0,2,1:T(8,128)(2,1)}, bf16[32,2,44,128]{3,0,2,1:T(8,128)(2,1)}, u32[]{:S(2)}, u32[]{:S(2)}) collective-permute-start(bf16[32,2,44,128]{3,0,2,1:T(8,128)(2,1)} %copy.69), channel_id=1, source_target_pairs={{0,192},{32,224},{64,0},{96,32},{128,64},{160,96},{192,128},{224,1... | collective-permute-start | bytes 2162696 | tf_op jit(solution)/shard_map/ppermute | solution.py:21
  76.0 3.7 %collective-permute-start = (bf16[32,2,44,128]{3,0,2,1:T(8,128)(2,1)}, bf16[32,2,44,128]{3,0,2,1:T(8,128)(2,1)}, u32[]{:S(2)}, u32[]{:S(2)}) collective-permute-start(bf16[32,2,44,128]{3,0,2,1:T(8,128)(2,1)} %copy.69), channel_id=1, source_target_pairs={{0,224},{32,0},{64,32},{96,64},{128,96},{160,128},{192,160},{224,1... | collective-permute-start | bytes 2162696 | tf_op jit(solution)/shard_map/ppermute | solution.py:21
  79.7 22.7 %collective-permute-done.4 = bf16[32,2,44,128]{3,0,2,1:T(8,128)(2,1)} collective-permute-done((bf16[32,2,44,128]{3,0,2,1:T(8,128)(2,1)}, bf16[32,2,44,128]{3,0,2,1:T(8,128)(2,1)}, u32[]{:S(2)}, u32[]{:S(2)}) %collective-permute-start.4) | collective-permute-done | bytes 720928 | tf_op jit(solution)/shard_map/ppermute | solution.py:21
  102.5 3.9 %collective-permute-start.7 = (bf16[32,2,44,128]{3,0,2,1:T(8,128)(2,1)}, bf16[32,2,44,128]{3,0,2,1:T(8,128)(2,1)S(1)}, u32[]{:S(2)}, u32[]{:S(2)}) collective-permute-start(bf16[32,2,44,128]{3,0,2,1:T(8,128)(2,1)} %copy.80), channel_id=1, source_target_pairs={{0,128},{32,160},{64,192},{96,224},{1,129},{33,161},{65,193},{97,2... | collective-permute-start | bytes 2162696 | tf_op jit(solution)/shard_map/ppermute | solution.py:112
  112.8 2.3 %copy.83.refs_1_ = bf16[32,2,44,128]{3,2,1,0:T(8,128)(2,1)} copy(bf16[32,2,44,128]{3,0,2,1:T(8,128)(2,1)} %collective-permute-done.3) | data formatting | bytes 1441792 | tf_op jit(solution)/shard_map/ppermute | solution.py:21
  115.1 4.0 %shard_map.46 = f32[1,128,256]{2,1,0:T(8,128)} custom-call(bf16[32,2,44,128]{3,2,1,0:T(8,128)(2,1)} %get-tuple-element.10.own_ref.refs_0_, bf16[32,2,44,128]{3,2,1,0:T(8,128)(2,1)} %copy.89.refs_0_), custom_call_target="tpu_custom_call" | custom-call | flops 369098752 | bytes 1572864 | tf_op jit(solution)/shard_map/pallas_call | solution.py:76
  119.1 4.0 %shard_map.45 = f32[1,128,256]{2,1,0:T(8,128)} custom-call(bf16[32,2,44,128]{3,2,1,0:T(8,128)(2,1)} %get-tuple-element.10.own_ref.refs_0_, bf16[32,2,44,128]{3,2,1,0:T(8,128)(2,1)} %copy.86.refs_0_), custom_call_target="tpu_custom_call" | custom-call | flops 369098752 | bytes 1572864 | tf_op jit(solution)/shard_map/pallas_call | solution.py:76
  123.1 5.3 %shard_map.44 = f32[2,128,256]{2,1,0:T(8,128)} custom-call(bf16[32,2,44,128]{3,2,1,0:T(8,128)(2,1)} %get-tuple-element.10.own_ref.refs_0_, bf16[32,2,44,128]{3,2,1,0:T(8,128)(2,1)} %get-tuple-element.10.own_ref.refs_0_, bf16[32,2,44,128]{3,2,1,0:T(8,128)(2,1)} %copy.83.refs_1_), custom_call_target="tpu_custom_call" | custom-call | flops 738197504 | bytes 2424832 | tf_op jit(solution)/shard_map/pallas_call | solution.py:76
  129.8 2.3 %copy.78.refs_0_ = bf16[32,2,44,128]{3,2,1,0:T(8,128)(2,1)} copy(bf16[32,2,44,128]{3,0,2,1:T(8,128)(2,1)} %collective-permute-done.2) | data formatting | bytes 1441792 | tf_op jit(solution)/shard_map/ppermute | solution.py:21
  132.0 4.1 %collective-permute-done.1 = bf16[32,2,44,128]{3,0,2,1:T(8,128)(2,1)} collective-permute-done((bf16[32,2,44,128]{3,0,2,1:T(8,128)(2,1)}, bf16[32,2,44,128]{3,0,2,1:T(8,128)(2,1)}, u32[]{:S(2)}, u32[]{:S(2)}) %collective-permute-start.1) | collective-permute-done | bytes 720928 | tf_op jit(solution)/shard_map/ppermute | solution.py:21
  138.4 13.2 %collective-permute-done = bf16[32,2,44,128]{3,0,2,1:T(8,128)(2,1)} collective-permute-done((bf16[32,2,44,128]{3,0,2,1:T(8,128)(2,1)}, bf16[32,2,44,128]{3,0,2,1:T(8,128)(2,1)}, u32[]{:S(2)}, u32[]{:S(2)}) %collective-permute-start) | collective-permute-done | bytes 720928 | tf_op jit(solution)/shard_map/ppermute | solution.py:21
  151.6 2.3 %copy.72.refs_1_ = bf16[32,2,44,128]{3,2,1,0:T(8,128)(2,1)} copy(bf16[32,2,44,128]{3,0,2,1:T(8,128)(2,1)} %collective-permute-done) | data formatting | bytes 1441792 | tf_op jit(solution)/shard_map/ppermute | solution.py:21
  153.9 4.0 %shard_map.43 = f32[1,128,256]{2,1,0:T(8,128)} custom-call(bf16[32,2,44,128]{3,2,1,0:T(8,128)(2,1)} %get-tuple-element.9.own_ref.refs_0_, bf16[32,2,44,128]{3,2,1,0:T(8,128)(2,1)} %copy.78.refs_0_), custom_call_target="tpu_custom_call" | custom-call | flops 369098752 | bytes 1572864 | tf_op jit(solution)/shard_map/pallas_call | solution.py:76
  157.8 4.0 %shard_map.42 = f32[1,128,256]{2,1,0:T(8,128)} custom-call(bf16[32,2,44,128]{3,2,1,0:T(8,128)(2,1)} %get-tuple-element.9.own_ref.refs_0_, bf16[32,2,44,128]{3,2,1,0:T(8,128)(2,1)} %copy.75.refs_0_), custom_call_target="tpu_custom_call" | custom-call | flops 369098752 | bytes 1572864 | tf_op jit(solution)/shard_map/pallas_call | solution.py:76
  161.8 5.3 %shard_map.41 = f32[2,128,256]{2,1,0:T(8,128)} custom-call(bf16[32,2,44,128]{3,2,1,0:T(8,128)(2,1)} %get-tuple-element.9.own_ref.refs_0_, bf16[32,2,44,128]{3,2,1,0:T(8,128)(2,1)} %get-tuple-element.9.own_ref.refs_0_, bf16[32,2,44,128]{3,2,1,0:T(8,128)(2,1)} %copy.72.refs_1_), custom_call_target="tpu_custom_call" | custom-call | flops 738197504 | bytes 2424832 | tf_op jit(solution)/shard_map/pallas_call | solution.py:76
  170.2 4.0 %shard_map.47 = f32[1,128,256]{2,1,0:T(8,128)} custom-call(bf16[32,2,44,128]{3,2,1,0:T(8,128)(2,1)} %get-tuple-element.8.own_ref, bf16[32,2,44,128]{3,2,1,0:T(8,128)(2,1)} %copy_select_fusion.refs_0_), custom_call_target="tpu_custom_call" | custom-call | flops 369098752 | bytes 1572864 | tf_op jit(solution)/shard_map/pallas_call | solution.py:76
  (44 shorter events, 24.7 us)
Async XLA Ops:
  11.0 31.2 %all-to-all-start.1 = ((bf16[32,2,44,128]{3,1,2,0:T(2,128)(2,1)}), bf16[32,2,44,128]{3,1,2,0:T(2,128)(2,1)S(1)}, u32[]{:S(2)}, u32[]{:S(2)}) async-start(bf16[32,2,44,128]{3,1,2,0:T(2,128)(2,1)} %copy.79), calls=%async_computation.1 | async-start | bytes 1441792 | tf_op jit(solution)/shard_map/all_to_all | solution.py:106
  42.2 25.9 %all-to-all-start = ((bf16[32,2,44,128]{3,1,2,0:T(2,128)(2,1)}), bf16[32,2,44,128]{3,1,2,0:T(2,128)(2,1)S(1)}, u32[]{:S(2)}, u32[]{:S(2)}) async-start(bf16[32,2,44,128]{3,1,2,0:T(2,128)(2,1)} %copy.68), calls=%async_computation | async-start | bytes 1441792 | tf_op jit(solution)/shard_map/all_to_all | solution.py:106
  48.0 28.0 %collective-permute-start.5 = (bf16[32,2,44,128]{3,0,2,1:T(8,128)(2,1)}, bf16[32,2,44,128]{3,0,2,1:T(8,128)(2,1)S(1)}, u32[]{:S(2)}, u32[]{:S(2)}) collective-permute-start(bf16[32,2,44,128]{3,0,2,1:T(8,128)(2,1)} %copy.80), channel_id=1, source_target_pairs={{0,160},{32,192},{64,224},{96,0},{128,32},{160,64},{192,96},{224,1... | collective-permute-start | bytes 2162696 | tf_op jit(solution)/shard_map/ppermute | solution.py:21
  51.2 51.3 %collective-permute-start.4 = (bf16[32,2,44,128]{3,0,2,1:T(8,128)(2,1)}, bf16[32,2,44,128]{3,0,2,1:T(8,128)(2,1)}, u32[]{:S(2)}, u32[]{:S(2)}) collective-permute-start(bf16[32,2,44,128]{3,0,2,1:T(8,128)(2,1)} %copy.80), channel_id=1, source_target_pairs={{0,192},{32,224},{64,0},{96,32},{128,64},{160,96},{192,128},{224,1... | collective-permute-start | bytes 2162696 | tf_op jit(solution)/shard_map/ppermute | solution.py:21
  54.9 51.5 %collective-permute-start.3 = (bf16[32,2,44,128]{3,0,2,1:T(8,128)(2,1)}, bf16[32,2,44,128]{3,0,2,1:T(8,128)(2,1)}, u32[]{:S(2)}, u32[]{:S(2)}) collective-permute-start(bf16[32,2,44,128]{3,0,2,1:T(8,128)(2,1)} %copy.80), channel_id=1, source_target_pairs={{0,224},{32,0},{64,32},{96,64},{128,96},{160,128},{192,160},{224,1... | collective-permute-start | bytes 2162696 | tf_op jit(solution)/shard_map/ppermute | solution.py:21
  69.1 60.6 %collective-permute-start.2 = (bf16[32,2,44,128]{3,0,2,1:T(8,128)(2,1)}, bf16[32,2,44,128]{3,0,2,1:T(8,128)(2,1)}, u32[]{:S(2)}, u32[]{:S(2)}) collective-permute-start(bf16[32,2,44,128]{3,0,2,1:T(8,128)(2,1)} %copy.69), channel_id=1, source_target_pairs={{0,160},{32,192},{64,224},{96,0},{128,32},{160,64},{192,96},{224,1... | collective-permute-start | bytes 2162696 | tf_op jit(solution)/shard_map/ppermute | solution.py:21
  72.3 63.8 %collective-permute-start.1 = (bf16[32,2,44,128]{3,0,2,1:T(8,128)(2,1)}, bf16[32,2,44,128]{3,0,2,1:T(8,128)(2,1)}, u32[]{:S(2)}, u32[]{:S(2)}) collective-permute-start(bf16[32,2,44,128]{3,0,2,1:T(8,128)(2,1)} %copy.69), channel_id=1, source_target_pairs={{0,192},{32,224},{64,0},{96,32},{128,64},{160,96},{192,128},{224,1... | collective-permute-start | bytes 2162696 | tf_op jit(solution)/shard_map/ppermute | solution.py:21
  76.0 3.7 %copy-start = (bf16[32,2,44,128]{3,0,2,1:T(8,128)(2,1)}, bf16[32,2,44,128]{3,0,2,1:T(8,128)(2,1)S(1)}, u32[]{:S(2)}) copy-start(bf16[32,2,44,128]{3,0,2,1:T(8,128)(2,1)S(1)} %collective-permute-done.5) | copy-start | bytes 2162692
  76.0 75.5 %collective-permute-start = (bf16[32,2,44,128]{3,0,2,1:T(8,128)(2,1)}, bf16[32,2,44,128]{3,0,2,1:T(8,128)(2,1)}, u32[]{:S(2)}, u32[]{:S(2)}) collective-permute-start(bf16[32,2,44,128]{3,0,2,1:T(8,128)(2,1)} %copy.69), channel_id=1, source_target_pairs={{0,224},{32,0},{64,32},{96,64},{128,96},{160,128},{192,160},{224,1... | collective-permute-start | bytes 2162696 | tf_op jit(solution)/shard_map/ppermute | solution.py:21
  102.5 6.9 %copy-start.1 = (bf16[32,2,44,128]{3,0,2,1:T(8,128)(2,1)S(1)}, bf16[32,2,44,128]{3,0,2,1:T(8,128)(2,1)}, u32[]{:S(2)}) copy-start(bf16[32,2,44,128]{3,0,2,1:T(8,128)(2,1)} %copy-done) | copy-start | bytes 2162692
  102.5 66.0 %collective-permute-start.7 = (bf16[32,2,44,128]{3,0,2,1:T(8,128)(2,1)}, bf16[32,2,44,128]{3,0,2,1:T(8,128)(2,1)S(1)}, u32[]{:S(2)}, u32[]{:S(2)}) collective-permute-start(bf16[32,2,44,128]{3,0,2,1:T(8,128)(2,1)} %copy.80), channel_id=1, source_target_pairs={{0,128},{32,160},{64,192},{96,224},{1,129},{33,161},{65,193},{97,2... | collective-permute-start | bytes 2162696 | tf_op jit(solution)/shard_map/ppermute | solution.py:112
  106.4 62.3 %collective-permute-start.6 = (bf16[32,2,44,128]{3,0,2,1:T(8,128)(2,1)}, bf16[32,2,44,128]{3,0,2,1:T(8,128)(2,1)S(1)}, u32[]{:S(2)}, u32[]{:S(2)}) collective-permute-start(bf16[32,2,44,128]{3,0,2,1:T(8,128)(2,1)} %copy.69), channel_id=1, source_target_pairs={{128,0},{160,32},{192,64},{224,96},{129,1},{161,33},{193,65},{225,... | collective-permute-start | bytes 2162696 | tf_op jit(solution)/shard_map/ppermute | solution.py:112
  119.1 9.3 %copy-start.2 = (f32[1,128,256]{2,1,0:T(8,128)S(1)}, f32[1,128,256]{2,1,0:T(8,128)}, u32[]{:S(2)}) copy-start(f32[1,128,256]{2,1,0:T(8,128)} %shard_map.46) | copy-start | bytes 393220
  157.8 9.3 %copy-start.3 = (f32[1,128,256]{2,1,0:T(8,128)S(1)}, f32[1,128,256]{2,1,0:T(8,128)}, u32[]{:S(2)}) copy-start(f32[1,128,256]{2,1,0:T(8,128)} %shard_map.43) | copy-start | bytes 393220
  168.2 7.1 %copy-start.4 = (f32[2]{0:T(128)S(1)}, f32[2]{0:T(128)}, u32[]{:S(2)}) copy-start(f32[2]{0:T(128)} %constant.41.clone) | copy-start | bytes 28

commit v9 on v6

--- a/solution.py
+++ b/solution.py
@@ -2,6 +2,8 @@
 import math
 
 import jax
+import ml_dtypes
+import numpy as np
 import jax.numpy as jnp
 from jax import lax
 from jax.experimental import pallas as pl
@@ -21,18 +23,15 @@
 
 
 def dft_table(sample_count, frequency_count, first_bin):
-    positions = jnp.arange(sample_count, dtype=jnp.int32)
-    bin_numbers = jnp.arange(frequency_count, dtype=jnp.int32) + first_bin
+    positions = np.arange(sample_count, dtype=np.int64)
+    bin_numbers = np.arange(frequency_count, dtype=np.int64) + first_bin
     phase_index = bin_numbers[:, None] * positions[None, :] % sample_count
-    phase_angle = 2.0 * math.pi / sample_count * phase_index.astype(jnp.float32)
-    hann_taper = 0.5 - 0.5 * jnp.cos(2.0 * math.pi / sample_count * positions.astype(jnp.float32))
-    cosine = hann_taper[None, :] * jnp.cos(phase_angle)
-    sine_part = -hann_taper[None, :] * jnp.sin(phase_angle)
-    return (
-        jnp.stack([cosine, sine_part], axis=1)
-        .reshape(2 * frequency_count, sample_count)
-        .astype(jnp.bfloat16)
-    )
+    phase_angle = 2.0 * math.pi / sample_count * phase_index
+    hann_taper = 0.5 - 0.5 * np.cos(2.0 * math.pi / sample_count * positions)
+    cosine = hann_taper[None, :] * np.cos(phase_angle)
+    sine_part = -hann_taper[None, :] * np.sin(phase_angle)
+    table = np.stack([cosine, sine_part], axis=1).reshape(2 * frequency_count, sample_count)
+    return jnp.asarray(table.astype(np.float32).astype(ml_dtypes.bfloat16))
 
 
 def whiten(records, taper_table, overall_scale):

time: 178 us -> 177 us (level)
  no operation moved by 1% of the time
where the time goes in v9:
time: 177 us; the launch traced here: 175 us
  waiting for transfers between devices  75.7 us (43%)
  starting transfers between devices  39.1 us (22%)
  Pallas kernels  25.9 us (15%)
  local copies, waits for them, and re-layouts  19.8 us (11%)
  other arithmetic  7.01 us (4%)
  matrix products  6.79 us (4%)
    ppermute x6, waiting for transfers between devices, shifted(): return lax.ppermute(value, axis, pairs)  42 us
    all_to_all x2, waiting for transfers between devices, body(): lax.all_to_all(spectra[half], 'tm', split_axis=0, concat_axis=0, tiled=True)  31.6 us
    pallas_call x7, Pallas kernels, pair_stack(): pl.pallas_call(functools.partial(pair_kernel, step), out_shape=jax.ShapeD...  25.9 us
    ppermute x6, starting transfers between devices, shifted(): return lax.ppermute(value, axis, pairs)  18.8 us
    all_to_all x2, starting transfers between devices, body(): lax.all_to_all(spectra[half], 'tm', split_axis=0, concat_axis=0, tiled=True)  14.9 us
    ppermute x6, local copies, waits for them, and re-layouts, shifted(): return lax.ppermute(value, axis, pairs)  12.6 us
    dot_general x1, matrix products, whiten(): jnp.einsum('ks,wcs->kwc', taper_table, records, preferred_element_type=jn...  6.79 us
    ppermute x2, starting transfers between devices, body(): far_recv.append(lax.ppermute(blocks, 'chan', pairs))  5.4 us
  transfers between devices with their start and end apart: 10, of which 7 were waited for; matrix products, arithmetic and copies ran while one was open for 11% of the time, Pallas kernels for 13%

profile of v9, /device:TPU:2, one launch (start us, length us, event | category | flops | bytes accessed | tf_op | source)
XLA Modules:
  0.0 175.2 jit_solution(9196972708339088443)
XLA Ops:
  0.6 6.8 %multiply_reduce_fusion = (f32[44,128]{1,0:T(8,128)S(1)}, f32[128,44,128]{2,0,1:T(8,128)S(1)}) fusion(bf16[128,1024,1]{1,0,2:T(8,128)(2,1)} %constant.24, bf16[44,128,1024]{2,1,0:T(8,128)(2,1)} %param.3), kind=kOutput, calls=%fused_computation.1 | convolution fusion | flops 1477831168 | bytes 14702592 | tf_op jit(solution)/shard_map/ks,wcs->kwc/dot_general | solution.py:38
  9.3 10.1 %all-to-all-start.1 = ((bf16[32,2,44,128]{3,1,2,0:T(2,128)(2,1)}), bf16[32,2,44,128]{3,1,2,0:T(2,128)(2,1)S(1)}, u32[]{:S(2)}, u32[]{:S(2)}) async-start(bf16[32,2,44,128]{3,1,2,0:T(2,128)(2,1)} %copy.48), calls=%async_computation.1 | async-start | bytes 1441792 | tf_op jit(solution)/shard_map/all_to_all | solution.py:99
  20.8 19.7 %all-to-all-done.1 = bf16[32,2,44,128]{3,1,2,0:T(2,128)(2,1)S(1)} async-done(((bf16[32,2,44,128]{3,1,2,0:T(2,128)(2,1)}), bf16[32,2,44,128]{3,1,2,0:T(2,128)(2,1)S(1)}, u32[]{:S(2)}, u32[]{:S(2)}) %all-to-all-start.1) | async-done | bytes 720928 | tf_op jit(solution)/shard_map/all_to_all | solution.py:99
  40.5 4.8 %all-to-all-start = ((bf16[32,2,44,128]{3,1,2,0:T(2,128)(2,1)}), bf16[32,2,44,128]{3,1,2,0:T(2,128)(2,1)S(1)}, u32[]{:S(2)}, u32[]{:S(2)}) async-start(bf16[32,2,44,128]{3,1,2,0:T(2,128)(2,1)} %copy.37), calls=%async_computation | async-start | bytes 1441792 | tf_op jit(solution)/shard_map/all_to_all | solution.py:99
  46.3 3.1 %collective-permute-start.5 = (bf16[32,2,44,128]{3,0,2,1:T(8,128)(2,1)}, bf16[32,2,44,128]{3,0,2,1:T(8,128)(2,1)S(1)}, u32[]{:S(2)}, u32[]{:S(2)}) collective-permute-start(bf16[32,2,44,128]{3,0,2,1:T(8,128)(2,1)} %copy.49), channel_id=1, source_target_pairs={{0,160},{32,192},{64,224},{96,0},{128,32},{160,64},{192,96},{224,1... | collective-permute-start | bytes 2162696 | tf_op jit(solution)/shard_map/ppermute | solution.py:22
  49.4 3.7 %collective-permute-start.4 = (bf16[32,2,44,128]{3,0,2,1:T(8,128)(2,1)}, bf16[32,2,44,128]{3,0,2,1:T(8,128)(2,1)}, u32[]{:S(2)}, u32[]{:S(2)}) collective-permute-start(bf16[32,2,44,128]{3,0,2,1:T(8,128)(2,1)} %copy.49), channel_id=1, source_target_pairs={{0,192},{32,224},{64,0},{96,32},{128,64},{160,96},{192,128},{224,1... | collective-permute-start | bytes 2162696 | tf_op jit(solution)/shard_map/ppermute | solution.py:22
  54.5 11.9 %all-to-all-done = bf16[32,2,44,128]{3,1,2,0:T(2,128)(2,1)S(1)} async-done(((bf16[32,2,44,128]{3,1,2,0:T(2,128)(2,1)}), bf16[32,2,44,128]{3,1,2,0:T(2,128)(2,1)S(1)}, u32[]{:S(2)}, u32[]{:S(2)}) %all-to-all-start) | async-done | bytes 720928 | tf_op jit(solution)/shard_map/all_to_all | solution.py:99
  67.4 3.1 %collective-permute-start.2 = (bf16[32,2,44,128]{3,0,2,1:T(8,128)(2,1)}, bf16[32,2,44,128]{3,0,2,1:T(8,128)(2,1)}, u32[]{:S(2)}, u32[]{:S(2)}) collective-permute-start(bf16[32,2,44,128]{3,0,2,1:T(8,128)(2,1)} %copy.38), channel_id=1, source_target_pairs={{0,160},{32,192},{64,224},{96,0},{128,32},{160,64},{192,96},{224,1... | collective-permute-start | bytes 2162696 | tf_op jit(solution)/shard_map/ppermute | solution.py:22
  70.6 3.7 %collective-permute-start.1 = (bf16[32,2,44,128]{3,0,2,1:T(8,128)(2,1)}, bf16[32,2,44,128]{3,0,2,1:T(8,128)(2,1)}, u32[]{:S(2)}, u32[]{:S(2)}) collective-permute-start(bf16[32,2,44,128]{3,0,2,1:T(8,128)(2,1)} %copy.38), channel_id=1, source_target_pairs={{0,192},{32,224},{64,0},{96,32},{128,64},{160,96},{192,128},{224,1... | collective-permute-start | bytes 2162696 | tf_op jit(solution)/shard_map/ppermute | solution.py:22
  74.3 3.7 %collective-permute-start = (bf16[32,2,44,128]{3,0,2,1:T(8,128)(2,1)}, bf16[32,2,44,128]{3,0,2,1:T(8,128)(2,1)}, u32[]{:S(2)}, u32[]{:S(2)}) collective-permute-start(bf16[32,2,44,128]{3,0,2,1:T(8,128)(2,1)} %copy.38), channel_id=1, source_target_pairs={{0,224},{32,0},{64,32},{96,64},{128,96},{160,128},{192,160},{224,1... | collective-permute-start | bytes 2162696 | tf_op jit(solution)/shard_map/ppermute | solution.py:22
  78.0 22.7 %collective-permute-done.4 = bf16[32,2,44,128]{3,0,2,1:T(8,128)(2,1)} collective-permute-done((bf16[32,2,44,128]{3,0,2,1:T(8,128)(2,1)}, bf16[32,2,44,128]{3,0,2,1:T(8,128)(2,1)}, u32[]{:S(2)}, u32[]{:S(2)}) %collective-permute-start.4) | collective-permute-done | bytes 720928 | tf_op jit(solution)/shard_map/ppermute | solution.py:22
  100.7 3.9 %collective-permute-start.7 = (bf16[32,2,44,128]{3,0,2,1:T(8,128)(2,1)}, bf16[32,2,44,128]{3,0,2,1:T(8,128)(2,1)S(1)}, u32[]{:S(2)}, u32[]{:S(2)}) collective-permute-start(bf16[32,2,44,128]{3,0,2,1:T(8,128)(2,1)} %copy.49), channel_id=1, source_target_pairs={{0,128},{32,160},{64,192},{96,224},{1,129},{33,161},{65,193},{97,2... | collective-permute-start | bytes 2162696 | tf_op jit(solution)/shard_map/ppermute | solution.py:105
  111.1 2.3 %copy.52.refs_1_ = bf16[32,2,44,128]{3,2,1,0:T(8,128)(2,1)} copy(bf16[32,2,44,128]{3,0,2,1:T(8,128)(2,1)} %collective-permute-done.3) | data formatting | bytes 1441792 | tf_op jit(solution)/shard_map/ppermute | solution.py:22
  113.4 3.3 %shard_map.55 = f32[1,128,256]{2,1,0:T(8,128)} custom-call(bf16[32,2,44,128]{3,2,1,0:T(8,128)(2,1)} %get-tuple-element.8.own_ref.refs_0_, bf16[32,2,44,128]{3,2,1,0:T(8,128)(2,1)} %copy.58.refs_0_), custom_call_target="tpu_custom_call" | custom-call | flops 369098752 | bytes 1572864 | tf_op jit(solution)/shard_map/pallas_call | solution.py:69
  116.7 3.4 %shard_map.54 = f32[1,128,256]{2,1,0:T(8,128)} custom-call(bf16[32,2,44,128]{3,2,1,0:T(8,128)(2,1)} %get-tuple-element.8.own_ref.refs_0_, bf16[32,2,44,128]{3,2,1,0:T(8,128)(2,1)} %copy.55.refs_0_), custom_call_target="tpu_custom_call" | custom-call | flops 369098752 | bytes 1572864 | tf_op jit(solution)/shard_map/pallas_call | solution.py:69
  120.1 4.5 %shard_map.53 = f32[2,128,256]{2,1,0:T(8,128)} custom-call(bf16[32,2,44,128]{3,2,1,0:T(8,128)(2,1)} %get-tuple-element.8.own_ref.refs_0_, bf16[32,2,44,128]{3,2,1,0:T(8,128)(2,1)} %get-tuple-element.8.own_ref.refs_0_, bf16[32,2,44,128]{3,2,1,0:T(8,128)(2,1)} %copy.52.refs_1_), custom_call_target="tpu_custom_call" | custom-call | flops 738197504 | bytes 2424832 | tf_op jit(solution)/shard_map/pallas_call | solution.py:69
  126.0 2.3 %copy.47.refs_0_ = bf16[32,2,44,128]{3,2,1,0:T(8,128)(2,1)} copy(bf16[32,2,44,128]{3,0,2,1:T(8,128)(2,1)} %collective-permute-done.2) | data formatting | bytes 1441792 | tf_op jit(solution)/shard_map/ppermute | solution.py:22
  128.3 6.1 %collective-permute-done.1 = bf16[32,2,44,128]{3,0,2,1:T(8,128)(2,1)} collective-permute-done((bf16[32,2,44,128]{3,0,2,1:T(8,128)(2,1)}, bf16[32,2,44,128]{3,0,2,1:T(8,128)(2,1)}, u32[]{:S(2)}, u32[]{:S(2)}) %collective-permute-start.1) | collective-permute-done | bytes 720928 | tf_op jit(solution)/shard_map/ppermute | solution.py:22
  136.7 13.2 %collective-permute-done = bf16[32,2,44,128]{3,0,2,1:T(8,128)(2,1)} collective-permute-done((bf16[32,2,44,128]{3,0,2,1:T(8,128)(2,1)}, bf16[32,2,44,128]{3,0,2,1:T(8,128)(2,1)}, u32[]{:S(2)}, u32[]{:S(2)}) %collective-permute-start) | collective-permute-done | bytes 720928 | tf_op jit(solution)/shard_map/ppermute | solution.py:22
  149.8 2.3 %copy.41.refs_1_ = bf16[32,2,44,128]{3,2,1,0:T(8,128)(2,1)} copy(bf16[32,2,44,128]{3,0,2,1:T(8,128)(2,1)} %collective-permute-done) | data formatting | bytes 1441792 | tf_op jit(solution)/shard_map/ppermute | solution.py:22
  152.2 3.3 %shard_map.52 = f32[1,128,256]{2,1,0:T(8,128)} custom-call(bf16[32,2,44,128]{3,2,1,0:T(8,128)(2,1)} %get-tuple-element.7.own_ref.refs_0_, bf16[32,2,44,128]{3,2,1,0:T(8,128)(2,1)} %copy.47.refs_0_), custom_call_target="tpu_custom_call" | custom-call | flops 369098752 | bytes 1572864 | tf_op jit(solution)/shard_map/pallas_call | solution.py:69
  155.5 3.4 %shard_map.51 = f32[1,128,256]{2,1,0:T(8,128)} custom-call(bf16[32,2,44,128]{3,2,1,0:T(8,128)(2,1)} %get-tuple-element.7.own_ref.refs_0_, bf16[32,2,44,128]{3,2,1,0:T(8,128)(2,1)} %copy.44.refs_0_), custom_call_target="tpu_custom_call" | custom-call | flops 369098752 | bytes 1572864 | tf_op jit(solution)/shard_map/pallas_call | solution.py:69
  158.8 4.7 %shard_map.50 = f32[2,128,256]{2,1,0:T(8,128)} custom-call(bf16[32,2,44,128]{3,2,1,0:T(8,128)(2,1)} %get-tuple-element.7.own_ref.refs_0_, bf16[32,2,44,128]{3,2,1,0:T(8,128)(2,1)} %get-tuple-element.7.own_ref.refs_0_, bf16[32,2,44,128]{3,2,1,0:T(8,128)(2,1)} %copy.41.refs_1_), custom_call_target="tpu_custom_call" | custom-call | flops 738197504 | bytes 2424832 | tf_op jit(solution)/shard_map/pallas_call | solution.py:69
  168.5 3.3 %shard_map.56 = f32[1,128,256]{2,1,0:T(8,128)} custom-call(bf16[32,2,44,128]{3,2,1,0:T(8,128)(2,1)} %get-tuple-element.6.own_ref, bf16[32,2,44,128]{3,2,1,0:T(8,128)(2,1)} %copy_select_fusion.refs_0_), custom_call_target="tpu_custom_call" | custom-call | flops 369098752 | bytes 1572864 | tf_op jit(solution)/shard_map/pallas_call | solution.py:69
  (38 shorter events, 24.9 us)
Async XLA Ops:
  9.3 31.2 %all-to-all-start.1 = ((bf16[32,2,44,128]{3,1,2,0:T(2,128)(2,1)}), bf16[32,2,44,128]{3,1,2,0:T(2,128)(2,1)S(1)}, u32[]{:S(2)}, u32[]{:S(2)}) async-start(bf16[32,2,44,128]{3,1,2,0:T(2,128)(2,1)} %copy.48), calls=%async_computation.1 | async-start | bytes 1441792 | tf_op jit(solution)/shard_map/all_to_all | solution.py:99
  40.5 25.9 %all-to-all-start = ((bf16[32,2,44,128]{3,1,2,0:T(2,128)(2,1)}), bf16[32,2,44,128]{3,1,2,0:T(2,128)(2,1)S(1)}, u32[]{:S(2)}, u32[]{:S(2)}) async-start(bf16[32,2,44,128]{3,1,2,0:T(2,128)(2,1)} %copy.37), calls=%async_computation | async-start | bytes 1441792 | tf_op jit(solution)/shard_map/all_to_all | solution.py:99
  46.3 28.0 %collective-permute-start.5 = (bf16[32,2,44,128]{3,0,2,1:T(8,128)(2,1)}, bf16[32,2,44,128]{3,0,2,1:T(8,128)(2,1)S(1)}, u32[]{:S(2)}, u32[]{:S(2)}) collective-permute-start(bf16[32,2,44,128]{3,0,2,1:T(8,128)(2,1)} %copy.49), channel_id=1, source_target_pairs={{0,160},{32,192},{64,224},{96,0},{128,32},{160,64},{192,96},{224,1... | collective-permute-start | bytes 2162696 | tf_op jit(solution)/shard_map/ppermute | solution.py:22
  49.4 51.3 %collective-permute-start.4 = (bf16[32,2,44,128]{3,0,2,1:T(8,128)(2,1)}, bf16[32,2,44,128]{3,0,2,1:T(8,128)(2,1)}, u32[]{:S(2)}, u32[]{:S(2)}) collective-permute-start(bf16[32,2,44,128]{3,0,2,1:T(8,128)(2,1)} %copy.49), channel_id=1, source_target_pairs={{0,192},{32,224},{64,0},{96,32},{128,64},{160,96},{192,128},{224,1... | collective-permute-start | bytes 2162696 | tf_op jit(solution)/shard_map/ppermute | solution.py:22
  53.2 51.5 %collective-permute-start.3 = (bf16[32,2,44,128]{3,0,2,1:T(8,128)(2,1)}, bf16[32,2,44,128]{3,0,2,1:T(8,128)(2,1)}, u32[]{:S(2)}, u32[]{:S(2)}) collective-permute-start(bf16[32,2,44,128]{3,0,2,1:T(8,128)(2,1)} %copy.49), channel_id=1, source_target_pairs={{0,224},{32,0},{64,32},{96,64},{128,96},{160,128},{192,160},{224,1... | collective-permute-start | bytes 2162696 | tf_op jit(solution)/shard_map/ppermute | solution.py:22
  67.4 58.6 %collective-permute-start.2 = (bf16[32,2,44,128]{3,0,2,1:T(8,128)(2,1)}, bf16[32,2,44,128]{3,0,2,1:T(8,128)(2,1)}, u32[]{:S(2)}, u32[]{:S(2)}) collective-permute-start(bf16[32,2,44,128]{3,0,2,1:T(8,128)(2,1)} %copy.38), channel_id=1, source_target_pairs={{0,160},{32,192},{64,224},{96,0},{128,32},{160,64},{192,96},{224,1... | collective-permute-start | bytes 2162696 | tf_op jit(solution)/shard_map/ppermute | solution.py:22
  70.6 63.8 %collective-permute-start.1 = (bf16[32,2,44,128]{3,0,2,1:T(8,128)(2,1)}, bf16[32,2,44,128]{3,0,2,1:T(8,128)(2,1)}, u32[]{:S(2)}, u32[]{:S(2)}) collective-permute-start(bf16[32,2,44,128]{3,0,2,1:T(8,128)(2,1)} %copy.38), channel_id=1, source_target_pairs={{0,192},{32,224},{64,0},{96,32},{128,64},{160,96},{192,128},{224,1... | collective-permute-start | bytes 2162696 | tf_op jit(solution)/shard_map/ppermute | solution.py:22
  74.3 3.7 %copy-start = (bf16[32,2,44,128]{3,0,2,1:T(8,128)(2,1)}, bf16[32,2,44,128]{3,0,2,1:T(8,128)(2,1)S(1)}, u32[]{:S(2)}) copy-start(bf16[32,2,44,128]{3,0,2,1:T(8,128)(2,1)S(1)} %collective-permute-done.5) | copy-start | bytes 2162692
  74.3 75.5 %collective-permute-start = (bf16[32,2,44,128]{3,0,2,1:T(8,128)(2,1)}, bf16[32,2,44,128]{3,0,2,1:T(8,128)(2,1)}, u32[]{:S(2)}, u32[]{:S(2)}) collective-permute-start(bf16[32,2,44,128]{3,0,2,1:T(8,128)(2,1)} %copy.38), channel_id=1, source_target_pairs={{0,224},{32,0},{64,32},{96,64},{128,96},{160,128},{192,160},{224,1... | collective-permute-start | bytes 2162696 | tf_op jit(solution)/shard_map/ppermute | solution.py:22
  100.7 6.9 %copy-start.1 = (bf16[32,2,44,128]{3,0,2,1:T(8,128)(2,1)S(1)}, bf16[32,2,44,128]{3,0,2,1:T(8,128)(2,1)}, u32[]{:S(2)}) copy-start(bf16[32,2,44,128]{3,0,2,1:T(8,128)(2,1)} %copy-done) | copy-start | bytes 2162692
  100.7 64.3 %collective-permute-start.7 = (bf16[32,2,44,128]{3,0,2,1:T(8,128)(2,1)}, bf16[32,2,44,128]{3,0,2,1:T(8,128)(2,1)S(1)}, u32[]{:S(2)}, u32[]{:S(2)}) collective-permute-start(bf16[32,2,44,128]{3,0,2,1:T(8,128)(2,1)} %copy.49), channel_id=1, source_target_pairs={{0,128},{32,160},{64,192},{96,224},{1,129},{33,161},{65,193},{97,2... | collective-permute-start | bytes 2162696 | tf_op jit(solution)/shard_map/ppermute | solution.py:105
  104.7 62.3 %collective-permute-start.6 = (bf16[32,2,44,128]{3,0,2,1:T(8,128)(2,1)}, bf16[32,2,44,128]{3,0,2,1:T(8,128)(2,1)S(1)}, u32[]{:S(2)}, u32[]{:S(2)}) collective-permute-start(bf16[32,2,44,128]{3,0,2,1:T(8,128)(2,1)} %copy.38), channel_id=1, source_target_pairs={{128,0},{160,32},{192,64},{224,96},{129,1},{161,33},{193,65},{225,... | collective-permute-start | bytes 2162696 | tf_op jit(solution)/shard_map/ppermute | solution.py:105
  116.7 7.9 %copy-start.2 = (f32[1,128,256]{2,1,0:T(8,128)S(1)}, f32[1,128,256]{2,1,0:T(8,128)}, u32[]{:S(2)}) copy-start(f32[1,128,256]{2,1,0:T(8,128)} %shard_map.55) | copy-start | bytes 393220
  155.5 8.1 %copy-start.3 = (f32[1,128,256]{2,1,0:T(8,128)S(1)}, f32[1,128,256]{2,1,0:T(8,128)}, u32[]{:S(2)}) copy-start(f32[1,128,256]{2,1,0:T(8,128)} %shard_map.52) | copy-start | bytes 393220
  164.6 8.3 %copy-start.4 = (f32[2]{0:T(128)S(1)}, f32[2]{0:T(128)}, u32[]{:S(2)}) copy-start(f32[2]{0:T(128)} %constant.22.clone) | copy-start | bytes 28

commit v10 on v9

--- a/solution.py
+++ b/solution.py
@@ -41,7 +41,7 @@
     return (spectra * factor[None]).astype(jnp.bfloat16)
 
 
-def pair_kernel(group_count, own_ref, *refs):
+def pair_kernel(group_count, turn, own_ref, *refs):
     mate_refs, out_ref = refs[:-1], refs[-1]
     chans = out_ref.shape[-2]
     contract = (((0,), (0,)), ((), ()))
@@ -60,14 +60,23 @@
             both = jnp.concatenate([real, imag], axis=1)
             out_ref[index] += both.astype(jnp.bfloat16).astype(jnp.float32)
 
+    if turn:
+        upper = lax.axis_index("chan") >= lax.axis_size("chan") // 2
 
-def pair_stack(own, mates):
+        @pl.when(jnp.logical_and(upper, pl.program_id(0) == pl.num_programs(0) - 1))
+        def _():
+            real = out_ref[0, :, :chans]
+            imag = out_ref[0, :, chans:]
+            out_ref[0] = jnp.concatenate([real.T, -imag.T], axis=1)
+
+
+def pair_stack(own, mates, turn=False):
     groups, _, width, chans = own.shape
     step = GROUPS_PER_STEP
     spec = pl.BlockSpec((step, 2, width, chans), lambda n: (n, 0, 0, 0))
     count = len(mates)
     return pl.pallas_call(
-        functools.partial(pair_kernel, step),
+        functools.partial(pair_kernel, step, turn),
         out_shape=jax.ShapeDtypeStruct((count, chans, 2 * chans), jnp.float32),
         grid=(groups // step,),
         in_specs=[spec] * (count + 1),
@@ -110,9 +119,7 @@
 
     far_own = jnp.where(lower_half, own_h[0], own_h[1])
     far_mate = jnp.where(lower_half, far_recv[0], far_recv[1])
-    product = pair_stack(far_own, [far_mate]).reshape(chans, 2, chans)
-    turned = product.transpose(2, 1, 0) * jnp.array([1.0, -1.0], jnp.float32)[None, :, None]
-    cross_far = jnp.where(lower_half, product, turned).reshape(1, chans, 2, chans)
+    cross_far = pair_stack(far_own, [far_mate], turn=True).reshape(1, chans, 2, chans)
     return (cross_near, cross_far)
 
 

time: 177 us -> 176 us (level)
  transfers between devices with their start and end apart: 10 -> 10, of which waited for: 7 -> 7; matrix products, arithmetic and copies ran while one was open for 11% -> 12% of each run, Pallas kernels for 13% -> 13%
where the time goes in v10:
time: 176 us; the launch traced here: 175 us
  waiting for transfers between devices  75.8 us (43%)
  starting transfers between devices  39.1 us (22%)
  Pallas kernels  25.8 us (15%)
  local copies, waits for them, and re-layouts  19.7 us (11%)
  other arithmetic  6.94 us (4%)
  matrix products  6.79 us (4%)
    ppermute x6, waiting for transfers between devices, shifted(): return lax.ppermute(value, axis, pairs)  41.9 us
    all_to_all x2, waiting for transfers between devices, body(): lax.all_to_all(spectra[half], 'tm', split_axis=0, concat_axis=0, tiled=True)  31.6 us
    pallas_call x7, Pallas kernels, pair_stack(): pl.pallas_call(functools.partial(pair_kernel, step, turn), out_shape=jax....  25.8 us
    ppermute x6, starting transfers between devices, shifted(): return lax.ppermute(value, axis, pairs)  18.8 us
    all_to_all x2, starting transfers between devices, body(): lax.all_to_all(spectra[half], 'tm', split_axis=0, concat_axis=0, tiled=True)  14.9 us
    ppermute x6, local copies, waits for them, and re-layouts, shifted(): return lax.ppermute(value, axis, pairs)  12.7 us
    dot_general x1, matrix products, whiten(): jnp.einsum('ks,wcs->kwc', taper_table, records, preferred_element_type=jn...  6.79 us
    ppermute x2, starting transfers between devices, body(): far_recv.append(lax.ppermute(blocks, 'chan', pairs))  5.41 us
  transfers between devices with their start and end apart: 10, of which 7 were waited for; matrix products, arithmetic and copies ran while one was open for 12% of the time, Pallas kernels for 13%

profile of v10, /device:TPU:2, one launch (start us, length us, event | category | flops | bytes accessed | tf_op | source)
XLA Modules:
  0.0 174.9 jit_solution(16684621968004693470)
XLA Ops:
  0.6 6.8 %multiply_reduce_fusion = (f32[44,128]{1,0:T(8,128)S(1)}, f32[128,44,128]{2,0,1:T(8,128)S(1)}) fusion(bf16[128,1024,1]{1,0,2:T(8,128)(2,1)} %constant.21, bf16[44,128,1024]{2,1,0:T(8,128)(2,1)} %param.2), kind=kOutput, calls=%fused_computation.1 | convolution fusion | flops 1477831168 | bytes 14702592 | tf_op jit(solution)/shard_map/ks,wcs->kwc/dot_general | solution.py:38
  9.3 10.1 %all-to-all-start.1 = ((bf16[32,2,44,128]{3,1,2,0:T(2,128)(2,1)}), bf16[32,2,44,128]{3,1,2,0:T(2,128)(2,1)S(1)}, u32[]{:S(2)}, u32[]{:S(2)}) async-start(bf16[32,2,44,128]{3,1,2,0:T(2,128)(2,1)} %copy.17), calls=%async_computation.1 | async-start | bytes 1441792 | tf_op jit(solution)/shard_map/all_to_all | solution.py:108
  20.8 19.8 %all-to-all-done.1 = bf16[32,2,44,128]{3,1,2,0:T(2,128)(2,1)S(1)} async-done(((bf16[32,2,44,128]{3,1,2,0:T(2,128)(2,1)}), bf16[32,2,44,128]{3,1,2,0:T(2,128)(2,1)S(1)}, u32[]{:S(2)}, u32[]{:S(2)}) %all-to-all-start.1) | async-done | bytes 720928 | tf_op jit(solution)/shard_map/all_to_all | solution.py:108
  40.5 4.8 %all-to-all-start = ((bf16[32,2,44,128]{3,1,2,0:T(2,128)(2,1)}), bf16[32,2,44,128]{3,1,2,0:T(2,128)(2,1)S(1)}, u32[]{:S(2)}, u32[]{:S(2)}) async-start(bf16[32,2,44,128]{3,1,2,0:T(2,128)(2,1)} %copy.6), calls=%async_computation | async-start | bytes 1441792 | tf_op jit(solution)/shard_map/all_to_all | solution.py:108
  46.3 3.1 %collective-permute-start.5 = (bf16[32,2,44,128]{3,0,2,1:T(8,128)(2,1)}, bf16[32,2,44,128]{3,0,2,1:T(8,128)(2,1)S(1)}, u32[]{:S(2)}, u32[]{:S(2)}) collective-permute-start(bf16[32,2,44,128]{3,0,2,1:T(8,128)(2,1)} %copy.18), channel_id=1, source_target_pairs={{0,160},{32,192},{64,224},{96,0},{128,32},{160,64},{192,96},{224,1... | collective-permute-start | bytes 2162696 | tf_op jit(solution)/shard_map/ppermute | solution.py:22
  49.4 3.7 %collective-permute-start.4 = (bf16[32,2,44,128]{3,0,2,1:T(8,128)(2,1)}, bf16[32,2,44,128]{3,0,2,1:T(8,128)(2,1)}, u32[]{:S(2)}, u32[]{:S(2)}) collective-permute-start(bf16[32,2,44,128]{3,0,2,1:T(8,128)(2,1)} %copy.18), channel_id=1, source_target_pairs={{0,192},{32,224},{64,0},{96,32},{128,64},{160,96},{192,128},{224,1... | collective-permute-start | bytes 2162696 | tf_op jit(solution)/shard_map/ppermute | solution.py:22
  54.5 11.9 %all-to-all-done = bf16[32,2,44,128]{3,1,2,0:T(2,128)(2,1)S(1)} async-done(((bf16[32,2,44,128]{3,1,2,0:T(2,128)(2,1)}), bf16[32,2,44,128]{3,1,2,0:T(2,128)(2,1)S(1)}, u32[]{:S(2)}, u32[]{:S(2)}) %all-to-all-start) | async-done | bytes 720928 | tf_op jit(solution)/shard_map/all_to_all | solution.py:108
  67.4 3.1 %collective-permute-start.2 = (bf16[32,2,44,128]{3,0,2,1:T(8,128)(2,1)}, bf16[32,2,44,128]{3,0,2,1:T(8,128)(2,1)}, u32[]{:S(2)}, u32[]{:S(2)}) collective-permute-start(bf16[32,2,44,128]{3,0,2,1:T(8,128)(2,1)} %copy.7), channel_id=1, source_target_pairs={{0,160},{32,192},{64,224},{96,0},{128,32},{160,64},{192,96},{224,1... | collective-permute-start | bytes 2162696 | tf_op jit(solution)/shard_map/ppermute | solution.py:22
  70.6 3.7 %collective-permute-start.1 = (bf16[32,2,44,128]{3,0,2,1:T(8,128)(2,1)}, bf16[32,2,44,128]{3,0,2,1:T(8,128)(2,1)}, u32[]{:S(2)}, u32[]{:S(2)}) collective-permute-start(bf16[32,2,44,128]{3,0,2,1:T(8,128)(2,1)} %copy.7), channel_id=1, source_target_pairs={{0,192},{32,224},{64,0},{96,32},{128,64},{160,96},{192,128},{224,1... | collective-permute-start | bytes 2162696 | tf_op jit(solution)/shard_map/ppermute | solution.py:22
  74.3 3.7 %collective-permute-start = (bf16[32,2,44,128]{3,0,2,1:T(8,128)(2,1)}, bf16[32,2,44,128]{3,0,2,1:T(8,128)(2,1)}, u32[]{:S(2)}, u32[]{:S(2)}) collective-permute-start(bf16[32,2,44,128]{3,0,2,1:T(8,128)(2,1)} %copy.7), channel_id=1, source_target_pairs={{0,224},{32,0},{64,32},{96,64},{128,96},{160,128},{192,160},{224,1... | collective-permute-start | bytes 2162696 | tf_op jit(solution)/shard_map/ppermute | solution.py:22
  78.0 22.7 %collective-permute-done.4 = bf16[32,2,44,128]{3,0,2,1:T(8,128)(2,1)} collective-permute-done((bf16[32,2,44,128]{3,0,2,1:T(8,128)(2,1)}, bf16[32,2,44,128]{3,0,2,1:T(8,128)(2,1)}, u32[]{:S(2)}, u32[]{:S(2)}) %collective-permute-start.4) | collective-permute-done | bytes 720928 | tf_op jit(solution)/shard_map/ppermute | solution.py:22
  100.7 3.9 %collective-permute-start.7 = (bf16[32,2,44,128]{3,0,2,1:T(8,128)(2,1)}, bf16[32,2,44,128]{3,0,2,1:T(8,128)(2,1)S(1)}, u32[]{:S(2)}, u32[]{:S(2)}) collective-permute-start(bf16[32,2,44,128]{3,0,2,1:T(8,128)(2,1)} %copy.18), channel_id=1, source_target_pairs={{0,128},{32,160},{64,192},{96,224},{1,129},{33,161},{65,193},{97,2... | collective-permute-start | bytes 2162696 | tf_op jit(solution)/shard_map/ppermute | solution.py:114
  111.1 2.3 %copy.21.refs_1_ = bf16[32,2,44,128]{3,2,1,0:T(8,128)(2,1)} copy(bf16[32,2,44,128]{3,0,2,1:T(8,128)(2,1)} %collective-permute-done.3) | data formatting | bytes 1441792 | tf_op jit(solution)/shard_map/ppermute | solution.py:22
  113.4 3.3 %shard_map.46 = f32[1,128,256]{2,1,0:T(8,128)} custom-call(bf16[32,2,44,128]{3,2,1,0:T(8,128)(2,1)} %get-tuple-element.6.own_ref.refs_0_, bf16[32,2,44,128]{3,2,1,0:T(8,128)(2,1)} %copy.27.refs_0_), custom_call_target="tpu_custom_call" | custom-call | flops 369098752 | bytes 1572864 | tf_op jit(solution)/shard_map/pallas_call | solution.py:78
  116.7 3.4 %shard_map.45 = f32[1,128,256]{2,1,0:T(8,128)} custom-call(bf16[32,2,44,128]{3,2,1,0:T(8,128)(2,1)} %get-tuple-element.6.own_ref.refs_0_, bf16[32,2,44,128]{3,2,1,0:T(8,128)(2,1)} %copy.24.refs_0_), custom_call_target="tpu_custom_call" | custom-call | flops 369098752 | bytes 1572864 | tf_op jit(solution)/shard_map/pallas_call | solution.py:78
  120.1 4.6 %shard_map.44 = f32[2,128,256]{2,1,0:T(8,128)} custom-call(bf16[32,2,44,128]{3,2,1,0:T(8,128)(2,1)} %get-tuple-element.6.own_ref.refs_0_, bf16[32,2,44,128]{3,2,1,0:T(8,128)(2,1)} %get-tuple-element.6.own_ref.refs_0_, bf16[32,2,44,128]{3,2,1,0:T(8,128)(2,1)} %copy.21.refs_1_), custom_call_target="tpu_custom_call" | custom-call | flops 738197504 | bytes 2424832 | tf_op jit(solution)/shard_map/pallas_call | solution.py:78
  126.0 2.3 %copy.16.refs_0_ = bf16[32,2,44,128]{3,2,1,0:T(8,128)(2,1)} copy(bf16[32,2,44,128]{3,0,2,1:T(8,128)(2,1)} %collective-permute-done.2) | data formatting | bytes 1441792 | tf_op jit(solution)/shard_map/ppermute | solution.py:22
  128.3 6.1 %collective-permute-done.1 = bf16[32,2,44,128]{3,0,2,1:T(8,128)(2,1)} collective-permute-done((bf16[32,2,44,128]{3,0,2,1:T(8,128)(2,1)}, bf16[32,2,44,128]{3,0,2,1:T(8,128)(2,1)}, u32[]{:S(2)}, u32[]{:S(2)}) %collective-permute-start.1) | collective-permute-done | bytes 720928 | tf_op jit(solution)/shard_map/ppermute | solution.py:22
  136.7 13.2 %collective-permute-done = bf16[32,2,44,128]{3,0,2,1:T(8,128)(2,1)} collective-permute-done((bf16[32,2,44,128]{3,0,2,1:T(8,128)(2,1)}, bf16[32,2,44,128]{3,0,2,1:T(8,128)(2,1)}, u32[]{:S(2)}, u32[]{:S(2)}) %collective-permute-start) | collective-permute-done | bytes 720928 | tf_op jit(solution)/shard_map/ppermute | solution.py:22
  149.8 2.3 %copy.10.refs_1_ = bf16[32,2,44,128]{3,2,1,0:T(8,128)(2,1)} copy(bf16[32,2,44,128]{3,0,2,1:T(8,128)(2,1)} %collective-permute-done) | data formatting | bytes 1441792 | tf_op jit(solution)/shard_map/ppermute | solution.py:22
  152.2 3.3 %shard_map.43 = f32[1,128,256]{2,1,0:T(8,128)} custom-call(bf16[32,2,44,128]{3,2,1,0:T(8,128)(2,1)} %get-tuple-element.5.own_ref.refs_0_, bf16[32,2,44,128]{3,2,1,0:T(8,128)(2,1)} %copy.16.refs_0_), custom_call_target="tpu_custom_call" | custom-call | flops 369098752 | bytes 1572864 | tf_op jit(solution)/shard_map/pallas_call | solution.py:78
  155.5 3.4 %shard_map.42 = f32[1,128,256]{2,1,0:T(8,128)} custom-call(bf16[32,2,44,128]{3,2,1,0:T(8,128)(2,1)} %get-tuple-element.5.own_ref.refs_0_, bf16[32,2,44,128]{3,2,1,0:T(8,128)(2,1)} %copy.13.refs_0_), custom_call_target="tpu_custom_call" | custom-call | flops 369098752 | bytes 1572864 | tf_op jit(solution)/shard_map/pallas_call | solution.py:78
  158.8 4.6 %shard_map.41 = f32[2,128,256]{2,1,0:T(8,128)} custom-call(bf16[32,2,44,128]{3,2,1,0:T(8,128)(2,1)} %get-tuple-element.5.own_ref.refs_0_, bf16[32,2,44,128]{3,2,1,0:T(8,128)(2,1)} %get-tuple-element.5.own_ref.refs_0_, bf16[32,2,44,128]{3,2,1,0:T(8,128)(2,1)} %copy.10.refs_1_), custom_call_target="tpu_custom_call" | custom-call | flops 738197504 | bytes 2424832 | tf_op jit(solution)/shard_map/pallas_call | solution.py:78
  168.5 3.3 %shard_map.47 = f32[1,128,256]{2,1,0:T(8,128)} custom-call(bf16[32,2,44,128]{3,2,1,0:T(8,128)(2,1)} %get-tuple-element.4.own_ref, bf16[32,2,44,128]{3,2,1,0:T(8,128)(2,1)} %copy_select_fusion.refs_0_), custom_call_target="tpu_custom_call" | custom-call | flops 369098752 | bytes 1572864 | tf_op jit(solution)/shard_map/pallas_call | solution.py:78
  (33 shorter events, 24.8 us)
Async XLA Ops:
  9.3 31.2 %all-to-all-start.1 = ((bf16[32,2,44,128]{3,1,2,0:T(2,128)(2,1)}), bf16[32,2,44,128]{3,1,2,0:T(2,128)(2,1)S(1)}, u32[]{:S(2)}, u32[]{:S(2)}) async-start(bf16[32,2,44,128]{3,1,2,0:T(2,128)(2,1)} %copy.17), calls=%async_computation.1 | async-start | bytes 1441792 | tf_op jit(solution)/shard_map/all_to_all | solution.py:108
  40.5 25.9 %all-to-all-start = ((bf16[32,2,44,128]{3,1,2,0:T(2,128)(2,1)}), bf16[32,2,44,128]{3,1,2,0:T(2,128)(2,1)S(1)}, u32[]{:S(2)}, u32[]{:S(2)}) async-start(bf16[32,2,44,128]{3,1,2,0:T(2,128)(2,1)} %copy.6), calls=%async_computation | async-start | bytes 1441792 | tf_op jit(solution)/shard_map/all_to_all | solution.py:108
  46.3 28.0 %collective-permute-start.5 = (bf16[32,2,44,128]{3,0,2,1:T(8,128)(2,1)}, bf16[32,2,44,128]{3,0,2,1:T(8,128)(2,1)S(1)}, u32[]{:S(2)}, u32[]{:S(2)}) collective-permute-start(bf16[32,2,44,128]{3,0,2,1:T(8,128)(2,1)} %copy.18), channel_id=1, source_target_pairs={{0,160},{32,192},{64,224},{96,0},{128,32},{160,64},{192,96},{224,1... | collective-permute-start | bytes 2162696 | tf_op jit(solution)/shard_map/ppermute | solution.py:22
  49.4 51.3 %collective-permute-start.4 = (bf16[32,2,44,128]{3,0,2,1:T(8,128)(2,1)}, bf16[32,2,44,128]{3,0,2,1:T(8,128)(2,1)}, u32[]{:S(2)}, u32[]{:S(2)}) collective-permute-start(bf16[32,2,44,128]{3,0,2,1:T(8,128)(2,1)} %copy.18), channel_id=1, source_target_pairs={{0,192},{32,224},{64,0},{96,32},{128,64},{160,96},{192,128},{224,1... | collective-permute-start | bytes 2162696 | tf_op jit(solution)/shard_map/ppermute | solution.py:22
  53.2 51.5 %collective-permute-start.3 = (bf16[32,2,44,128]{3,0,2,1:T(8,128)(2,1)}, bf16[32,2,44,128]{3,0,2,1:T(8,128)(2,1)}, u32[]{:S(2)}, u32[]{:S(2)}) collective-permute-start(bf16[32,2,44,128]{3,0,2,1:T(8,128)(2,1)} %copy.18), channel_id=1, source_target_pairs={{0,224},{32,0},{64,32},{96,64},{128,96},{160,128},{192,160},{224,1... | collective-permute-start | bytes 2162696 | tf_op jit(solution)/shard_map/ppermute | solution.py:22
  67.4 58.6 %collective-permute-start.2 = (bf16[32,2,44,128]{3,0,2,1:T(8,128)(2,1)}, bf16[32,2,44,128]{3,0,2,1:T(8,128)(2,1)}, u32[]{:S(2)}, u32[]{:S(2)}) collective-permute-start(bf16[32,2,44,128]{3,0,2,1:T(8,128)(2,1)} %copy.7), channel_id=1, source_target_pairs={{0,160},{32,192},{64,224},{96,0},{128,32},{160,64},{192,96},{224,1... | collective-permute-start | bytes 2162696 | tf_op jit(solution)/shard_map/ppermute | solution.py:22
  70.6 63.8 %collective-permute-start.1 = (bf16[32,2,44,128]{3,0,2,1:T(8,128)(2,1)}, bf16[32,2,44,128]{3,0,2,1:T(8,128)(2,1)}, u32[]{:S(2)}, u32[]{:S(2)}) collective-permute-start(bf16[32,2,44,128]{3,0,2,1:T(8,128)(2,1)} %copy.7), channel_id=1, source_target_pairs={{0,192},{32,224},{64,0},{96,32},{128,64},{160,96},{192,128},{224,1... | collective-permute-start | bytes 2162696 | tf_op jit(solution)/shard_map/ppermute | solution.py:22
  74.3 3.7 %copy-start = (bf16[32,2,44,128]{3,0,2,1:T(8,128)(2,1)}, bf16[32,2,44,128]{3,0,2,1:T(8,128)(2,1)S(1)}, u32[]{:S(2)}) copy-start(bf16[32,2,44,128]{3,0,2,1:T(8,128)(2,1)S(1)} %collective-permute-done.5) | copy-start | bytes 2162692
  74.3 75.5 %collective-permute-start = (bf16[32,2,44,128]{3,0,2,1:T(8,128)(2,1)}, bf16[32,2,44,128]{3,0,2,1:T(8,128)(2,1)}, u32[]{:S(2)}, u32[]{:S(2)}) collective-permute-start(bf16[32,2,44,128]{3,0,2,1:T(8,128)(2,1)} %copy.7), channel_id=1, source_target_pairs={{0,224},{32,0},{64,32},{96,64},{128,96},{160,128},{192,160},{224,1... | collective-permute-start | bytes 2162696 | tf_op jit(solution)/shard_map/ppermute | solution.py:22
  100.7 6.9 %copy-start.1 = (bf16[32,2,44,128]{3,0,2,1:T(8,128)(2,1)S(1)}, bf16[32,2,44,128]{3,0,2,1:T(8,128)(2,1)}, u32[]{:S(2)}) copy-start(bf16[32,2,44,128]{3,0,2,1:T(8,128)(2,1)} %copy-done) | copy-start | bytes 2162692
  100.7 64.3 %collective-permute-start.7 = (bf16[32,2,44,128]{3,0,2,1:T(8,128)(2,1)}, bf16[32,2,44,128]{3,0,2,1:T(8,128)(2,1)S(1)}, u32[]{:S(2)}, u32[]{:S(2)}) collective-permute-start(bf16[32,2,44,128]{3,0,2,1:T(8,128)(2,1)} %copy.18), channel_id=1, source_target_pairs={{0,128},{32,160},{64,192},{96,224},{1,129},{33,161},{65,193},{97,2... | collective-permute-start | bytes 2162696 | tf_op jit(solution)/shard_map/ppermute | solution.py:114
  104.7 62.3 %collective-permute-start.6 = (bf16[32,2,44,128]{3,0,2,1:T(8,128)(2,1)}, bf16[32,2,44,128]{3,0,2,1:T(8,128)(2,1)S(1)}, u32[]{:S(2)}, u32[]{:S(2)}) collective-permute-start(bf16[32,2,44,128]{3,0,2,1:T(8,128)(2,1)} %copy.7), channel_id=1, source_target_pairs={{128,0},{160,32},{192,64},{224,96},{129,1},{161,33},{193,65},{225,... | collective-permute-start | bytes 2162696 | tf_op jit(solution)/shard_map/ppermute | solution.py:114
  116.7 7.9 %copy-start.2 = (f32[1,128,256]{2,1,0:T(8,128)S(1)}, f32[1,128,256]{2,1,0:T(8,128)}, u32[]{:S(2)}) copy-start(f32[1,128,256]{2,1,0:T(8,128)} %shard_map.46) | copy-start | bytes 393220
  155.5 7.9 %copy-start.3 = (f32[1,128,256]{2,1,0:T(8,128)S(1)}, f32[1,128,256]{2,1,0:T(8,128)}, u32[]{:S(2)}) copy-start(f32[1,128,256]{2,1,0:T(8,128)} %shard_map.43) | copy-start | bytes 393220

commit v11 on v10

--- a/solution.py
+++ b/solution.py
@@ -65,9 +65,10 @@
 
         @pl.when(jnp.logical_and(upper, pl.program_id(0) == pl.num_programs(0) - 1))
         def _():
-            real = out_ref[0, :, :chans]
-            imag = out_ref[0, :, chans:]
-            out_ref[0] = jnp.concatenate([real.T, -imag.T], axis=1)
+            last = len(mate_refs) - 1
+            real = out_ref[last, :, :chans]
+            imag = out_ref[last, :, chans:]
+            out_ref[last] = jnp.concatenate([real.T, -imag.T], axis=1)
 
 
 def pair_stack(own, mates, turn=False):
@@ -103,7 +104,7 @@
 
     near = []
     own_h = []
-    far_recv = []
+    far_parts = []
     for half in range(2):
         blocks = lax.all_to_all(spectra[half], "tm", split_axis=0, concat_axis=0, tiled=True)
         own_h.append(blocks)
@@ -111,15 +112,14 @@
             pairs = [(s, s - half_count) for s in range(half_count, chan_count)]
         else:
             pairs = [(s, s + half_count) for s in range(half_count)]
-        far_recv.append(lax.ppermute(blocks, "chan", pairs))
+        far_recv = lax.ppermute(blocks, "chan", pairs)
         mates = [blocks] + [shifted(blocks, "chan", -offset) for offset in range(1, half_count)]
-        first = pair_stack(blocks, mates[:2])
-        near.append(jnp.concatenate([first] + [pair_stack(blocks, [mate]) for mate in mates[2:]], axis=0))
+        first = pair_stack(blocks, mates[:2] + [far_recv], turn=half == 1)
+        far_parts.append(first[2])
+        near.append(jnp.concatenate([first[:2]] + [pair_stack(blocks, [mate]) for mate in mates[2:]], axis=0))
     cross_near = jnp.stack(near, axis=0).reshape(1, 2, half_count, chans, 2, chans)
 
-    far_own = jnp.where(lower_half, own_h[0], own_h[1])
-    far_mate = jnp.where(lower_half, far_recv[0], far_recv[1])
-    cross_far = pair_stack(far_own, [far_mate], turn=True).reshape(1, chans, 2, chans)
+    cross_far = jnp.where(lower_half, far_parts[0], far_parts[1]).reshape(1, chans, 2, chans)
     return (cross_near, cross_far)
 
 

time: 176 us -> 206 us (1.17)
  waiting for transfers between devices: 75.8 us -> 101 us
  local copies, waits for them, and re-layouts: 19.7 us -> 25.7 us
  other arithmetic: 6.94 us -> 3.81 us
  starting transfers between devices: 39.1 us -> 41.4 us
    ppermute x2, waiting for transfers between devices: 2.25 us -> 15.9 us  [body(): far_recv = lax.ppermute(blocks, 'chan', pairs)]
    ppermute x6, waiting for transfers between devices: 41.9 us -> 53.9 us  [shifted(): return lax.ppermute(value, axis, pairs)]
    ppermute x0 -> x2, local copies, waits for them, and re-layouts: none -> 4.57 us  [body(): far_recv = lax.ppermute(blocks, 'chan', pairs)]
    ppermute x6, starting transfers between devices: 18.8 us -> 20.9 us  [shifted(): return lax.ppermute(value, axis, pairs)]
    pallas_call x7 -> x6, Pallas kernels: 25.8 us -> 25 us  [pair_stack(): pl.pallas_call(functools.partial(pair_kernel, step, turn), out_shape=jax....]
  transfers between devices with their start and end apart: 10 -> 10, of which waited for: 7 -> 10; matrix products, arithmetic and copies ran while one was open for 12% -> 10% of each run, Pallas kernels for 13% -> 9%
where the time goes in v11:
time: 206 us; the launch traced here: 205 us
  waiting for transfers between devices  101 us (49%)
  starting transfers between devices  41.4 us (20%)
  local copies, waits for them, and re-layouts  25.7 us (12%)
  Pallas kernels  25 us (12%)
  matrix products  6.79 us (3%)
  other arithmetic  3.81 us (2%)
    ppermute x6, waiting for transfers between devices, shifted(): return lax.ppermute(value, axis, pairs)  53.9 us
    all_to_all x2, waiting for transfers between devices, body(): lax.all_to_all(spectra[half], 'tm', split_axis=0, concat_axis=0, tiled=True)  31.6 us
    pallas_call x6, Pallas kernels, pair_stack(): pl.pallas_call(functools.partial(pair_kernel, step, turn), out_shape=jax....  25 us
    ppermute x6, starting transfers between devices, shifted(): return lax.ppermute(value, axis, pairs)  20.9 us
    ppermute x2, waiting for transfers between devices, body(): far_recv = lax.ppermute(blocks, 'chan', pairs)  15.9 us
    all_to_all x2, starting transfers between devices, body(): lax.all_to_all(spectra[half], 'tm', split_axis=0, concat_axis=0, tiled=True)  14.9 us
    ppermute x6, local copies, waits for them, and re-layouts, shifted(): return lax.ppermute(value, axis, pairs)  13.9 us
    dot_general x1, matrix products, whiten(): jnp.einsum('ks,wcs->kwc', taper_table, records, preferred_element_type=jn...  6.79 us
  transfers between devices with their start and end apart: 10, of which 10 were waited for; matrix products, arithmetic and copies ran while one was open for 10% of the time, Pallas kernels for 9%

profile of v11, /device:TPU:2, one launch (start us, length us, event | category | flops | bytes accessed | tf_op | source)
XLA Modules:
  0.0 205.0 jit_solution(3131166766305983276)
XLA Ops:
  0.6 6.8 %multiply_reduce_fusion = (f32[44,128]{1,0:T(8,128)S(1)}, f32[128,44,128]{2,0,1:T(8,128)S(1)}) fusion(bf16[128,1024,1]{1,0,2:T(8,128)(2,1)} %constant.21, bf16[44,128,1024]{2,1,0:T(8,128)(2,1)} %param.2), kind=kOutput, calls=%fused_computation.1 | convolution fusion | flops 1477831168 | bytes 14702592 | tf_op jit(solution)/shard_map/ks,wcs->kwc/dot_general | solution.py:38
  9.3 10.1 %all-to-all-start.1 = ((bf16[32,2,44,128]{3,1,2,0:T(2,128)(2,1)}), bf16[32,2,44,128]{3,1,2,0:T(2,128)(2,1)S(1)}, u32[]{:S(2)}, u32[]{:S(2)}) async-start(bf16[32,2,44,128]{3,1,2,0:T(2,128)(2,1)} %copy.19), calls=%async_computation.1 | async-start | bytes 1441792 | tf_op jit(solution)/shard_map/all_to_all | solution.py:109
  20.8 19.8 %all-to-all-done.1 = bf16[32,2,44,128]{3,1,2,0:T(2,128)(2,1)S(1)} async-done(((bf16[32,2,44,128]{3,1,2,0:T(2,128)(2,1)}), bf16[32,2,44,128]{3,1,2,0:T(2,128)(2,1)S(1)}, u32[]{:S(2)}, u32[]{:S(2)}) %all-to-all-start.1) | async-done | bytes 720928 | tf_op jit(solution)/shard_map/all_to_all | solution.py:109
  40.5 4.8 %all-to-all-start = ((bf16[32,2,44,128]{3,1,2,0:T(2,128)(2,1)}), bf16[32,2,44,128]{3,1,2,0:T(2,128)(2,1)S(1)}, u32[]{:S(2)}, u32[]{:S(2)}) async-start(bf16[32,2,44,128]{3,1,2,0:T(2,128)(2,1)} %copy.6), calls=%async_computation | async-start | bytes 1441792 | tf_op jit(solution)/shard_map/all_to_all | solution.py:109
  45.5 3.2 %collective-permute-start.7 = (bf16[32,2,44,128]{3,0,2,1:T(8,128)(2,1)S(1)}, bf16[32,2,44,128]{3,0,2,1:T(8,128)(2,1)}, u32[]{:S(2)}, u32[]{:S(2)}) collective-permute-start(bf16[32,2,44,128]{3,0,2,1:T(8,128)(2,1)S(1)} %copy.20), channel_id=1, source_target_pairs={{0,160},{32,192},{64,224},{96,0},{128,32},{160,64},{192,96},{224,1... | collective-permute-start | bytes 2162696 | tf_op jit(solution)/shard_map/ppermute | solution.py:22
  50.3 4.2 %collective-permute-start.5 = (bf16[32,2,44,128]{3,0,2,1:T(8,128)(2,1)S(1)}, bf16[32,2,44,128]{3,0,2,1:T(8,128)(2,1)}, u32[]{:S(2)}, u32[]{:S(2)}) collective-permute-start(bf16[32,2,44,128]{3,0,2,1:T(8,128)(2,1)S(1)} %copy.20), channel_id=1, source_target_pairs={{0,128},{32,160},{64,192},{96,224},{1,129},{33,161},{65,193},{97,2... | collective-permute-start | bytes 2162696 | tf_op jit(solution)/shard_map/ppermute | solution.py:115
  54.5 11.9 %all-to-all-done = bf16[32,2,44,128]{3,1,2,0:T(2,128)(2,1)S(1)} async-done(((bf16[32,2,44,128]{3,1,2,0:T(2,128)(2,1)}), bf16[32,2,44,128]{3,1,2,0:T(2,128)(2,1)S(1)}, u32[]{:S(2)}, u32[]{:S(2)}) %all-to-all-start) | async-done | bytes 720928 | tf_op jit(solution)/shard_map/all_to_all | solution.py:109
  66.5 3.2 %collective-permute-start.3 = (bf16[32,2,44,128]{3,0,2,1:T(8,128)(2,1)S(1)}, bf16[32,2,44,128]{3,0,2,1:T(8,128)(2,1)}, u32[]{:S(2)}, u32[]{:S(2)}) collective-permute-start(bf16[32,2,44,128]{3,0,2,1:T(8,128)(2,1)S(1)} %copy.7), channel_id=1, source_target_pairs={{0,160},{32,192},{64,224},{96,0},{128,32},{160,64},{192,96},{224,1... | collective-permute-start | bytes 2162696 | tf_op jit(solution)/shard_map/ppermute | solution.py:22
  71.2 6.6 %collective-permute-start.2 = (bf16[32,2,44,128]{3,0,2,1:T(8,128)(2,1)S(1)}, bf16[32,2,44,128]{3,0,2,1:T(8,128)(2,1)}, u32[]{:S(2)}, u32[]{:S(2)}) collective-permute-start(bf16[32,2,44,128]{3,0,2,1:T(8,128)(2,1)S(1)} %copy.7), channel_id=1, source_target_pairs={{0,192},{32,224},{64,0},{96,32},{128,64},{160,96},{192,128},{224,1... | collective-permute-start | bytes 2162696 | tf_op jit(solution)/shard_map/ppermute | solution.py:22
  77.8 8.8 %collective-permute-done.4 = bf16[32,2,44,128]{3,0,2,1:T(8,128)(2,1)} collective-permute-done((bf16[32,2,44,128]{3,0,2,1:T(8,128)(2,1)S(1)}, bf16[32,2,44,128]{3,0,2,1:T(8,128)(2,1)}, u32[]{:S(2)}, u32[]{:S(2)}) %collective-permute-start.4) | collective-permute-done | bytes 720928 | tf_op jit(solution)/shard_map/ppermute | solution.py:22
  86.6 6.2 %collective-permute-start = (bf16[32,2,44,128]{3,0,2,1:T(8,128)(2,1)S(1)}, bf16[32,2,44,128]{3,0,2,1:T(8,128)(2,1)}, u32[]{:S(2)}, u32[]{:S(2)}) collective-permute-start(bf16[32,2,44,128]{3,0,2,1:T(8,128)(2,1)S(1)} %copy.7), channel_id=1, source_target_pairs={{0,224},{32,0},{64,32},{96,64},{128,96},{160,128},{192,160},{224,1... | collective-permute-start | bytes 2162696 | tf_op jit(solution)/shard_map/ppermute | solution.py:22
  92.9 9.2 %collective-permute-done.5 = bf16[32,2,44,128]{3,0,2,1:T(8,128)(2,1)} collective-permute-done((bf16[32,2,44,128]{3,0,2,1:T(8,128)(2,1)S(1)}, bf16[32,2,44,128]{3,0,2,1:T(8,128)(2,1)}, u32[]{:S(2)}, u32[]{:S(2)}) %collective-permute-start.5) | collective-permute-done | bytes 720928 | tf_op jit(solution)/shard_map/ppermute | solution.py:115
  110.2 5.9 %shard_map.44 = f32[3,128,256]{2,1,0:T(8,128)} custom-call(bf16[32,2,44,128]{3,2,1,0:T(8,128)(2,1)} %copy.22.own_ref.refs_0_, bf16[32,2,44,128]{3,2,1,0:T(8,128)(2,1)} %copy.22.own_ref.refs_0_, bf16[32,2,44,128]{3,2,1,0:T(8,128)(2,1)} %copy.24.refs_1_, bf16[32,2,44,128]{3,2,1,0:T(8,128)(2,1)} %copy.25.refs_2_), custom_call_target="tpu_custom_call" | custom-call | flops 1107296256 | bytes 3276800 | tf_op jit(solution)/shard_map/pallas_call | solution.py:79
  116.1 2.4 %copy.31.refs_0_ = bf16[32,2,44,128]{3,2,1,0:T(8,128)(2,1)} copy(bf16[32,2,44,128]{3,0,2,1:T(8,128)(2,1)} %collective-permute-done.7) | data formatting | bytes 1441792 | tf_op jit(solution)/shard_map/ppermute | solution.py:22
  118.4 10.8 %collective-permute-done.6 = bf16[32,2,44,128]{3,0,2,1:T(8,128)(2,1)} collective-permute-done((bf16[32,2,44,128]{3,0,2,1:T(8,128)(2,1)S(1)}, bf16[32,2,44,128]{3,0,2,1:T(8,128)(2,1)}, u32[]{:S(2)}, u32[]{:S(2)}) %collective-permute-start.6) | collective-permute-done | bytes 720928 | tf_op jit(solution)/shard_map/ppermute | solution.py:22
  131.5 3.3 %shard_map.46 = f32[1,128,256]{2,1,0:T(8,128)} custom-call(bf16[32,2,44,128]{3,2,1,0:T(8,128)(2,1)} %copy.22.own_ref.refs_0_, bf16[32,2,44,128]{3,2,1,0:T(8,128)(2,1)} %copy.31.refs_0_), custom_call_target="tpu_custom_call" | custom-call | flops 369098752 | bytes 1572864 | tf_op jit(solution)/shard_map/pallas_call | solution.py:79
  134.8 3.3 %shard_map.45 = f32[1,128,256]{2,1,0:T(8,128)} custom-call(bf16[32,2,44,128]{3,2,1,0:T(8,128)(2,1)} %copy.22.own_ref.refs_0_, bf16[32,2,44,128]{3,2,1,0:T(8,128)(2,1)} %copy.28.refs_0_), custom_call_target="tpu_custom_call" | custom-call | flops 369098752 | bytes 1572864 | tf_op jit(solution)/shard_map/pallas_call | solution.py:79
  139.4 7.1 %collective-permute-done.3 = bf16[32,2,44,128]{3,0,2,1:T(8,128)(2,1)} collective-permute-done((bf16[32,2,44,128]{3,0,2,1:T(8,128)(2,1)S(1)}, bf16[32,2,44,128]{3,0,2,1:T(8,128)(2,1)}, u32[]{:S(2)}, u32[]{:S(2)}) %collective-permute-start.3) | collective-permute-done | bytes 720928 | tf_op jit(solution)/shard_map/ppermute | solution.py:22
  148.8 13.2 %collective-permute-done.2 = bf16[32,2,44,128]{3,0,2,1:T(8,128)(2,1)} collective-permute-done((bf16[32,2,44,128]{3,0,2,1:T(8,128)(2,1)S(1)}, bf16[32,2,44,128]{3,0,2,1:T(8,128)(2,1)}, u32[]{:S(2)}, u32[]{:S(2)}) %collective-permute-start.2) | collective-permute-done | bytes 720928 | tf_op jit(solution)/shard_map/ppermute | solution.py:22
  164.3 12.5 %collective-permute-done = bf16[32,2,44,128]{3,0,2,1:T(8,128)(2,1)} collective-permute-done((bf16[32,2,44,128]{3,0,2,1:T(8,128)(2,1)S(1)}, bf16[32,2,44,128]{3,0,2,1:T(8,128)(2,1)}, u32[]{:S(2)}, u32[]{:S(2)}) %collective-permute-start) | collective-permute-done | bytes 720928 | tf_op jit(solution)/shard_map/ppermute | solution.py:22
  179.1 3.3 %shard_map.43 = f32[1,128,256]{2,1,0:T(8,128)} custom-call(bf16[32,2,44,128]{3,2,1,0:T(8,128)(2,1)} %copy.9.own_ref.refs_0_, bf16[32,2,44,128]{3,2,1,0:T(8,128)(2,1)} %copy.18.refs_0_), custom_call_target="tpu_custom_call" | custom-call | flops 369098752 | bytes 1572864 | tf_op jit(solution)/shard_map/pallas_call | solution.py:79
  182.4 3.3 %shard_map.42 = f32[1,128,256]{2,1,0:T(8,128)} custom-call(bf16[32,2,44,128]{3,2,1,0:T(8,128)(2,1)} %copy.9.own_ref.refs_0_, bf16[32,2,44,128]{3,2,1,0:T(8,128)(2,1)} %copy.15.refs_0_), custom_call_target="tpu_custom_call" | custom-call | flops 369098752 | bytes 1572864 | tf_op jit(solution)/shard_map/pallas_call | solution.py:79
  185.8 6.7 %collective-permute-done.1 = bf16[32,2,44,128]{3,0,2,1:T(8,128)(2,1)} collective-permute-done((bf16[32,2,44,128]{3,0,2,1:T(8,128)(2,1)S(1)}, bf16[32,2,44,128]{3,0,2,1:T(8,128)(2,1)}, u32[]{:S(2)}, u32[]{:S(2)}) %collective-permute-start.1) | collective-permute-done | bytes 720928 | tf_op jit(solution)/shard_map/ppermute | solution.py:115
  194.7 5.9 %shard_map.41 = f32[3,128,256]{2,1,0:T(8,128)} custom-call(bf16[32,2,44,128]{3,2,1,0:T(8,128)(2,1)} %copy.9.own_ref.refs_0_, bf16[32,2,44,128]{3,2,1,0:T(8,128)(2,1)} %copy.9.own_ref.refs_0_, bf16[32,2,44,128]{3,2,1,0:T(8,128)(2,1)} %copy.11.refs_1_, bf16[32,2,44,128]{3,2,1,0:T(8,128)(2,1)} %copy.12.refs_2_), custom_call_target="tpu_custom_call" | custom-call | flops 1107296256 | bytes 3276800 | tf_op jit(solution)/shard_map/pallas_call | solution.py:79
  (36 shorter events, 31.8 us)
Async XLA Ops:
  9.3 31.2 %all-to-all-start.1 = ((bf16[32,2,44,128]{3,1,2,0:T(2,128)(2,1)}), bf16[32,2,44,128]{3,1,2,0:T(2,128)(2,1)S(1)}, u32[]{:S(2)}, u32[]{:S(2)}) async-start(bf16[32,2,44,128]{3,1,2,0:T(2,128)(2,1)} %copy.19), calls=%async_computation.1 | async-start | bytes 1441792 | tf_op jit(solution)/shard_map/all_to_all | solution.py:109
  40.5 25.9 %all-to-all-start = ((bf16[32,2,44,128]{3,1,2,0:T(2,128)(2,1)}), bf16[32,2,44,128]{3,1,2,0:T(2,128)(2,1)S(1)}, u32[]{:S(2)}, u32[]{:S(2)}) async-start(bf16[32,2,44,128]{3,1,2,0:T(2,128)(2,1)} %copy.6), calls=%async_computation | async-start | bytes 1441792 | tf_op jit(solution)/shard_map/all_to_all | solution.py:109
  45.5 25.7 %collective-permute-start.7 = (bf16[32,2,44,128]{3,0,2,1:T(8,128)(2,1)S(1)}, bf16[32,2,44,128]{3,0,2,1:T(8,128)(2,1)}, u32[]{:S(2)}, u32[]{:S(2)}) collective-permute-start(bf16[32,2,44,128]{3,0,2,1:T(8,128)(2,1)S(1)} %copy.20), channel_id=1, source_target_pairs={{0,160},{32,192},{64,224},{96,0},{128,32},{160,64},{192,96},{224,1... | collective-permute-start | bytes 2162696 | tf_op jit(solution)/shard_map/ppermute | solution.py:22
  48.7 38.0 %collective-permute-start.4 = (bf16[32,2,44,128]{3,0,2,1:T(8,128)(2,1)S(1)}, bf16[32,2,44,128]{3,0,2,1:T(8,128)(2,1)}, u32[]{:S(2)}, u32[]{:S(2)}) collective-permute-start(bf16[32,2,44,128]{3,0,2,1:T(8,128)(2,1)S(1)} %copy.20), channel_id=1, source_target_pairs={{0,224},{32,0},{64,32},{96,64},{128,96},{160,128},{192,160},{224,1... | collective-permute-start | bytes 2162696 | tf_op jit(solution)/shard_map/ppermute | solution.py:22
  50.3 51.8 %collective-permute-start.5 = (bf16[32,2,44,128]{3,0,2,1:T(8,128)(2,1)S(1)}, bf16[32,2,44,128]{3,0,2,1:T(8,128)(2,1)}, u32[]{:S(2)}, u32[]{:S(2)}) collective-permute-start(bf16[32,2,44,128]{3,0,2,1:T(8,128)(2,1)S(1)} %copy.20), channel_id=1, source_target_pairs={{0,128},{32,160},{64,192},{96,224},{1,129},{33,161},{65,193},{97,2... | collective-permute-start | bytes 2162696 | tf_op jit(solution)/shard_map/ppermute | solution.py:115
  54.5 74.7 %collective-permute-start.6 = (bf16[32,2,44,128]{3,0,2,1:T(8,128)(2,1)S(1)}, bf16[32,2,44,128]{3,0,2,1:T(8,128)(2,1)}, u32[]{:S(2)}, u32[]{:S(2)}) collective-permute-start(bf16[32,2,44,128]{3,0,2,1:T(8,128)(2,1)S(1)} %copy.20), channel_id=1, source_target_pairs={{0,192},{32,224},{64,0},{96,32},{128,64},{160,96},{192,128},{224,1... | collective-permute-start | bytes 2162696 | tf_op jit(solution)/shard_map/ppermute | solution.py:22
  66.5 80.0 %collective-permute-start.3 = (bf16[32,2,44,128]{3,0,2,1:T(8,128)(2,1)S(1)}, bf16[32,2,44,128]{3,0,2,1:T(8,128)(2,1)}, u32[]{:S(2)}, u32[]{:S(2)}) collective-permute-start(bf16[32,2,44,128]{3,0,2,1:T(8,128)(2,1)S(1)} %copy.7), channel_id=1, source_target_pairs={{0,160},{32,192},{64,224},{96,0},{128,32},{160,64},{192,96},{224,1... | collective-permute-start | bytes 2162696 | tf_op jit(solution)/shard_map/ppermute | solution.py:22
  71.2 90.8 %collective-permute-start.2 = (bf16[32,2,44,128]{3,0,2,1:T(8,128)(2,1)S(1)}, bf16[32,2,44,128]{3,0,2,1:T(8,128)(2,1)}, u32[]{:S(2)}, u32[]{:S(2)}) collective-permute-start(bf16[32,2,44,128]{3,0,2,1:T(8,128)(2,1)S(1)} %copy.7), channel_id=1, source_target_pairs={{0,192},{32,224},{64,0},{96,32},{128,64},{160,96},{192,128},{224,1... | collective-permute-start | bytes 2162696 | tf_op jit(solution)/shard_map/ppermute | solution.py:22
  86.6 90.1 %collective-permute-start = (bf16[32,2,44,128]{3,0,2,1:T(8,128)(2,1)S(1)}, bf16[32,2,44,128]{3,0,2,1:T(8,128)(2,1)}, u32[]{:S(2)}, u32[]{:S(2)}) collective-permute-start(bf16[32,2,44,128]{3,0,2,1:T(8,128)(2,1)S(1)} %copy.7), channel_id=1, source_target_pairs={{0,224},{32,0},{64,32},{96,64},{128,96},{160,128},{192,160},{224,1... | collective-permute-start | bytes 2162696 | tf_op jit(solution)/shard_map/ppermute | solution.py:22
  102.1 90.3 %collective-permute-start.1 = (bf16[32,2,44,128]{3,0,2,1:T(8,128)(2,1)S(1)}, bf16[32,2,44,128]{3,0,2,1:T(8,128)(2,1)}, u32[]{:S(2)}, u32[]{:S(2)}) collective-permute-start(bf16[32,2,44,128]{3,0,2,1:T(8,128)(2,1)S(1)} %copy.7), channel_id=1, source_target_pairs={{128,0},{160,32},{192,64},{224,96},{129,1},{161,33},{193,65},{225,... | collective-permute-start | bytes 2162696 | tf_op jit(solution)/shard_map/ppermute | solution.py:115
  116.1 22.1 %slice-start = ((f32[3,128,256]{2,1,0:T(8,128)}), f32[2,128,256]{2,1,0:T(8,128)S(1)}, s32[]{:S(2)}) async-start(f32[3,128,256]{2,1,0:T(8,128)} %shard_map.44), calls=%async_computation.2 | async-start | bytes 524288 | tf_op jit(solution)/shard_map/slice | solution.py:119
  185.8 15.8 %copy-start.1 = (f32[1,128,256]{2,1,0:T(8,128)S(1)}, f32[1,128,256]{2,1,0:T(8,128)}, u32[]{:S(2)}) copy-start(f32[1,128,256]{2,1,0:T(8,128)} %shard_map.43) | copy-start | bytes 393220
  185.8 15.8 %copy-start.2 = (f32[1,128,256]{2,1,0:T(8,128)S(1)}, f32[1,128,256]{2,1,0:T(8,128)}, u32[]{:S(2)}) copy-start(f32[1,128,256]{2,1,0:T(8,128)} %shard_map.42) | copy-start | bytes 393220
  194.7 7.2 %copy-start = (f32[3,128,256]{2,1,0:T(8,128)S(1)}, f32[3,128,256]{2,1,0:T(8,128)}, u32[]{:S(2)}) copy-start(f32[3,128,256]{2,1,0:T(8,128)} %shard_map.44) | copy-start | bytes 1179652

commit v12 on v10

--- a/solution.py
+++ b/solution.py
@@ -14,6 +14,7 @@
 FIRST_BIN = 32
 EPSILON = 1e-06
 GROUPS_PER_STEP = 16
+WHITEN_ROWS = 1408
 
 
 def shifted(value, axis, steps):
@@ -34,11 +35,37 @@
     return jnp.asarray(table.astype(np.float32).astype(ml_dtypes.bfloat16))
 
 
+def whiten_kernel(scale, table_ref, rows_ref, out_ref):
+    spectra = lax.dot_general(
+        table_ref[...], rows_ref[...], (((1,), (1,)), ((), ())), preferred_element_type=jnp.float32
+    )
+    mean_square = jnp.mean(spectra * spectra, axis=0, keepdims=True)
+    factor = scale / jnp.sqrt(mean_square + EPSILON)
+    out_ref[...] = (spectra * factor).astype(jnp.bfloat16)
+
+
 def whiten(records, taper_table, overall_scale):
-    spectra = jnp.einsum("ks,wcs->kwc", taper_table, records, preferred_element_type=jnp.float32)
-    mean_square = jnp.mean(spectra * spectra, axis=0)
-    factor = overall_scale / jnp.sqrt(mean_square + EPSILON)
-    return (spectra * factor[None]).astype(jnp.bfloat16)
+    windows, chans, samples = records.shape
+    rows = records.reshape(windows * chans, samples)
+    kinds = taper_table.shape[0]
+    step = WHITEN_ROWS
+    out = pl.pallas_call(
+        functools.partial(whiten_kernel, overall_scale),
+        out_shape=jax.ShapeDtypeStruct((kinds, windows * chans), jnp.bfloat16),
+        grid=(windows * chans // step,),
+        in_specs=[
+            pl.BlockSpec((kinds, samples), lambda i: (0, 0)),
+            pl.BlockSpec((step, samples), lambda i: (i, 0)),
+        ],
+        out_specs=pl.BlockSpec((kinds, step), lambda i: (0, i)),
+        compiler_params=pltpu.CompilerParams(vmem_limit_bytes=48 * 1024 * 1024),
+        cost_estimate=pl.CostEstimate(
+            flops=2 * kinds * windows * chans * samples,
+            bytes_accessed=2 * (windows * chans * samples + kinds * samples + kinds * windows * chans),
+            transcendentals=windows * chans,
+        ),
+    )(taper_table, rows)
+    return out.reshape(kinds, windows, chans)
 
 
 def pair_kernel(group_count, turn, own_ref, *refs):

time: 176 us -> 178 us (1.011)
  Pallas kernels: 25.8 us -> 32.9 us
  matrix products: 6.79 us -> 0 us
  local copies, waits for them, and re-layouts: 19.7 us -> 21.5 us
    pallas_call x0 -> x1, Pallas kernels: none -> 7.16 us  [whiten(): pl.pallas_call(functools.partial(whiten_kernel, overall_scale), out_shape...]
    dot_general x1 -> x0, matrix products: 6.79 us -> none  [whiten(): jnp.einsum('ks,wcs->kwc', taper_table, records, preferred_element_type=jn...]
    squeeze x2 -> x4, local copies, waits for them, and re-layouts: 2.72 us -> 3.62 us  [body(): spectra[half]]
where the time goes in v12:
time: 178 us; the launch traced here: 176 us
  waiting for transfers between devices  75.5 us (42%)
  starting transfers between devices  39.1 us (22%)
  Pallas kernels  32.9 us (18%)
  local copies, waits for them, and re-layouts  21.5 us (12%)
  other arithmetic  6.37 us (4%)
    ppermute x6, waiting for transfers between devices, shifted(): return lax.ppermute(value, axis, pairs)  42.1 us
    all_to_all x2, waiting for transfers between devices, body(): lax.all_to_all(spectra[half], 'tm', split_axis=0, concat_axis=0, tiled=True)  31.1 us
    pallas_call x7, Pallas kernels, pair_stack(): pl.pallas_call(functools.partial(pair_kernel, step, turn), out_shape=jax....  25.8 us
    ppermute x6, starting transfers between devices, shifted(): return lax.ppermute(value, axis, pairs)  18.8 us
    all_to_all x2, starting transfers between devices, body(): lax.all_to_all(spectra[half], 'tm', split_axis=0, concat_axis=0, tiled=True)  14.9 us
    ppermute x6, local copies, waits for them, and re-layouts, shifted(): return lax.ppermute(value, axis, pairs)  12.6 us
    pallas_call x1, Pallas kernels, whiten(): pl.pallas_call(functools.partial(whiten_kernel, overall_scale), out_shape...  7.16 us
    ppermute x2, starting transfers between devices, body(): far_recv.append(lax.ppermute(blocks, 'chan', pairs))  5.41 us
  transfers between devices with their start and end apart: 10, of which 7 were waited for; matrix products, arithmetic and copies ran while one was open for 12% of the time, Pallas kernels for 13%

profile of v12, /device:TPU:2, one launch (start us, length us, event | category | flops | bytes accessed | tf_op | source)
XLA Modules:
  0.0 176.2 jit_solution(5293557026985326723)
XLA Ops:
  1.6 7.2 %shard_map.41 = bf16[128,5632]{1,0:T(8,128)(2,1)S(1)} custom-call(bf16[128,1024]{1,0:T(8,128)(2,1)S(1)} %copy-done, bf16[5632,1024]{1,0:T(8,128)(2,1)} %bitcast.1), custom_call_target="tpu_custom_call" | custom-call | flops 1476395008 | bytes 13238272 | tf_op jit(solution)/shard_map/pallas_call | solution.py:52
  10.7 10.1 %all-to-all-start.1 = ((bf16[32,2,44,128]{3,1,2,0:T(2,128)(2,1)}), bf16[32,2,44,128]{3,1,2,0:T(2,128)(2,1)S(1)}, u32[]{:S(2)}, u32[]{:S(2)}) async-start(bf16[32,2,44,128]{3,1,2,0:T(2,128)(2,1)} %copy.15), calls=%async_computation.1 | async-start | bytes 1441792 | tf_op jit(solution)/shard_map/all_to_all | solution.py:135
  22.6 19.3 %all-to-all-done.1 = bf16[32,2,44,128]{3,1,2,0:T(2,128)(2,1)S(1)} async-done(((bf16[32,2,44,128]{3,1,2,0:T(2,128)(2,1)}), bf16[32,2,44,128]{3,1,2,0:T(2,128)(2,1)S(1)}, u32[]{:S(2)}, u32[]{:S(2)}) %all-to-all-start.1) | async-done | bytes 720928 | tf_op jit(solution)/shard_map/all_to_all | solution.py:135
  41.9 4.8 %all-to-all-start = ((bf16[32,2,44,128]{3,1,2,0:T(2,128)(2,1)}), bf16[32,2,44,128]{3,1,2,0:T(2,128)(2,1)S(1)}, u32[]{:S(2)}, u32[]{:S(2)}) async-start(bf16[32,2,44,128]{3,1,2,0:T(2,128)(2,1)} %copy.4), calls=%async_computation | async-start | bytes 1441792 | tf_op jit(solution)/shard_map/all_to_all | solution.py:135
  47.7 3.1 %collective-permute-start.5 = (bf16[32,2,44,128]{3,0,2,1:T(8,128)(2,1)}, bf16[32,2,44,128]{3,0,2,1:T(8,128)(2,1)S(1)}, u32[]{:S(2)}, u32[]{:S(2)}) collective-permute-start(bf16[32,2,44,128]{3,0,2,1:T(8,128)(2,1)} %copy.16), channel_id=1, source_target_pairs={{0,160},{32,192},{64,224},{96,0},{128,32},{160,64},{192,96},{224,1... | collective-permute-start | bytes 2162696 | tf_op jit(solution)/shard_map/ppermute | solution.py:23
  50.8 3.7 %collective-permute-start.4 = (bf16[32,2,44,128]{3,0,2,1:T(8,128)(2,1)}, bf16[32,2,44,128]{3,0,2,1:T(8,128)(2,1)}, u32[]{:S(2)}, u32[]{:S(2)}) collective-permute-start(bf16[32,2,44,128]{3,0,2,1:T(8,128)(2,1)} %copy.16), channel_id=1, source_target_pairs={{0,192},{32,224},{64,0},{96,32},{128,64},{160,96},{192,128},{224,1... | collective-permute-start | bytes 2162696 | tf_op jit(solution)/shard_map/ppermute | solution.py:23
  55.9 11.9 %all-to-all-done = bf16[32,2,44,128]{3,1,2,0:T(2,128)(2,1)S(1)} async-done(((bf16[32,2,44,128]{3,1,2,0:T(2,128)(2,1)}), bf16[32,2,44,128]{3,1,2,0:T(2,128)(2,1)S(1)}, u32[]{:S(2)}, u32[]{:S(2)}) %all-to-all-start) | async-done | bytes 720928 | tf_op jit(solution)/shard_map/all_to_all | solution.py:135
  68.8 3.1 %collective-permute-start.2 = (bf16[32,2,44,128]{3,0,2,1:T(8,128)(2,1)}, bf16[32,2,44,128]{3,0,2,1:T(8,128)(2,1)}, u32[]{:S(2)}, u32[]{:S(2)}) collective-permute-start(bf16[32,2,44,128]{3,0,2,1:T(8,128)(2,1)} %copy.5), channel_id=1, source_target_pairs={{0,160},{32,192},{64,224},{96,0},{128,32},{160,64},{192,96},{224,1... | collective-permute-start | bytes 2162696 | tf_op jit(solution)/shard_map/ppermute | solution.py:23
  71.9 3.7 %collective-permute-start.1 = (bf16[32,2,44,128]{3,0,2,1:T(8,128)(2,1)}, bf16[32,2,44,128]{3,0,2,1:T(8,128)(2,1)}, u32[]{:S(2)}, u32[]{:S(2)}) collective-permute-start(bf16[32,2,44,128]{3,0,2,1:T(8,128)(2,1)} %copy.5), channel_id=1, source_target_pairs={{0,192},{32,224},{64,0},{96,32},{128,64},{160,96},{192,128},{224,1... | collective-permute-start | bytes 2162696 | tf_op jit(solution)/shard_map/ppermute | solution.py:23
  75.6 3.7 %collective-permute-start = (bf16[32,2,44,128]{3,0,2,1:T(8,128)(2,1)}, bf16[32,2,44,128]{3,0,2,1:T(8,128)(2,1)}, u32[]{:S(2)}, u32[]{:S(2)}) collective-permute-start(bf16[32,2,44,128]{3,0,2,1:T(8,128)(2,1)} %copy.5), channel_id=1, source_target_pairs={{0,224},{32,0},{64,32},{96,64},{128,96},{160,128},{192,160},{224,1... | collective-permute-start | bytes 2162696 | tf_op jit(solution)/shard_map/ppermute | solution.py:23
  79.4 22.7 %collective-permute-done.4 = bf16[32,2,44,128]{3,0,2,1:T(8,128)(2,1)} collective-permute-done((bf16[32,2,44,128]{3,0,2,1:T(8,128)(2,1)}, bf16[32,2,44,128]{3,0,2,1:T(8,128)(2,1)}, u32[]{:S(2)}, u32[]{:S(2)}) %collective-permute-start.4) | collective-permute-done | bytes 720928 | tf_op jit(solution)/shard_map/ppermute | solution.py:23
  102.1 3.9 %collective-permute-start.7 = (bf16[32,2,44,128]{3,0,2,1:T(8,128)(2,1)}, bf16[32,2,44,128]{3,0,2,1:T(8,128)(2,1)S(1)}, u32[]{:S(2)}, u32[]{:S(2)}) collective-permute-start(bf16[32,2,44,128]{3,0,2,1:T(8,128)(2,1)} %copy.16), channel_id=1, source_target_pairs={{0,128},{32,160},{64,192},{96,224},{1,129},{33,161},{65,193},{97,2... | collective-permute-start | bytes 2162696 | tf_op jit(solution)/shard_map/ppermute | solution.py:141
  110.2 2.3 %copy.22.refs_0_ = bf16[32,2,44,128]{3,2,1,0:T(8,128)(2,1)} copy(bf16[32,2,44,128]{3,0,2,1:T(8,128)(2,1)} %collective-permute-done.4) | data formatting | bytes 1441792 | tf_op jit(solution)/shard_map/ppermute | solution.py:23
  114.8 3.3 %shard_map.47 = f32[1,128,256]{2,1,0:T(8,128)} custom-call(bf16[32,2,44,128]{3,2,1,0:T(8,128)(2,1)} %get-tuple-element.6.own_ref.refs_0_, bf16[32,2,44,128]{3,2,1,0:T(8,128)(2,1)} %copy.25.refs_0_), custom_call_target="tpu_custom_call" | custom-call | flops 369098752 | bytes 1572864 | tf_op jit(solution)/shard_map/pallas_call | solution.py:105
  118.1 3.3 %shard_map.46 = f32[1,128,256]{2,1,0:T(8,128)} custom-call(bf16[32,2,44,128]{3,2,1,0:T(8,128)(2,1)} %get-tuple-element.6.own_ref.refs_0_, bf16[32,2,44,128]{3,2,1,0:T(8,128)(2,1)} %copy.22.refs_0_), custom_call_target="tpu_custom_call" | custom-call | flops 369098752 | bytes 1572864 | tf_op jit(solution)/shard_map/pallas_call | solution.py:105
  121.4 4.6 %shard_map.45 = f32[2,128,256]{2,1,0:T(8,128)} custom-call(bf16[32,2,44,128]{3,2,1,0:T(8,128)(2,1)} %get-tuple-element.6.own_ref.refs_0_, bf16[32,2,44,128]{3,2,1,0:T(8,128)(2,1)} %get-tuple-element.6.own_ref.refs_0_, bf16[32,2,44,128]{3,2,1,0:T(8,128)(2,1)} %copy.19.refs_1_), custom_call_target="tpu_custom_call" | custom-call | flops 738197504 | bytes 2424832 | tf_op jit(solution)/shard_map/pallas_call | solution.py:105
  129.5 6.2 %collective-permute-done.1 = bf16[32,2,44,128]{3,0,2,1:T(8,128)(2,1)} collective-permute-done((bf16[32,2,44,128]{3,0,2,1:T(8,128)(2,1)}, bf16[32,2,44,128]{3,0,2,1:T(8,128)(2,1)}, u32[]{:S(2)}, u32[]{:S(2)}) %collective-permute-start.1) | collective-permute-done | bytes 720928 | tf_op jit(solution)/shard_map/ppermute | solution.py:23
  135.7 2.3 %copy.11.refs_0_ = bf16[32,2,44,128]{3,2,1,0:T(8,128)(2,1)} copy(bf16[32,2,44,128]{3,0,2,1:T(8,128)(2,1)} %collective-permute-done.1) | data formatting | bytes 1441792 | tf_op jit(solution)/shard_map/ppermute | solution.py:23
  138.0 13.2 %collective-permute-done = bf16[32,2,44,128]{3,0,2,1:T(8,128)(2,1)} collective-permute-done((bf16[32,2,44,128]{3,0,2,1:T(8,128)(2,1)}, bf16[32,2,44,128]{3,0,2,1:T(8,128)(2,1)}, u32[]{:S(2)}, u32[]{:S(2)}) %collective-permute-start) | collective-permute-done | bytes 720928 | tf_op jit(solution)/shard_map/ppermute | solution.py:23
  151.2 2.3 %copy.8.refs_1_ = bf16[32,2,44,128]{3,2,1,0:T(8,128)(2,1)} copy(bf16[32,2,44,128]{3,0,2,1:T(8,128)(2,1)} %collective-permute-done) | data formatting | bytes 1441792 | tf_op jit(solution)/shard_map/ppermute | solution.py:23
  153.5 3.3 %shard_map.44 = f32[1,128,256]{2,1,0:T(8,128)} custom-call(bf16[32,2,44,128]{3,2,1,0:T(8,128)(2,1)} %get-tuple-element.5.own_ref.refs_0_, bf16[32,2,44,128]{3,2,1,0:T(8,128)(2,1)} %copy.14.refs_0_), custom_call_target="tpu_custom_call" | custom-call | flops 369098752 | bytes 1572864 | tf_op jit(solution)/shard_map/pallas_call | solution.py:105
  156.8 3.3 %shard_map.43 = f32[1,128,256]{2,1,0:T(8,128)} custom-call(bf16[32,2,44,128]{3,2,1,0:T(8,128)(2,1)} %get-tuple-element.5.own_ref.refs_0_, bf16[32,2,44,128]{3,2,1,0:T(8,128)(2,1)} %copy.11.refs_0_), custom_call_target="tpu_custom_call" | custom-call | flops 369098752 | bytes 1572864 | tf_op jit(solution)/shard_map/pallas_call | solution.py:105
  160.1 4.6 %shard_map.42 = f32[2,128,256]{2,1,0:T(8,128)} custom-call(bf16[32,2,44,128]{3,2,1,0:T(8,128)(2,1)} %get-tuple-element.5.own_ref.refs_0_, bf16[32,2,44,128]{3,2,1,0:T(8,128)(2,1)} %get-tuple-element.5.own_ref.refs_0_, bf16[32,2,44,128]{3,2,1,0:T(8,128)(2,1)} %copy.8.refs_1_), custom_call_target="tpu_custom_call" | custom-call | flops 738197504 | bytes 2424832 | tf_op jit(solution)/shard_map/pallas_call | solution.py:105
  169.8 3.3 %shard_map.48 = f32[1,128,256]{2,1,0:T(8,128)} custom-call(bf16[32,2,44,128]{3,2,1,0:T(8,128)(2,1)} %get-tuple-element.4.own_ref, bf16[32,2,44,128]{3,2,1,0:T(8,128)(2,1)} %copy_select_fusion.refs_0_), custom_call_target="tpu_custom_call" | custom-call | flops 369098752 | bytes 1572864 | tf_op jit(solution)/shard_map/pallas_call | solution.py:105
  (39 shorter events, 26.1 us)
Async XLA Ops:
  0.6 1.0 copy-start
  10.7 31.2 %all-to-all-start.1 = ((bf16[32,2,44,128]{3,1,2,0:T(2,128)(2,1)}), bf16[32,2,44,128]{3,1,2,0:T(2,128)(2,1)S(1)}, u32[]{:S(2)}, u32[]{:S(2)}) async-start(bf16[32,2,44,128]{3,1,2,0:T(2,128)(2,1)} %copy.15), calls=%async_computation.1 | async-start | bytes 1441792 | tf_op jit(solution)/shard_map/all_to_all | solution.py:135
  41.9 25.9 %all-to-all-start = ((bf16[32,2,44,128]{3,1,2,0:T(2,128)(2,1)}), bf16[32,2,44,128]{3,1,2,0:T(2,128)(2,1)S(1)}, u32[]{:S(2)}, u32[]{:S(2)}) async-start(bf16[32,2,44,128]{3,1,2,0:T(2,128)(2,1)} %copy.4), calls=%async_computation | async-start | bytes 1441792 | tf_op jit(solution)/shard_map/all_to_all | solution.py:135
  47.7 28.0 %collective-permute-start.5 = (bf16[32,2,44,128]{3,0,2,1:T(8,128)(2,1)}, bf16[32,2,44,128]{3,0,2,1:T(8,128)(2,1)S(1)}, u32[]{:S(2)}, u32[]{:S(2)}) collective-permute-start(bf16[32,2,44,128]{3,0,2,1:T(8,128)(2,1)} %copy.16), channel_id=1, source_target_pairs={{0,160},{32,192},{64,224},{96,0},{128,32},{160,64},{192,96},{224,1... | collective-permute-start | bytes 2162696 | tf_op jit(solution)/shard_map/ppermute | solution.py:23
  50.8 51.3 %collective-permute-start.4 = (bf16[32,2,44,128]{3,0,2,1:T(8,128)(2,1)}, bf16[32,2,44,128]{3,0,2,1:T(8,128)(2,1)}, u32[]{:S(2)}, u32[]{:S(2)}) collective-permute-start(bf16[32,2,44,128]{3,0,2,1:T(8,128)(2,1)} %copy.16), channel_id=1, source_target_pairs={{0,192},{32,224},{64,0},{96,32},{128,64},{160,96},{192,128},{224,1... | collective-permute-start | bytes 2162696 | tf_op jit(solution)/shard_map/ppermute | solution.py:23
  54.6 51.5 %collective-permute-start.3 = (bf16[32,2,44,128]{3,0,2,1:T(8,128)(2,1)}, bf16[32,2,44,128]{3,0,2,1:T(8,128)(2,1)}, u32[]{:S(2)}, u32[]{:S(2)}) collective-permute-start(bf16[32,2,44,128]{3,0,2,1:T(8,128)(2,1)} %copy.16), channel_id=1, source_target_pairs={{0,224},{32,0},{64,32},{96,64},{128,96},{160,128},{192,160},{224,1... | collective-permute-start | bytes 2162696 | tf_op jit(solution)/shard_map/ppermute | solution.py:23
  68.8 58.5 %collective-permute-start.2 = (bf16[32,2,44,128]{3,0,2,1:T(8,128)(2,1)}, bf16[32,2,44,128]{3,0,2,1:T(8,128)(2,1)}, u32[]{:S(2)}, u32[]{:S(2)}) collective-permute-start(bf16[32,2,44,128]{3,0,2,1:T(8,128)(2,1)} %copy.5), channel_id=1, source_target_pairs={{0,160},{32,192},{64,224},{96,0},{128,32},{160,64},{192,96},{224,1... | collective-permute-start | bytes 2162696 | tf_op jit(solution)/shard_map/ppermute | solution.py:23
  71.9 63.8 %collective-permute-start.1 = (bf16[32,2,44,128]{3,0,2,1:T(8,128)(2,1)}, bf16[32,2,44,128]{3,0,2,1:T(8,128)(2,1)}, u32[]{:S(2)}, u32[]{:S(2)}) collective-permute-start(bf16[32,2,44,128]{3,0,2,1:T(8,128)(2,1)} %copy.5), channel_id=1, source_target_pairs={{0,192},{32,224},{64,0},{96,32},{128,64},{160,96},{192,128},{224,1... | collective-permute-start | bytes 2162696 | tf_op jit(solution)/shard_map/ppermute | solution.py:23
  75.6 3.7 %copy-start.1 = (bf16[32,2,44,128]{3,0,2,1:T(8,128)(2,1)}, bf16[32,2,44,128]{3,0,2,1:T(8,128)(2,1)S(1)}, u32[]{:S(2)}) copy-start(bf16[32,2,44,128]{3,0,2,1:T(8,128)(2,1)S(1)} %collective-permute-done.5) | copy-start | bytes 2162692
  75.6 75.5 %collective-permute-start = (bf16[32,2,44,128]{3,0,2,1:T(8,128)(2,1)}, bf16[32,2,44,128]{3,0,2,1:T(8,128)(2,1)}, u32[]{:S(2)}, u32[]{:S(2)}) collective-permute-start(bf16[32,2,44,128]{3,0,2,1:T(8,128)(2,1)} %copy.5), channel_id=1, source_target_pairs={{0,224},{32,0},{64,32},{96,64},{128,96},{160,128},{192,160},{224,1... | collective-permute-start | bytes 2162696 | tf_op jit(solution)/shard_map/ppermute | solution.py:23
  102.1 6.9 %copy-start.2 = (bf16[32,2,44,128]{3,0,2,1:T(8,128)(2,1)S(1)}, bf16[32,2,44,128]{3,0,2,1:T(8,128)(2,1)}, u32[]{:S(2)}) copy-start(bf16[32,2,44,128]{3,0,2,1:T(8,128)(2,1)} %copy-done.1) | copy-start | bytes 2162692
  102.1 64.3 %collective-permute-start.7 = (bf16[32,2,44,128]{3,0,2,1:T(8,128)(2,1)}, bf16[32,2,44,128]{3,0,2,1:T(8,128)(2,1)S(1)}, u32[]{:S(2)}, u32[]{:S(2)}) collective-permute-start(bf16[32,2,44,128]{3,0,2,1:T(8,128)(2,1)} %copy.16), channel_id=1, source_target_pairs={{0,128},{32,160},{64,192},{96,224},{1,129},{33,161},{65,193},{97,2... | collective-permute-start | bytes 2162696 | tf_op jit(solution)/shard_map/ppermute | solution.py:141
  106.0 62.3 %collective-permute-start.6 = (bf16[32,2,44,128]{3,0,2,1:T(8,128)(2,1)}, bf16[32,2,44,128]{3,0,2,1:T(8,128)(2,1)S(1)}, u32[]{:S(2)}, u32[]{:S(2)}) collective-permute-start(bf16[32,2,44,128]{3,0,2,1:T(8,128)(2,1)} %copy.5), channel_id=1, source_target_pairs={{128,0},{160,32},{192,64},{224,96},{129,1},{161,33},{193,65},{225,... | collective-permute-start | bytes 2162696 | tf_op jit(solution)/shard_map/ppermute | solution.py:141
  121.4 4.6 %copy-start.3 = (f32[1,128,256]{2,1,0:T(8,128)S(1)}, f32[1,128,256]{2,1,0:T(8,128)}, u32[]{:S(2)}) copy-start(f32[1,128,256]{2,1,0:T(8,128)} %shard_map.47) | copy-start | bytes 393220
  121.4 4.6 %copy-start.5 = (f32[1,128,256]{2,1,0:T(8,128)S(1)}, f32[1,128,256]{2,1,0:T(8,128)}, u32[]{:S(2)}) copy-start(f32[1,128,256]{2,1,0:T(8,128)} %shard_map.46) | copy-start | bytes 393220
  160.1 4.6 %copy-start.4 = (f32[1,128,256]{2,1,0:T(8,128)S(1)}, f32[1,128,256]{2,1,0:T(8,128)}, u32[]{:S(2)}) copy-start(f32[1,128,256]{2,1,0:T(8,128)} %shard_map.44) | copy-start | bytes 393220
  160.1 4.6 %copy-start.6 = (f32[1,128,256]{2,1,0:T(8,128)S(1)}, f32[1,128,256]{2,1,0:T(8,128)}, u32[]{:S(2)}) copy-start(f32[1,128,256]{2,1,0:T(8,128)} %shard_map.43) | copy-start | bytes 393220

commit v13 on v12

--- a/solution.py
+++ b/solution.py
@@ -36,12 +36,10 @@
 
 
 def whiten_kernel(scale, table_ref, rows_ref, out_ref):
-    spectra = lax.dot_general(
-        table_ref[...], rows_ref[...], (((1,), (1,)), ((), ())), preferred_element_type=jnp.float32
-    )
-    mean_square = jnp.mean(spectra * spectra, axis=0, keepdims=True)
+    spectra = jnp.dot(rows_ref[...], table_ref[...], preferred_element_type=jnp.float32)
+    mean_square = jnp.mean(spectra * spectra, axis=1, keepdims=True)
     factor = scale / jnp.sqrt(mean_square + EPSILON)
-    out_ref[...] = (spectra * factor).astype(jnp.bfloat16)
+    out_ref[...] = (spectra * factor).T.astype(jnp.bfloat16)
 
 
 def whiten(records, taper_table, overall_scale):
@@ -54,7 +52,7 @@
         out_shape=jax.ShapeDtypeStruct((kinds, windows * chans), jnp.bfloat16),
         grid=(windows * chans // step,),
         in_specs=[
-            pl.BlockSpec((kinds, samples), lambda i: (0, 0)),
+            pl.BlockSpec((samples, kinds), lambda i: (0, 0)),
             pl.BlockSpec((step, samples), lambda i: (i, 0)),
         ],
         out_specs=pl.BlockSpec((kinds, step), lambda i: (0, i)),
@@ -64,7 +62,7 @@
             bytes_accessed=2 * (windows * chans * samples + kinds * samples + kinds * windows * chans),
             transcendentals=windows * chans,
         ),
-    )(taper_table, rows)
+    )(taper_table.T, rows)
     return out.reshape(kinds, windows, chans)
 
 

time: 178 us -> 178 us (level)
  no operation moved by 1% of the time
where the time goes in v13:
time: 178 us; the launch traced here: 177 us
  waiting for transfers between devices  75.6 us (42%)
  starting transfers between devices  39.1 us (22%)
  Pallas kernels  33.3 us (19%)
  local copies, waits for them, and re-layouts  21.5 us (12%)
  other arithmetic  6.37 us (4%)
    ppermute x6, waiting for transfers between devices, shifted(): return lax.ppermute(value, axis, pairs)  42.1 us
    all_to_all x2, waiting for transfers between devices, body(): lax.all_to_all(spectra[half], 'tm', split_axis=0, concat_axis=0, tiled=True)  31.1 us
    pallas_call x7, Pallas kernels, pair_stack(): pl.pallas_call(functools.partial(pair_kernel, step, turn), out_shape=jax....  25.8 us
    ppermute x6, starting transfers between devices, shifted(): return lax.ppermute(value, axis, pairs)  18.8 us
    all_to_all x2, starting transfers between devices, body(): lax.all_to_all(spectra[half], 'tm', split_axis=0, concat_axis=0, tiled=True)  14.9 us
    ppermute x6, local copies, waits for them, and re-layouts, shifted(): return lax.ppermute(value, axis, pairs)  12.6 us
    pallas_call x1, Pallas kernels, whiten(): pl.pallas_call(functools.partial(whiten_kernel, overall_scale), out_shape...  7.51 us
    ppermute x2, starting transfers between devices, body(): far_recv.append(lax.ppermute(blocks, 'chan', pairs))  5.41 us
  transfers between devices with their start and end apart: 10, of which 7 were waited for; matrix products, arithmetic and copies ran while one was open for 12% of the time, Pallas kernels for 13%

profile of v13, /device:TPU:2, one launch (start us, length us, event | category | flops | bytes accessed | tf_op | source)
XLA Modules:
  0.0 176.6 jit_solution(692834062338385456)
XLA Ops:
  1.6 7.5 %shard_map.41 = bf16[128,5632]{1,0:T(8,128)(2,1)S(1)} custom-call(bf16[1024,128]{1,0:T(8,128)(2,1)S(1)} %copy-done, bf16[5632,1024]{1,0:T(8,128)(2,1)} %bitcast.1), custom_call_target="tpu_custom_call" | custom-call | flops 1476395008 | bytes 13238272 | tf_op jit(solution)/shard_map/pallas_call | solution.py:50
  11.0 10.1 %all-to-all-start.1 = ((bf16[32,2,44,128]{3,1,2,0:T(2,128)(2,1)}), bf16[32,2,44,128]{3,1,2,0:T(2,128)(2,1)S(1)}, u32[]{:S(2)}, u32[]{:S(2)}) async-start(bf16[32,2,44,128]{3,1,2,0:T(2,128)(2,1)} %copy.15), calls=%async_computation.1 | async-start | bytes 1441792 | tf_op jit(solution)/shard_map/all_to_all | solution.py:133
  22.9 19.3 %all-to-all-done.1 = bf16[32,2,44,128]{3,1,2,0:T(2,128)(2,1)S(1)} async-done(((bf16[32,2,44,128]{3,1,2,0:T(2,128)(2,1)}), bf16[32,2,44,128]{3,1,2,0:T(2,128)(2,1)S(1)}, u32[]{:S(2)}, u32[]{:S(2)}) %all-to-all-start.1) | async-done | bytes 720928 | tf_op jit(solution)/shard_map/all_to_all | solution.py:133
  42.2 4.8 %all-to-all-start = ((bf16[32,2,44,128]{3,1,2,0:T(2,128)(2,1)}), bf16[32,2,44,128]{3,1,2,0:T(2,128)(2,1)S(1)}, u32[]{:S(2)}, u32[]{:S(2)}) async-start(bf16[32,2,44,128]{3,1,2,0:T(2,128)(2,1)} %copy.4), calls=%async_computation | async-start | bytes 1441792 | tf_op jit(solution)/shard_map/all_to_all | solution.py:133
  48.0 3.1 %collective-permute-start.5 = (bf16[32,2,44,128]{3,0,2,1:T(8,128)(2,1)}, bf16[32,2,44,128]{3,0,2,1:T(8,128)(2,1)S(1)}, u32[]{:S(2)}, u32[]{:S(2)}) collective-permute-start(bf16[32,2,44,128]{3,0,2,1:T(8,128)(2,1)} %copy.16), channel_id=1, source_target_pairs={{0,160},{32,192},{64,224},{96,0},{128,32},{160,64},{192,96},{224,1... | collective-permute-start | bytes 2162696 | tf_op jit(solution)/shard_map/ppermute | solution.py:23
  51.2 3.7 %collective-permute-start.4 = (bf16[32,2,44,128]{3,0,2,1:T(8,128)(2,1)}, bf16[32,2,44,128]{3,0,2,1:T(8,128)(2,1)}, u32[]{:S(2)}, u32[]{:S(2)}) collective-permute-start(bf16[32,2,44,128]{3,0,2,1:T(8,128)(2,1)} %copy.16), channel_id=1, source_target_pairs={{0,192},{32,224},{64,0},{96,32},{128,64},{160,96},{192,128},{224,1... | collective-permute-start | bytes 2162696 | tf_op jit(solution)/shard_map/ppermute | solution.py:23
  56.2 11.9 %all-to-all-done = bf16[32,2,44,128]{3,1,2,0:T(2,128)(2,1)S(1)} async-done(((bf16[32,2,44,128]{3,1,2,0:T(2,128)(2,1)}), bf16[32,2,44,128]{3,1,2,0:T(2,128)(2,1)S(1)}, u32[]{:S(2)}, u32[]{:S(2)}) %all-to-all-start) | async-done | bytes 720928 | tf_op jit(solution)/shard_map/all_to_all | solution.py:133
  69.1 3.1 %collective-permute-start.2 = (bf16[32,2,44,128]{3,0,2,1:T(8,128)(2,1)}, bf16[32,2,44,128]{3,0,2,1:T(8,128)(2,1)}, u32[]{:S(2)}, u32[]{:S(2)}) collective-permute-start(bf16[32,2,44,128]{3,0,2,1:T(8,128)(2,1)} %copy.5), channel_id=1, source_target_pairs={{0,160},{32,192},{64,224},{96,0},{128,32},{160,64},{192,96},{224,1... | collective-permute-start | bytes 2162696 | tf_op jit(solution)/shard_map/ppermute | solution.py:23
  72.2 3.7 %collective-permute-start.1 = (bf16[32,2,44,128]{3,0,2,1:T(8,128)(2,1)}, bf16[32,2,44,128]{3,0,2,1:T(8,128)(2,1)}, u32[]{:S(2)}, u32[]{:S(2)}) collective-permute-start(bf16[32,2,44,128]{3,0,2,1:T(8,128)(2,1)} %copy.5), channel_id=1, source_target_pairs={{0,192},{32,224},{64,0},{96,32},{128,64},{160,96},{192,128},{224,1... | collective-permute-start | bytes 2162696 | tf_op jit(solution)/shard_map/ppermute | solution.py:23
  76.0 3.7 %collective-permute-start = (bf16[32,2,44,128]{3,0,2,1:T(8,128)(2,1)}, bf16[32,2,44,128]{3,0,2,1:T(8,128)(2,1)}, u32[]{:S(2)}, u32[]{:S(2)}) collective-permute-start(bf16[32,2,44,128]{3,0,2,1:T(8,128)(2,1)} %copy.5), channel_id=1, source_target_pairs={{0,224},{32,0},{64,32},{96,64},{128,96},{160,128},{192,160},{224,1... | collective-permute-start | bytes 2162696 | tf_op jit(solution)/shard_map/ppermute | solution.py:23
  79.7 22.7 %collective-permute-done.4 = bf16[32,2,44,128]{3,0,2,1:T(8,128)(2,1)} collective-permute-done((bf16[32,2,44,128]{3,0,2,1:T(8,128)(2,1)}, bf16[32,2,44,128]{3,0,2,1:T(8,128)(2,1)}, u32[]{:S(2)}, u32[]{:S(2)}) %collective-permute-start.4) | collective-permute-done | bytes 720928 | tf_op jit(solution)/shard_map/ppermute | solution.py:23
  102.4 3.9 %collective-permute-start.7 = (bf16[32,2,44,128]{3,0,2,1:T(8,128)(2,1)}, bf16[32,2,44,128]{3,0,2,1:T(8,128)(2,1)S(1)}, u32[]{:S(2)}, u32[]{:S(2)}) collective-permute-start(bf16[32,2,44,128]{3,0,2,1:T(8,128)(2,1)} %copy.16), channel_id=1, source_target_pairs={{0,128},{32,160},{64,192},{96,224},{1,129},{33,161},{65,193},{97,2... | collective-permute-start | bytes 2162696 | tf_op jit(solution)/shard_map/ppermute | solution.py:139
  110.5 2.3 %copy.22.refs_0_ = bf16[32,2,44,128]{3,2,1,0:T(8,128)(2,1)} copy(bf16[32,2,44,128]{3,0,2,1:T(8,128)(2,1)} %collective-permute-done.4) | data formatting | bytes 1441792 | tf_op jit(solution)/shard_map/ppermute | solution.py:23
  115.1 3.3 %shard_map.47 = f32[1,128,256]{2,1,0:T(8,128)} custom-call(bf16[32,2,44,128]{3,2,1,0:T(8,128)(2,1)} %get-tuple-element.6.own_ref.refs_0_, bf16[32,2,44,128]{3,2,1,0:T(8,128)(2,1)} %copy.25.refs_0_), custom_call_target="tpu_custom_call" | custom-call | flops 369098752 | bytes 1572864 | tf_op jit(solution)/shard_map/pallas_call | solution.py:103
  118.4 3.3 %shard_map.46 = f32[1,128,256]{2,1,0:T(8,128)} custom-call(bf16[32,2,44,128]{3,2,1,0:T(8,128)(2,1)} %get-tuple-element.6.own_ref.refs_0_, bf16[32,2,44,128]{3,2,1,0:T(8,128)(2,1)} %copy.22.refs_0_), custom_call_target="tpu_custom_call" | custom-call | flops 369098752 | bytes 1572864 | tf_op jit(solution)/shard_map/pallas_call | solution.py:103
  121.7 4.6 %shard_map.45 = f32[2,128,256]{2,1,0:T(8,128)} custom-call(bf16[32,2,44,128]{3,2,1,0:T(8,128)(2,1)} %get-tuple-element.6.own_ref.refs_0_, bf16[32,2,44,128]{3,2,1,0:T(8,128)(2,1)} %get-tuple-element.6.own_ref.refs_0_, bf16[32,2,44,128]{3,2,1,0:T(8,128)(2,1)} %copy.19.refs_1_), custom_call_target="tpu_custom_call" | custom-call | flops 738197504 | bytes 2424832 | tf_op jit(solution)/shard_map/pallas_call | solution.py:103
  129.9 6.2 %collective-permute-done.1 = bf16[32,2,44,128]{3,0,2,1:T(8,128)(2,1)} collective-permute-done((bf16[32,2,44,128]{3,0,2,1:T(8,128)(2,1)}, bf16[32,2,44,128]{3,0,2,1:T(8,128)(2,1)}, u32[]{:S(2)}, u32[]{:S(2)}) %collective-permute-start.1) | collective-permute-done | bytes 720928 | tf_op jit(solution)/shard_map/ppermute | solution.py:23
  136.1 2.3 %copy.11.refs_0_ = bf16[32,2,44,128]{3,2,1,0:T(8,128)(2,1)} copy(bf16[32,2,44,128]{3,0,2,1:T(8,128)(2,1)} %collective-permute-done.1) | data formatting | bytes 1441792 | tf_op jit(solution)/shard_map/ppermute | solution.py:23
  138.4 13.2 %collective-permute-done = bf16[32,2,44,128]{3,0,2,1:T(8,128)(2,1)} collective-permute-done((bf16[32,2,44,128]{3,0,2,1:T(8,128)(2,1)}, bf16[32,2,44,128]{3,0,2,1:T(8,128)(2,1)}, u32[]{:S(2)}, u32[]{:S(2)}) %collective-permute-start) | collective-permute-done | bytes 720928 | tf_op jit(solution)/shard_map/ppermute | solution.py:23
  151.5 2.3 %copy.8.refs_1_ = bf16[32,2,44,128]{3,2,1,0:T(8,128)(2,1)} copy(bf16[32,2,44,128]{3,0,2,1:T(8,128)(2,1)} %collective-permute-done) | data formatting | bytes 1441792 | tf_op jit(solution)/shard_map/ppermute | solution.py:23
  153.8 3.3 %shard_map.44 = f32[1,128,256]{2,1,0:T(8,128)} custom-call(bf16[32,2,44,128]{3,2,1,0:T(8,128)(2,1)} %get-tuple-element.5.own_ref.refs_0_, bf16[32,2,44,128]{3,2,1,0:T(8,128)(2,1)} %copy.14.refs_0_), custom_call_target="tpu_custom_call" | custom-call | flops 369098752 | bytes 1572864 | tf_op jit(solution)/shard_map/pallas_call | solution.py:103
  157.2 3.3 %shard_map.43 = f32[1,128,256]{2,1,0:T(8,128)} custom-call(bf16[32,2,44,128]{3,2,1,0:T(8,128)(2,1)} %get-tuple-element.5.own_ref.refs_0_, bf16[32,2,44,128]{3,2,1,0:T(8,128)(2,1)} %copy.11.refs_0_), custom_call_target="tpu_custom_call" | custom-call | flops 369098752 | bytes 1572864 | tf_op jit(solution)/shard_map/pallas_call | solution.py:103
  160.5 4.6 %shard_map.42 = f32[2,128,256]{2,1,0:T(8,128)} custom-call(bf16[32,2,44,128]{3,2,1,0:T(8,128)(2,1)} %get-tuple-element.5.own_ref.refs_0_, bf16[32,2,44,128]{3,2,1,0:T(8,128)(2,1)} %get-tuple-element.5.own_ref.refs_0_, bf16[32,2,44,128]{3,2,1,0:T(8,128)(2,1)} %copy.8.refs_1_), custom_call_target="tpu_custom_call" | custom-call | flops 738197504 | bytes 2424832 | tf_op jit(solution)/shard_map/pallas_call | solution.py:103
  170.2 3.3 %shard_map.48 = f32[1,128,256]{2,1,0:T(8,128)} custom-call(bf16[32,2,44,128]{3,2,1,0:T(8,128)(2,1)} %get-tuple-element.4.own_ref, bf16[32,2,44,128]{3,2,1,0:T(8,128)(2,1)} %copy_select_fusion.refs_0_), custom_call_target="tpu_custom_call" | custom-call | flops 369098752 | bytes 1572864 | tf_op jit(solution)/shard_map/pallas_call | solution.py:103
  (39 shorter events, 26.1 us)
Async XLA Ops:
  0.6 1.0 copy-start
  11.0 31.2 %all-to-all-start.1 = ((bf16[32,2,44,128]{3,1,2,0:T(2,128)(2,1)}), bf16[32,2,44,128]{3,1,2,0:T(2,128)(2,1)S(1)}, u32[]{:S(2)}, u32[]{:S(2)}) async-start(bf16[32,2,44,128]{3,1,2,0:T(2,128)(2,1)} %copy.15), calls=%async_computation.1 | async-start | bytes 1441792 | tf_op jit(solution)/shard_map/all_to_all | solution.py:133
  42.2 25.9 %all-to-all-start = ((bf16[32,2,44,128]{3,1,2,0:T(2,128)(2,1)}), bf16[32,2,44,128]{3,1,2,0:T(2,128)(2,1)S(1)}, u32[]{:S(2)}, u32[]{:S(2)}) async-start(bf16[32,2,44,128]{3,1,2,0:T(2,128)(2,1)} %copy.4), calls=%async_computation | async-start | bytes 1441792 | tf_op jit(solution)/shard_map/all_to_all | solution.py:133
  48.0 28.0 %collective-permute-start.5 = (bf16[32,2,44,128]{3,0,2,1:T(8,128)(2,1)}, bf16[32,2,44,128]{3,0,2,1:T(8,128)(2,1)S(1)}, u32[]{:S(2)}, u32[]{:S(2)}) collective-permute-start(bf16[32,2,44,128]{3,0,2,1:T(8,128)(2,1)} %copy.16), channel_id=1, source_target_pairs={{0,160},{32,192},{64,224},{96,0},{128,32},{160,64},{192,96},{224,1... | collective-permute-start | bytes 2162696 | tf_op jit(solution)/shard_map/ppermute | solution.py:23
  51.2 51.3 %collective-permute-start.4 = (bf16[32,2,44,128]{3,0,2,1:T(8,128)(2,1)}, bf16[32,2,44,128]{3,0,2,1:T(8,128)(2,1)}, u32[]{:S(2)}, u32[]{:S(2)}) collective-permute-start(bf16[32,2,44,128]{3,0,2,1:T(8,128)(2,1)} %copy.16), channel_id=1, source_target_pairs={{0,192},{32,224},{64,0},{96,32},{128,64},{160,96},{192,128},{224,1... | collective-permute-start | bytes 2162696 | tf_op jit(solution)/shard_map/ppermute | solution.py:23
  54.9 51.5 %collective-permute-start.3 = (bf16[32,2,44,128]{3,0,2,1:T(8,128)(2,1)}, bf16[32,2,44,128]{3,0,2,1:T(8,128)(2,1)}, u32[]{:S(2)}, u32[]{:S(2)}) collective-permute-start(bf16[32,2,44,128]{3,0,2,1:T(8,128)(2,1)} %copy.16), channel_id=1, source_target_pairs={{0,224},{32,0},{64,32},{96,64},{128,96},{160,128},{192,160},{224,1... | collective-permute-start | bytes 2162696 | tf_op jit(solution)/shard_map/ppermute | solution.py:23
  69.1 58.5 %collective-permute-start.2 = (bf16[32,2,44,128]{3,0,2,1:T(8,128)(2,1)}, bf16[32,2,44,128]{3,0,2,1:T(8,128)(2,1)}, u32[]{:S(2)}, u32[]{:S(2)}) collective-permute-start(bf16[32,2,44,128]{3,0,2,1:T(8,128)(2,1)} %copy.5), channel_id=1, source_target_pairs={{0,160},{32,192},{64,224},{96,0},{128,32},{160,64},{192,96},{224,1... | collective-permute-start | bytes 2162696 | tf_op jit(solution)/shard_map/ppermute | solution.py:23
  72.2 63.8 %collective-permute-start.1 = (bf16[32,2,44,128]{3,0,2,1:T(8,128)(2,1)}, bf16[32,2,44,128]{3,0,2,1:T(8,128)(2,1)}, u32[]{:S(2)}, u32[]{:S(2)}) collective-permute-start(bf16[32,2,44,128]{3,0,2,1:T(8,128)(2,1)} %copy.5), channel_id=1, source_target_pairs={{0,192},{32,224},{64,0},{96,32},{128,64},{160,96},{192,128},{224,1... | collective-permute-start | bytes 2162696 | tf_op jit(solution)/shard_map/ppermute | solution.py:23
  76.0 3.7 %copy-start.1 = (bf16[32,2,44,128]{3,0,2,1:T(8,128)(2,1)}, bf16[32,2,44,128]{3,0,2,1:T(8,128)(2,1)S(1)}, u32[]{:S(2)}) copy-start(bf16[32,2,44,128]{3,0,2,1:T(8,128)(2,1)S(1)} %collective-permute-done.5) | copy-start | bytes 2162692
  76.0 75.5 %collective-permute-start = (bf16[32,2,44,128]{3,0,2,1:T(8,128)(2,1)}, bf16[32,2,44,128]{3,0,2,1:T(8,128)(2,1)}, u32[]{:S(2)}, u32[]{:S(2)}) collective-permute-start(bf16[32,2,44,128]{3,0,2,1:T(8,128)(2,1)} %copy.5), channel_id=1, source_target_pairs={{0,224},{32,0},{64,32},{96,64},{128,96},{160,128},{192,160},{224,1... | collective-permute-start | bytes 2162696 | tf_op jit(solution)/shard_map/ppermute | solution.py:23
  102.4 6.9 %copy-start.2 = (bf16[32,2,44,128]{3,0,2,1:T(8,128)(2,1)S(1)}, bf16[32,2,44,128]{3,0,2,1:T(8,128)(2,1)}, u32[]{:S(2)}) copy-start(bf16[32,2,44,128]{3,0,2,1:T(8,128)(2,1)} %copy-done.1) | copy-start | bytes 2162692
  102.4 64.3 %collective-permute-start.7 = (bf16[32,2,44,128]{3,0,2,1:T(8,128)(2,1)}, bf16[32,2,44,128]{3,0,2,1:T(8,128)(2,1)S(1)}, u32[]{:S(2)}, u32[]{:S(2)}) collective-permute-start(bf16[32,2,44,128]{3,0,2,1:T(8,128)(2,1)} %copy.16), channel_id=1, source_target_pairs={{0,128},{32,160},{64,192},{96,224},{1,129},{33,161},{65,193},{97,2... | collective-permute-start | bytes 2162696 | tf_op jit(solution)/shard_map/ppermute | solution.py:139
  106.4 62.3 %collective-permute-start.6 = (bf16[32,2,44,128]{3,0,2,1:T(8,128)(2,1)}, bf16[32,2,44,128]{3,0,2,1:T(8,128)(2,1)S(1)}, u32[]{:S(2)}, u32[]{:S(2)}) collective-permute-start(bf16[32,2,44,128]{3,0,2,1:T(8,128)(2,1)} %copy.5), channel_id=1, source_target_pairs={{128,0},{160,32},{192,64},{224,96},{129,1},{161,33},{193,65},{225,... | collective-permute-start | bytes 2162696 | tf_op jit(solution)/shard_map/ppermute | solution.py:139
  121.7 4.6 %copy-start.3 = (f32[1,128,256]{2,1,0:T(8,128)S(1)}, f32[1,128,256]{2,1,0:T(8,128)}, u32[]{:S(2)}) copy-start(f32[1,128,256]{2,1,0:T(8,128)} %shard_map.47) | copy-start | bytes 393220
  121.7 4.6 %copy-start.5 = (f32[1,128,256]{2,1,0:T(8,128)S(1)}, f32[1,128,256]{2,1,0:T(8,128)}, u32[]{:S(2)}) copy-start(f32[1,128,256]{2,1,0:T(8,128)} %shard_map.46) | copy-start | bytes 393220
  160.5 4.6 %copy-start.4 = (f32[1,128,256]{2,1,0:T(8,128)S(1)}, f32[1,128,256]{2,1,0:T(8,128)}, u32[]{:S(2)}) copy-start(f32[1,128,256]{2,1,0:T(8,128)} %shard_map.44) | copy-start | bytes 393220
  160.5 4.6 %copy-start.6 = (f32[1,128,256]{2,1,0:T(8,128)S(1)}, f32[1,128,256]{2,1,0:T(8,128)}, u32[]{:S(2)}) copy-start(f32[1,128,256]{2,1,0:T(8,128)} %shard_map.43) | copy-start | bytes 393220

commit v14 on v10

--- a/solution.py
+++ b/solution.py
@@ -42,7 +42,10 @@
 
 
 def pair_kernel(group_count, turn, own_ref, *refs):
-    mate_refs, out_ref = refs[:-1], refs[-1]
+    if turn:
+        mate_refs, final_ref, out_ref = refs[:-2], refs[-2], refs[-1]
+    else:
+        mate_refs, out_ref = refs[:-1], refs[-1]
     chans = out_ref.shape[-2]
     contract = (((0,), (0,)), ((), ()))
 
@@ -62,12 +65,17 @@
 
     if turn:
         upper = lax.axis_index("chan") >= lax.axis_size("chan") // 2
+        last = pl.program_id(0) == pl.num_programs(0) - 1
 
-        @pl.when(jnp.logical_and(upper, pl.program_id(0) == pl.num_programs(0) - 1))
+        @pl.when(jnp.logical_and(last, jnp.logical_not(upper)))
         def _():
-            real = out_ref[0, :, :chans]
-            imag = out_ref[0, :, chans:]
-            out_ref[0] = jnp.concatenate([real.T, -imag.T], axis=1)
+            final_ref[:, 0, :] = out_ref[0, :, :chans]
+            final_ref[:, 1, :] = out_ref[0, :, chans:]
+
+        @pl.when(jnp.logical_and(last, upper))
+        def _():
+            final_ref[:, 0, :] = out_ref[0, :, :chans].T
+            final_ref[:, 1, :] = -out_ref[0, :, chans:].T
 
 
 def pair_stack(own, mates, turn=False):
@@ -75,12 +83,22 @@
     step = GROUPS_PER_STEP
     spec = pl.BlockSpec((step, 2, width, chans), lambda n: (n, 0, 0, 0))
     count = len(mates)
+    total_shape = (count, chans, 2 * chans)
+    if turn:
+        out_shape = jax.ShapeDtypeStruct((chans, 2, chans), jnp.float32)
+        out_spec = pl.BlockSpec((chans, 2, chans), lambda n: (0, 0, 0))
+        scratch = [pltpu.VMEM(total_shape, jnp.float32)]
+    else:
+        out_shape = jax.ShapeDtypeStruct(total_shape, jnp.float32)
+        out_spec = pl.BlockSpec(total_shape, lambda n: (0, 0, 0))
+        scratch = []
     return pl.pallas_call(
         functools.partial(pair_kernel, step, turn),
-        out_shape=jax.ShapeDtypeStruct((count, chans, 2 * chans), jnp.float32),
+        out_shape=out_shape,
         grid=(groups // step,),
         in_specs=[spec] * (count + 1),
-        out_specs=pl.BlockSpec((count, chans, 2 * chans), lambda n: (0, 0, 0)),
+        out_specs=out_spec,
+        scratch_shapes=scratch,
         cost_estimate=pl.CostEstimate(
             flops=2 * count * groups * 2 * width * 4 * chans * chans,
             bytes_accessed=2 * (count + 1) * groups * 2 * width * chans + 4 * count * chans * 2 * chans,

time: 176 us -> 174 us (0.989)
  transfers between devices with their start and end apart: 10 -> 10, of which waited for: 7 -> 6; matrix products, arithmetic and copies ran while one was open for 12% -> 13% of each run, Pallas kernels for 13% -> 13%
where the time goes in v14:
time: 174 us; the launch traced here: 172 us
  waiting for transfers between devices  74.2 us (43%)
  starting transfers between devices  39.1 us (22%)
  Pallas kernels  26.1 us (15%)
  local copies, waits for them, and re-layouts  18 us (10%)
  other arithmetic  6.98 us (4%)
  matrix products  6.79 us (4%)
    ppermute x6, waiting for transfers between devices, shifted(): return lax.ppermute(value, axis, pairs)  41.9 us
    all_to_all x2, waiting for transfers between devices, body(): lax.all_to_all(spectra[half], 'tm', split_axis=0, concat_axis=0, tiled=True)  31.6 us
    pallas_call x7, Pallas kernels, pair_stack(): pl.pallas_call(functools.partial(pair_kernel, step, turn), out_shape=out_...  26.1 us
    ppermute x6, starting transfers between devices, shifted(): return lax.ppermute(value, axis, pairs)  18.8 us
    all_to_all x2, starting transfers between devices, body(): lax.all_to_all(spectra[half], 'tm', split_axis=0, concat_axis=0, tiled=True)  14.9 us
    ppermute x6, local copies, waits for them, and re-layouts, shifted(): return lax.ppermute(value, axis, pairs)  12.7 us
    dot_general x1, matrix products, whiten(): jnp.einsum('ks,wcs->kwc', taper_table, records, preferred_element_type=jn...  6.79 us
    ppermute x2, starting transfers between devices, body(): far_recv.append(lax.ppermute(blocks, 'chan', pairs))  5.41 us
  transfers between devices with their start and end apart: 10, of which 6 were waited for; matrix products, arithmetic and copies ran while one was open for 13% of the time, Pallas kernels for 13%

profile of v14, /device:TPU:2, one launch (start us, length us, event | category | flops | bytes accessed | tf_op | source)
XLA Modules:
  0.0 171.9 jit_solution(6748407474312610695)
XLA Ops:
  0.6 6.8 %multiply_reduce_fusion = (f32[44,128]{1,0:T(8,128)S(1)}, f32[128,44,128]{2,0,1:T(8,128)S(1)}) fusion(bf16[128,1024,1]{1,0,2:T(8,128)(2,1)} %constant.21, bf16[44,128,1024]{2,1,0:T(8,128)(2,1)} %param.2), kind=kOutput, calls=%fused_computation.1 | convolution fusion | flops 1477831168 | bytes 14702592 | tf_op jit(solution)/shard_map/ks,wcs->kwc/dot_general | solution.py:38
  9.3 10.1 %all-to-all-start.1 = ((bf16[32,2,44,128]{3,1,2,0:T(2,128)(2,1)}), bf16[32,2,44,128]{3,1,2,0:T(2,128)(2,1)S(1)}, u32[]{:S(2)}, u32[]{:S(2)}) async-start(bf16[32,2,44,128]{3,1,2,0:T(2,128)(2,1)} %copy.17), calls=%async_computation.1 | async-start | bytes 1441792 | tf_op jit(solution)/shard_map/all_to_all | solution.py:126
  20.8 19.8 %all-to-all-done.1 = bf16[32,2,44,128]{3,1,2,0:T(2,128)(2,1)S(1)} async-done(((bf16[32,2,44,128]{3,1,2,0:T(2,128)(2,1)}), bf16[32,2,44,128]{3,1,2,0:T(2,128)(2,1)S(1)}, u32[]{:S(2)}, u32[]{:S(2)}) %all-to-all-start.1) | async-done | bytes 720928 | tf_op jit(solution)/shard_map/all_to_all | solution.py:126
  40.5 4.8 %all-to-all-start = ((bf16[32,2,44,128]{3,1,2,0:T(2,128)(2,1)}), bf16[32,2,44,128]{3,1,2,0:T(2,128)(2,1)S(1)}, u32[]{:S(2)}, u32[]{:S(2)}) async-start(bf16[32,2,44,128]{3,1,2,0:T(2,128)(2,1)} %copy.6), calls=%async_computation | async-start | bytes 1441792 | tf_op jit(solution)/shard_map/all_to_all | solution.py:126
  46.3 3.1 %collective-permute-start.5 = (bf16[32,2,44,128]{3,0,2,1:T(8,128)(2,1)}, bf16[32,2,44,128]{3,0,2,1:T(8,128)(2,1)S(1)}, u32[]{:S(2)}, u32[]{:S(2)}) collective-permute-start(bf16[32,2,44,128]{3,0,2,1:T(8,128)(2,1)} %copy.18), channel_id=1, source_target_pairs={{0,160},{32,192},{64,224},{96,0},{128,32},{160,64},{192,96},{224,1... | collective-permute-start | bytes 2162696 | tf_op jit(solution)/shard_map/ppermute | solution.py:22
  49.4 3.7 %collective-permute-start.4 = (bf16[32,2,44,128]{3,0,2,1:T(8,128)(2,1)}, bf16[32,2,44,128]{3,0,2,1:T(8,128)(2,1)}, u32[]{:S(2)}, u32[]{:S(2)}) collective-permute-start(bf16[32,2,44,128]{3,0,2,1:T(8,128)(2,1)} %copy.18), channel_id=1, source_target_pairs={{0,192},{32,224},{64,0},{96,32},{128,64},{160,96},{192,128},{224,1... | collective-permute-start | bytes 2162696 | tf_op jit(solution)/shard_map/ppermute | solution.py:22
  54.5 11.9 %all-to-all-done = bf16[32,2,44,128]{3,1,2,0:T(2,128)(2,1)S(1)} async-done(((bf16[32,2,44,128]{3,1,2,0:T(2,128)(2,1)}), bf16[32,2,44,128]{3,1,2,0:T(2,128)(2,1)S(1)}, u32[]{:S(2)}, u32[]{:S(2)}) %all-to-all-start) | async-done | bytes 720928 | tf_op jit(solution)/shard_map/all_to_all | solution.py:126
  67.4 3.1 %collective-permute-start.2 = (bf16[32,2,44,128]{3,0,2,1:T(8,128)(2,1)}, bf16[32,2,44,128]{3,0,2,1:T(8,128)(2,1)}, u32[]{:S(2)}, u32[]{:S(2)}) collective-permute-start(bf16[32,2,44,128]{3,0,2,1:T(8,128)(2,1)} %copy.7), channel_id=1, source_target_pairs={{0,160},{32,192},{64,224},{96,0},{128,32},{160,64},{192,96},{224,1... | collective-permute-start | bytes 2162696 | tf_op jit(solution)/shard_map/ppermute | solution.py:22
  70.6 3.7 %collective-permute-start.1 = (bf16[32,2,44,128]{3,0,2,1:T(8,128)(2,1)}, bf16[32,2,44,128]{3,0,2,1:T(8,128)(2,1)}, u32[]{:S(2)}, u32[]{:S(2)}) collective-permute-start(bf16[32,2,44,128]{3,0,2,1:T(8,128)(2,1)} %copy.7), channel_id=1, source_target_pairs={{0,192},{32,224},{64,0},{96,32},{128,64},{160,96},{192,128},{224,1... | collective-permute-start | bytes 2162696 | tf_op jit(solution)/shard_map/ppermute | solution.py:22
  74.3 3.7 %collective-permute-start = (bf16[32,2,44,128]{3,0,2,1:T(8,128)(2,1)}, bf16[32,2,44,128]{3,0,2,1:T(8,128)(2,1)}, u32[]{:S(2)}, u32[]{:S(2)}) collective-permute-start(bf16[32,2,44,128]{3,0,2,1:T(8,128)(2,1)} %copy.7), channel_id=1, source_target_pairs={{0,224},{32,0},{64,32},{96,64},{128,96},{160,128},{192,160},{224,1... | collective-permute-start | bytes 2162696 | tf_op jit(solution)/shard_map/ppermute | solution.py:22
  78.0 22.7 %collective-permute-done.4 = bf16[32,2,44,128]{3,0,2,1:T(8,128)(2,1)} collective-permute-done((bf16[32,2,44,128]{3,0,2,1:T(8,128)(2,1)}, bf16[32,2,44,128]{3,0,2,1:T(8,128)(2,1)}, u32[]{:S(2)}, u32[]{:S(2)}) %collective-permute-start.4) | collective-permute-done | bytes 720928 | tf_op jit(solution)/shard_map/ppermute | solution.py:22
  100.7 3.9 %collective-permute-start.7 = (bf16[32,2,44,128]{3,0,2,1:T(8,128)(2,1)}, bf16[32,2,44,128]{3,0,2,1:T(8,128)(2,1)S(1)}, u32[]{:S(2)}, u32[]{:S(2)}) collective-permute-start(bf16[32,2,44,128]{3,0,2,1:T(8,128)(2,1)} %copy.18), channel_id=1, source_target_pairs={{0,128},{32,160},{64,192},{96,224},{1,129},{33,161},{65,193},{97,2... | collective-permute-start | bytes 2162696 | tf_op jit(solution)/shard_map/ppermute | solution.py:132
  111.1 2.3 %copy.21.refs_1_ = bf16[32,2,44,128]{3,2,1,0:T(8,128)(2,1)} copy(bf16[32,2,44,128]{3,0,2,1:T(8,128)(2,1)} %collective-permute-done.3) | data formatting | bytes 1441792 | tf_op jit(solution)/shard_map/ppermute | solution.py:22
  113.4 3.3 %shard_map.46 = f32[1,128,256]{2,1,0:T(8,128)} custom-call(bf16[32,2,44,128]{3,2,1,0:T(8,128)(2,1)} %get-tuple-element.6.own_ref.refs_0_, bf16[32,2,44,128]{3,2,1,0:T(8,128)(2,1)} %copy.27.refs_0_), custom_call_target="tpu_custom_call" | custom-call | flops 369098752 | bytes 1572864 | tf_op jit(solution)/shard_map/pallas_call | solution.py:95
  116.8 3.4 %shard_map.45 = f32[1,128,256]{2,1,0:T(8,128)} custom-call(bf16[32,2,44,128]{3,2,1,0:T(8,128)(2,1)} %get-tuple-element.6.own_ref.refs_0_, bf16[32,2,44,128]{3,2,1,0:T(8,128)(2,1)} %copy.24.refs_0_), custom_call_target="tpu_custom_call" | custom-call | flops 369098752 | bytes 1572864 | tf_op jit(solution)/shard_map/pallas_call | solution.py:95
  120.1 4.6 %shard_map.44 = f32[2,128,256]{2,1,0:T(8,128)} custom-call(bf16[32,2,44,128]{3,2,1,0:T(8,128)(2,1)} %get-tuple-element.6.own_ref.refs_0_, bf16[32,2,44,128]{3,2,1,0:T(8,128)(2,1)} %get-tuple-element.6.own_ref.refs_0_, bf16[32,2,44,128]{3,2,1,0:T(8,128)(2,1)} %copy.21.refs_1_), custom_call_target="tpu_custom_call" | custom-call | flops 738197504 | bytes 2424832 | tf_op jit(solution)/shard_map/pallas_call | solution.py:95
  126.1 2.3 %copy.16.refs_0_ = bf16[32,2,44,128]{3,2,1,0:T(8,128)(2,1)} copy(bf16[32,2,44,128]{3,0,2,1:T(8,128)(2,1)} %collective-permute-done.2) | data formatting | bytes 1441792 | tf_op jit(solution)/shard_map/ppermute | solution.py:22
  128.4 6.0 %collective-permute-done.1 = bf16[32,2,44,128]{3,0,2,1:T(8,128)(2,1)} collective-permute-done((bf16[32,2,44,128]{3,0,2,1:T(8,128)(2,1)}, bf16[32,2,44,128]{3,0,2,1:T(8,128)(2,1)}, u32[]{:S(2)}, u32[]{:S(2)}) %collective-permute-start.1) | collective-permute-done | bytes 720928 | tf_op jit(solution)/shard_map/ppermute | solution.py:22
  134.4 2.3 %copy.13.refs_0_ = bf16[32,2,44,128]{3,2,1,0:T(8,128)(2,1)} copy(bf16[32,2,44,128]{3,0,2,1:T(8,128)(2,1)} %collective-permute-done.1) | data formatting | bytes 1441792 | tf_op jit(solution)/shard_map/ppermute | solution.py:22
  136.7 13.2 %collective-permute-done = bf16[32,2,44,128]{3,0,2,1:T(8,128)(2,1)} collective-permute-done((bf16[32,2,44,128]{3,0,2,1:T(8,128)(2,1)}, bf16[32,2,44,128]{3,0,2,1:T(8,128)(2,1)}, u32[]{:S(2)}, u32[]{:S(2)}) %collective-permute-start) | collective-permute-done | bytes 720928 | tf_op jit(solution)/shard_map/ppermute | solution.py:22
  152.1 3.3 %shard_map.43 = f32[1,128,256]{2,1,0:T(8,128)} custom-call(bf16[32,2,44,128]{3,2,1,0:T(8,128)(2,1)} %get-tuple-element.5.own_ref.refs_0_, bf16[32,2,44,128]{3,2,1,0:T(8,128)(2,1)} %copy.16.refs_0_), custom_call_target="tpu_custom_call" | custom-call | flops 369098752 | bytes 1572864 | tf_op jit(solution)/shard_map/pallas_call | solution.py:95
  155.5 3.4 %shard_map.42 = f32[1,128,256]{2,1,0:T(8,128)} custom-call(bf16[32,2,44,128]{3,2,1,0:T(8,128)(2,1)} %get-tuple-element.5.own_ref.refs_0_, bf16[32,2,44,128]{3,2,1,0:T(8,128)(2,1)} %copy.13.refs_0_), custom_call_target="tpu_custom_call" | custom-call | flops 369098752 | bytes 1572864 | tf_op jit(solution)/shard_map/pallas_call | solution.py:95
  158.8 4.7 %shard_map.41 = f32[2,128,256]{2,1,0:T(8,128)} custom-call(bf16[32,2,44,128]{3,2,1,0:T(8,128)(2,1)} %get-tuple-element.5.own_ref.refs_0_, bf16[32,2,44,128]{3,2,1,0:T(8,128)(2,1)} %get-tuple-element.5.own_ref.refs_0_, bf16[32,2,44,128]{3,2,1,0:T(8,128)(2,1)} %copy.10.refs_1_), custom_call_target="tpu_custom_call" | custom-call | flops 738197504 | bytes 2424832 | tf_op jit(solution)/shard_map/pallas_call | solution.py:95
  168.5 3.4 %shard_map.47 = f32[128,2,128]{2,1,0:T(2,128)} custom-call(bf16[32,2,44,128]{3,2,1,0:T(8,128)(2,1)} %get-tuple-element.4.own_ref, bf16[32,2,44,128]{3,2,1,0:T(8,128)(2,1)} %copy_select_fusion.refs_0_), custom_call_target="tpu_custom_call" | custom-call | flops 369098752 | bytes 1572864 | tf_op jit(solution)/shard_map/pallas_call | solution.py:95
  (32 shorter events, 21.6 us)
Async XLA Ops:
  9.3 31.2 %all-to-all-start.1 = ((bf16[32,2,44,128]{3,1,2,0:T(2,128)(2,1)}), bf16[32,2,44,128]{3,1,2,0:T(2,128)(2,1)S(1)}, u32[]{:S(2)}, u32[]{:S(2)}) async-start(bf16[32,2,44,128]{3,1,2,0:T(2,128)(2,1)} %copy.17), calls=%async_computation.1 | async-start | bytes 1441792 | tf_op jit(solution)/shard_map/all_to_all | solution.py:126
  40.5 25.9 %all-to-all-start = ((bf16[32,2,44,128]{3,1,2,0:T(2,128)(2,1)}), bf16[32,2,44,128]{3,1,2,0:T(2,128)(2,1)S(1)}, u32[]{:S(2)}, u32[]{:S(2)}) async-start(bf16[32,2,44,128]{3,1,2,0:T(2,128)(2,1)} %copy.6), calls=%async_computation | async-start | bytes 1441792 | tf_op jit(solution)/shard_map/all_to_all | solution.py:126
  46.3 28.0 %collective-permute-start.5 = (bf16[32,2,44,128]{3,0,2,1:T(8,128)(2,1)}, bf16[32,2,44,128]{3,0,2,1:T(8,128)(2,1)S(1)}, u32[]{:S(2)}, u32[]{:S(2)}) collective-permute-start(bf16[32,2,44,128]{3,0,2,1:T(8,128)(2,1)} %copy.18), channel_id=1, source_target_pairs={{0,160},{32,192},{64,224},{96,0},{128,32},{160,64},{192,96},{224,1... | collective-permute-start | bytes 2162696 | tf_op jit(solution)/shard_map/ppermute | solution.py:22
  49.4 51.3 %collective-permute-start.4 = (bf16[32,2,44,128]{3,0,2,1:T(8,128)(2,1)}, bf16[32,2,44,128]{3,0,2,1:T(8,128)(2,1)}, u32[]{:S(2)}, u32[]{:S(2)}) collective-permute-start(bf16[32,2,44,128]{3,0,2,1:T(8,128)(2,1)} %copy.18), channel_id=1, source_target_pairs={{0,192},{32,224},{64,0},{96,32},{128,64},{160,96},{192,128},{224,1... | collective-permute-start | bytes 2162696 | tf_op jit(solution)/shard_map/ppermute | solution.py:22
  53.2 51.5 %collective-permute-start.3 = (bf16[32,2,44,128]{3,0,2,1:T(8,128)(2,1)}, bf16[32,2,44,128]{3,0,2,1:T(8,128)(2,1)}, u32[]{:S(2)}, u32[]{:S(2)}) collective-permute-start(bf16[32,2,44,128]{3,0,2,1:T(8,128)(2,1)} %copy.18), channel_id=1, source_target_pairs={{0,224},{32,0},{64,32},{96,64},{128,96},{160,128},{192,160},{224,1... | collective-permute-start | bytes 2162696 | tf_op jit(solution)/shard_map/ppermute | solution.py:22
  67.4 58.6 %collective-permute-start.2 = (bf16[32,2,44,128]{3,0,2,1:T(8,128)(2,1)}, bf16[32,2,44,128]{3,0,2,1:T(8,128)(2,1)}, u32[]{:S(2)}, u32[]{:S(2)}) collective-permute-start(bf16[32,2,44,128]{3,0,2,1:T(8,128)(2,1)} %copy.7), channel_id=1, source_target_pairs={{0,160},{32,192},{64,224},{96,0},{128,32},{160,64},{192,96},{224,1... | collective-permute-start | bytes 2162696 | tf_op jit(solution)/shard_map/ppermute | solution.py:22
  70.6 63.8 %collective-permute-start.1 = (bf16[32,2,44,128]{3,0,2,1:T(8,128)(2,1)}, bf16[32,2,44,128]{3,0,2,1:T(8,128)(2,1)}, u32[]{:S(2)}, u32[]{:S(2)}) collective-permute-start(bf16[32,2,44,128]{3,0,2,1:T(8,128)(2,1)} %copy.7), channel_id=1, source_target_pairs={{0,192},{32,224},{64,0},{96,32},{128,64},{160,96},{192,128},{224,1... | collective-permute-start | bytes 2162696 | tf_op jit(solution)/shard_map/ppermute | solution.py:22
  74.3 3.7 %copy-start = (bf16[32,2,44,128]{3,0,2,1:T(8,128)(2,1)}, bf16[32,2,44,128]{3,0,2,1:T(8,128)(2,1)S(1)}, u32[]{:S(2)}) copy-start(bf16[32,2,44,128]{3,0,2,1:T(8,128)(2,1)S(1)} %collective-permute-done.5) | copy-start | bytes 2162692
  74.3 75.5 %collective-permute-start = (bf16[32,2,44,128]{3,0,2,1:T(8,128)(2,1)}, bf16[32,2,44,128]{3,0,2,1:T(8,128)(2,1)}, u32[]{:S(2)}, u32[]{:S(2)}) collective-permute-start(bf16[32,2,44,128]{3,0,2,1:T(8,128)(2,1)} %copy.7), channel_id=1, source_target_pairs={{0,224},{32,0},{64,32},{96,64},{128,96},{160,128},{192,160},{224,1... | collective-permute-start | bytes 2162696 | tf_op jit(solution)/shard_map/ppermute | solution.py:22
  100.7 7.0 %copy-start.1 = (bf16[32,2,44,128]{3,0,2,1:T(8,128)(2,1)S(1)}, bf16[32,2,44,128]{3,0,2,1:T(8,128)(2,1)}, u32[]{:S(2)}) copy-start(bf16[32,2,44,128]{3,0,2,1:T(8,128)(2,1)} %copy-done) | copy-start | bytes 2162692
  100.7 65.6 %collective-permute-start.7 = (bf16[32,2,44,128]{3,0,2,1:T(8,128)(2,1)}, bf16[32,2,44,128]{3,0,2,1:T(8,128)(2,1)S(1)}, u32[]{:S(2)}, u32[]{:S(2)}) collective-permute-start(bf16[32,2,44,128]{3,0,2,1:T(8,128)(2,1)} %copy.18), channel_id=1, source_target_pairs={{0,128},{32,160},{64,192},{96,224},{1,129},{33,161},{65,193},{97,2... | collective-permute-start | bytes 2162696 | tf_op jit(solution)/shard_map/ppermute | solution.py:132
  104.7 62.3 %collective-permute-start.6 = (bf16[32,2,44,128]{3,0,2,1:T(8,128)(2,1)}, bf16[32,2,44,128]{3,0,2,1:T(8,128)(2,1)S(1)}, u32[]{:S(2)}, u32[]{:S(2)}) collective-permute-start(bf16[32,2,44,128]{3,0,2,1:T(8,128)(2,1)} %copy.7), channel_id=1, source_target_pairs={{128,0},{160,32},{192,64},{224,96},{129,1},{161,33},{193,65},{225,... | collective-permute-start | bytes 2162696 | tf_op jit(solution)/shard_map/ppermute | solution.py:132
  116.8 8.0 %copy-start.2 = (f32[1,128,256]{2,1,0:T(8,128)S(1)}, f32[1,128,256]{2,1,0:T(8,128)}, u32[]{:S(2)}) copy-start(f32[1,128,256]{2,1,0:T(8,128)} %shard_map.46) | copy-start | bytes 393220
  155.4 8.1 %copy-start.3 = (f32[1,128,256]{2,1,0:T(8,128)S(1)}, f32[1,128,256]{2,1,0:T(8,128)}, u32[]{:S(2)}) copy-start(f32[1,128,256]{2,1,0:T(8,128)} %shard_map.43) | copy-start | bytes 393220

commit v15 on v14

--- a/solution.py
+++ b/solution.py
@@ -56,7 +56,10 @@
     for group in range(group_count):
         rows = jnp.concatenate([own_ref[group, 0], own_ref[group, 1]], axis=1)
         for index, mate_ref in enumerate(mate_refs):
-            cols = jnp.concatenate([mate_ref[group, 0], mate_ref[group, 1]], axis=1)
+            if turn:
+                cols = jnp.concatenate([mate_ref[0, :, group, :], mate_ref[1, :, group, :]], axis=1)
+            else:
+                cols = jnp.concatenate([mate_ref[group, 0], mate_ref[group, 1]], axis=1)
             prod = lax.dot_general(rows, cols, contract, preferred_element_type=jnp.float32)
             real = prod[:chans, :chans] + prod[chans:, chans:]
             imag = prod[chans:, :chans] - prod[:chans, chans:]
@@ -84,7 +87,10 @@
     spec = pl.BlockSpec((step, 2, width, chans), lambda n: (n, 0, 0, 0))
     count = len(mates)
     total_shape = (count, chans, 2 * chans)
+    mate_spec = spec
     if turn:
+        mates = [mate.transpose(1, 2, 0, 3) for mate in mates]
+        mate_spec = pl.BlockSpec((2, width, step, chans), lambda n: (0, 0, n, 0))
         out_shape = jax.ShapeDtypeStruct((chans, 2, chans), jnp.float32)
         out_spec = pl.BlockSpec((chans, 2, chans), lambda n: (0, 0, 0))
         scratch = [pltpu.VMEM(total_shape, jnp.float32)]
@@ -96,7 +102,7 @@
         functools.partial(pair_kernel, step, turn),
         out_shape=out_shape,
         grid=(groups // step,),
-        in_specs=[spec] * (count + 1),
+        in_specs=[spec] + [mate_spec] * count,
         out_specs=out_spec,
         scratch_shapes=scratch,
         cost_estimate=pl.CostEstimate(

time: 174 us -> 190 us (1.092)
  waiting for transfers between devices: 74.2 us -> 90.9 us
    all_to_all x2, waiting for transfers between devices: 31.6 us -> 40.8 us  [body(): lax.all_to_all(spectra[half], 'tm', split_axis=0, concat_axis=0, tiled=True)]
    ppermute x6, waiting for transfers between devices: 41.9 us -> 50.1 us  [shifted(): return lax.ppermute(value, axis, pairs)]
    ppermute x6, local copies, waits for them, and re-layouts: 12.7 us -> 10.4 us  [shifted(): return lax.ppermute(value, axis, pairs)]
    ppermute x6, starting transfers between devices: 18.8 us -> 16.5 us  [shifted(): return lax.ppermute(value, axis, pairs)]
    ppermute x2, starting transfers between devices: 5.41 us -> 7.6 us  [body(): far_recv.append(lax.ppermute(blocks, 'chan', pairs))]
  transfers between devices with their start and end apart: 10 -> 10, of which waited for: 6 -> 6; matrix products, arithmetic and copies ran while one was open for 13% -> 10% of each run, Pallas kernels for 13% -> 12%
where the time goes in v15:
time: 190 us; the launch traced here: 187 us
  waiting for transfers between devices  90.9 us (48%)
  starting transfers between devices  39 us (21%)
  Pallas kernels  26.2 us (14%)
  local copies, waits for them, and re-layouts  16.9 us (9%)
  matrix products  6.79 us (4%)
  other arithmetic  6.27 us (3%)
    ppermute x6, waiting for transfers between devices, shifted(): return lax.ppermute(value, axis, pairs)  50.1 us
    all_to_all x2, waiting for transfers between devices, body(): lax.all_to_all(spectra[half], 'tm', split_axis=0, concat_axis=0, tiled=True)  40.8 us
    pallas_call x7, Pallas kernels, pair_stack(): pl.pallas_call(functools.partial(pair_kernel, step, turn), out_shape=out_...  26.2 us
    ppermute x6, starting transfers between devices, shifted(): return lax.ppermute(value, axis, pairs)  16.5 us
    all_to_all x2, starting transfers between devices, body(): lax.all_to_all(spectra[half], 'tm', split_axis=0, concat_axis=0, tiled=True)  14.9 us
    ppermute x6, local copies, waits for them, and re-layouts, shifted(): return lax.ppermute(value, axis, pairs)  10.4 us
    ppermute x2, starting transfers between devices, body(): far_recv.append(lax.ppermute(blocks, 'chan', pairs))  7.6 us
    dot_general x1, matrix products, whiten(): jnp.einsum('ks,wcs->kwc', taper_table, records, preferred_element_type=jn...  6.79 us
  transfers between devices with their start and end apart: 10, of which 6 were waited for; matrix products, arithmetic and copies ran while one was open for 10% of the time, Pallas kernels for 12%

profile of v15, /device:TPU:2, one launch (start us, length us, event | category | flops | bytes accessed | tf_op | source)
XLA Modules:
  0.0 186.9 jit_solution(16794954005032931607)
XLA Ops:
  0.6 6.8 %multiply_reduce_fusion = (f32[44,128]{1,0:T(8,128)S(1)}, f32[128,44,128]{2,0,1:T(8,128)S(1)}) fusion(bf16[128,1024,1]{1,0,2:T(8,128)(2,1)} %constant.21, bf16[44,128,1024]{2,1,0:T(8,128)(2,1)} %param.2), kind=kOutput, calls=%fused_computation.1 | convolution fusion | flops 1477831168 | bytes 14702592 | tf_op jit(solution)/shard_map/ks,wcs->kwc/dot_general | solution.py:38
  9.3 10.1 %all-to-all-start.1 = ((bf16[32,2,44,128]{3,1,2,0:T(2,128)(2,1)}), bf16[32,2,44,128]{3,1,2,0:T(2,128)(2,1)S(1)}, u32[]{:S(2)}, u32[]{:S(2)}) async-start(bf16[32,2,44,128]{3,1,2,0:T(2,128)(2,1)} %copy.54), calls=%async_computation.1 | async-start | bytes 1441792 | tf_op jit(solution)/shard_map/all_to_all | solution.py:132
  20.8 19.8 %all-to-all-done.1 = bf16[32,2,44,128]{3,1,2,0:T(2,128)(2,1)S(1)} async-done(((bf16[32,2,44,128]{3,1,2,0:T(2,128)(2,1)}), bf16[32,2,44,128]{3,1,2,0:T(2,128)(2,1)S(1)}, u32[]{:S(2)}, u32[]{:S(2)}) %all-to-all-start.1) | async-done | bytes 720928 | tf_op jit(solution)/shard_map/all_to_all | solution.py:132
  40.5 4.8 %all-to-all-start = ((bf16[32,2,44,128]{3,1,2,0:T(2,128)(2,1)}), bf16[32,2,44,128]{3,1,2,0:T(2,128)(2,1)S(1)}, u32[]{:S(2)}, u32[]{:S(2)}) async-start(bf16[32,2,44,128]{3,1,2,0:T(2,128)(2,1)} %copy.43), calls=%async_computation | async-start | bytes 1441792 | tf_op jit(solution)/shard_map/all_to_all | solution.py:132
  45.3 21.1 %all-to-all-done = bf16[32,2,44,128]{3,1,2,0:T(2,128)(2,1)S(1)} async-done(((bf16[32,2,44,128]{3,1,2,0:T(2,128)(2,1)}), bf16[32,2,44,128]{3,1,2,0:T(2,128)(2,1)S(1)}, u32[]{:S(2)}, u32[]{:S(2)}) %all-to-all-start) | async-done | bytes 720928 | tf_op jit(solution)/shard_map/all_to_all | solution.py:132
  67.8 3.1 %collective-permute-start.5 = (bf16[32,2,44,128]{3,0,2,1:T(8,128)(2,1)}, bf16[32,2,44,128]{3,0,2,1:T(8,128)(2,1)S(1)}, u32[]{:S(2)}, u32[]{:S(2)}) collective-permute-start(bf16[32,2,44,128]{3,0,2,1:T(8,128)(2,1)} %get-tuple-element.6), channel_id=1, source_target_pairs={{0,160},{32,192},{64,224},{96,0},{128,32},{160,64},{192,96},{224,1... | collective-permute-start | bytes 2162696 | tf_op jit(solution)/shard_map/ppermute | solution.py:22
  70.9 3.7 %collective-permute-start.4 = (bf16[32,2,44,128]{3,0,2,1:T(8,128)(2,1)}, bf16[32,2,44,128]{3,0,2,1:T(8,128)(2,1)S(1)}, u32[]{:S(2)}, u32[]{:S(2)}) collective-permute-start(bf16[32,2,44,128]{3,0,2,1:T(8,128)(2,1)} %get-tuple-element.6), channel_id=1, source_target_pairs={{0,192},{32,224},{64,0},{96,32},{128,64},{160,96},{192,128},{224,1... | collective-permute-start | bytes 2162696 | tf_op jit(solution)/shard_map/ppermute | solution.py:22
  76.0 2.2 %collective-permute-start.2 = (bf16[32,2,44,128]{3,0,2,1:T(8,128)(2,1)}, bf16[32,2,44,128]{3,0,2,1:T(8,128)(2,1)}, u32[]{:S(2)}, u32[]{:S(2)}) collective-permute-start(bf16[32,2,44,128]{3,0,2,1:T(8,128)(2,1)} %get-tuple-element.5), channel_id=1, source_target_pairs={{0,160},{32,192},{64,224},{96,0},{128,32},{160,64},{192,96},{224,1... | collective-permute-start | bytes 2162696 | tf_op jit(solution)/shard_map/ppermute | solution.py:22
  79.0 9.8 %collective-permute-done.5 = bf16[32,2,44,128]{3,0,2,1:T(8,128)(2,1)S(1)} collective-permute-done((bf16[32,2,44,128]{3,0,2,1:T(8,128)(2,1)}, bf16[32,2,44,128]{3,0,2,1:T(8,128)(2,1)S(1)}, u32[]{:S(2)}, u32[]{:S(2)}) %collective-permute-start.5) | collective-permute-done | bytes 720928 | tf_op jit(solution)/shard_map/ppermute | solution.py:22
  88.8 5.3 %collective-permute-start = (bf16[32,2,44,128]{3,0,2,1:T(8,128)(2,1)}, bf16[32,2,44,128]{3,0,2,1:T(8,128)(2,1)}, u32[]{:S(2)}, u32[]{:S(2)}) collective-permute-start(bf16[32,2,44,128]{3,0,2,1:T(8,128)(2,1)} %get-tuple-element.5), channel_id=1, source_target_pairs={{0,224},{32,0},{64,32},{96,64},{128,96},{160,128},{192,160},{224,1... | collective-permute-start | bytes 2162696 | tf_op jit(solution)/shard_map/ppermute | solution.py:22
  94.1 26.2 %collective-permute-done.4 = bf16[32,2,44,128]{3,0,2,1:T(8,128)(2,1)S(1)} collective-permute-done((bf16[32,2,44,128]{3,0,2,1:T(8,128)(2,1)}, bf16[32,2,44,128]{3,0,2,1:T(8,128)(2,1)S(1)}, u32[]{:S(2)}, u32[]{:S(2)}) %collective-permute-start.4) | collective-permute-done | bytes 720928 | tf_op jit(solution)/shard_map/ppermute | solution.py:22
  121.6 6.3 %collective-permute-start.7 = (bf16[32,2,44,128]{3,0,2,1:T(8,128)(2,1)}, bf16[32,2,44,128]{3,0,2,1:T(8,128)(2,1)S(1)}, u32[]{:S(2)}, u32[]{:S(2)}) collective-permute-start(bf16[32,2,44,128]{3,0,2,1:T(8,128)(2,1)} %get-tuple-element.6), channel_id=1, source_target_pairs={{0,128},{32,160},{64,192},{96,224},{1,129},{33,161},{65,193},{97,2... | collective-permute-start | bytes 2162696 | tf_op jit(solution)/shard_map/ppermute | solution.py:138
  134.7 3.3 %shard_map.46 = f32[1,128,256]{2,1,0:T(8,128)} custom-call(bf16[32,2,44,128]{3,2,1,0:T(8,128)(2,1)} %copy.56.own_ref.refs_0_, bf16[32,2,44,128]{3,2,1,0:T(8,128)(2,1)} %copy.64.refs_0_), custom_call_target="tpu_custom_call" | custom-call | flops 369098752 | bytes 1572864 | tf_op jit(solution)/shard_map/pallas_call | solution.py:101
  138.0 3.4 %shard_map.45 = f32[1,128,256]{2,1,0:T(8,128)} custom-call(bf16[32,2,44,128]{3,2,1,0:T(8,128)(2,1)} %copy.56.own_ref.refs_0_, bf16[32,2,44,128]{3,2,1,0:T(8,128)(2,1)} %copy.61.refs_0_), custom_call_target="tpu_custom_call" | custom-call | flops 369098752 | bytes 1572864 | tf_op jit(solution)/shard_map/pallas_call | solution.py:101
  141.4 4.7 %shard_map.44 = f32[2,128,256]{2,1,0:T(8,128)} custom-call(bf16[32,2,44,128]{3,2,1,0:T(8,128)(2,1)} %copy.56.own_ref.refs_0_, bf16[32,2,44,128]{3,2,1,0:T(8,128)(2,1)} %copy.56.own_ref.refs_0_, bf16[32,2,44,128]{3,2,1,0:T(8,128)(2,1)} %copy.58.refs_1_), custom_call_target="tpu_custom_call" | custom-call | flops 738197504 | bytes 2424832 | tf_op jit(solution)/shard_map/pallas_call | solution.py:101
  147.4 2.3 %copy.53.refs_0_ = bf16[32,2,44,128]{3,2,1,0:T(8,128)(2,1)} copy(bf16[32,2,44,128]{3,0,2,1:T(8,128)(2,1)} %collective-permute-done.2) | data formatting | bytes 1441792 | tf_op jit(solution)/shard_map/ppermute | solution.py:22
  150.6 2.3 %copy.50.refs_0_ = bf16[32,2,44,128]{3,2,1,0:T(8,128)(2,1)} copy(bf16[32,2,44,128]{3,0,2,1:T(8,128)(2,1)} %collective-permute-done.1) | data formatting | bytes 1441792 | tf_op jit(solution)/shard_map/ppermute | solution.py:22
  152.9 13.2 %collective-permute-done = bf16[32,2,44,128]{3,0,2,1:T(8,128)(2,1)} collective-permute-done((bf16[32,2,44,128]{3,0,2,1:T(8,128)(2,1)}, bf16[32,2,44,128]{3,0,2,1:T(8,128)(2,1)}, u32[]{:S(2)}, u32[]{:S(2)}) %collective-permute-start) | collective-permute-done | bytes 720928 | tf_op jit(solution)/shard_map/ppermute | solution.py:22
  166.0 2.3 %copy.47.refs_1_ = bf16[32,2,44,128]{3,2,1,0:T(8,128)(2,1)} copy(bf16[32,2,44,128]{3,0,2,1:T(8,128)(2,1)} %collective-permute-done) | data formatting | bytes 1441792 | tf_op jit(solution)/shard_map/ppermute | solution.py:22
  168.3 3.3 %shard_map.43 = f32[1,128,256]{2,1,0:T(8,128)} custom-call(bf16[32,2,44,128]{3,2,1,0:T(8,128)(2,1)} %copy.45.own_ref.refs_0_, bf16[32,2,44,128]{3,2,1,0:T(8,128)(2,1)} %copy.53.refs_0_), custom_call_target="tpu_custom_call" | custom-call | flops 369098752 | bytes 1572864 | tf_op jit(solution)/shard_map/pallas_call | solution.py:101
  171.7 3.4 %shard_map.42 = f32[1,128,256]{2,1,0:T(8,128)} custom-call(bf16[32,2,44,128]{3,2,1,0:T(8,128)(2,1)} %copy.45.own_ref.refs_0_, bf16[32,2,44,128]{3,2,1,0:T(8,128)(2,1)} %copy.50.refs_0_), custom_call_target="tpu_custom_call" | custom-call | flops 369098752 | bytes 1572864 | tf_op jit(solution)/shard_map/pallas_call | solution.py:101
  175.0 4.6 %shard_map.41 = f32[2,128,256]{2,1,0:T(8,128)} custom-call(bf16[32,2,44,128]{3,2,1,0:T(8,128)(2,1)} %copy.45.own_ref.refs_0_, bf16[32,2,44,128]{3,2,1,0:T(8,128)(2,1)} %copy.45.own_ref.refs_0_, bf16[32,2,44,128]{3,2,1,0:T(8,128)(2,1)} %copy.47.refs_1_), custom_call_target="tpu_custom_call" | custom-call | flops 738197504 | bytes 2424832 | tf_op jit(solution)/shard_map/pallas_call | solution.py:101
  181.0 1.4 pad_maximum_fusion
  183.4 3.5 %shard_map.47 = f32[128,2,128]{2,1,0:T(2,128)} custom-call(bf16[32,2,44,128]{3,2,1,0:T(8,128)(2,1)} %copy.69.own_ref, bf16[2,44,32,128]{3,2,1,0:T(8,128)(2,1)} %select_bitcast_fusion.refs_0_), custom_call_target="tpu_custom_call" | custom-call | flops 369098752 | bytes 1572864 | tf_op jit(solution)/shard_map/pallas_call | solution.py:101
  (29 shorter events, 19.2 us)
Async XLA Ops:
  9.3 31.2 %all-to-all-start.1 = ((bf16[32,2,44,128]{3,1,2,0:T(2,128)(2,1)}), bf16[32,2,44,128]{3,1,2,0:T(2,128)(2,1)S(1)}, u32[]{:S(2)}, u32[]{:S(2)}) async-start(bf16[32,2,44,128]{3,1,2,0:T(2,128)(2,1)} %copy.54), calls=%async_computation.1 | async-start | bytes 1441792 | tf_op jit(solution)/shard_map/all_to_all | solution.py:132
  40.5 25.9 %all-to-all-start = ((bf16[32,2,44,128]{3,1,2,0:T(2,128)(2,1)}), bf16[32,2,44,128]{3,1,2,0:T(2,128)(2,1)S(1)}, u32[]{:S(2)}, u32[]{:S(2)}) async-start(bf16[32,2,44,128]{3,1,2,0:T(2,128)(2,1)} %copy.43), calls=%async_computation | async-start | bytes 1441792 | tf_op jit(solution)/shard_map/all_to_all | solution.py:132
  67.8 21.1 %collective-permute-start.5 = (bf16[32,2,44,128]{3,0,2,1:T(8,128)(2,1)}, bf16[32,2,44,128]{3,0,2,1:T(8,128)(2,1)S(1)}, u32[]{:S(2)}, u32[]{:S(2)}) collective-permute-start(bf16[32,2,44,128]{3,0,2,1:T(8,128)(2,1)} %get-tuple-element.6), channel_id=1, source_target_pairs={{0,160},{32,192},{64,224},{96,0},{128,32},{160,64},{192,96},{224,1... | collective-permute-start | bytes 2162696 | tf_op jit(solution)/shard_map/ppermute | solution.py:22
  70.9 49.4 %collective-permute-start.4 = (bf16[32,2,44,128]{3,0,2,1:T(8,128)(2,1)}, bf16[32,2,44,128]{3,0,2,1:T(8,128)(2,1)S(1)}, u32[]{:S(2)}, u32[]{:S(2)}) collective-permute-start(bf16[32,2,44,128]{3,0,2,1:T(8,128)(2,1)} %get-tuple-element.6), channel_id=1, source_target_pairs={{0,192},{32,224},{64,0},{96,32},{128,64},{160,96},{192,128},{224,1... | collective-permute-start | bytes 2162696 | tf_op jit(solution)/shard_map/ppermute | solution.py:22
  74.6 47.0 %collective-permute-start.3 = (bf16[32,2,44,128]{3,0,2,1:T(8,128)(2,1)}, bf16[32,2,44,128]{3,0,2,1:T(8,128)(2,1)S(1)}, u32[]{:S(2)}, u32[]{:S(2)}) collective-permute-start(bf16[32,2,44,128]{3,0,2,1:T(8,128)(2,1)} %get-tuple-element.6), channel_id=1, source_target_pairs={{0,224},{32,0},{64,32},{96,64},{128,96},{160,128},{192,160},{224,1... | collective-permute-start | bytes 2162696 | tf_op jit(solution)/shard_map/ppermute | solution.py:22
  76.0 71.4 %collective-permute-start.2 = (bf16[32,2,44,128]{3,0,2,1:T(8,128)(2,1)}, bf16[32,2,44,128]{3,0,2,1:T(8,128)(2,1)}, u32[]{:S(2)}, u32[]{:S(2)}) collective-permute-start(bf16[32,2,44,128]{3,0,2,1:T(8,128)(2,1)} %get-tuple-element.5), channel_id=1, source_target_pairs={{0,160},{32,192},{64,224},{96,0},{128,32},{160,64},{192,96},{224,1... | collective-permute-start | bytes 2162696 | tf_op jit(solution)/shard_map/ppermute | solution.py:22
  78.2 72.4 %collective-permute-start.1 = (bf16[32,2,44,128]{3,0,2,1:T(8,128)(2,1)}, bf16[32,2,44,128]{3,0,2,1:T(8,128)(2,1)}, u32[]{:S(2)}, u32[]{:S(2)}) collective-permute-start(bf16[32,2,44,128]{3,0,2,1:T(8,128)(2,1)} %get-tuple-element.5), channel_id=1, source_target_pairs={{0,192},{32,224},{64,0},{96,32},{128,64},{160,96},{192,128},{224,1... | collective-permute-start | bytes 2162696 | tf_op jit(solution)/shard_map/ppermute | solution.py:22
  88.8 77.2 %collective-permute-start = (bf16[32,2,44,128]{3,0,2,1:T(8,128)(2,1)}, bf16[32,2,44,128]{3,0,2,1:T(8,128)(2,1)}, u32[]{:S(2)}, u32[]{:S(2)}) collective-permute-start(bf16[32,2,44,128]{3,0,2,1:T(8,128)(2,1)} %get-tuple-element.5), channel_id=1, source_target_pairs={{0,224},{32,0},{64,32},{96,64},{128,96},{160,128},{192,160},{224,1... | collective-permute-start | bytes 2162696 | tf_op jit(solution)/shard_map/ppermute | solution.py:22
  120.3 62.1 %collective-permute-start.6 = (bf16[32,2,44,128]{3,0,2,1:T(8,128)(2,1)}, bf16[32,2,44,128]{3,0,2,1:T(8,128)(2,1)S(1)}, u32[]{:S(2)}, u32[]{:S(2)}) collective-permute-start(bf16[32,2,44,128]{3,0,2,1:T(8,128)(2,1)} %get-tuple-element.5), channel_id=1, source_target_pairs={{128,0},{160,32},{192,64},{224,96},{129,1},{161,33},{193,65},{225,... | collective-permute-start | bytes 2162696 | tf_op jit(solution)/shard_map/ppermute | solution.py:138
  121.6 60.8 %collective-permute-start.7 = (bf16[32,2,44,128]{3,0,2,1:T(8,128)(2,1)}, bf16[32,2,44,128]{3,0,2,1:T(8,128)(2,1)S(1)}, u32[]{:S(2)}, u32[]{:S(2)}) collective-permute-start(bf16[32,2,44,128]{3,0,2,1:T(8,128)(2,1)} %get-tuple-element.6), channel_id=1, source_target_pairs={{0,128},{32,160},{64,192},{96,224},{1,129},{33,161},{65,193},{97,2... | collective-permute-start | bytes 2162696 | tf_op jit(solution)/shard_map/ppermute | solution.py:138
  138.0 8.1 %copy-start = (f32[1,128,256]{2,1,0:T(8,128)S(1)}, f32[1,128,256]{2,1,0:T(8,128)}, u32[]{:S(2)}) copy-start(f32[1,128,256]{2,1,0:T(8,128)} %shard_map.46) | copy-start | bytes 393220
  171.7 8.0 %copy-start.1 = (f32[1,128,256]{2,1,0:T(8,128)S(1)}, f32[1,128,256]{2,1,0:T(8,128)}, u32[]{:S(2)}) copy-start(f32[1,128,256]{2,1,0:T(8,128)} %shard_map.43) | copy-start | bytes 393220

commit v16 on v15

--- a/solution.py
+++ b/solution.py
@@ -55,11 +55,13 @@
 
     for group in range(group_count):
         rows = jnp.concatenate([own_ref[group, 0], own_ref[group, 1]], axis=1)
-        for index, mate_ref in enumerate(mate_refs):
-            if turn:
-                cols = jnp.concatenate([mate_ref[0, :, group, :], mate_ref[1, :, group, :]], axis=1)
-            else:
-                cols = jnp.concatenate([mate_ref[group, 0], mate_ref[group, 1]], axis=1)
+        if turn:
+            lower = lax.axis_index("chan") < lax.axis_size("chan") // 2
+            pairs = [[jnp.concatenate([ref[0, :, group, :], ref[1, :, group, :]], axis=1) for ref in mate_refs]]
+            pairs = [jnp.where(lower, pairs[0][0], pairs[0][1])]
+        else:
+            pairs = [jnp.concatenate([ref[group, 0], ref[group, 1]], axis=1) for ref in mate_refs]
+        for index, cols in enumerate(pairs):
             prod = lax.dot_general(rows, cols, contract, preferred_element_type=jnp.float32)
             real = prod[:chans, :chans] + prod[chans:, chans:]
             imag = prod[chans:, :chans] - prod[:chans, chans:]
@@ -89,6 +91,8 @@
     total_shape = (count, chans, 2 * chans)
     mate_spec = spec
     if turn:
+        count = 1
+        total_shape = (count, chans, 2 * chans)
         mates = [mate.transpose(1, 2, 0, 3) for mate in mates]
         mate_spec = pl.BlockSpec((2, width, step, chans), lambda n: (0, 0, n, 0))
         out_shape = jax.ShapeDtypeStruct((chans, 2, chans), jnp.float32)
@@ -102,7 +106,7 @@
         functools.partial(pair_kernel, step, turn),
         out_shape=out_shape,
         grid=(groups // step,),
-        in_specs=[spec] + [mate_spec] * count,
+        in_specs=[spec] + [mate_spec] * len(mates),
         out_specs=out_spec,
         scratch_shapes=scratch,
         cost_estimate=pl.CostEstimate(
@@ -142,8 +146,7 @@
     cross_near = jnp.stack(near, axis=0).reshape(1, 2, half_count, chans, 2, chans)
 
     far_own = jnp.where(lower_half, own_h[0], own_h[1])
-    far_mate = jnp.where(lower_half, far_recv[0], far_recv[1])
-    cross_far = pair_stack(far_own, [far_mate], turn=True).reshape(1, chans, 2, chans)
+    cross_far = pair_stack(far_own, far_recv, turn=True).reshape(1, chans, 2, chans)
     return (cross_near, cross_far)
 
 

time: 190 us -> 173 us (0.911)
  waiting for transfers between devices: 90.9 us -> 72.1 us
  starting transfers between devices: 39 us -> 41.5 us
    ppermute x6, waiting for transfers between devices: 50.1 us -> 39 us  [shifted(): return lax.ppermute(value, axis, pairs)]
    all_to_all x2, waiting for transfers between devices: 40.8 us -> 32.4 us  [body(): lax.all_to_all(spectra[half], 'tm', split_axis=0, concat_axis=0, tiled=True)]
    ppermute x6, local copies, waits for them, and re-layouts: 10.4 us -> 13.7 us  [shifted(): return lax.ppermute(value, axis, pairs)]
    ppermute x6, starting transfers between devices: 16.5 us -> 19.4 us  [shifted(): return lax.ppermute(value, axis, pairs)]
  transfers between devices with their start and end apart: 10 -> 10, of which waited for: 6 -> 7; matrix products, arithmetic and copies ran while one was open for 10% -> 12% of each run, Pallas kernels for 12% -> 13%
where the time goes in v16:
time: 173 us; the launch traced here: 171 us
  waiting for transfers between devices  72.1 us (42%)
  starting transfers between devices  41.5 us (24%)
  Pallas kernels  27.4 us (16%)
  local copies, waits for them, and re-layouts  17.3 us (10%)
  matrix products  6.79 us (4%)
  other arithmetic  5.5 us (3%)
    ppermute x6, waiting for transfers between devices, shifted(): return lax.ppermute(value, axis, pairs)  39 us
    all_to_all x2, waiting for transfers between devices, body(): lax.all_to_all(spectra[half], 'tm', split_axis=0, concat_axis=0, tiled=True)  32.4 us
    pallas_call x7, Pallas kernels, pair_stack(): pl.pallas_call(functools.partial(pair_kernel, step, turn), out_shape=out_...  27.4 us
    ppermute x6, starting transfers between devices, shifted(): return lax.ppermute(value, axis, pairs)  19.4 us
    all_to_all x2, starting transfers between devices, body(): lax.all_to_all(spectra[half], 'tm', split_axis=0, concat_axis=0, tiled=True)  14.9 us
    ppermute x6, local copies, waits for them, and re-layouts, shifted(): return lax.ppermute(value, axis, pairs)  13.7 us
    ppermute x2, starting transfers between devices, body(): far_recv.append(lax.ppermute(blocks, 'chan', pairs))  7.22 us
    dot_general x1, matrix products, whiten(): jnp.einsum('ks,wcs->kwc', taper_table, records, preferred_element_type=jn...  6.79 us
  transfers between devices with their start and end apart: 10, of which 7 were waited for; matrix products, arithmetic and copies ran while one was open for 12% of the time, Pallas kernels for 13%

profile of v16, /device:TPU:2, one launch (start us, length us, event | category | flops | bytes accessed | tf_op | source)
XLA Modules:
  0.0 171.4 jit_solution(962083051315242743)
XLA Ops:
  0.6 6.8 %multiply_reduce_fusion = (f32[44,128]{1,0:T(8,128)S(1)}, f32[128,44,128]{2,0,1:T(8,128)S(1)}) fusion(bf16[128,1024,1]{1,0,2:T(8,128)(2,1)} %constant.21, bf16[44,128,1024]{2,1,0:T(8,128)(2,1)} %param.2), kind=kOutput, calls=%fused_computation.1 | convolution fusion | flops 1477831168 | bytes 14702592 | tf_op jit(solution)/shard_map/ks,wcs->kwc/dot_general | solution.py:38
  9.3 10.1 %all-to-all-start.1 = ((bf16[32,2,44,128]{3,1,2,0:T(2,128)(2,1)}), bf16[32,2,44,128]{3,1,2,0:T(2,128)(2,1)S(1)}, u32[]{:S(2)}, u32[]{:S(2)}) async-start(bf16[32,2,44,128]{3,1,2,0:T(2,128)(2,1)} %copy.51), calls=%async_computation.1 | async-start | bytes 1441792 | tf_op jit(solution)/shard_map/all_to_all | solution.py:136
  20.8 19.8 %all-to-all-done.1 = bf16[32,2,44,128]{3,1,2,0:T(2,128)(2,1)S(1)} async-done(((bf16[32,2,44,128]{3,1,2,0:T(2,128)(2,1)}), bf16[32,2,44,128]{3,1,2,0:T(2,128)(2,1)S(1)}, u32[]{:S(2)}, u32[]{:S(2)}) %all-to-all-start.1) | async-done | bytes 720928 | tf_op jit(solution)/shard_map/all_to_all | solution.py:136
  40.6 4.8 %all-to-all-start = ((bf16[32,2,44,128]{3,1,2,0:T(2,128)(2,1)}), bf16[32,2,44,128]{3,1,2,0:T(2,128)(2,1)S(1)}, u32[]{:S(2)}, u32[]{:S(2)}) async-start(bf16[32,2,44,128]{3,1,2,0:T(2,128)(2,1)} %copy.40), calls=%async_computation | async-start | bytes 1441792 | tf_op jit(solution)/shard_map/all_to_all | solution.py:136
  45.5 3.2 %collective-permute-start.5 = (bf16[32,2,44,128]{3,0,2,1:T(8,128)(2,1)S(1)}, bf16[32,2,44,128]{3,0,2,1:T(8,128)(2,1)}, u32[]{:S(2)}, u32[]{:S(2)}) collective-permute-start(bf16[32,2,44,128]{3,0,2,1:T(8,128)(2,1)S(1)} %copy.52), channel_id=1, source_target_pairs={{0,160},{32,192},{64,224},{96,0},{128,32},{160,64},{192,96},{224,1... | collective-permute-start | bytes 2162696 | tf_op jit(solution)/shard_map/ppermute | solution.py:22
  48.7 3.7 %collective-permute-start.4 = (bf16[32,2,44,128]{3,0,2,1:T(8,128)(2,1)S(1)}, bf16[32,2,44,128]{3,0,2,1:T(8,128)(2,1)}, u32[]{:S(2)}, u32[]{:S(2)}) collective-permute-start(bf16[32,2,44,128]{3,0,2,1:T(8,128)(2,1)S(1)} %copy.52), channel_id=1, source_target_pairs={{0,192},{32,224},{64,0},{96,32},{128,64},{160,96},{192,128},{224,1... | collective-permute-start | bytes 2162696 | tf_op jit(solution)/shard_map/ppermute | solution.py:22
  53.8 12.6 %all-to-all-done = bf16[32,2,44,128]{3,1,2,0:T(2,128)(2,1)S(1)} async-done(((bf16[32,2,44,128]{3,1,2,0:T(2,128)(2,1)}), bf16[32,2,44,128]{3,1,2,0:T(2,128)(2,1)S(1)}, u32[]{:S(2)}, u32[]{:S(2)}) %all-to-all-start) | async-done | bytes 720928 | tf_op jit(solution)/shard_map/all_to_all | solution.py:136
  66.6 3.2 %collective-permute-start.2 = (bf16[32,2,44,128]{3,0,2,1:T(8,128)(2,1)S(1)}, bf16[32,2,44,128]{3,0,2,1:T(8,128)(2,1)}, u32[]{:S(2)}, u32[]{:S(2)}) collective-permute-start(bf16[32,2,44,128]{3,0,2,1:T(8,128)(2,1)S(1)} %copy.41), channel_id=1, source_target_pairs={{0,160},{32,192},{64,224},{96,0},{128,32},{160,64},{192,96},{224,1... | collective-permute-start | bytes 2162696 | tf_op jit(solution)/shard_map/ppermute | solution.py:22
  69.8 3.7 %collective-permute-start.1 = (bf16[32,2,44,128]{3,0,2,1:T(8,128)(2,1)S(1)}, bf16[32,2,44,128]{3,0,2,1:T(8,128)(2,1)}, u32[]{:S(2)}, u32[]{:S(2)}) collective-permute-start(bf16[32,2,44,128]{3,0,2,1:T(8,128)(2,1)S(1)} %copy.41), channel_id=1, source_target_pairs={{0,192},{32,224},{64,0},{96,32},{128,64},{160,96},{192,128},{224,1... | collective-permute-start | bytes 2162696 | tf_op jit(solution)/shard_map/ppermute | solution.py:22
  73.5 4.1 %collective-permute-start = (bf16[32,2,44,128]{3,0,2,1:T(8,128)(2,1)S(1)}, bf16[32,2,44,128]{3,0,2,1:T(8,128)(2,1)}, u32[]{:S(2)}, u32[]{:S(2)}) collective-permute-start(bf16[32,2,44,128]{3,0,2,1:T(8,128)(2,1)S(1)} %copy.41), channel_id=1, source_target_pairs={{0,224},{32,0},{64,32},{96,64},{128,96},{160,128},{192,160},{224,1... | collective-permute-start | bytes 2162696 | tf_op jit(solution)/shard_map/ppermute | solution.py:22
  77.7 22.3 %collective-permute-done.4 = bf16[32,2,44,128]{3,0,2,1:T(8,128)(2,1)} collective-permute-done((bf16[32,2,44,128]{3,0,2,1:T(8,128)(2,1)S(1)}, bf16[32,2,44,128]{3,0,2,1:T(8,128)(2,1)}, u32[]{:S(2)}, u32[]{:S(2)}) %collective-permute-start.4) | collective-permute-done | bytes 720928 | tf_op jit(solution)/shard_map/ppermute | solution.py:22
  103.1 5.9 %collective-permute-start.7 = (bf16[32,2,44,128]{3,0,2,1:T(8,128)(2,1)S(1)}, bf16[32,2,44,128]{3,0,2,1:T(8,128)(2,1)}, u32[]{:S(2)}, u32[]{:S(2)}) collective-permute-start(bf16[32,2,44,128]{3,0,2,1:T(8,128)(2,1)S(1)} %copy.52), channel_id=1, source_target_pairs={{0,128},{32,160},{64,192},{96,224},{1,129},{33,161},{65,193},{97,2... | collective-permute-start | bytes 2162696 | tf_op jit(solution)/shard_map/ppermute | solution.py:142
  110.6 2.3 %copy.61.refs_0_ = bf16[32,2,44,128]{3,2,1,0:T(8,128)(2,1)} copy(bf16[32,2,44,128]{3,0,2,1:T(8,128)(2,1)} %collective-permute-done.5) | data formatting | bytes 1441792 | tf_op jit(solution)/shard_map/ppermute | solution.py:22
  112.9 2.3 %copy.58.refs_0_ = bf16[32,2,44,128]{3,2,1,0:T(8,128)(2,1)} copy(bf16[32,2,44,128]{3,0,2,1:T(8,128)(2,1)} %collective-permute-done.4) | data formatting | bytes 1441792 | tf_op jit(solution)/shard_map/ppermute | solution.py:22
  117.4 3.3 %shard_map.46 = f32[1,128,256]{2,1,0:T(8,128)} custom-call(bf16[32,2,44,128]{3,2,1,0:T(8,128)(2,1)} %get-tuple-element.6.own_ref.refs_0_, bf16[32,2,44,128]{3,2,1,0:T(8,128)(2,1)} %copy.61.refs_0_), custom_call_target="tpu_custom_call" | custom-call | flops 369098752 | bytes 1572864 | tf_op jit(solution)/shard_map/pallas_call | solution.py:105
  120.7 3.3 %shard_map.45 = f32[1,128,256]{2,1,0:T(8,128)} custom-call(bf16[32,2,44,128]{3,2,1,0:T(8,128)(2,1)} %get-tuple-element.6.own_ref.refs_0_, bf16[32,2,44,128]{3,2,1,0:T(8,128)(2,1)} %copy.58.refs_0_), custom_call_target="tpu_custom_call" | custom-call | flops 369098752 | bytes 1572864 | tf_op jit(solution)/shard_map/pallas_call | solution.py:105
  124.1 4.6 %shard_map.44 = f32[2,128,256]{2,1,0:T(8,128)} custom-call(bf16[32,2,44,128]{3,2,1,0:T(8,128)(2,1)} %get-tuple-element.6.own_ref.refs_0_, bf16[32,2,44,128]{3,2,1,0:T(8,128)(2,1)} %get-tuple-element.6.own_ref.refs_0_, bf16[32,2,44,128]{3,2,1,0:T(8,128)(2,1)} %copy.55.refs_1_), custom_call_target="tpu_custom_call" | custom-call | flops 738197504 | bytes 2424832 | tf_op jit(solution)/shard_map/pallas_call | solution.py:105
  130.1 2.3 %copy.50.refs_0_ = bf16[32,2,44,128]{3,2,1,0:T(8,128)(2,1)} copy(bf16[32,2,44,128]{3,0,2,1:T(8,128)(2,1)} %collective-permute-done.2) | data formatting | bytes 1441792 | tf_op jit(solution)/shard_map/ppermute | solution.py:22
  136.3 13.2 %collective-permute-done = bf16[32,2,44,128]{3,0,2,1:T(8,128)(2,1)} collective-permute-done((bf16[32,2,44,128]{3,0,2,1:T(8,128)(2,1)S(1)}, bf16[32,2,44,128]{3,0,2,1:T(8,128)(2,1)}, u32[]{:S(2)}, u32[]{:S(2)}) %collective-permute-start) | collective-permute-done | bytes 720928 | tf_op jit(solution)/shard_map/ppermute | solution.py:22
  149.5 2.3 %copy.44.refs_1_ = bf16[32,2,44,128]{3,2,1,0:T(8,128)(2,1)} copy(bf16[32,2,44,128]{3,0,2,1:T(8,128)(2,1)} %collective-permute-done) | data formatting | bytes 1441792 | tf_op jit(solution)/shard_map/ppermute | solution.py:22
  151.8 3.3 %shard_map.43 = f32[1,128,256]{2,1,0:T(8,128)} custom-call(bf16[32,2,44,128]{3,2,1,0:T(8,128)(2,1)} %get-tuple-element.5.own_ref.refs_0_, bf16[32,2,44,128]{3,2,1,0:T(8,128)(2,1)} %copy.50.refs_0_), custom_call_target="tpu_custom_call" | custom-call | flops 369098752 | bytes 1572864 | tf_op jit(solution)/shard_map/pallas_call | solution.py:105
  155.1 3.3 %shard_map.42 = f32[1,128,256]{2,1,0:T(8,128)} custom-call(bf16[32,2,44,128]{3,2,1,0:T(8,128)(2,1)} %get-tuple-element.5.own_ref.refs_0_, bf16[32,2,44,128]{3,2,1,0:T(8,128)(2,1)} %copy.47.refs_0_), custom_call_target="tpu_custom_call" | custom-call | flops 369098752 | bytes 1572864 | tf_op jit(solution)/shard_map/pallas_call | solution.py:105
  158.4 4.7 %shard_map.41 = f32[2,128,256]{2,1,0:T(8,128)} custom-call(bf16[32,2,44,128]{3,2,1,0:T(8,128)(2,1)} %get-tuple-element.5.own_ref.refs_0_, bf16[32,2,44,128]{3,2,1,0:T(8,128)(2,1)} %get-tuple-element.5.own_ref.refs_0_, bf16[32,2,44,128]{3,2,1,0:T(8,128)(2,1)} %copy.44.refs_1_), custom_call_target="tpu_custom_call" | custom-call | flops 738197504 | bytes 2424832 | tf_op jit(solution)/shard_map/pallas_call | solution.py:105
  166.7 4.7 %shard_map.47 = f32[128,2,128]{2,1,0:T(2,128)} custom-call(bf16[32,2,44,128]{3,2,1,0:T(8,128)(2,1)} %get-tuple-element.4.own_ref, bf16[2,44,32,128]{3,2,1,0:T(8,128)(2,1)} %bitcast.3.refs_0_, bf16[2,44,32,128]{3,2,1,0:T(8,128)(2,1)} %bitcast.4.refs_1_), custom_call_target="tpu_custom_call" | custom-call | flops 369098752 | bytes 1572864 | tf_op jit(solution)/shard_map/pallas_call | solution.py:105
  (27 shorter events, 20.5 us)
Async XLA Ops:
  9.3 31.2 %all-to-all-start.1 = ((bf16[32,2,44,128]{3,1,2,0:T(2,128)(2,1)}), bf16[32,2,44,128]{3,1,2,0:T(2,128)(2,1)S(1)}, u32[]{:S(2)}, u32[]{:S(2)}) async-start(bf16[32,2,44,128]{3,1,2,0:T(2,128)(2,1)} %copy.51), calls=%async_computation.1 | async-start | bytes 1441792 | tf_op jit(solution)/shard_map/all_to_all | solution.py:136
  40.6 25.9 %all-to-all-start = ((bf16[32,2,44,128]{3,1,2,0:T(2,128)(2,1)}), bf16[32,2,44,128]{3,1,2,0:T(2,128)(2,1)S(1)}, u32[]{:S(2)}, u32[]{:S(2)}) async-start(bf16[32,2,44,128]{3,1,2,0:T(2,128)(2,1)} %copy.40), calls=%async_computation | async-start | bytes 1441792 | tf_op jit(solution)/shard_map/all_to_all | solution.py:136
  45.5 28.0 %collective-permute-start.5 = (bf16[32,2,44,128]{3,0,2,1:T(8,128)(2,1)S(1)}, bf16[32,2,44,128]{3,0,2,1:T(8,128)(2,1)}, u32[]{:S(2)}, u32[]{:S(2)}) collective-permute-start(bf16[32,2,44,128]{3,0,2,1:T(8,128)(2,1)S(1)} %copy.52), channel_id=1, source_target_pairs={{0,160},{32,192},{64,224},{96,0},{128,32},{160,64},{192,96},{224,1... | collective-permute-start | bytes 2162696 | tf_op jit(solution)/shard_map/ppermute | solution.py:22
  48.7 51.3 %collective-permute-start.4 = (bf16[32,2,44,128]{3,0,2,1:T(8,128)(2,1)S(1)}, bf16[32,2,44,128]{3,0,2,1:T(8,128)(2,1)}, u32[]{:S(2)}, u32[]{:S(2)}) collective-permute-start(bf16[32,2,44,128]{3,0,2,1:T(8,128)(2,1)S(1)} %copy.52), channel_id=1, source_target_pairs={{0,192},{32,224},{64,0},{96,32},{128,64},{160,96},{192,128},{224,1... | collective-permute-start | bytes 2162696 | tf_op jit(solution)/shard_map/ppermute | solution.py:22
  52.4 50.7 %collective-permute-start.3 = (bf16[32,2,44,128]{3,0,2,1:T(8,128)(2,1)S(1)}, bf16[32,2,44,128]{3,0,2,1:T(8,128)(2,1)}, u32[]{:S(2)}, u32[]{:S(2)}) collective-permute-start(bf16[32,2,44,128]{3,0,2,1:T(8,128)(2,1)S(1)} %copy.52), channel_id=1, source_target_pairs={{0,224},{32,0},{64,32},{96,64},{128,96},{160,128},{192,160},{224,1... | collective-permute-start | bytes 2162696 | tf_op jit(solution)/shard_map/ppermute | solution.py:22
  66.6 63.5 %collective-permute-start.2 = (bf16[32,2,44,128]{3,0,2,1:T(8,128)(2,1)S(1)}, bf16[32,2,44,128]{3,0,2,1:T(8,128)(2,1)}, u32[]{:S(2)}, u32[]{:S(2)}) collective-permute-start(bf16[32,2,44,128]{3,0,2,1:T(8,128)(2,1)S(1)} %copy.41), channel_id=1, source_target_pairs={{0,160},{32,192},{64,224},{96,0},{128,32},{160,64},{192,96},{224,1... | collective-permute-start | bytes 2162696 | tf_op jit(solution)/shard_map/ppermute | solution.py:22
  69.8 64.2 %collective-permute-start.1 = (bf16[32,2,44,128]{3,0,2,1:T(8,128)(2,1)S(1)}, bf16[32,2,44,128]{3,0,2,1:T(8,128)(2,1)}, u32[]{:S(2)}, u32[]{:S(2)}) collective-permute-start(bf16[32,2,44,128]{3,0,2,1:T(8,128)(2,1)S(1)} %copy.41), channel_id=1, source_target_pairs={{0,192},{32,224},{64,0},{96,32},{128,64},{160,96},{192,128},{224,1... | collective-permute-start | bytes 2162696 | tf_op jit(solution)/shard_map/ppermute | solution.py:22
  73.5 75.9 %collective-permute-start = (bf16[32,2,44,128]{3,0,2,1:T(8,128)(2,1)S(1)}, bf16[32,2,44,128]{3,0,2,1:T(8,128)(2,1)}, u32[]{:S(2)}, u32[]{:S(2)}) collective-permute-start(bf16[32,2,44,128]{3,0,2,1:T(8,128)(2,1)S(1)} %copy.41), channel_id=1, source_target_pairs={{0,224},{32,0},{64,32},{96,64},{128,96},{160,128},{192,160},{224,1... | collective-permute-start | bytes 2162696 | tf_op jit(solution)/shard_map/ppermute | solution.py:22
  100.0 66.7 %collective-permute-start.6 = (bf16[32,2,44,128]{3,0,2,1:T(8,128)(2,1)S(1)}, bf16[32,2,44,128]{3,0,2,1:T(8,128)(2,1)}, u32[]{:S(2)}, u32[]{:S(2)}) collective-permute-start(bf16[32,2,44,128]{3,0,2,1:T(8,128)(2,1)S(1)} %copy.41), channel_id=1, source_target_pairs={{128,0},{160,32},{192,64},{224,96},{129,1},{161,33},{193,65},{225,... | collective-permute-start | bytes 2162696 | tf_op jit(solution)/shard_map/ppermute | solution.py:142
  103.1 63.5 %collective-permute-start.7 = (bf16[32,2,44,128]{3,0,2,1:T(8,128)(2,1)S(1)}, bf16[32,2,44,128]{3,0,2,1:T(8,128)(2,1)}, u32[]{:S(2)}, u32[]{:S(2)}) collective-permute-start(bf16[32,2,44,128]{3,0,2,1:T(8,128)(2,1)S(1)} %copy.52), channel_id=1, source_target_pairs={{0,128},{32,160},{64,192},{96,224},{1,129},{33,161},{65,193},{97,2... | collective-permute-start | bytes 2162696 | tf_op jit(solution)/shard_map/ppermute | solution.py:142
  120.7 8.0 %copy-start = (f32[1,128,256]{2,1,0:T(8,128)S(1)}, f32[1,128,256]{2,1,0:T(8,128)}, u32[]{:S(2)}) copy-start(f32[1,128,256]{2,1,0:T(8,128)} %shard_map.46) | copy-start | bytes 393220
  155.1 8.1 %copy-start.1 = (f32[1,128,256]{2,1,0:T(8,128)S(1)}, f32[1,128,256]{2,1,0:T(8,128)}, u32[]{:S(2)}) copy-start(f32[1,128,256]{2,1,0:T(8,128)} %shard_map.43) | copy-start | bytes 393220
